TPU v7x, 32 devices: a whole 2x2x4 slice. The times are simulated.
32 devices in a mesh: dp: 16 (over z, y, core), tensor: 2 (over x).
Axes of the slice: x: 2, y: 2, z: 4, core: 2. Of those that a mesh axis runs over, the one named last changes fastest.
Arguments:
- source_embed: bfloat16 [16, 1024, 768], P('dp', 'tensor'), may hold values from -6 to 6
- target_embed: bfloat16 [16, 512, 768], P('dp', 'tensor'), may hold values from -6 to 6
- out_cotangent: bfloat16 [16, 512, 768], P('dp', 'tensor'), may hold values from -6 to 6
- row_flags: int32 [16, 1024], P('dp', 'tensor'), may hold values from 0 to 2, as said below
- source_mask: int32 [16, 1024], P('dp'), may hold values from 0 to 1, as said below
- target_mask: int32 [16, 512], P('dp'), may hold values from 0 to 1, as said below
- attention_weights: float32 [12, 768, 768], P(None, 'dp', 'tensor'), may hold values from -6 to 6
- feed_weights: float32 [4, 768, 3072], P(None, 'dp', 'tensor'), may hold values from -6 to 6
- rows_attention: float32 [12, 768], P(None, 'dp'), may hold values from 2457.6 to 2457600
- columns_attention: float32 [12, 768], P(None, 'tensor'), may hold values from 2457.6 to 2457600
- rows_feed: float32 [4, 768], P(None, 'dp'), may hold values from 7.3728 to 7372.8
- columns_feed: float32 [4, 3072], P(None, 'tensor'), may hold values from 7.3728 to 7372.8
- vector_params: float32 [14, 768], replicated, may hold values from -6 to 6
- vector_moments: float32 [14, 768], P(None, 'dp'), may hold values from 4915.2 to 4915200
Outputs:
- decoder_out: bfloat16 [16, 512, 768], P('dp', 'tensor')
- source_gradient: float32 [16, 1024, 768], P('dp', 'tensor')
- target_gradient: float32 [16, 512, 768], P('dp', 'tensor')
- attention_gradients: float32 [12, 768, 768], P(None, 'dp', 'tensor')
- feed_gradients: float32 [4, 768, 3072], P(None, 'dp', 'tensor')
- vector_gradients: float32 [14, 768], P(None, 'dp')
- attention_updated: float32 [12, 768, 768], P(None, 'dp', 'tensor')
- feed_updated: float32 [4, 768, 3072], P(None, 'dp', 'tensor')
- vector_updated: float32 [14, 768], P(None, 'dp')
- rows_attention_next: float32 [12, 768], P(None, 'dp')
- columns_attention_next: float32 [12, 768], P(None, 'tensor')
- rows_feed_next: float32 [4, 768], P(None, 'dp')
- columns_feed_next: float32 [4, 3072], P(None, 'tensor')
- vector_moments_next: float32 [14, 768], P(None, 'dp')
- final_norm_gradients: float32 [2, 768], P(None, 'dp')
Inputs may be any that keep to these rules, and one draw needn't show every extreme that they name: `row_flags`: 0 keeps a source row, 1 marks a gap-sentence row and 2 a masked-token row. `source_mask`: each row is ones followed by zeros with 512 or more ones; the first row is all ones. `target_mask`: each row is ones followed by zeros with 256 or more ones; the first row is all ones.
All inputs are finite; a program needn't handle non-finite values.
Results may differ from a plain program's by a relative error of at most 0.019.
Values may be sent and summed in bfloat16 or wider, within the bound.
A program may use at most 256 MiB of HBM per device.

v0:
```python
import jax
import jax.numpy as jnp
from jax import lax
from jax.sharding import PartitionSpec as P

D = 768
HEAD_DIM = 64
FF = 3072


norm_epsilon = 1e-05
decay_rate = 1.0 - 2.0 ** (-0.8)
step_rate = 0.2
masked_score = -1e30


def gelu_exact(values):
    return jax.nn.gelu(values, approximate=False)


def layer_norm(values, norm_gain, norm_shift):
    centre = jnp.mean(values, axis=-1, keepdims=True)
    centred = values - centre
    spread = jnp.mean(centred * centred, axis=-1, keepdims=True)
    return centred * lax.rsqrt(spread + norm_epsilon) * norm_gain + norm_shift


def gather_rows(local_rows):
    return lax.all_gather(local_rows, "tensor", axis=0, tiled=True)


def branch_total(partial_rows):
    return lax.psum_scatter(
        partial_rows.astype(jnp.bfloat16), "tensor", scatter_dimension=0, tiled=True
    ).astype(jnp.float32)


def gather_gradient(local_rows):
    return lax.all_gather(local_rows, "tensor", axis=0, tiled=True)


def input_total(partial_rows):
    return lax.psum_scatter(
        partial_rows.astype(jnp.bfloat16), "tensor", scatter_dimension=0, tiled=True
    ).astype(jnp.float32)


def project(left_side, right_side):
    return jnp.dot(left_side, right_side, preferred_element_type=jnp.float32)


def project_back(left_side, right_side):
    return jnp.einsum("tx,dx->td", left_side, right_side, preferred_element_type=jnp.float32)


def weight_product(left_side, right_side):
    return jnp.einsum("td,tx->dx", left_side, right_side, preferred_element_type=jnp.float32)


def split_heads(matrix):
    return matrix.reshape(matrix.shape[0], matrix.shape[1] // HEAD_DIM, HEAD_DIM)


def block_scores(query_block, key_heads, first_row, key_valid, causal):
    scores = jnp.einsum(
        "qhd,khd->hqk", query_block, key_heads, preferred_element_type=jnp.float32
    ) * HEAD_DIM ** (-0.5)
    allowed = jnp.broadcast_to(key_valid[None, :], (query_block.shape[0], key_valid.shape[0]))
    if causal:
        query_place = first_row + lax.broadcasted_iota(jnp.int32, allowed.shape, 0)
        key_place = lax.broadcasted_iota(jnp.int32, allowed.shape, 1)
        allowed = allowed & (key_place <= query_place)
    return jnp.where(allowed[None], scores, masked_score)


def attend_forward(query_rows, key_rows, value_rows, key_valid, causal):
    query_heads = split_heads(query_rows)
    key_heads = split_heads(key_rows)
    value_heads = split_heads(value_rows)
    block_rows = min(512, query_rows.shape[0])
    outputs = []
    totals = []
    for first_row in range(0, query_rows.shape[0], block_rows):
        scores = block_scores(
            query_heads[first_row : first_row + block_rows], key_heads, first_row, key_valid, causal
        )
        row_peak = jnp.max(scores, axis=-1, keepdims=True)
        weights = jnp.exp(scores - row_peak)
        row_total = jnp.sum(weights, axis=-1, keepdims=True)
        weights_low = (weights / row_total).astype(jnp.bfloat16)
        attended = jnp.einsum(
            "hqk,khd->qhd", weights_low, value_heads, preferred_element_type=jnp.float32
        )
        outputs.append(attended.astype(jnp.bfloat16))
        totals.append(row_peak[:, :, 0] + jnp.log(row_total[:, :, 0]))
    attended = jnp.concatenate(outputs, axis=0)
    return (attended.reshape(query_rows.shape), jnp.concatenate(totals, axis=1))


def attend_backward(grad_attended, query_rows, key_rows, value_rows, log_totals, key_valid, causal):
    query_heads = split_heads(query_rows)
    key_heads = split_heads(key_rows)
    value_heads = split_heads(value_rows)
    grad_heads = split_heads(grad_attended)
    block_rows = min(512, query_rows.shape[0])
    grad_queries = []
    grad_keys = jnp.zeros(key_heads.shape, jnp.float32)
    grad_values = jnp.zeros(value_heads.shape, jnp.float32)
    for first_row in range(0, query_rows.shape[0], block_rows):
        last_row = first_row + block_rows
        query_block = query_heads[first_row:last_row]
        grad_block = grad_heads[first_row:last_row]
        scores = block_scores(query_block, key_heads, first_row, key_valid, causal)
        weights = jnp.exp(scores - log_totals[:, first_row:last_row, None])
        grad_weights = jnp.einsum(
            "qhd,khd->hqk", grad_block, value_heads, preferred_element_type=jnp.float32
        )
        row_dot = jnp.sum(weights * grad_weights, axis=-1, keepdims=True)
        grad_scores = (weights * (grad_weights - row_dot)).astype(jnp.bfloat16)
        grad_queries.append(
            jnp.einsum("hqk,khd->qhd", grad_scores, key_heads, preferred_element_type=jnp.float32)
            * HEAD_DIM ** (-0.5)
        )
        grad_keys = grad_keys + jnp.einsum(
            "hqk,qhd->khd", grad_scores, query_block, preferred_element_type=jnp.float32
        ) * HEAD_DIM ** (-0.5)
        grad_values = grad_values + jnp.einsum(
            "hqk,qhd->khd",
            weights.astype(jnp.bfloat16),
            grad_block,
            preferred_element_type=jnp.float32,
        )
    grad_query = (
        jnp.concatenate(grad_queries, axis=0).reshape(query_rows.shape).astype(jnp.bfloat16)
    )
    return (
        grad_query,
        grad_keys.reshape(key_rows.shape).astype(jnp.bfloat16),
        grad_values.reshape(value_rows.shape).astype(jnp.bfloat16),
    )


def attention_forward(residual, vectors, norm_row, memory_rows, matrices, key_valid, causal):
    normed = gather_rows(
        layer_norm(residual, vectors[norm_row], vectors[norm_row + 1]).astype(jnp.bfloat16)
    )
    source_rows = normed if memory_rows is None else memory_rows
    query_rows = project(normed, matrices[0]).astype(jnp.bfloat16)
    key_rows = project(source_rows, matrices[1]).astype(jnp.bfloat16)
    value_rows = project(source_rows, matrices[2]).astype(jnp.bfloat16)
    attended, log_totals = attend_forward(query_rows, key_rows, value_rows, key_valid, causal)
    branch = branch_total(project_back(attended, matrices[3]))
    stored = {
        "normed": normed,
        "source": source_rows,
        "query": query_rows,
        "key": key_rows,
        "value": value_rows,
        "attended": attended,
        "totals": log_totals,
    }
    return (residual + branch, stored)


def feed_forward(residual, vectors, norm_row, matrices):
    normed = gather_rows(
        layer_norm(residual, vectors[norm_row], vectors[norm_row + 1]).astype(jnp.bfloat16)
    )
    before = project(normed, matrices[0])
    hidden = gelu_exact(before).astype(jnp.bfloat16)
    branch = branch_total(project_back(hidden, matrices[1]))
    return (residual + branch, {"normed": normed, "hidden": hidden, "before": before})


def accumulate(parts_list, first_index, new_terms):
    for offset, new_term in enumerate(new_terms):
        position = first_index + offset
        parts_list[position] = new_term


def norm_backward(residual, vectors, norm_row, grad_normed):
    unused_out, norm_back = jax.vjp(layer_norm, residual, vectors[norm_row], vectors[norm_row + 1])
    return norm_back(grad_normed)


def attention_backward(grad_residual, stored, matrices, key_valid, causal):
    grad_full = gather_gradient(grad_residual.astype(jnp.bfloat16))
    grad_output = weight_product(grad_full, stored["attended"])
    grad_attended = project(grad_full, matrices[3]).astype(jnp.bfloat16)
    grad_query, grad_key, grad_value = attend_backward(
        grad_attended,
        stored["query"],
        stored["key"],
        stored["value"],
        stored["totals"],
        key_valid,
        causal,
    )
    weight_terms = [
        weight_product(stored["normed"], grad_query),
        weight_product(stored["source"], grad_key),
        weight_product(stored["source"], grad_value),
        grad_output,
    ]
    from_query = project_back(grad_query, matrices[0])
    from_source = project_back(grad_key, matrices[1]) + project_back(grad_value, matrices[2])
    return (weight_terms, from_query, from_source)


def self_backward(
    grad_residual,
    residual,
    vectors,
    norm_row,
    stored,
    matrices,
    key_valid,
    causal,
    attention_parts,
    first_index,
    vector_parts,
):
    weight_terms, from_query, from_source = attention_backward(
        grad_residual, stored, matrices, key_valid, causal
    )
    accumulate(attention_parts, first_index, weight_terms)
    grad_input, grad_gain, grad_shift = norm_backward(
        residual, vectors, norm_row, input_total(from_query + from_source)
    )
    accumulate(vector_parts, norm_row, [grad_gain, grad_shift])
    return grad_residual + grad_input


def feed_backward(
    grad_residual,
    residual,
    vectors,
    norm_row,
    stored,
    matrices,
    feed_parts,
    first_index,
    vector_parts,
):
    grad_full = gather_gradient(grad_residual.astype(jnp.bfloat16))
    grad_second = weight_product(grad_full, stored["hidden"])
    grad_hidden = project(grad_full, matrices[1])
    unused_value, gelu_back = jax.vjp(gelu_exact, stored["before"])
    grad_hidden = gelu_back(grad_hidden)[0].astype(jnp.bfloat16)
    grad_first = weight_product(stored["normed"], grad_hidden)
    accumulate(feed_parts, first_index, [grad_first, grad_second])
    grad_input, grad_gain, grad_shift = norm_backward(
        residual, vectors, norm_row, input_total(project_back(grad_hidden, matrices[0]))
    )
    accumulate(vector_parts, norm_row, [grad_gain, grad_shift])
    return grad_residual + grad_input


def factored_step(weights, grads, rows_next, columns_next, row_level, mean_square):
    estimate = rows_next[:, :, None] * columns_next[:, None, :] / row_level[:, None, None]
    return weights - step_rate * jnp.sqrt(mean_square)[:, None, None] * grads * lax.rsqrt(estimate)


def on_device(
    source_embed,
    target_embed,
    out_cotangent,
    row_flags,
    source_mask,
    target_mask,
    attention_weights,
    feed_weights,
    rows_attention,
    columns_attention,
    rows_feed,
    columns_feed,
    vector_params,
    vector_moments,
):
    attention_low, feed_low = (
        lax.all_gather(attention_weights.astype(jnp.bfloat16), "dp", axis=1, tiled=True),
        lax.all_gather(feed_weights.astype(jnp.bfloat16), "dp", axis=1, tiled=True),
    )
    half_target = target_embed.shape[1]
    target_offset = lax.axis_index("tensor") * half_target
    pair_index = 0
    row_kinds = row_flags[pair_index]
    start_rows = jnp.where(
        (row_kinds == 1)[:, None],
        vector_params[12][None, :],
        jnp.where(
            (row_kinds == 2)[:, None],
            vector_params[13][None, :],
            source_embed[pair_index].astype(jnp.float32),
        ),
    )
    source_valid = source_mask[pair_index] > 0
    target_valid = target_mask[pair_index] > 0
    encoder_mid, kept_first = attention_forward(
        start_rows, vector_params, 0, None, attention_low[0:4], source_valid, False
    )
    encoder_final, kept_second = feed_forward(encoder_mid, vector_params, 2, feed_low[0:2])
    memory_rows = gather_rows(
        layer_norm(encoder_final, vector_params[4], vector_params[5]).astype(jnp.bfloat16)
    )
    target_rows = target_embed[pair_index].astype(jnp.float32)
    decoder_one, kept_third = attention_forward(
        target_rows, vector_params, 6, None, attention_low[4:8], target_valid, True
    )
    decoder_two, kept_fourth = attention_forward(
        decoder_one, vector_params, 8, memory_rows, attention_low[8:12], source_valid, False
    )
    decoder_three, kept_fifth = feed_forward(decoder_two, vector_params, 10, feed_low[2:4])
    decoder_rows = [decoder_three.astype(jnp.bfloat16)]
    records = [
        {
            "start": start_rows,
            "source_valid": source_valid,
            "target_valid": target_valid,
            "encoder_mid": encoder_mid,
            "encoder_final": encoder_final,
            "target": target_rows,
            "decoder_one": decoder_one,
            "decoder_two": decoder_two,
            "kept_first": kept_first,
            "kept_second": kept_second,
            "kept_third": kept_third,
            "kept_fourth": kept_fourth,
            "kept_fifth": kept_fifth,
        }
    ]
    attention_parts = [None] * 12
    feed_parts = [None] * 4
    vector_parts = [None] * 14
    pair_index = 0
    record = records[pair_index]
    row_keep = lax.dynamic_slice_in_dim(target_mask[pair_index], target_offset, half_target) > 0
    grad_three = jnp.where(row_keep[:, None], out_cotangent[pair_index].astype(jnp.float32), 0.0)
    grad_two = feed_backward(
        grad_three,
        record["decoder_two"],
        vector_params,
        10,
        record["kept_fifth"],
        feed_low[2:4],
        feed_parts,
        2,
        vector_parts,
    )
    weight_terms, from_query, from_source = attention_backward(
        grad_two, record["kept_fourth"], attention_low[8:12], record["source_valid"], False
    )
    accumulate(attention_parts, 8, weight_terms)
    query_local = lax.psum_scatter(
        from_query.astype(jnp.bfloat16), "tensor", scatter_dimension=0, tiled=True
    ).astype(jnp.float32)
    memory_local = lax.psum_scatter(
        from_source.astype(jnp.bfloat16), "tensor", scatter_dimension=0, tiled=True
    ).astype(jnp.float32)
    grad_input, grad_gain, grad_shift = norm_backward(
        record["decoder_one"], vector_params, 8, query_local
    )
    accumulate(vector_parts, 8, [grad_gain, grad_shift])
    grad_one = grad_two + grad_input
    grad_encoder, grad_gain, grad_shift = norm_backward(
        record["encoder_final"], vector_params, 4, memory_local
    )
    accumulate(vector_parts, 4, [grad_gain, grad_shift])
    encoder_grads = [grad_encoder]
    target_grads = [
        self_backward(
            grad_one,
            record["target"],
            vector_params,
            6,
            record["kept_third"],
            attention_low[4:8],
            record["target_valid"],
            True,
            attention_parts,
            4,
            vector_parts,
        )
    ]
    pair_index = 0
    record = records[pair_index]
    grad_mid = feed_backward(
        encoder_grads[pair_index],
        record["encoder_mid"],
        vector_params,
        2,
        record["kept_second"],
        feed_low[0:2],
        feed_parts,
        0,
        vector_parts,
    )
    grad_start = self_backward(
        grad_mid,
        record["start"],
        vector_params,
        0,
        record["kept_first"],
        attention_low[0:4],
        record["source_valid"],
        False,
        attention_parts,
        0,
        vector_parts,
    )
    row_kinds = row_flags[pair_index]
    source_grads = [jnp.where((row_kinds == 0)[:, None], grad_start, 0.0)]
    accumulate(
        vector_parts,
        12,
        [
            jnp.sum(jnp.where((row_kinds == 1)[:, None], grad_start, 0.0), axis=0),
            jnp.sum(jnp.where((row_kinds == 2)[:, None], grad_start, 0.0), axis=0),
        ],
    )
    attention_grad, feed_grad, vector_grad = (
        lax.psum_scatter(jnp.stack(attention_parts), "dp", scatter_dimension=1, tiled=True),
        lax.psum_scatter(jnp.stack(feed_parts), "dp", scatter_dimension=1, tiled=True),
        lax.psum_scatter(jnp.stack(vector_parts), "dp", scatter_dimension=1, tiled=True),
    )
    attention_square = attention_grad * attention_grad
    feed_square = feed_grad * feed_grad
    attention_rowsum, feed_rowsum, vector_grad, attention_weightrows, feed_weightrows = lax.psum(
        (
            jnp.sum(attention_square, axis=2),
            jnp.sum(feed_square, axis=2),
            vector_grad,
            jnp.sum(attention_weights * attention_weights, axis=2),
            jnp.sum(feed_weights * feed_weights, axis=2),
        ),
        "tensor",
    )
    rows_attention_next = decay_rate * rows_attention + (1.0 - decay_rate) * attention_rowsum / D
    rows_feed_next = decay_rate * rows_feed + (1.0 - decay_rate) * feed_rowsum / FF
    column_attention, column_feed, total_attention, total_feed, scale_attention, scale_feed = (
        lax.psum(
            (
                jnp.sum(attention_square, axis=1),
                jnp.sum(feed_square, axis=1),
                jnp.sum(rows_attention_next, axis=1),
                jnp.sum(rows_feed_next, axis=1),
                jnp.sum(attention_weightrows, axis=1),
                jnp.sum(feed_weightrows, axis=1),
            ),
            "dp",
        )
    )
    columns_attention_next = (
        decay_rate * columns_attention + (1.0 - decay_rate) * column_attention / D
    )
    columns_feed_next = decay_rate * columns_feed + (1.0 - decay_rate) * column_feed / D
    attention_updated = factored_step(
        attention_weights,
        attention_grad,
        rows_attention_next,
        columns_attention_next,
        total_attention / D,
        scale_attention / (D * D),
    )
    feed_updated = factored_step(
        feed_weights,
        feed_grad,
        rows_feed_next,
        columns_feed_next,
        total_feed / D,
        scale_feed / (D * FF),
    )
    local_width = vector_moments.shape[1]
    vector_local = lax.dynamic_slice_in_dim(
        vector_params, lax.axis_index("dp") * local_width, local_width, 1
    )
    vector_moments_next = (
        decay_rate * vector_moments + (1.0 - decay_rate) * vector_grad * vector_grad
    )
    vector_scale = jnp.sqrt(jnp.mean(vector_params * vector_params, axis=1))
    vector_updated = vector_local - step_rate * vector_scale[:, None] * vector_grad * lax.rsqrt(
        vector_moments_next
    )
    return (
        jnp.stack(decoder_rows),
        jnp.stack(source_grads),
        jnp.stack(target_grads),
        attention_grad,
        feed_grad,
        vector_grad,
        attention_updated,
        feed_updated,
        vector_updated,
        rows_attention_next,
        columns_attention_next,
        rows_feed_next,
        columns_feed_next,
        vector_moments_next,
        vector_grad[10:12],
    )


def solution(mesh):
    placed = (
        P("dp", "tensor", None),
        P("dp", "tensor", None),
        P("dp", "tensor", None),
        P("dp", "tensor"),
        P("dp", None),
        P("dp", None),
        P(None, "dp", "tensor"),
        P(None, "dp", "tensor"),
        P(None, "dp"),
        P(None, "tensor"),
        P(None, "dp"),
        P(None, "tensor"),
        P(),
        P(None, "dp"),
    )
    return jax.shard_map(
        on_device,
        mesh=mesh,
        in_specs=placed,
        out_specs=(
            P("dp", "tensor", None),
            P("dp", "tensor", None),
            P("dp", "tensor", None),
            P(None, "dp", "tensor"),
            P(None, "dp", "tensor"),
            P(None, "dp"),
            P(None, "dp", "tensor"),
            P(None, "dp", "tensor"),
            P(None, "dp"),
            P(None, "dp"),
            P(None, "tensor"),
            P(None, "dp"),
            P(None, "tensor"),
            P(None, "dp"),
            P(None, "dp"),
        ),
        check_vma=False,
    )
```

profile of v0, /device:TPU:0, one launch (start us, length us, event | category | flops | bytes accessed | tf_op | source)
XLA Modules:
  0.0 1323.4 jit_solution(13901343917661911310)
XLA Ops:
  18.7 28.4 %all-gather.10.cloned.1.call-done = bf16[1024,768]{1,0:T(8,128)(2,1)} async-done(((bf16[512,768]{1,0:T(8,128)(2,1)}), bf16[1024,768]{1,0:T(8,128)(2,1)}) %all-gather.10.cloned.1.call-update) | async-done | bytes 1572880 | tf_op jit(solution)/shard_map/all_gather | solution.py:29
  47.1 69.4 %all-gather.8.cloned.1.call-done = bf16[12,768,384]{2,1,0:T(8,128)(2,1)} async-done(((bf16[12,48,384]{2,1,0:T(8,128)(2,1)}), bf16[12,768,384]{2,1,0:T(8,128)(2,1)}) %all-gather.8.cloned.1.call-update) | async-done | bytes 7077904 | tf_op jit(solution)/shard_map/all_gather | solution.py:281
  149.5 22.9 %reduce-scatter.19.cloned.1.call-done = bf16[512,768]{1,0:T(8,128)(2,1)} async-done(((bf16[1024,768]{1,0:T(8,128)(2,1)}), bf16[512,768]{1,0:T(8,128)(2,1)}) %reduce-scatter.19.cloned.1.call-update) | async-done | bytes 786448 | tf_op jit(solution)/shard_map/reduce_scatter | solution.py:33
  179.6 77.3 %all-gather.14.cloned.1.call-done = bf16[4,768,1536]{2,1,0:T(8,128)(2,1)} async-done(((bf16[4,48,1536]{2,1,0:T(8,128)(2,1)}), bf16[4,768,1536]{2,1,0:T(8,128)(2,1)}) %all-gather.14.cloned.1.call-update) | async-done | bytes 9437200 | tf_op jit(solution)/shard_map/all_gather | solution.py:282
  256.9 27.4 %all-gather.12.cloned.1.call-done = bf16[1024,768]{1,0:T(8,128)(2,1)} async-done(((bf16[512,768]{1,0:T(8,128)(2,1)}), bf16[1024,768]{1,0:T(8,128)(2,1)}) %all-gather.12.cloned.1.call-update) | async-done | bytes 1572880 | tf_op jit(solution)/shard_map/all_gather | solution.py:29
  284.3 19.5 %multiply_convert_fusion.4 = (bf16[1024,1536]{1,0:T(8,128)(2,1)S(1)}, f32[1024,1536]{1,0:T(8,128)}, f32[1024,1536]{1,0:T(8,128)}) fusion(bf16[1024,768]{1,0:T(8,128)(2,1)} %all-gather.12.cloned.1.call-done, bf16[4,768,1536]{2,1,0:T(8,128)(2,1)} %all-gather.14.cloned.1.call-done), kind=kOutput, calls=%fused_computation.37 | convolution fusion | flops 2518155264 | bytes 19660800 | tf_op jit(solution)/shard_map/dot_general | solution.py:49
  311.0 16.5 %all_gather.39 = bf16[512,768]{1,0:T(8,128)(2,1)S(1)} all-gather(bf16[256,768]{1,0:T(8,128)(2,1)S(1)} %fusion.120), channel_id=1, replica_groups=mesh['dp'=16,'tensor'=2] {'tensor'}, dimensions={0}, use_global_device_ids=true | all-gather | bytes 1179648 | tf_op jit(solution)/shard_map/all_gather | solution.py:29
  346.1 15.0 %reduce-scatter.17.cloned.1.call-done = bf16[256,768]{1,0:T(8,128)(2,1)} async-done(((bf16[512,768]{1,0:T(8,128)(2,1)}), bf16[256,768]{1,0:T(8,128)(2,1)}) %reduce-scatter.17.cloned.1.call-update) | async-done | bytes 393232 | tf_op jit(solution)/shard_map/reduce_scatter | solution.py:33
  365.3 16.9 %all_gather.45 = bf16[512,768]{1,0:T(8,128)(2,1)S(1)} all-gather(bf16[256,768]{1,0:T(8,128)(2,1)S(1)} %add_convert_fusion.11), channel_id=1, replica_groups=mesh['dp'=16,'tensor'=2] {'tensor'}, dimensions={0}, use_global_device_ids=true | all-gather | bytes 1179648 | tf_op jit(solution)/shard_map/all_gather | solution.py:29
  385.4 9.0 all-gather.16.cloned.1.call-done
  414.9 18.8 %all_gather.47 = bf16[512,768]{1,0:T(8,128)(2,1)} all-gather(bf16[256,768]{1,0:T(8,128)(2,1)S(1)} %fusion.133), channel_id=1, replica_groups=mesh['dp'=16,'tensor'=2] {'tensor'}, dimensions={0}, use_global_device_ids=true | all-gather | bytes 1179648 | tf_op jit(solution)/shard_map/all_gather | solution.py:39
  439.4 11.9 all_gather.46
  451.3 10.2 multiply_convert_fusion.5
  473.0 11.7 reduce-scatter.27.cloned.1.call-done
  488.1 17.0 %reduce-scatter.25.cloned.1.call-done = bf16[256,768]{1,0:T(8,128)(2,1)} async-done(((bf16[512,768]{1,0:T(8,128)(2,1)}), bf16[256,768]{1,0:T(8,128)(2,1)}) %reduce-scatter.25.cloned.1.call-update) | async-done | bytes 393232 | tf_op jit(solution)/shard_map/reduce_scatter | solution.py:33
  509.7 12.1 all_gather.48
  524.3 10.3 multiply_reduce_fusion.2
  563.5 16.3 %reduce-scatter.29.cloned.1.call-done = bf16[512,768]{1,0:T(8,128)(2,1)} async-done(((bf16[1024,768]{1,0:T(8,128)(2,1)}), bf16[512,768]{1,0:T(8,128)(2,1)}) %reduce-scatter.29.cloned.1.call-update) | async-done | bytes 786448 | tf_op jit(solution)/shard_map/reduce_scatter | solution.py:357
  587.2 13.0 reduce-scatter.35.cloned.1.call-done
  607.2 19.1 %all_gather.51 = bf16[512,768]{1,0:T(8,128)(2,1)S(1)} all-gather(bf16[256,768]{1,0:T(8,128)(2,1)S(1)} %get-tuple-element.83), channel_id=1, replica_groups=mesh['dp'=16,'tensor'=2] {'tensor'}, dimensions={0}, use_global_device_ids=true | all-gather | bytes 1179648 | tf_op jit(solution)/shard_map/all_gather | solution.py:39
  628.2 7.6 all-gather.18.cloned.1.call-done
  635.8 9.7 add_convert_fusion
  669.3 9.6 reduce-scatter.31.cloned.1.call-done
  692.0 7.2 reduce-scatter.37.cloned.1.call-done
  707.1 21.3 %all-gather.20.cloned.1.call-done = bf16[1024,768]{1,0:T(8,128)(2,1)} async-done(((bf16[512,768]{1,0:T(8,128)(2,1)}), bf16[1024,768]{1,0:T(8,128)(2,1)}) %all-gather.20.cloned.1.call-update) | async-done | bytes 1572880 | tf_op jit(solution)/shard_map/all_gather | solution.py:39
  738.0 21.0 %multiply_reduce_fusion.1 = (f32[6,512]{1,0:T(8,128)}, f32[6,512]{1,0:T(8,128)}, f32[6,512,1024]{2,1,0:T(8,128)}) fusion(f32[6,512]{1,0:T(8,128)} %get-tuple-element.123, f32[6,512,1024]{2,1,0:T(8,128)} %copy-done.1, pred[1024]{0:T(1024)(128)(4,1)S(1)} %copy-done.120, f32[6,512,1024]{2,1,0:T(8,128)} %fusion.181, f32[6,512]{1,0:T(8,128)} %get-tuple-element.122, ...), kind=kOutput, calls=%fused_computation.5 | convolution fusion | flops 434104320 | bytes 51561472 | tf_op jit(solution)/shard_map/qhd,khd->hqk/dot_general | solution.py:115
  759.0 17.4 %multiply_convert_fusion.1 = (bf16[6,512,1024]{2,1,0:T(8,128)(2,1)S(1)}, bf16[6,512,1024]{2,1,0:T(8,128)(2,1)S(1)}) fusion(f32[6,512,1024]{2,1,0:T(8,128)} %get-tuple-element.119, f32[6,512]{1,0:T(8,128)} %get-tuple-element.59, f32[6,512]{1,0:T(8,128)} %get-tuple-element.123, f32[6,512,1024]{2,1,0:T(8,128)} %copy-done.1, pred[1024]{0:T(1024)(128)(4,1)S(1)} %copy-done.120, ...), kind=kLoop, calls=%fused_computation.4 | loop fusion | flops 37748736 | bytes 62964736 | tf_op jit(solution)/shard_map/convert_element_type | solution.py:119
  863.3 30.6 %reduce-scatter.43.cloned.1.call-done = f32[48,14]{1,0:T(8,128)} async-done(((f32[768,14]{1,0:T(8,128)}), f32[48,14]{1,0:T(8,128)}) %reduce-scatter.43.cloned.1.call-update) | async-done | bytes 2704
  894.7 148.4 %reduce-scatter.39.cloned.1.call-done = f32[12,48,384]{2,1,0:T(8,128)} async-done(((f32[12,768,384]{2,1,0:T(8,128)}), f32[12,48,384]{2,1,0:T(8,128)}) %reduce-scatter.39.cloned.1.call-update) | async-done | bytes 884752 | tf_op jit(solution)/shard_map/reduce_scatter | solution.py:422
  1044.5 197.2 %reduce-scatter.41.cloned.1.call-done = f32[4,48,1536]{2,1,0:T(8,128)} async-done(((f32[4,768,1536]{2,1,0:T(8,128)}), f32[4,48,1536]{2,1,0:T(8,128)}) %reduce-scatter.41.cloned.1.call-update) | async-done | bytes 1179664 | tf_op jit(solution)/shard_map/reduce_scatter | solution.py:423
  1243.3 8.3 all-reduce.1
  1252.2 57.8 %all-reduce = (f32[12]{0:T(128)S(1)}, f32[12,384]{1,0:T(8,128)S(1)}, f32[12]{0:T(128)S(1)}, f32[4]{0:T(128)S(1)}, f32[4,1536]{1,0:T(4,128)S(1)}, /*index=5*/f32[4]{0:T(128)S(1)}) all-reduce(f32[12]{0:T(128)S(1)} %get-tuple-element.80, f32[12,384]{1,0:T(8,128)S(1)} %get-tuple-element.29, ...), channel_id=1, replica_groups=mesh['dp'=16,'tensor'=2] {'dp'}, use_global_device_ids=true, to_apply=%region_74.75 | all-reduce | flops 10784 | bytes 86272 | tf_op jit(solution)/shard_map/psum | solution.py:441
  (636 shorter events, 327.2 us)
Async XLA Ops:
  7.2 39.9 %all-gather.10.cloned.1.call-start = ((), (), s32[]{:S(2)}) async-start(), calls=%async_computation.16 | async-start | bytes 2359296 | tf_op jit(solution)/shard_map/all_gather | solution.py:29
  9.2 170.2 %copy-start.101 = (f32[768]{0:T(1024)}, f32[768]{0:T(1024)S(1)}, u32[]{:S(2)}) copy-start(f32[768]{0:T(1024)S(1)} %get-tuple-element.55) | copy-start | bytes 9220
  17.0 99.5 %all-gather.8.cloned.1.call-start = ((), (), s32[]{:S(2)}) async-start(), calls=%async_computation.14 | async-start | bytes 7520256 | tf_op jit(solution)/shard_map/all_gather | solution.py:281
  18.6 153.8 %reduce-scatter.19.cloned.1.call-start = ((), (), s32[]{:S(2)}) async-start(), calls=%async_computation.17 | async-start | bytes 2359296 | tf_op jit(solution)/shard_map/reduce_scatter | solution.py:33
  147.6 109.3 %all-gather.14.cloned.1.call-start = ((), (), s32[]{:S(2)}) async-start(), calls=%async_computation.19 | async-start | bytes 10027008 | tf_op jit(solution)/shard_map/all_gather | solution.py:282
  149.4 134.8 %all-gather.12.cloned.1.call-start = ((), (), s32[]{:S(2)}) async-start(), calls=%async_computation.18 | async-start | bytes 2359296 | tf_op jit(solution)/shard_map/all_gather | solution.py:29
  178.3 162.6 %reduce-scatter.21.cloned.1.call-start = ((), (), s32[]{:S(2)}) async-start(), calls=%async_computation.20 | async-start | bytes 2359296 | tf_op jit(solution)/shard_map/reduce_scatter | solution.py:33
  178.5 125.2 %copy-start.133 = (f32[256]{0:T(256)}, f32[256]{0:T(256)S(1)}, u32[]{:S(2)}) copy-start(f32[256]{0:T(256)S(1)} %broadcast_multiply_fusion.5) | copy-start | bytes 3076
  178.8 125.0 %copy-start.155 = (f32[256]{0:T(256)}, f32[256]{0:T(256)S(1)}, u32[]{:S(2)}) copy-start(f32[256]{0:T(256)S(1)} %fusion.147) | copy-start | bytes 3076
  310.9 50.2 %reduce-scatter.17.cloned.1.call-start = ((), (), s32[]{:S(2)}) async-start(), calls=%async_computation.15 | async-start | bytes 1179648 | tf_op jit(solution)/shard_map/reduce_scatter | solution.py:33
  340.7 53.7 %all-gather.16.cloned.1.call-start = ((), (), s32[]{:S(2)}) async-start(), calls=%async_computation.21 | async-start | bytes 2359296 | tf_op jit(solution)/shard_map/all_gather | solution.py:29
  346.1 90.0 %reduce-scatter.23.cloned.1.call-start = ((), (), s32[]{:S(2)}) async-start(), calls=%async_computation.22 | async-start | bytes 1179648 | tf_op jit(solution)/shard_map/reduce_scatter | solution.py:33
  412.4 72.3 %reduce-scatter.27.cloned.1.call-start = ((), (), s32[]{:S(2)}) async-start(), calls=%async_computation.24 | async-start | bytes 1179648 | tf_op jit(solution)/shard_map/reduce_scatter | solution.py:43
  467.1 38.0 %reduce-scatter.25.cloned.1.call-start = ((), (), s32[]{:S(2)}) async-start(), calls=%async_computation.23 | async-start | bytes 1179648 | tf_op jit(solution)/shard_map/reduce_scatter | solution.py:33
  471.7 108.2 %reduce-scatter.29.cloned.1.call-start = ((), (), s32[]{:S(2)}) async-start(), calls=%async_computation.25 | async-start | bytes 2359296 | tf_op jit(solution)/shard_map/reduce_scatter | solution.py:357
  553.5 46.6 %reduce-scatter.35.cloned.1.call-start = ((), (), s32[]{:S(2)}) async-start(), calls=%async_computation.30 | async-start | bytes 1179648 | tf_op jit(solution)/shard_map/reduce_scatter | solution.py:354
  562.1 73.7 %all-gather.18.cloned.1.call-start = ((), (), s32[]{:S(2)}) async-start(), calls=%async_computation.26 | async-start | bytes 2359296 | tf_op jit(solution)/shard_map/all_gather | solution.py:39
  586.9 92.0 %reduce-scatter.31.cloned.1.call-start = ((), (), s32[]{:S(2)}) async-start(), calls=%async_computation.27 | async-start | bytes 2359296 | tf_op jit(solution)/shard_map/reduce_scatter | solution.py:43
  652.7 46.5 %reduce-scatter.37.cloned.1.call-start = ((), (), s32[]{:S(2)}) async-start(), calls=%async_computation.31 | async-start | bytes 1179648 | tf_op jit(solution)/shard_map/reduce_scatter | solution.py:43
  669.3 59.1 %all-gather.20.cloned.1.call-start = ((), (), s32[]{:S(2)}) async-start(), calls=%async_computation.28 | async-start | bytes 2359296 | tf_op jit(solution)/shard_map/all_gather | solution.py:39
  687.7 140.1 %reduce-scatter.33.cloned.1.call-start = ((), (), s32[]{:S(2)}) async-start(), calls=%async_computation.29 | async-start | bytes 2359296 | tf_op jit(solution)/shard_map/reduce_scatter | solution.py:43
  801.6 92.3 %reduce-scatter.43.cloned.1.call-start = ((), (), s32[]{:S(2)}) async-start(), calls=%async_computation.34 | async-start | bytes 417792
  838.2 205.0 %reduce-scatter.39.cloned.1.call-start = ((), (), s32[]{:S(2)}) async-start(), calls=%async_computation.32 | async-start | bytes 15040512 | tf_op jit(solution)/shard_map/reduce_scatter | solution.py:422
  840.9 400.8 %reduce-scatter.41.cloned.1.call-start = ((), (), s32[]{:S(2)}) async-start(), calls=%async_computation.33 | async-start | bytes 20054016 | tf_op jit(solution)/shard_map/reduce_scatter | solution.py:423
  861.9 381.4 %copy-start.141 = (f32[12,48]{1,0:T(8,128)S(1)}, f32[12,48]{1,0:T(8,128)}, u32[]{:S(2)}) copy-start(f32[12,48]{1,0:T(8,128)} %get-tuple-element.101) | copy-start | bytes 6916
  861.9 381.4 %copy-start.178 = (f32[4,48]{1,0:T(4,128)S(1)}, f32[4,48]{1,0:T(4,128)}, u32[]{:S(2)}) copy-start(f32[4,48]{1,0:T(4,128)} %get-tuple-element.99) | copy-start | bytes 2308
  861.9 390.0 %copy-start.176 = (f32[12,48]{1,0:T(8,128)S(1)}, f32[12,48]{1,0:T(8,128)}, u32[]{:S(2)}) copy-start(f32[12,48]{1,0:T(8,128)} %param.22) | copy-start | bytes 6916
  862.0 390.1 %copy-start.182 = (f32[4,48]{1,0:T(4,128)S(1)}, f32[4,48]{1,0:T(4,128)}, u32[]{:S(2)}) copy-start(f32[4,48]{1,0:T(4,128)} %param.24) | copy-start | bytes 2308
  862.0 448.6 %copy-start.147 = (f32[12,384]{1,0:T(8,128)S(1)}, f32[12,384]{1,0:T(8,128)}, u32[]{:S(2)}) copy-start(f32[12,384]{1,0:T(8,128)} %param.23) | copy-start | bytes 55300
  862.0 448.6 %copy-start.148 = (f32[4,1536]{1,0:T(4,128)S(1)}, f32[4,1536]{1,0:T(4,128)}, u32[]{:S(2)}) copy-start(f32[4,1536]{1,0:T(4,128)} %param.25) | copy-start | bytes 73732
  862.0 448.6 %copy-start.177 = (f32[14,48]{1,0:T(8,128)S(1)}, f32[14,48]{1,0:T(8,128)}, u32[]{:S(2)}) copy-start(f32[14,48]{1,0:T(8,128)} %param.27) | copy-start | bytes 8068
  863.3 451.3 %copy-start.23 = (f32[4,48,1536]{2,1,0:T(8,128)S(1)}, f32[4,48,1536]{2,1,0:T(8,128)}, u32[]{:S(2)}) copy-start(f32[4,48,1536]{2,1,0:T(8,128)} %param.21) | copy-start | bytes 3538948
  (190 other events, 2250.1 us)
Sparse Core Ops, SparseCore 0:
  17.1 29.8 all-gather.9
  49.9 66.4 all-gather.7
  147.7 24.6 reduce-scatter.18
  175.3 81.4 all-gather.13
  258.9 25.3 all-gather.11
  311.0 29.7 reduce-scatter.20
  343.7 17.4 reduce-scatter.16
  363.3 31.0 all-gather.15
  412.5 23.5 reduce-scatter.22
  467.3 17.4 reduce-scatter.26
  487.6 17.4 reduce-scatter.24
  553.7 26.1 reduce-scatter.28
  582.7 17.3 reduce-scatter.34
  602.1 33.6 all-gather.17
  652.8 26.0 reduce-scatter.30
  681.7 17.4 reduce-scatter.36
  701.2 27.1 all-gather.19
  801.7 26.0 reduce-scatter.32
  838.3 55.5 reduce-scatter.42
  898.5 144.5 reduce-scatter.38
  1047.8 193.8 reduce-scatter.40
where the time goes:
time: 1330 us; the launch traced here: 1320 us
  waiting for transfers between devices  735 us (55%)
  matrix products  242 us (18%)
  blocking collectives  161 us (12%)
  other arithmetic  126 us (9%)
  local copies, waits for them, and re-layouts  39.9 us (3%)
  between operations  17.3 us (1%)
    reduce_scatter x1, waiting for transfers between devices, on_device(): lax.psum_scatter(jnp.stack(feed_parts), 'dp', scatter_dimension=1, tiled=...  197 us
    reduce_scatter x1, waiting for transfers between devices, on_device(): lax.psum_scatter(jnp.stack(attention_parts), 'dp', scatter_dimension=1, t...  148 us
    all_gather x1, waiting for transfers between devices, on_device(): lax.all_gather(feed_weights.astype(jnp.bfloat16), 'dp', axis=1, tiled=True)  77.3 us
    all_gather x1, waiting for transfers between devices, on_device(): lax.all_gather(attention_weights.astype(jnp.bfloat16), 'dp', axis=1, tile...  69.4 us
    dot_general x16, matrix products, project(): return jnp.dot(left_side, right_side, preferred_element_type=jnp.float32)  65.9 us
    all_gather x3, waiting for transfers between devices, gather_rows(): return lax.all_gather(local_rows, 'tensor', axis=0, tiled=True)  64.8 us
    psum x1, blocking collectives, on_device(): lax.psum((jnp.sum(attention_square, axis=1), jnp.sum(feed_square, axis=1)...  57.8 us
    reduce_scatter x5, waiting for transfers between devices, branch_total(): lax.psum_scatter(partial_rows.astype(jnp.bfloat16), 'tensor', scatter_dim...  57.4 us
  transfers between devices with their start and end apart: 21, of which 21 were waited for; matrix products, arithmetic and copies ran while one was open for 11% of the time, Pallas kernels for 0%

commit v1 on v0

v1 whole, which is shorter than its diff:
```python
import jax
import jax.numpy as jnp
from jax import lax
from jax.sharding import Mesh
from jax.sharding import PartitionSpec as P

HEAD_DIM = 64
norm_epsilon = 1e-05
decay_rate = 1.0 - 2.0 ** (-0.8)
step_rate = 0.2
masked_score = -1e30
low = jnp.bfloat16
wide = jnp.float32


def gelu_exact(values):
    return jax.nn.gelu(values, approximate=False)


def layer_norm(values, norm_gain, norm_shift):
    centre = jnp.mean(values, axis=-1, keepdims=True)
    centred = values - centre
    spread = jnp.mean(centred * centred, axis=-1, keepdims=True)
    return centred * lax.rsqrt(spread + norm_epsilon) * norm_gain + norm_shift


def swap_chips(array):
    return lax.ppermute(array, ("c", "x"), [(0, 0), (1, 2), (2, 1), (3, 3)])


def other_core(array):
    return lax.ppermute(array, "c", [(0, 1), (1, 0)])


def both_halves(own_half):
    received = other_core(own_half)
    first = lax.axis_index("c") == 0
    return jnp.concatenate(
        [jnp.where(first, own_half, received), jnp.where(first, received, own_half)], axis=0
    )


def core_sum(partial_rows):
    sent = partial_rows.astype(low)
    return sent.astype(wide) + other_core(sent).astype(wide)


def ring_next(array):
    size = lax.axis_size("z")
    return lax.ppermute(array, "z", [(i, (i + 1) % size) for i in range(size)])


def holds():
    return lax.axis_index("c") == lax.axis_index("x")


def spread_blocks(blocks, order):
    held = blocks[None, None]
    for axis in order:
        if axis == "x":
            received = lax.ppermute(held, ("c", "x"), [(0, 1), (3, 2)])
            held = jnp.where(holds(), held, received)
        elif axis == "y":
            received = lax.ppermute(held, "y", [(0, 1), (1, 0)])
            first = lax.axis_index("y") == 0
            held = jnp.concatenate(
                [jnp.where(first, held, received), jnp.where(first, received, held)], axis=1
            )
        else:
            size = lax.axis_size("z")
            if size != 4:
                held = lax.all_gather(held, "z", axis=0, tiled=True)
                continue
            place = lax.axis_index("z")
            whole = jnp.zeros((size,) + held.shape[1:], held.dtype)
            moving = held
            for step in range(size):
                where_from = lax.rem(place + size - step, size)
                whole = lax.dynamic_update_slice_in_dim(whole, moving, where_from, 0)
                if step < size - 1:
                    moving = ring_next(moving)
            held = whole
    return held


def reduce_blocks(parts, order):
    held = parts
    for position, axis in enumerate(order):
        final = position == len(order) - 1
        kind = wide if final else low
        if axis == "x":
            received = lax.ppermute(held, ("c", "x"), [(1, 0), (2, 3)])
            held = (held.astype(wide) + received.astype(wide)).astype(kind)
        elif axis == "y":
            mine = lax.axis_index("y")
            sent = lax.dynamic_slice_in_dim(held, 1 - mine, 1, 1)
            kept = lax.dynamic_slice_in_dim(held, mine, 1, 1)
            received = lax.ppermute(sent, "y", [(0, 1), (1, 0)])
            held = (kept.astype(wide) + received.astype(wide)).astype(kind)
        else:
            size = lax.axis_size("z")
            if size != 4:
                held = lax.psum_scatter(held, "z", scatter_dimension=0, tiled=True).astype(kind)
                continue
            place = lax.axis_index("z")
            moving = lax.dynamic_slice_in_dim(held, lax.rem(place + size - 1, size), 1, 0)
            for step in range(1, size):
                received = ring_next(moving)
                kept = lax.dynamic_slice_in_dim(held, lax.rem(place + size - 1 - step, size), 1, 0)
                last = step == size - 1
                moving = (kept.astype(wide) + received.astype(wide)).astype(kind if last else low)
            held = moving
    return held[0, 0]


def gather_weights(blocks, order):
    received = lax.ppermute(blocks, ("c", "x"), [(2, 0), (1, 3)])
    first = lax.axis_index("c") == 0
    both = jnp.concatenate(
        [jnp.where(first, blocks, received), jnp.where(first, received, blocks)], axis=0
    )
    spread = spread_blocks(both, order)
    return spread.reshape(-1, spread.shape[-1])


def scatter_gradient(gradient, order):
    depth, columns = gradient.shape
    z_size, y_size = lax.axis_size("z"), lax.axis_size("y")
    rows = depth // (z_size * y_size)
    total = reduce_blocks(gradient.astype(low).reshape(z_size, y_size, rows, columns), order)
    core = lax.axis_index("c")
    half = rows // 2
    kept = lax.dynamic_slice_in_dim(total, core * half, half, 0)
    sent = lax.dynamic_slice_in_dim(total, (1 - core) * half, half, 0)
    received = lax.ppermute(sent, ("c", "x"), [(0, 2), (3, 1)])
    return jnp.where(holds(), kept, received)


def data_sum(values):
    values = values + other_core(values)
    if lax.axis_size("z") != 4:
        return lax.psum(values, ("z", "y"))
    values = values + lax.ppermute(values, "y", [(0, 1), (1, 0)])
    values = values + lax.ppermute(values, "z", [(0, 1), (1, 0), (2, 3), (3, 2)])
    return values + lax.ppermute(values, "z", [(0, 2), (2, 0), (1, 3), (3, 1)])


def tensor_sum(values):
    return values + lax.ppermute(values, "x", [(0, 1), (1, 0)])


def project(left_side, right_side):
    return jnp.dot(left_side, right_side, preferred_element_type=wide)


def project_back(left_side, right_side):
    return jnp.einsum("tx,dx->td", left_side, right_side, preferred_element_type=wide)


def weight_product(left_side, right_side):
    return jnp.einsum("td,tx->dx", left_side, right_side, preferred_element_type=wide)


def split_heads(matrix):
    return matrix.reshape(matrix.shape[0], matrix.shape[1] // HEAD_DIM, HEAD_DIM)


def block_scores(query_block, key_heads, first_row, key_valid, causal):
    scores = jnp.einsum(
        "qhd,khd->hqk", query_block, key_heads, preferred_element_type=wide
    ) * HEAD_DIM ** (-0.5)
    allowed = jnp.broadcast_to(key_valid[None, :], (query_block.shape[0], key_valid.shape[0]))
    if causal:
        query_place = first_row + lax.broadcasted_iota(jnp.int32, allowed.shape, 0)
        key_place = lax.broadcasted_iota(jnp.int32, allowed.shape, 1)
        allowed = allowed & (key_place <= query_place)
    return jnp.where(allowed[None], scores, masked_score)


def attend_forward(query_rows, key_rows, value_rows, key_valid, causal):
    query_heads = split_heads(query_rows)
    key_heads = split_heads(key_rows)
    value_heads = split_heads(value_rows)
    scores = block_scores(query_heads, key_heads, 0, key_valid, causal)
    row_peak = jnp.max(scores, axis=-1, keepdims=True)
    weights = jnp.exp(scores - row_peak)
    row_total = jnp.sum(weights, axis=-1, keepdims=True)
    weights_low = (weights / row_total).astype(low)
    attended = jnp.einsum("hqk,khd->qhd", weights_low, value_heads, preferred_element_type=wide)
    totals = row_peak[:, :, 0] + jnp.log(row_total[:, :, 0])
    return attended.astype(low).reshape(query_rows.shape), totals


def attend_backward(grad_attended, query_rows, key_rows, value_rows, log_totals, key_valid, causal):
    query_heads = split_heads(query_rows)
    key_heads = split_heads(key_rows)
    value_heads = split_heads(value_rows)
    grad_heads = split_heads(grad_attended)
    scale = HEAD_DIM ** (-0.5)
    scores = block_scores(query_heads, key_heads, 0, key_valid, causal)
    weights = jnp.exp(scores - log_totals[:, :, None])
    grad_weights = jnp.einsum("qhd,khd->hqk", grad_heads, value_heads, preferred_element_type=wide)
    row_dot = jnp.sum(weights * grad_weights, axis=-1, keepdims=True)
    grad_scores = (weights * (grad_weights - row_dot)).astype(low)
    grad_query = jnp.einsum("hqk,khd->qhd", grad_scores, key_heads, preferred_element_type=wide)
    grad_key = jnp.einsum("hqk,qhd->khd", grad_scores, query_heads, preferred_element_type=wide)
    grad_value = jnp.einsum(
        "hqk,qhd->khd", weights.astype(low), grad_heads, preferred_element_type=wide
    )
    return (
        (grad_query * scale).reshape(query_rows.shape).astype(low),
        (grad_key * scale).reshape(key_rows.shape).astype(low),
        grad_value.reshape(value_rows.shape).astype(low),
    )


def attention_forward(residual, vectors, norm_row, memory_rows, weights, key_valid, causal):
    width = weights.shape[1] // 4
    normed = layer_norm(residual, vectors[norm_row], vectors[norm_row + 1]).astype(low)
    source_rows = normed if memory_rows is None else memory_rows
    query_rows = project(normed, weights[:, :width]).astype(low)
    key_rows = project(source_rows, weights[:, width : 2 * width]).astype(low)
    value_rows = project(source_rows, weights[:, 2 * width : 3 * width]).astype(low)
    attended, log_totals = attend_forward(query_rows, key_rows, value_rows, key_valid, causal)
    branch = core_sum(project_back(attended, weights[:, 3 * width :]))
    stored = {
        "normed": normed,
        "source": source_rows,
        "query": query_rows,
        "key": key_rows,
        "value": value_rows,
        "attended": attended,
        "totals": log_totals,
    }
    return residual + branch, stored


def feed_forward(residual, vectors, norm_row, weights):
    width = weights.shape[1] // 2
    normed = layer_norm(residual, vectors[norm_row], vectors[norm_row + 1]).astype(low)
    before = project(normed, weights[:, :width])
    hidden = gelu_exact(before).astype(low)
    branch = core_sum(project_back(hidden, weights[:, width:]))
    return residual + branch, {"normed": normed, "hidden": hidden, "before": before}


def norm_backward(residual, vectors, norm_row, grad_normed):
    unused_out, norm_back = jax.vjp(layer_norm, residual, vectors[norm_row], vectors[norm_row + 1])
    return norm_back(grad_normed)


def attention_backward(grad_residual, stored, weights, key_valid, causal):
    width = weights.shape[1] // 4
    grad_branch = grad_residual.astype(low)
    grad_output = weight_product(grad_branch, stored["attended"])
    grad_attended = project(grad_branch, weights[:, 3 * width :]).astype(low)
    grad_query, grad_key, grad_value = attend_backward(
        grad_attended,
        stored["query"],
        stored["key"],
        stored["value"],
        stored["totals"],
        key_valid,
        causal,
    )
    weight_terms = jnp.concatenate(
        [
            weight_product(stored["normed"], grad_query).astype(low),
            weight_product(stored["source"], grad_key).astype(low),
            weight_product(stored["source"], grad_value).astype(low),
            grad_output.astype(low),
        ],
        axis=1,
    )
    from_query = project_back(grad_query, weights[:, :width])
    from_source = project_back(grad_key, weights[:, width : 2 * width]) + project_back(
        grad_value, weights[:, 2 * width : 3 * width]
    )
    return weight_terms, from_query, from_source


def feed_backward(grad_residual, residual, vectors, norm_row, stored, weights):
    width = weights.shape[1] // 2
    grad_branch = grad_residual.astype(low)
    grad_second = weight_product(grad_branch, stored["hidden"])
    grad_hidden = project(grad_branch, weights[:, width:])
    unused_value, gelu_back = jax.vjp(gelu_exact, stored["before"])
    grad_hidden = gelu_back(grad_hidden)[0].astype(low)
    grad_first = weight_product(stored["normed"], grad_hidden)
    weight_terms = jnp.concatenate([grad_first.astype(low), grad_second.astype(low)], axis=1)
    grad_input, grad_gain, grad_shift = norm_backward(
        residual, vectors, norm_row, core_sum(project_back(grad_hidden, weights[:, :width]))
    )
    return grad_residual + grad_input, weight_terms, [grad_gain, grad_shift]


def factored_step(weights, grads, rows_next, columns_next, row_level, mean_square):
    estimate = rows_next[:, :, None] * columns_next[:, None, :] / row_level[:, None, None]
    return weights - step_rate * jnp.sqrt(mean_square)[:, None, None] * grads * lax.rsqrt(estimate)


ORDERS = ("zyx", "zxy", "xyz")


def on_device(
    source_embed,
    target_embed,
    out_cotangent,
    row_flags,
    source_mask,
    target_mask,
    attention_weights,
    feed_weights,
    rows_attention,
    columns_attention,
    rows_feed,
    columns_feed,
    vector_params,
    vector_moments,
):
    core = lax.axis_index("c")
    local_rows, half_width = attention_weights.shape[1:]
    half_units = feed_weights.shape[2]
    depth = vector_params.shape[1]
    units_all = 2 * half_units

    def attention_group(block):
        part = attention_weights[4 * block : 4 * block + 4].astype(low)
        return part.transpose(1, 0, 2).reshape(local_rows, 4 * half_width)

    def feed_group(index):
        part = feed_weights[2 * index : 2 * index + 2].astype(low)
        return part.transpose(1, 0, 2).reshape(local_rows, 2 * half_units)

    source_half = swap_chips(source_embed[0])
    flags_half = swap_chips(row_flags[0])
    source_all = both_halves(source_half)
    flags_all = both_halves(flags_half)
    masks = swap_chips(jnp.concatenate([source_mask[0], target_mask[0]]))
    source_valid = masks[: source_mask.shape[1]] > 0
    target_valid = masks[source_mask.shape[1] :] > 0
    target_all = both_halves(swap_chips(target_embed[0]))
    cotangent_all = both_halves(swap_chips(out_cotangent[0]))

    encoder_attention = gather_weights(attention_group(0), "zyx")
    decoder_attention = gather_weights(attention_group(1), "xyz")
    encoder_feed = gather_weights(feed_group(0), "zxy")
    cross_attention = gather_weights(attention_group(2), "zyx")
    decoder_feed_first = gather_weights(feed_group(1)[:, :half_units], "zyx")
    decoder_feed_second = gather_weights(feed_group(1)[:, half_units:], "xyz")
    decoder_feed = jnp.concatenate([decoder_feed_first, decoder_feed_second], axis=1)

    start_rows = jnp.where(
        (flags_all == 1)[:, None],
        vector_params[12][None, :],
        jnp.where((flags_all == 2)[:, None], vector_params[13][None, :], source_all.astype(wide)),
    )
    target_rows = target_all.astype(wide)

    encoder_mid, kept_first = attention_forward(
        start_rows, vector_params, 0, None, encoder_attention, source_valid, False
    )
    decoder_one, kept_third = attention_forward(
        target_rows, vector_params, 6, None, decoder_attention, target_valid, True
    )
    encoder_final, kept_second = feed_forward(encoder_mid, vector_params, 2, encoder_feed)
    memory_rows = layer_norm(encoder_final, vector_params[4], vector_params[5]).astype(low)
    decoder_two, kept_fourth = attention_forward(
        decoder_one, vector_params, 8, memory_rows, cross_attention, source_valid, False
    )
    decoder_three, kept_fifth = feed_forward(decoder_two, vector_params, 10, decoder_feed)

    def own_half(rows):
        half = rows.shape[0] // 2
        return lax.dynamic_slice_in_dim(rows, core * half, half, 0)

    decoder_out = swap_chips(own_half(decoder_three.astype(low)))

    grad_three = jnp.where(target_valid[:, None], cotangent_all.astype(wide), 0.0)
    vector_parts = [None] * 14
    grad_two, decoder_feed_terms, vector_parts[10:12] = feed_backward(
        grad_three, decoder_two, vector_params, 10, kept_fifth, decoder_feed
    )
    decoder_feed_grad = scatter_gradient(decoder_feed_terms, "xyz")
    cross_terms, from_query, from_source = attention_backward(
        grad_two, kept_fourth, cross_attention, source_valid, False
    )
    cross_grad = scatter_gradient(cross_terms, "zyx")
    grad_memory, vector_parts[4], vector_parts[5] = norm_backward(
        encoder_final, vector_params, 4, core_sum(from_source)
    )
    grad_input, vector_parts[8], vector_parts[9] = norm_backward(
        decoder_one, vector_params, 8, core_sum(from_query)
    )
    grad_one = grad_two + grad_input
    grad_mid, encoder_feed_terms, vector_parts[2:4] = feed_backward(
        grad_memory, encoder_mid, vector_params, 2, kept_second, encoder_feed
    )
    encoder_feed_grad = scatter_gradient(encoder_feed_terms, "yxz")
    decoder_terms, from_query, from_source = attention_backward(
        grad_one, kept_third, decoder_attention, target_valid, True
    )
    decoder_grad = scatter_gradient(decoder_terms, "zyx")
    grad_input, vector_parts[6], vector_parts[7] = norm_backward(
        target_rows, vector_params, 6, core_sum(from_query + from_source)
    )
    target_grad = swap_chips(own_half((grad_one + grad_input).astype(low))).astype(wide)
    encoder_terms, from_query, from_source = attention_backward(
        grad_mid, kept_first, encoder_attention, source_valid, False
    )
    grad_input, vector_parts[0], vector_parts[1] = norm_backward(
        start_rows, vector_params, 0, core_sum(from_query + from_source)
    )
    grad_start = grad_mid + grad_input
    vector_parts[12] = jnp.sum(jnp.where((flags_all == 1)[:, None], grad_start, 0.0), axis=0)
    vector_parts[13] = jnp.sum(jnp.where((flags_all == 2)[:, None], grad_start, 0.0), axis=0)
    source_grad = swap_chips(own_half(grad_start.astype(low))).astype(wide)
    source_grad = jnp.where((row_flags[0] == 0)[:, None], source_grad, 0.0)

    vector_terms = jnp.stack(vector_parts, axis=1).astype(low)
    vector_terms = jnp.pad(vector_terms, ((0, 0), (0, 128 - vector_terms.shape[1])))
    tail_first = scatter_gradient(
        jnp.concatenate([encoder_terms[:, : 2 * half_width], vector_terms], axis=1), "xyz"
    )
    tail_second = scatter_gradient(encoder_terms[:, 2 * half_width :], "zyx")
    vector_grad = tail_first[:, 2 * half_width : 2 * half_width + 14].T
    encoder_grad = jnp.concatenate([tail_first[:, : 2 * half_width], tail_second], axis=1)

    def as_matrices(rows, count):
        return rows.reshape(local_rows, count, -1).transpose(1, 0, 2)

    attention_grad = jnp.concatenate(
        [as_matrices(part, 4) for part in (encoder_grad, decoder_grad, cross_grad)], axis=0
    )
    feed_grad = jnp.concatenate(
        [as_matrices(part, 2) for part in (encoder_feed_grad, decoder_feed_grad)], axis=0
    )

    weight_squares = jnp.concatenate(
        [
            jnp.sum(attention_weights * attention_weights, axis=(1, 2)),
            jnp.sum(feed_weights * feed_weights, axis=(1, 2)),
            jnp.sum(rows_attention, axis=1) * 0.5,
            jnp.sum(rows_feed, axis=1) * 0.5,
        ]
    )
    early_sums = data_sum(tensor_sum(weight_squares))
    scale_attention, scale_feed = early_sums[:12], early_sums[12:16]
    rows_total_attention, rows_total_feed = early_sums[16:28], early_sums[28:32]
    attention_square = attention_grad * attention_grad
    feed_square = feed_grad * feed_grad
    row_sums = tensor_sum(
        jnp.concatenate([jnp.sum(attention_square, axis=2), jnp.sum(feed_square, axis=2)], axis=0)
    )
    column_attention = jnp.sum(attention_square, axis=1)
    column_feed = jnp.sum(feed_square, axis=1)
    square_totals = jnp.sum(row_sums, axis=1)
    column_sums = data_sum(
        jnp.concatenate([column_attention.reshape(-1), column_feed.reshape(-1), square_totals])
    )
    column_attention = column_sums[: column_attention.size].reshape(column_attention.shape)
    column_feed = column_sums[column_attention.size : -16].reshape(column_feed.shape)
    square_totals = column_sums[-16:]
    keep, take = decay_rate, 1.0 - decay_rate
    rows_attention_next = keep * rows_attention + take * row_sums[:12] / depth
    rows_feed_next = keep * rows_feed + take * row_sums[12:] / units_all
    total_attention = keep * rows_total_attention + take * square_totals[:12] / depth
    total_feed = keep * rows_total_feed + take * square_totals[12:] / units_all
    columns_attention_next = keep * columns_attention + take * column_attention / depth
    columns_feed_next = keep * columns_feed + take * column_feed / depth
    attention_updated = factored_step(
        attention_weights,
        attention_grad,
        rows_attention_next,
        columns_attention_next,
        total_attention / depth,
        scale_attention / (depth * depth),
    )
    feed_updated = factored_step(
        feed_weights,
        feed_grad,
        rows_feed_next,
        columns_feed_next,
        total_feed / depth,
        scale_feed / (depth * units_all),
    )
    local_width = vector_moments.shape[1]
    place = (lax.axis_index("z") * lax.axis_size("y") + lax.axis_index("y")) * 2 + core
    vector_local = lax.dynamic_slice_in_dim(vector_params, place * local_width, local_width, 1)
    vector_moments_next = keep * vector_moments + take * vector_grad * vector_grad
    vector_scale = jnp.sqrt(jnp.mean(vector_params * vector_params, axis=1))
    vector_updated = vector_local - step_rate * vector_scale[:, None] * vector_grad * lax.rsqrt(
        vector_moments_next
    )
    return (
        decoder_out[None],
        source_grad[None],
        target_grad[None],
        attention_grad,
        feed_grad,
        vector_grad,
        attention_updated,
        feed_updated,
        vector_updated,
        rows_attention_next,
        columns_attention_next,
        rows_feed_next,
        columns_feed_next,
        vector_moments_next,
        vector_grad[10:12],
    )


def solution(mesh):
    groups = mesh.shape["dp"] // 4
    inner = Mesh(mesh.devices.reshape(groups, 2, 2, 2), ("z", "y", "c", "x"))
    data = ("z", "y", "c")
    rows3, rows2 = P(data, "x", None), P(data, "x")
    matrix, row_spec, column_spec = P(None, data, "x"), P(None, data), P(None, "x")
    return jax.shard_map(
        on_device,
        mesh=inner,
        in_specs=(
            rows3,
            rows3,
            rows3,
            rows2,
            P(data, None),
            P(data, None),
            matrix,
            matrix,
            row_spec,
            column_spec,
            row_spec,
            column_spec,
            P(),
            row_spec,
        ),
        out_specs=(
            rows3,
            rows3,
            rows3,
            matrix,
            matrix,
            row_spec,
            matrix,
            matrix,
            row_spec,
            row_spec,
            column_spec,
            row_spec,
            column_spec,
            row_spec,
            row_spec,
        ),
        check_vma=False,
    )
```

time: 1330 us -> 1010 us (0.76)
  waiting for transfers between devices: 735 us -> 443 us
  blocking collectives: 161 us -> 0 us
  starting transfers between devices: 1.48 us -> 138 us
  matrix products: 242 us -> 193 us
  local copies, waits for them, and re-layouts: 39.9 us -> 74.3 us
  other arithmetic: 126 us -> 149 us
    reduce_scatter x13 -> x0, waiting for transfers between devices: 464 us -> none  [the longest x1 197 us: on_device(): lax.psum_scatter(jnp.stack(feed_parts), 'dp', scatter_dimension=1, tiled=...]
    ppermute x0 -> x105, waiting for transfers between devices: none -> 443 us  [the longest x36 207 us: ring_next(): return lax.ppermute(array, 'z', [(i, (i + 1) % size) for i in range(size)])]
    all_gather x7 -> x0, waiting for transfers between devices: 240 us -> none  [the longest x1 77.3 us: on_device(): lax.all_gather(feed_weights.astype(jnp.bfloat16), 'dp', axis=1, tiled=True)]
    ppermute x0 -> x105, starting transfers between devices: none -> 138 us  [the longest x6 21 us: spread_blocks(): received = lax.ppermute(held, ('c', 'x'), [(0, 1), (3, 2)])]
    all_gather x6 -> x0, blocking collectives: 95.3 us -> none  [the longest x3 50 us: gather_gradient(): return lax.all_gather(local_rows, 'tensor', axis=0, tiled=True)]
    psum x2 -> x0, blocking collectives: 66.1 us -> none  [the longest x1 57.8 us: on_device(): lax.psum((jnp.sum(attention_square, axis=1), jnp.sum(feed_square, axis=1)...]
    dot_general x60 -> x57, matrix products: 209 us -> 163 us  [the longest x16 49.2 us: project(): return jnp.dot(left_side, right_side, preferred_element_type=wide)]
    unnamed x22 -> x0, waiting for transfers between devices: 30.9 us -> none
  transfers between devices with their start and end apart: 21 -> 105, of which waited for: 21 -> 45; matrix products, arithmetic and copies ran while one was open for 11% -> 37% of each run, Pallas kernels for 0% -> 0%
where the time goes in v1:
time: 1010 us; the launch traced here: 1000 us
  waiting for transfers between devices  443 us (44%)
  matrix products  193 us (19%)
  other arithmetic  149 us (15%)
  starting transfers between devices  138 us (14%)
  local copies, waits for them, and re-layouts  74.3 us (7%)
    ppermute x36, waiting for transfers between devices, ring_next(): return lax.ppermute(array, 'z', [(i, (i + 1) % size) for i in range(size)])  207 us
    ppermute x6, waiting for transfers between devices, reduce_blocks(): received = lax.ppermute(sent, 'y', [(0, 1), (1, 0)])  103 us
    ppermute x6, waiting for transfers between devices, spread_blocks(): received = lax.ppermute(held, 'y', [(0, 1), (1, 0)])  56.8 us
    dot_general x16, matrix products, project(): return jnp.dot(left_side, right_side, preferred_element_type=wide)  49.2 us
    dot_general x16, matrix products, project_back(): jnp.einsum('tx,dx->td', left_side, right_side, preferred_element_type=wide)  37.9 us
    ppermute x6, waiting for transfers between devices, reduce_blocks(): received = lax.ppermute(held, ('c', 'x'), [(1, 0), (2, 3)])  29.6 us
    unnamed x373, local copies, waits for them, and re-layouts  29.4 us
    dot_general x16, matrix products, weight_product(): jnp.einsum('td,tx->dx', left_side, right_side, preferred_element_type=wide)  28.4 us
  transfers between devices with their start and end apart: 105, of which 45 were waited for; matrix products, arithmetic and copies ran while one was open for 37% of the time, Pallas kernels for 0%

profile of v1, /device:TPU:0, one launch (start us, length us, event | category | flops | bytes accessed | tf_op | source)
XLA Modules:
  0.0 1003.1 jit_solution(11214159748811096042)
XLA Ops:
  13.1 7.2 collective-permute-start.11
  56.4 9.3 collective-permute-done.29
  68.5 8.9 collective-permute-done.36
  79.1 7.9 collective-permute-done.43
  87.0 10.4 %collective-permute-done.30 = bf16[1,1,96,1536]{3,2,1,0:T(8,128)(2,1)S(1)} collective-permute-done((bf16[1,1,96,1536]{3,2,1,0:T(8,128)(2,1)S(1)}, bf16[1,1,96,1536]{3,2,1,0:T(8,128)(2,1)S(1)}, u32[]{:S(2)}, u32[]{:S(2)}) %collective-permute-start.30) | collective-permute-done | bytes 294944 | tf_op jit(solution)/shard_map/ppermute | solution.py:50
  97.8 9.2 collective-permute-done.16
  118.8 31.6 %collective-permute-done.31 = bf16[1,1,96,1536]{3,2,1,0:T(8,128)(2,1)S(1)} collective-permute-done((bf16[1,1,96,1536]{3,2,1,0:T(8,128)(2,1)S(1)}, bf16[1,1,96,1536]{3,2,1,0:T(8,128)(2,1)S(1)}, u32[]{:S(2)}, u32[]{:S(2)}) %collective-permute-start.31) | collective-permute-done | bytes 294944 | tf_op jit(solution)/shard_map/ppermute | solution.py:50
  150.3 6.3 collective-permute-done.17
  165.3 10.3 %collective-permute-done.23 = bf16[1,1,96,3072]{3,2,1,0:T(8,128)(2,1)S(1)} collective-permute-done((bf16[1,1,96,3072]{3,2,1,0:T(8,128)(2,1)S(1)}, bf16[1,1,96,3072]{3,2,1,0:T(8,128)(2,1)S(1)}, u32[]{:S(2)}, u32[]{:S(2)}) %collective-permute-start.23) | collective-permute-done | bytes 589856 | tf_op jit(solution)/shard_map/ppermute | solution.py:50
  189.8 11.2 %collective-permute-done.45 = bf16[1,2,96,1536]{3,2,1,0:T(8,128)(2,1)} collective-permute-done((bf16[1,2,96,1536]{3,2,1,0:T(8,128)(2,1)S(1)}, bf16[1,2,96,1536]{3,2,1,0:T(8,128)(2,1)}, u32[]{:S(2)}, u32[]{:S(2)}) %collective-permute-start.45) | collective-permute-done | bytes 589856 | tf_op jit(solution)/shard_map/ppermute | solution.py:50
  202.1 11.4 %collective-permute-done.24 = bf16[1,1,96,3072]{3,2,1,0:T(8,128)(2,1)S(1)} collective-permute-done((bf16[1,1,96,3072]{3,2,1,0:T(8,128)(2,1)S(1)}, bf16[1,1,96,3072]{3,2,1,0:T(8,128)(2,1)S(1)}, u32[]{:S(2)}, u32[]{:S(2)}) %collective-permute-start.24) | collective-permute-done | bytes 589856 | tf_op jit(solution)/shard_map/ppermute | solution.py:50
  222.6 12.7 %collective-permute-done.39 = bf16[4,1,96,1536]{3,2,1,0:T(8,128)(2,1)S(1)} collective-permute-done((bf16[4,1,96,1536]{3,2,1,0:T(8,128)(2,1)S(1)}, bf16[4,1,96,1536]{3,2,1,0:T(8,128)(2,1)S(1)}, u32[]{:S(2)}, u32[]{:S(2)}) %collective-permute-start.39) | collective-permute-done | bytes 1179680 | tf_op jit(solution)/shard_map/ppermute | solution.py:64
  248.5 19.7 %collective-permute-done.19 = bf16[4,2,96,1536]{3,2,1,0:T(8,128)(2,1)S(1)} collective-permute-done((bf16[4,2,96,1536]{3,2,1,0:T(8,128)(2,1)S(1)}, bf16[4,2,96,1536]{3,2,1,0:T(8,128)(2,1)S(1)}, u32[]{:S(2)}, u32[]{:S(2)}) %collective-permute-start.19) | collective-permute-done | bytes 2359328 | tf_op jit(solution)/shard_map/ppermute | solution.py:61
  288.4 10.6 %fusion.72 = bf16[6,64,1024]{2,1,0:T(8,128)(2,1)S(1)} fusion(bf16[1024,6,64]{0,2,1:T(8,128)(2,1)} %bitcast.351, f32[6,1024,1024]{1,2,0:T(8,128)} %copy-done, f32[6,1024]{1,0:T(8,128)S(1)} %fusion, f32[6,1024]{1,0:T(8,128)S(1)} %get-tuple-element.204), kind=kOutput, calls=%fused_computation.191 | convolution fusion | flops 824573952 | bytes 26787840 | tf_op jit(solution)/shard_map/hqk,khd->qhd/dot_general | solution.py:189
  320.8 36.3 %collective-permute-done.26 = bf16[4,1,96,3072]{3,2,1,0:T(8,128)(2,1)S(1)} collective-permute-done((bf16[4,1,96,3072]{3,2,1,0:T(8,128)(2,1)S(1)}, bf16[4,1,96,3072]{3,2,1,0:T(8,128)(2,1)S(1)}, u32[]{:S(2)}, u32[]{:S(2)}) %collective-permute-start.26) | collective-permute-done | bytes 2359328 | tf_op jit(solution)/shard_map/ppermute | solution.py:64
  357.9 18.9 %multiply_convert_fusion.3 = (bf16[1024,1536]{1,0:T(8,128)(2,1)S(1)}, f32[1024,1536]{1,0:T(8,128)}, f32[1024,1536]{1,0:T(8,128)}) fusion(bf16[768,3072]{1,0:T(8,128)(2,1)S(1)} %bitcast.290, f32[1024,768]{1,0:T(8,128)S(1)} %get-tuple-element.141, f32[768]{0:T(1024)S(1)} %get-tuple-element.105, f32[768]{0:T(1024)S(1)} %get-tuple-element.106, ...), kind=kOutput, calls=%fused_computation.28 | convolution fusion | flops 2522087424 | bytes 21250048 | tf_op jit(solution)/shard_map/dot_general | solution.py:153
  401.8 7.8 multiply_convert_fusion.4
  436.1 6.7 multiply_reduce_fusion.1
  444.5 6.7 multiply_convert_fusion.1
  537.9 8.7 add_convert_fusion.1
  577.0 51.5 %collective-permute-done.80 = bf16[1,1,96,1536]{3,2,1,0:T(8,128)(2,1)S(1)} collective-permute-done((bf16[1,1,96,1536]{3,2,1,0:T(8,128)(2,1)S(1)}, bf16[1,1,96,1536]{3,2,1,0:T(8,128)(2,1)S(1)}, u32[]{:S(2)}, u32[]{:S(2)}) %collective-permute-start.80) | collective-permute-done | bytes 294944 | tf_op jit(solution)/shard_map/ppermute | solution.py:98
  651.8 11.2 %fusion.69 = bf16[6,64,1024]{2,1,0:T(8,128)(2,1)} fusion(bf16[1024,6,64]{0,2,1:T(8,128)(2,1)S(1)} %bitcast.278, f32[6,1024,1024]{1,2,0:T(8,128)} %copy-done, f32[6,1024]{1,0:T(8,128)S(1)} %copy-done.88), kind=kOutput, calls=%fused_computation.185 | convolution fusion | flops 818282496 | bytes 26763264 | tf_op jit(solution)/shard_map/hqk,qhd->khd/dot_general | solution.py:207
  663.0 16.3 %multiply_reduce_fusion = (f32[6,1024]{1,0:T(8,128)}, f32[6,1024,1024]{1,2,0:T(8,128)}) fusion(f32[6,1024,1024]{1,2,0:T(8,128)} %copy-done, f32[6,1024]{1,0:T(8,128)S(1)} %copy-done.88, bf16[1024,6,64]{0,2,1:T(8,128)(2,1)S(1)} %bitcast.279, bf16[1024,6,64]{0,2,1:T(8,128)(2,1)} %bitcast.352), kind=kOutput, calls=%fused_computation.1 | convolution fusion | flops 824174592 | bytes 51953664 | tf_op jit(solution)/shard_map/qhd,khd->hqk/dot_general | solution.py:202
  696.3 16.9 %multiply_convert_fusion = bf16[6,1024,1024]{1,2,0:T(8,128)(2,1)S(1)} fusion(f32[6,1024,1024]{1,2,0:T(8,128)} %get-tuple-element.213, f32[6,1024,1024]{1,2,0:T(8,128)} %copy-done, f32[6,1024]{1,0:T(8,128)S(1)} %copy-done.98, f32[6,1024]{1,0:T(8,128)S(1)} %copy-done.89), kind=kLoop, calls=%fused_computation | loop fusion | flops 25165824 | bytes 62963712 | tf_op jit(solution)/shard_map/convert_element_type | solution.py:204
  753.8 51.4 %collective-permute-done.68 = bf16[1,1,96,768]{3,2,1,0:T(8,128)(2,1)S(1)} collective-permute-done((bf16[1,1,96,768]{3,2,1,0:T(8,128)(2,1)S(1)}, bf16[1,1,96,768]{3,2,1,0:T(8,128)(2,1)S(1)}, u32[]{:S(2)}, u32[]{:S(2)}) %collective-permute-start.68) | collective-permute-done | bytes 147488 | tf_op jit(solution)/shard_map/ppermute | solution.py:98
  823.5 7.4 collective-permute-start.55
  850.7 23.5 %collective-permute-done.84 = bf16[4,1,96,3072]{3,2,1,0:T(8,128)(2,1)} collective-permute-done((bf16[4,1,96,3072]{3,2,1,0:T(8,128)(2,1)S(1)}, bf16[4,1,96,3072]{3,2,1,0:T(8,128)(2,1)}, u32[]{:S(2)}, u32[]{:S(2)}) %collective-permute-start.84) | collective-permute-done | bytes 2359328 | tf_op jit(solution)/shard_map/ppermute | solution.py:92
  877.9 8.2 collective-permute-done.61
  886.5 16.0 %collective-permute-done.62 = bf16[1,1,96,896]{3,2,1,0:T(8,128)(2,1)S(1)} collective-permute-done((bf16[1,1,96,896]{3,2,1,0:T(8,128)(2,1)S(1)}, bf16[1,1,96,896]{3,2,1,0:T(8,128)(2,1)S(1)}, u32[]{:S(2)}, u32[]{:S(2)}) %collective-permute-start.62) | collective-permute-done | bytes 172064 | tf_op jit(solution)/shard_map/ppermute | solution.py:50
  902.8 16.0 %collective-permute-done.63 = bf16[1,1,96,896]{3,2,1,0:T(8,128)(2,1)S(1)} collective-permute-done((bf16[1,1,96,896]{3,2,1,0:T(8,128)(2,1)S(1)}, bf16[1,1,96,896]{3,2,1,0:T(8,128)(2,1)S(1)}, u32[]{:S(2)}, u32[]{:S(2)}) %collective-permute-start.63) | collective-permute-done | bytes 172064 | tf_op jit(solution)/shard_map/ppermute | solution.py:50
  921.2 10.3 %collective-permute-done.86 = bf16[1,1,96,3072]{3,2,1,0:T(8,128)(2,1)S(1)} collective-permute-done((bf16[1,1,96,3072]{3,2,1,0:T(8,128)(2,1)S(1)}, bf16[1,1,96,3072]{3,2,1,0:T(8,128)(2,1)S(1)}, u32[]{:S(2)}, u32[]{:S(2)}) %collective-permute-start.86) | collective-permute-done | bytes 589856 | tf_op jit(solution)/shard_map/ppermute | solution.py:50
  933.8 10.3 %collective-permute-done.93 = bf16[1,1,96,3072]{3,2,1,0:T(8,128)(2,1)S(1)} collective-permute-done((bf16[1,1,96,3072]{3,2,1,0:T(8,128)(2,1)}, bf16[1,1,96,3072]{3,2,1,0:T(8,128)(2,1)S(1)}, u32[]{:S(2)}, u32[]{:S(2)}) %collective-permute-start.93) | collective-permute-done | bytes 589856 | tf_op jit(solution)/shard_map/ppermute | solution.py:50
  (895 shorter events, 507.3 us)
Async XLA Ops:
  3.5 63.9 %collective-permute-start = (bf16[256,768]{1,0:T(8,128)(2,1)}, bf16[256,768]{1,0:T(8,128)(2,1)S(1)}, u32[]{:S(2)}, u32[]{:S(2)}) collective-permute-start(bf16[256,768]{1,0:T(8,128)(2,1)} %bitcast.368), channel_id=1, source_target_pairs={{0,0},{1,2},{2,1},{3,3},{4,4},{5,6},{6,5},{7,7},{8,8},{9,10},{10,9... | collective-permute-start | bytes 1179656 | tf_op jit(solution)/shard_map/ppermute | solution.py:28
  5.2 63.4 %collective-permute-start.49 = (bf16[256,768]{1,0:T(8,128)(2,1)}, bf16[256,768]{1,0:T(8,128)(2,1)S(1)}, u32[]{:S(2)}, u32[]{:S(2)}) collective-permute-start(bf16[256,768]{1,0:T(8,128)(2,1)} %bitcast.369), channel_id=1, source_target_pairs={{0,0},{1,2},{2,1},{3,3},{4,4},{5,6},{6,5},{7,7},{8,8},{9,10},{10,9... | collective-permute-start | bytes 1179656 | tf_op jit(solution)/shard_map/ppermute | solution.py:28
  29.8 85.6 %collective-permute-start.12 = (bf16[512,768]{1,0:T(8,128)(2,1)}, bf16[512,768]{1,0:T(8,128)(2,1)S(1)}, u32[]{:S(2)}, u32[]{:S(2)}) collective-permute-start(bf16[512,768]{1,0:T(8,128)(2,1)} %bitcast.367), channel_id=1, source_target_pairs={{0,0},{1,2},{2,1},{3,3},{4,4},{5,6},{6,5},{7,7},{8,8},{9,10},{10,9... | collective-permute-start | bytes 2359304 | tf_op jit(solution)/shard_map/ppermute | solution.py:28
  67.4 42.9 %collective-permute-start.22 = (bf16[1,1,96,3072]{3,2,1,0:T(8,128)(2,1)S(1)}, bf16[1,1,96,3072]{3,2,1,0:T(8,128)(2,1)S(1)}, u32[]{:S(2)}, u32[]{:S(2)}) collective-permute-start(bf16[1,1,96,3072]{3,2,1,0:T(8,128)(2,1)S(1)} %maximum_bitcast_fusion), channel_id=1, source_target_pairs={{0,8},{8,16},{16,24},{24,0},{1,9},{9,17},{17,25},{25,1},{2,10},{10... | collective-permute-start | bytes 1769480 | tf_op jit(solution)/shard_map/ppermute | solution.py:50
  107.3 57.2 %collective-permute-start.5 = (bf16[1,2,96,1536]{3,2,1,0:T(8,128)(2,1)S(1)}, bf16[1,2,96,1536]{3,2,1,0:T(8,128)(2,1)S(1)}, u32[]{:S(2)}, u32[]{:S(2)}) collective-permute-start(bf16[1,2,96,1536]{3,2,1,0:T(8,128)(2,1)S(1)} %get-tuple-element.172), channel_id=1, source_target_pairs={{0,8},{8,16},{16,24},{24,0},{1,9},{9,17},{17,25},{25,1},{2,10},{10... | collective-permute-start | bytes 1769480 | tf_op jit(solution)/shard_map/ppermute | solution.py:50
  108.6 56.6 %collective-permute-start.44 = (bf16[1,2,96,1536]{3,2,1,0:T(8,128)(2,1)S(1)}, bf16[1,2,96,1536]{3,2,1,0:T(8,128)(2,1)S(1)}, u32[]{:S(2)}, u32[]{:S(2)}) collective-permute-start(bf16[1,2,96,1536]{3,2,1,0:T(8,128)(2,1)S(1)} %get-tuple-element.164), channel_id=1, source_target_pairs={{0,8},{8,16},{16,24},{24,0},{1,9},{9,17},{17,25},{25,1},{2,10},{10... | collective-permute-start | bytes 1769480 | tf_op jit(solution)/shard_map/ppermute | solution.py:50
  118.7 57.7 %collective-permute-start.13 = (bf16[512,768]{1,0:T(8,128)(2,1)S(1)}, bf16[512,768]{1,0:T(8,128)(2,1)S(1)}, u32[]{:S(2)}, u32[]{:S(2)}) collective-permute-start(bf16[512,768]{1,0:T(8,128)(2,1)S(1)} %collective-permute-done.12), channel_id=1, source_target_pairs={{0,2},{2,0},{1,3},{3,1},{4,6},{6,4},{5,7},{7,5},{8,10},{10,8},{9,1... | collective-permute-start | bytes 2359304 | tf_op jit(solution)/shard_map/ppermute | solution.py:32
  163.0 51.4 %collective-permute-start.18 = (bf16[4,1,96,1536]{3,2,1,0:T(8,128)(2,1)S(1)}, bf16[4,1,96,1536]{3,2,1,0:T(8,128)(2,1)S(1)}, u32[]{:S(2)}, u32[]{:S(2)}) collective-permute-start(bf16[4,1,96,1536]{3,2,1,0:T(8,128)(2,1)S(1)} %constant_dynamic-update-slice_fusion.16), channel_id=1, source_target_pairs={{0,4},{4,0},{1,5},{5,1},{2,6},{6,2},{3,7},{7,3},{8,12},{12,8},{9,1... | collective-permute-start | bytes 3538952 | tf_op jit(solution)/shard_map/ppermute | solution.py:64
  164.5 53.8 %collective-permute-start.32 = (bf16[4,1,96,1536]{3,2,1,0:T(8,128)(2,1)S(1)}, bf16[4,1,96,1536]{3,2,1,0:T(8,128)(2,1)S(1)}, u32[]{:S(2)}, u32[]{:S(2)}) collective-permute-start(bf16[4,1,96,1536]{3,2,1,0:T(8,128)(2,1)S(1)} %constant_dynamic-update-slice_fusion.8), channel_id=1, source_target_pairs={{0,4},{4,0},{1,5},{5,1},{2,6},{6,2},{3,7},{7,3},{8,12},{12,8},{9,1... | collective-permute-start | bytes 3538952 | tf_op jit(solution)/shard_map/ppermute | solution.py:64
  188.2 47.0 %collective-permute-start.39 = (bf16[4,1,96,1536]{3,2,1,0:T(8,128)(2,1)S(1)}, bf16[4,1,96,1536]{3,2,1,0:T(8,128)(2,1)S(1)}, u32[]{:S(2)}, u32[]{:S(2)}) collective-permute-start(bf16[4,1,96,1536]{3,2,1,0:T(8,128)(2,1)S(1)} %constant_dynamic-update-slice_fusion.4), channel_id=1, source_target_pairs={{0,4},{4,0},{1,5},{5,1},{2,6},{6,2},{3,7},{7,3},{8,12},{12,8},{9,1... | collective-permute-start | bytes 3538952 | tf_op jit(solution)/shard_map/ppermute | solution.py:64
  213.5 93.9 %collective-permute-start.46 = (bf16[1,2,96,1536]{3,2,1,0:T(8,128)(2,1)}, bf16[1,2,96,1536]{3,2,1,0:T(8,128)(2,1)}, u32[]{:S(2)}, u32[]{:S(2)}) collective-permute-start(bf16[1,2,96,1536]{3,2,1,0:T(8,128)(2,1)} %collective-permute-done.45), channel_id=1, source_target_pairs={{0,8},{8,16},{16,24},{24,0},{1,9},{9,17},{17,25},{25,1},{2,10},{10... | collective-permute-start | bytes 1769480 | tf_op jit(solution)/shard_map/ppermute | solution.py:50
  214.4 87.1 %collective-permute-start.25 = (bf16[4,1,96,3072]{3,2,1,0:T(8,128)(2,1)}, bf16[4,1,96,3072]{3,2,1,0:T(8,128)(2,1)}, u32[]{:S(2)}, u32[]{:S(2)}) collective-permute-start(bf16[4,1,96,3072]{3,2,1,0:T(8,128)(2,1)} %constant_dynamic-update-slice_fusion.12), channel_id=1, source_target_pairs={{0,1},{3,2},{4,5},{7,6},{8,9},{11,10},{12,13},{15,14},{16,17},{19,... | collective-permute-start | bytes 7077896 | tf_op jit(solution)/shard_map/ppermute | solution.py:61
  218.3 49.9 %collective-permute-start.19 = (bf16[4,2,96,1536]{3,2,1,0:T(8,128)(2,1)S(1)}, bf16[4,2,96,1536]{3,2,1,0:T(8,128)(2,1)S(1)}, u32[]{:S(2)}, u32[]{:S(2)}) collective-permute-start(bf16[4,2,96,1536]{3,2,1,0:T(8,128)(2,1)S(1)} %pad_maximum_fusion.3), channel_id=1, source_target_pairs={{0,1},{3,2},{4,5},{7,6},{8,9},{11,10},{12,13},{15,14},{16,17},{19,... | collective-permute-start | bytes 7077896 | tf_op jit(solution)/shard_map/ppermute | solution.py:61
  235.3 146.9 %collective-permute-start.33 = (bf16[4,2,96,1536]{3,2,1,0:T(8,128)(2,1)}, bf16[4,2,96,1536]{3,2,1,0:T(8,128)(2,1)}, u32[]{:S(2)}, u32[]{:S(2)}) collective-permute-start(bf16[4,2,96,1536]{3,2,1,0:T(8,128)(2,1)} %pad_maximum_fusion.4), channel_id=1, source_target_pairs={{0,1},{3,2},{4,5},{7,6},{8,9},{11,10},{12,13},{15,14},{16,17},{19,... | collective-permute-start | bytes 7077896 | tf_op jit(solution)/shard_map/ppermute | solution.py:61
  248.5 66.6 %collective-permute-start.9 = (bf16[512,768]{1,0:T(8,128)(2,1)}, bf16[512,768]{1,0:T(8,128)(2,1)}, u32[]{:S(2)}, u32[]{:S(2)}) collective-permute-start(bf16[512,768]{1,0:T(8,128)(2,1)} %convolution_convert_fusion.15), channel_id=1, source_target_pairs={{0,2},{2,0},{1,3},{3,1},{4,6},{6,4},{5,7},{7,5},{8,10},{10,8},{9,1... | collective-permute-start | bytes 2359304 | tf_op jit(solution)/shard_map/ppermute | solution.py:32
  303.5 53.6 %collective-permute-start.26 = (bf16[4,1,96,3072]{3,2,1,0:T(8,128)(2,1)S(1)}, bf16[4,1,96,3072]{3,2,1,0:T(8,128)(2,1)S(1)}, u32[]{:S(2)}, u32[]{:S(2)}) collective-permute-start(bf16[4,1,96,3072]{3,2,1,0:T(8,128)(2,1)S(1)} %broadcast_select_fusion), channel_id=1, source_target_pairs={{0,4},{4,0},{1,5},{5,1},{2,6},{6,2},{3,7},{7,3},{8,12},{12,8},{9,1... | collective-permute-start | bytes 7077896 | tf_op jit(solution)/shard_map/ppermute | solution.py:64
  307.4 91.8 %collective-permute-start.40 = (bf16[4,2,96,1536]{3,2,1,0:T(8,128)(2,1)}, bf16[4,2,96,1536]{3,2,1,0:T(8,128)(2,1)}, u32[]{:S(2)}, u32[]{:S(2)}) collective-permute-start(bf16[4,2,96,1536]{3,2,1,0:T(8,128)(2,1)} %pad_maximum_fusion.5), channel_id=1, source_target_pairs={{0,1},{3,2},{4,5},{7,6},{8,9},{11,10},{12,13},{15,14},{16,17},{19,... | collective-permute-start | bytes 7077896 | tf_op jit(solution)/shard_map/ppermute | solution.py:61
  427.9 309.6 %collective-permute-start.89 = (bf16[4,2,96,3072]{3,2,1,0:T(8,128)(2,1)}, bf16[4,2,96,3072]{3,2,1,0:T(8,128)(2,1)}, u32[]{:S(2)}, u32[]{:S(2)}) collective-permute-start(bf16[4,2,96,3072]{3,2,1,0:T(8,128)(2,1)} %bitcast.93), channel_id=1, source_target_pairs={{1,0},{2,3},{5,4},{6,7},{9,8},{10,11},{13,12},{14,15},{17,16},{18,... | collective-permute-start | bytes 14155784 | tf_op jit(solution)/shard_map/ppermute | solution.py:92
  482.3 49.2 %collective-permute-start.52 = (bf16[1024,768]{1,0:T(8,128)(2,1)}, bf16[1024,768]{1,0:T(8,128)(2,1)}, u32[]{:S(2)}, u32[]{:S(2)}) collective-permute-start(bf16[1024,768]{1,0:T(8,128)(2,1)} %add_convert_fusion.6), channel_id=1, source_target_pairs={{0,2},{2,0},{1,3},{3,1},{4,6},{6,4},{5,7},{7,5},{8,10},{10,8},{9,1... | collective-permute-start | bytes 4718600 | tf_op jit(solution)/shard_map/ppermute | solution.py:32
  519.1 49.7 %collective-permute-start.57 = (bf16[512,768]{1,0:T(8,128)(2,1)S(1)}, bf16[512,768]{1,0:T(8,128)(2,1)S(1)}, u32[]{:S(2)}, u32[]{:S(2)}) collective-permute-start(bf16[512,768]{1,0:T(8,128)(2,1)S(1)} %add_convert_fusion.13), channel_id=1, source_target_pairs={{0,2},{2,0},{1,3},{3,1},{4,6},{6,4},{5,7},{7,5},{8,10},{10,8},{9,1... | collective-permute-start | bytes 2359304 | tf_op jit(solution)/shard_map/ppermute | solution.py:32
  522.7 50.8 %collective-permute-start.79 = (bf16[1,2,96,1536]{3,2,1,0:T(8,128)(2,1)}, bf16[1,2,96,1536]{3,2,1,0:T(8,128)(2,1)S(1)}, u32[]{:S(2)}, u32[]{:S(2)}) collective-permute-start(bf16[1,2,96,1536]{3,2,1,0:T(8,128)(2,1)} %add_convert_fusion.22), channel_id=1, source_target_pairs={{0,8},{8,16},{16,24},{24,0},{1,9},{9,17},{17,25},{25,1},{2,10},{10... | collective-permute-start | bytes 1769480 | tf_op jit(solution)/shard_map/ppermute | solution.py:50
  531.2 43.1 %collective-permute-start.72 = (bf16[1,2,96,1536]{3,2,1,0:T(8,128)(2,1)}, bf16[1,2,96,1536]{3,2,1,0:T(8,128)(2,1)S(1)}, u32[]{:S(2)}, u32[]{:S(2)}) collective-permute-start(bf16[1,2,96,1536]{3,2,1,0:T(8,128)(2,1)} %add_convert_fusion.26), channel_id=1, source_target_pairs={{0,8},{8,16},{16,24},{24,0},{1,9},{9,17},{17,25},{25,1},{2,10},{10... | collective-permute-start | bytes 1769480 | tf_op jit(solution)/shard_map/ppermute | solution.py:50
  560.7 82.5 %collective-permute-start.53 = (bf16[1024,768]{1,0:T(8,128)(2,1)S(1)}, bf16[1024,768]{1,0:T(8,128)(2,1)S(1)}, u32[]{:S(2)}, u32[]{:S(2)}) collective-permute-start(bf16[1024,768]{1,0:T(8,128)(2,1)S(1)} %fusion.54), channel_id=1, source_target_pairs={{0,2},{2,0},{1,3},{3,1},{4,6},{6,4},{5,7},{7,5},{8,10},{10,8},{9,1... | collective-permute-start | bytes 4718600 | tf_op jit(solution)/shard_map/ppermute | solution.py:32
  568.8 181.9 %collective-permute-start.83 = (bf16[4,1,96,3072]{3,2,1,0:T(8,128)(2,1)}, bf16[4,1,96,3072]{3,2,1,0:T(8,128)(2,1)}, u32[]{:S(2)}, u32[]{:S(2)}) collective-permute-start(bf16[4,1,96,3072]{3,2,1,0:T(8,128)(2,1)} %constant_dynamic-slice_fusion.4), channel_id=1, source_target_pairs={{0,4},{4,0},{1,5},{5,1},{2,6},{6,2},{3,7},{7,3},{8,12},{12,8},{9,1... | collective-permute-start | bytes 7077896 | tf_op jit(solution)/shard_map/ppermute | solution.py:98
  574.4 54.1 %collective-permute-start.80 = (bf16[1,1,96,1536]{3,2,1,0:T(8,128)(2,1)S(1)}, bf16[1,1,96,1536]{3,2,1,0:T(8,128)(2,1)S(1)}, u32[]{:S(2)}, u32[]{:S(2)}) collective-permute-start(bf16[1,1,96,1536]{3,2,1,0:T(8,128)(2,1)S(1)} %constant_dynamic-slice_fusion.5), channel_id=1, source_target_pairs={{0,4},{4,0},{1,5},{5,1},{2,6},{6,2},{3,7},{7,3},{8,12},{12,8},{9,1... | collective-permute-start | bytes 884744 | tf_op jit(solution)/shard_map/ppermute | solution.py:98
  575.1 54.8 %collective-permute-start.73 = (bf16[1,2,96,1536]{3,2,1,0:T(8,128)(2,1)S(1)}, bf16[1,2,96,1536]{3,2,1,0:T(8,128)(2,1)S(1)}, u32[]{:S(2)}, u32[]{:S(2)}) collective-permute-start(bf16[1,2,96,1536]{3,2,1,0:T(8,128)(2,1)S(1)} %add_convert_fusion.25), channel_id=1, source_target_pairs={{0,8},{8,16},{16,24},{24,0},{1,9},{9,17},{17,25},{25,1},{2,10},{10... | collective-permute-start | bytes 1769480 | tf_op jit(solution)/shard_map/ppermute | solution.py:50
  638.7 193.0 %collective-permute-start.82 = (f32[48,1536]{1,0:T(8,128)}, f32[48,1536]{1,0:T(8,128)}, u32[]{:S(2)}, u32[]{:S(2)}) collective-permute-start(f32[48,1536]{1,0:T(8,128)} %dynamic-slice_bitcast_fusion.2), channel_id=1, source_target_pairs={{0,2},{3,1},{4,6},{7,5},{8,10},{11,9},{12,14},{15,13},{16,18},{19,... | collective-permute-start | bytes 884744 | tf_op jit(solution)/shard_map/ppermute | solution.py:135
  641.4 47.9 %collective-permute-start.75 = (bf16[1,1,96,1536]{3,2,1,0:T(8,128)(2,1)}, bf16[1,1,96,1536]{3,2,1,0:T(8,128)(2,1)}, u32[]{:S(2)}, u32[]{:S(2)}) collective-permute-start(bf16[1,1,96,1536]{3,2,1,0:T(8,128)(2,1)} %add_convert_fusion.28), channel_id=1, source_target_pairs={{1,0},{2,3},{5,4},{6,7},{9,8},{10,11},{13,12},{14,15},{17,16},{18,... | collective-permute-start | bytes 884744 | tf_op jit(solution)/shard_map/ppermute | solution.py:92
  691.2 141.7 %collective-permute-start.76 = (f32[48,1536]{1,0:T(8,128)}, f32[48,1536]{1,0:T(8,128)}, u32[]{:S(2)}, u32[]{:S(2)}) collective-permute-start(f32[48,1536]{1,0:T(8,128)} %dynamic-slice_bitcast_fusion.3), channel_id=1, source_target_pairs={{0,2},{3,1},{4,6},{7,5},{8,10},{11,9},{12,14},{15,13},{16,18},{19,... | collective-permute-start | bytes 884744 | tf_op jit(solution)/shard_map/ppermute | solution.py:135
  737.4 69.2 %collective-permute-start.54 = (bf16[1024,768]{1,0:T(8,128)(2,1)S(1)}, bf16[1024,768]{1,0:T(8,128)(2,1)S(1)}, u32[]{:S(2)}, u32[]{:S(2)}) collective-permute-start(bf16[1024,768]{1,0:T(8,128)(2,1)S(1)} %add_convert_fusion.5), channel_id=1, source_target_pairs={{0,2},{2,0},{1,3},{3,1},{4,6},{6,4},{5,7},{7,5},{8,10},{10,8},{9,1... | collective-permute-start | bytes 4718600 | tf_op jit(solution)/shard_map/ppermute | solution.py:32
  749.0 97.3 %collective-permute-start.90 = (bf16[4,1,96,3072]{3,2,1,0:T(8,128)(2,1)}, bf16[4,1,96,3072]{3,2,1,0:T(8,128)(2,1)}, u32[]{:S(2)}, u32[]{:S(2)}) collective-permute-start(bf16[4,1,96,3072]{3,2,1,0:T(8,128)(2,1)} %constant_dynamic-slice_fusion.2), channel_id=1, source_target_pairs={{0,4},{4,0},{1,5},{5,1},{2,6},{6,2},{3,7},{7,3},{8,12},{12,8},{9,1... | collective-permute-start | bytes 7077896 | tf_op jit(solution)/shard_map/ppermute | solution.py:98
  750.7 54.5 %collective-permute-start.68 = (bf16[1,1,96,768]{3,2,1,0:T(8,128)(2,1)S(1)}, bf16[1,1,96,768]{3,2,1,0:T(8,128)(2,1)S(1)}, u32[]{:S(2)}, u32[]{:S(2)}) collective-permute-start(bf16[1,1,96,768]{3,2,1,0:T(8,128)(2,1)S(1)} %constant_dynamic-slice_fusion.9), channel_id=1, source_target_pairs={{0,4},{4,0},{1,5},{5,1},{2,6},{6,2},{3,7},{7,3},{8,12},{12,8},{9,1... | collective-permute-start | bytes 442376 | tf_op jit(solution)/shard_map/ppermute | solution.py:98
  (253 other events, 5673.6 us)

commit v2 on v1

--- a/solution.py
+++ b/solution.py
@@ -1,6 +1,10 @@
+import functools
+
 import jax
 import jax.numpy as jnp
 from jax import lax
+from jax.experimental import pallas as pl
+from jax.experimental.pallas import tpu as pltpu
 from jax.sharding import Mesh
 from jax.sharding import PartitionSpec as P
 
@@ -11,6 +15,7 @@
 masked_score = -1e30
 low = jnp.bfloat16
 wide = jnp.float32
+MESH = pl.DeviceIdType.MESH
 
 
 def gelu_exact(values):
@@ -149,6 +154,385 @@
     return values + lax.ppermute(values, "x", [(0, 1), (1, 0)])
 
 
+def column_cuts(columns):
+    tiles = columns // 128
+    first = (tiles * 42 + 50) // 100
+    second = (tiles * 36 + 50) // 100
+    edges = [0, first * 128, (first + second) * 128, columns]
+    return list(zip(edges[:-1], edges[1:]))
+
+
+class Place:
+    def __init__(self):
+        self.z, self.y, self.c, self.x = (lax.axis_index(name) for name in "zycx")
+        self.holds = self.c == self.x
+
+    def block(self, which):
+        back, same_y = which
+        z = lax.rem(self.z + 4 - back, 4)
+        return z * 2 + (self.y if same_y else 1 - self.y)
+
+    def target(self, axis):
+        if axis == "z":
+            return {"z": lax.rem(self.z + 1, 4)}
+        if axis == "z_back":
+            return {"z": lax.rem(self.z + 3, 4)}
+        return {axis: 1 - getattr(self, axis)}
+
+
+def greet(place):
+    barrier = pltpu.get_barrier_semaphore()
+    for axis in ("c", "x", "y", "z", "z_back"):
+        pl.semaphore_signal(
+            barrier, inc=1, device_id=place.target(axis), device_id_type=MESH
+        )
+    pl.semaphore_wait(barrier, 5)
+
+
+def gather_kernel(own_ref, out_ref, local_sem, send_sems, recv_sems):
+    place = Place()
+    rows = own_ref.shape[0]
+    cuts = column_cuts(own_ref.shape[1])
+    holds = place.holds
+    greet(place)
+    own_block = place.block((0, True))
+    own_rows = out_ref.at[own_block, pl.ds(place.c * rows, rows), :]
+    to_other = pltpu.make_async_remote_copy(
+        src_ref=own_ref,
+        dst_ref=own_rows,
+        send_sem=send_sems.at[72],
+        recv_sem=recv_sems.at[24],
+        device_id=place.target("c"),
+        device_id_type=MESH,
+    )
+    to_self = pltpu.make_async_copy(own_ref, own_rows, local_sem)
+    pl.when(jnp.logical_not(holds))(lambda: to_other.start())
+
+    @pl.when(holds)
+    def _():
+        to_self.start()
+        to_self.wait()
+        to_other.wait_recv()
+
+    pending = []
+
+    def copy(group, which, axis):
+        begin, end = cuts[group]
+        block = place.block(which)
+        piece = out_ref.at[block, :, pl.ds(begin, end - begin)]
+        number = {"z": 0, "y": 1, "x": 2}[axis]
+        return pltpu.make_async_remote_copy(
+            src_ref=piece,
+            dst_ref=piece,
+            send_sem=send_sems.at[(group * 8 + block) * 3 + number],
+            recv_sem=recv_sems.at[group * 8 + block],
+            device_id=place.target(axis),
+            device_id_type=MESH,
+        )
+
+    def send(group, which, axis, who):
+        copy(group, which, axis).start()
+        pending.append((functools.partial(copy, group, which, axis), who))
+
+    def arrive(group, block):
+        copy(group, block, "x").wait_recv()
+
+    here, there = (lambda back: (back, True)), (lambda back: (back, False))
+    first, second, third = 0, 1, 2
+
+    @pl.when(holds)
+    def _():
+        send(first, here(0), "x", True)
+        send(second, here(0), "y", True)
+        send(third, here(0), "z", True)
+        send(third, here(0), "y", True)
+        send(third, here(0), "x", True)
+        send(first, here(0), "z", True)
+        send(first, here(0), "y", True)
+        send(second, here(0), "z", True)
+        send(second, here(0), "x", True)
+
+    @pl.when(jnp.logical_not(holds))
+    def _():
+        arrive(third, here(0))
+        send(third, here(0), "z", False)
+        send(third, here(0), "y", False)
+
+    for back in range(1, 5):
+
+        @pl.when(holds)
+        def _():
+            if back < 4:
+                arrive(first, here(back))
+                if back < 3:
+                    send(first, here(back), "z", True)
+                send(first, here(back), "y", True)
+                send(first, here(back), "x", True)
+                arrive(second, here(back))
+                if back < 3:
+                    send(second, here(back), "z", True)
+                send(second, here(back), "x", True)
+                send(second, here(back), "y", True)
+            arrive(first, there(back - 1))
+            send(first, there(back - 1), "x", True)
+
+        @pl.when(jnp.logical_not(holds))
+        def _():
+            arrive(second, here(back - 1))
+            send(second, here(back - 1), "y", False)
+
+        if back < 4:
+            if back == 1:
+                arrive(third, there(0))
+                send(third, there(0), "z", None)
+            arrive(third, here(back))
+            if back < 3:
+                send(third, here(back), "z", None)
+            arrive(third, there(back))
+            if back < 3:
+                send(third, there(back), "z", None)
+    for back in range(4):
+        arrive(second, there(back))
+
+    @pl.when(jnp.logical_not(holds))
+    def _():
+        for back in range(4):
+            arrive(first, here(back))
+            arrive(first, there(back))
+        to_other.wait_send()
+        for one, who in pending:
+            if who is False:
+                one().wait_send()
+
+    @pl.when(holds)
+    def _():
+        for one, who in pending:
+            if who is True:
+                one().wait_send()
+
+    for one, who in pending:
+        if who is None:
+            one().wait_send()
+
+
+def gather_all(own):
+    rows, columns = own.shape
+    return pl.pallas_call(
+        gather_kernel,
+        out_shape=jax.ShapeDtypeStruct((8, 2 * rows, columns), own.dtype),
+        in_specs=[pl.BlockSpec(memory_space=pl.ANY)],
+        out_specs=pl.BlockSpec(memory_space=pl.ANY),
+        scratch_shapes=[
+            pltpu.SemaphoreType.DMA,
+            pltpu.SemaphoreType.DMA((73,)),
+            pltpu.SemaphoreType.DMA((25,)),
+        ],
+        compiler_params=pltpu.CompilerParams(collective_id=0, has_side_effects=True),
+        name="gather_weights",
+    )(own)
+
+
+def scatter_kernel(widths, *refs):
+    count = len(widths)
+    grads = refs[:count]
+    out_ref, total, final = refs[count : count + 3]
+    buffers = refs[count + 3 : count + 6]
+    load_sems, send_sems, recv_sems, end_sem = refs[count + 6 :]
+    place = Place()
+    holds = place.holds
+    rows = total.shape[1]
+    columns = total.shape[2]
+    cuts = column_cuts(columns)
+    loads = []
+    begin = 0
+    for number, width in enumerate(widths):
+        one = pltpu.make_async_copy(
+            grads[number], total.at[:, :, pl.ds(begin, width)], load_sems.at[number]
+        )
+        one.start()
+        loads.append(one)
+        begin += width
+    greet(place)
+    for one in loads:
+        one.wait()
+    here, there = (lambda back: (back, True)), (lambda back: (back, False))
+    pending = []
+    slots = {}
+
+    def copy(group, which, slot, axis):
+        begin, end = cuts[group]
+        block = place.block(which)
+        return pltpu.make_async_remote_copy(
+            src_ref=total.at[block, :, pl.ds(begin, end - begin)],
+            dst_ref=buffers[group].at[slot],
+            send_sem=send_sems.at[group * 16 + slot],
+            recv_sem=recv_sems.at[group * 16 + slot],
+            device_id=place.target(axis),
+            device_id_type=MESH,
+        )
+
+    def send(group, which, slot, axis, who):
+        copy(group, which, slot, axis).start()
+        pending.append((functools.partial(copy, group, which, slot, axis), who))
+
+    def add(group, which, slot, last=False):
+        copy(group, which, slot, "x").wait_recv()
+        block = place.block(which)
+        begin, end = cuts[group]
+        part = pl.ds(begin, end - begin)
+
+        @pl.loop(0, rows // 16)
+        def _(step):
+            at = pl.ds(pl.multiple_of(step * 16, 16), 16)
+            held = total[block, at, part]
+            came = buffers[group][slot, at, :]
+            if last:
+                final[at, part] = held.astype(wide) + came.astype(wide)
+            else:
+                total[block, at, part] = held + came
+
+    first, second, third = 0, 1, 2
+    for which, offset in ((there, 3), (here, 0)):
+        send(third, which(3), offset + 2, "z_back", None)
+    for back in (3, 2, 1, 0):
+        send(second, there(back), back, "y", None)
+
+    @pl.when(jnp.logical_not(holds))
+    def _():
+        for back in (3, 2, 1, 0):
+            send(first, there(back), 4 + back, "x", False)
+            send(first, here(back), back, "x", False)
+
+    for back in (3, 2, 1, 0):
+        if back < 3:
+            for which, offset in ((there, 3), (here, 0)):
+                add(third, which(back), offset + back)
+                if back > 0:
+                    send(third, which(back), offset + back - 1, "z_back", None)
+                elif offset == 3:
+                    send(third, which(0), 6, "y", None)
+        add(second, here(back), back)
+
+        @pl.when(jnp.logical_not(holds))
+        def _():
+            send(second, here(back), 4 + back, "x", False)
+
+        @pl.when(holds)
+        def _():
+            add(first, there(back), 4 + back)
+            send(first, there(back), 8 + back, "y", True)
+            add(first, here(back), back)
+            add(first, here(back), 8 + back, last=False)
+            if back < 3:
+                add(first, here(back), 12 + back, last=back == 0)
+            if back > 0:
+                send(first, here(back), 12 + back - 1, "z_back", True)
+
+    add(third, here(0), 6)
+
+    @pl.when(jnp.logical_not(holds))
+    def _():
+        send(third, here(0), 7, "x", False)
+
+    end_copy = pltpu.make_async_remote_copy(
+        src_ref=final.at[pl.ds((1 - place.c) * (rows // 2), rows // 2), :],
+        dst_ref=out_ref,
+        send_sem=end_sem.at[0],
+        recv_sem=end_sem.at[1],
+        device_id=place.target("c"),
+        device_id_type=MESH,
+    )
+    keep_copy = pltpu.make_async_copy(
+        final.at[pl.ds(place.c * (rows // 2), rows // 2), :], out_ref, end_sem.at[2]
+    )
+
+    @pl.when(holds)
+    def _():
+        for back in (3, 2, 1, 0):
+            add(second, here(back), 4 + back)
+            if back < 3:
+                add(second, here(back), 8 + back, last=back == 0)
+            if back > 0:
+                send(second, here(back), 8 + back - 1, "z_back", True)
+        add(third, here(0), 7, last=True)
+        end_copy.start()
+        keep_copy.start()
+        keep_copy.wait()
+        end_copy.wait_send()
+        for one, who in pending:
+            if who is True:
+                one().wait_send()
+
+    @pl.when(jnp.logical_not(holds))
+    def _():
+        end_copy.wait_recv()
+        for one, who in pending:
+            if who is False:
+                one().wait_send()
+
+    for one, who in pending:
+        if who is None:
+            one().wait_send()
+
+
+def scatter_all(parts):
+    depth = parts[0].shape[0]
+    widths = [part.shape[1] for part in parts]
+    columns = sum(widths)
+    rows = depth // 8
+    cuts = column_cuts(columns)
+    return pl.pallas_call(
+        functools.partial(scatter_kernel, widths),
+        out_shape=jax.ShapeDtypeStruct((rows // 2, columns), wide),
+        in_specs=[pl.BlockSpec(memory_space=pl.ANY)] * len(parts),
+        out_specs=pl.BlockSpec(memory_space=pl.ANY),
+        scratch_shapes=[
+            pltpu.VMEM((8, rows, columns), low),
+            pltpu.VMEM((rows, columns), wide),
+            pltpu.VMEM((15, rows, cuts[0][1] - cuts[0][0]), low),
+            pltpu.VMEM((11, rows, cuts[1][1] - cuts[1][0]), low),
+            pltpu.VMEM((8, rows, cuts[2][1] - cuts[2][0]), low),
+            pltpu.SemaphoreType.DMA((len(parts),)),
+            pltpu.SemaphoreType.DMA((48,)),
+            pltpu.SemaphoreType.DMA((48,)),
+            pltpu.SemaphoreType.DMA((3,)),
+        ],
+        compiler_params=pltpu.CompilerParams(
+            collective_id=1, has_side_effects=True, vmem_limit_bytes=56 << 20
+        ),
+        name="scatter_gradients",
+    )(*[part.reshape(8, rows, part.shape[1]) for part in parts])
+
+
+def fits_kernels():
+    return lax.axis_size("z") == 4
+
+
+def gather_groups(groups):
+    if fits_kernels():
+        whole = gather_all(jnp.concatenate(groups, axis=1))
+        whole = whole.reshape(-1, whole.shape[2])
+        pieces = []
+        begin = 0
+        for group in groups:
+            pieces.append(whole[:, begin : begin + group.shape[1]])
+            begin += group.shape[1]
+        return pieces
+    return [gather_weights(group, "zyx") for group in groups]
+
+
+def scatter_groups(groups):
+    if fits_kernels():
+        whole = scatter_all(groups)
+        pieces = []
+        begin = 0
+        for group in groups:
+            pieces.append(whole[:, begin : begin + group.shape[1]])
+            begin += group.shape[1]
+        return pieces
+    return [scatter_gradient(group, "xyz") for group in groups]
+
+
 def project(left_side, right_side):
     return jnp.dot(left_side, right_side, preferred_element_type=wide)
 
@@ -342,13 +726,9 @@
     target_all = both_halves(swap_chips(target_embed[0]))
     cotangent_all = both_halves(swap_chips(out_cotangent[0]))
 
-    encoder_attention = gather_weights(attention_group(0), "zyx")
-    decoder_attention = gather_weights(attention_group(1), "xyz")
-    encoder_feed = gather_weights(feed_group(0), "zxy")
-    cross_attention = gather_weights(attention_group(2), "zyx")
-    decoder_feed_first = gather_weights(feed_group(1)[:, :half_units], "zyx")
-    decoder_feed_second = gather_weights(feed_group(1)[:, half_units:], "xyz")
-    decoder_feed = jnp.concatenate([decoder_feed_first, decoder_feed_second], axis=1)
+    encoder_attention, decoder_attention, cross_attention, encoder_feed, decoder_feed = gather_groups(
+        [attention_group(0), attention_group(1), attention_group(2), feed_group(0), feed_group(1)]
+    )
 
     start_rows = jnp.where(
         (flags_all == 1)[:, None],
@@ -381,11 +761,9 @@
     grad_two, decoder_feed_terms, vector_parts[10:12] = feed_backward(
         grad_three, decoder_two, vector_params, 10, kept_fifth, decoder_feed
     )
-    decoder_feed_grad = scatter_gradient(decoder_feed_terms, "xyz")
     cross_terms, from_query, from_source = attention_backward(
         grad_two, kept_fourth, cross_attention, source_valid, False
     )
-    cross_grad = scatter_gradient(cross_terms, "zyx")
     grad_memory, vector_parts[4], vector_parts[5] = norm_backward(
         encoder_final, vector_params, 4, core_sum(from_source)
     )
@@ -396,11 +774,9 @@
     grad_mid, encoder_feed_terms, vector_parts[2:4] = feed_backward(
         grad_memory, encoder_mid, vector_params, 2, kept_second, encoder_feed
     )
-    encoder_feed_grad = scatter_gradient(encoder_feed_terms, "yxz")
     decoder_terms, from_query, from_source = attention_backward(
         grad_one, kept_third, decoder_attention, target_valid, True
     )
-    decoder_grad = scatter_gradient(decoder_terms, "zyx")
     grad_input, vector_parts[6], vector_parts[7] = norm_backward(
         target_rows, vector_params, 6, core_sum(from_query + from_source)
     )
@@ -419,12 +795,19 @@
 
     vector_terms = jnp.stack(vector_parts, axis=1).astype(low)
     vector_terms = jnp.pad(vector_terms, ((0, 0), (0, 128 - vector_terms.shape[1])))
-    tail_first = scatter_gradient(
-        jnp.concatenate([encoder_terms[:, : 2 * half_width], vector_terms], axis=1), "xyz"
-    )
-    tail_second = scatter_gradient(encoder_terms[:, 2 * half_width :], "zyx")
-    vector_grad = tail_first[:, 2 * half_width : 2 * half_width + 14].T
-    encoder_grad = jnp.concatenate([tail_first[:, : 2 * half_width], tail_second], axis=1)
+    (encoder_grad, decoder_grad, cross_grad, encoder_feed_grad, decoder_feed_grad, vector_grad) = (
+        scatter_groups(
+            [
+                encoder_terms,
+                decoder_terms,
+                cross_terms,
+                encoder_feed_terms,
+                decoder_feed_terms,
+                vector_terms,
+            ]
+        )
+    )
+    vector_grad = vector_grad[:, :14].T
 
     def as_matrices(rows, count):
         return rows.reshape(local_rows, count, -1).transpose(1, 0, 2)

time: 1010 us -> 800 us (0.79)
  waiting for transfers between devices: 443 us -> 13.5 us
  Pallas kernels: 0 us -> 353 us
  starting transfers between devices: 138 us -> 45.2 us
  local copies, waits for them, and re-layouts: 74.3 us -> 43.1 us
  other arithmetic: 149 us -> 120 us
  matrix products: 193 us -> 214 us
    ppermute x72 -> x0, waiting for transfers between devices: 430 us -> none  [the longest x36 207 us: ring_next(): return lax.ppermute(array, 'z', [(i, (i + 1) % size) for i in range(size)])]
    pallas_call x0 -> x2, Pallas kernels: none -> 353 us  [the longest x1 179 us: scatter_all(): pl.pallas_call(functools.partial(scatter_kernel, widths), out_shape=jax.S...]
    ppermute x72 -> x0, starting transfers between devices: 88.6 us -> none  [the longest x6 21 us: spread_blocks(): received = lax.ppermute(held, ('c', 'x'), [(0, 1), (3, 2)])]
    convert_element_type x24 -> x0, other arithmetic: 24.3 us -> none  [the longest x3 9.95 us: reduce_blocks(): held = (held.astype(wide) + received.astype(wide)).astype(kind)]
    dot_general x16, matrix products: 49.2 us -> 65.9 us  [project(): return jnp.dot(left_side, right_side, preferred_element_type=wide)]
    unnamed x373 -> x326, local copies, waits for them, and re-layouts: 29.4 us -> 17.5 us
  transfers between devices with their start and end apart: 105 -> 33, of which waited for: 45 -> 9; matrix products, arithmetic and copies ran while one was open for 37% -> 39% of each run, Pallas kernels for 0% -> 22%
where the time goes in v2:
time: 800 us; the launch traced here: 793 us
  Pallas kernels  353 us (44%)
  matrix products  214 us (27%)
  other arithmetic  120 us (15%)
  starting transfers between devices  45.2 us (6%)
  local copies, waits for them, and re-layouts  43.1 us (5%)
  waiting for transfers between devices  13.5 us (2%)
    pallas_call x1, Pallas kernels, scatter_all(): pl.pallas_call(functools.partial(scatter_kernel, widths), out_shape=jax.S...  179 us
    pallas_call x1, Pallas kernels, gather_all(): pl.pallas_call(gather_kernel, out_shape=jax.ShapeDtypeStruct((8, 2 * rows...  174 us
    dot_general x16, matrix products, project(): return jnp.dot(left_side, right_side, preferred_element_type=wide)  65.9 us
    dot_general x16, matrix products, project_back(): jnp.einsum('tx,dx->td', left_side, right_side, preferred_element_type=wide)  46.6 us
    convert_element_type x3, other arithmetic, attend_backward(): grad_scores = (weights * (grad_weights - row_dot)).astype(low)  26.2 us
    ppermute x8, starting transfers between devices, swap_chips(): return lax.ppermute(array, ('c', 'x'), [(0, 0), (1, 2), (2, 1), (3, 3)])  23.8 us
    dot_general x3, matrix products, attend_backward(): jnp.einsum('qhd,khd->hqk', grad_heads, value_heads, preferred_element_typ...  23.7 us
    dot_general x3, matrix products, attend_forward(): jnp.einsum('hqk,khd->qhd', weights_low, value_heads, preferred_element_ty...  19.3 us
  transfers between devices with their start and end apart: 33, of which 9 were waited for; matrix products, arithmetic and copies ran while one was open for 39% of the time, Pallas kernels for 22%

profile of v2, /device:TPU:0, one launch (start us, length us, event | category | flops | bytes accessed | tf_op | source)
XLA Modules:
  0.0 792.5 jit_solution(8192931932453892158)
XLA Ops:
  6.9 4.5 collective-permute-start.13
  16.6 6.2 collective-permute-start.5
  23.5 174.1 %gather_weights.1 = bf16[8,96,10752]{2,1,0:T(8,128)(2,1)} custom-call(bf16[48,10752]{1,0:T(8,128)(2,1)} %copy-done.48), custom_call_target="tpu_custom_call" | custom-call | tf_op jit(solution)/shard_map/gather_weights/pallas_call | solution.py:320
  204.3 3.8 fusion.176
  224.5 6.1 fusion.175
  234.4 4.5 copy-done
  238.9 10.8 %fusion.87 = bf16[6,64,1024]{2,1,0:T(8,128)(2,1)S(1)} fusion(bf16[1024,6,64]{0,2,1:T(8,128)(2,1)} %bitcast.293, f32[6,1024,1024]{1,2,0:T(8,128)} %copy-done, f32[6,1024]{1,0:T(8,128)S(1)} %fusion, f32[6,1024]{1,0:T(8,128)S(1)} %get-tuple-element.146), kind=kOutput, calls=%fused_computation.183 | convolution fusion | flops 824573952 | bytes 26787840 | tf_op jit(solution)/shard_map/hqk,khd->qhd/dot_general | solution.py:573
  254.1 3.8 fusion.18
  258.0 4.1 fusion.97
  268.9 20.2 %multiply_convert_fusion.3 = (bf16[1024,1536]{1,0:T(8,128)(2,1)S(1)}, f32[1024,1536]{1,0:T(8,128)}, f32[1024,1536]{1,0:T(8,128)}) fusion(bf16[768,10752]{1,0:T(8,128)(2,1)} %bitcast.213, f32[1024,768]{1,0:T(8,128)S(1)} %get-tuple-element.113, f32[768]{0:T(1024)S(1)} %copy-done.142, f32[768]{0:T(1024)S(1)} %copy-done.109, f32[1024]{0:T(1024)S(1)} %fusion.141, ...), kind=kOutput, calls=%fused_computation.27 | convolution fusion | flops 2522087424 | bytes 21248000 | tf_op jit(solution)/shard_map/dot_general | solution.py:537
  289.1 6.8 fusion.66
  317.9 4.4 fusion.98
  327.2 9.5 %multiply_convert_fusion.4 = (bf16[512,1536]{1,0:T(8,128)(2,1)S(1)}, f32[512,1536]{1,0:T(8,128)S(1)}, f32[512,1536]{1,0:T(8,128)S(1)}) fusion(bf16[768,10752]{1,0:T(8,128)(2,1)} %bitcast.219, f32[512,768]{1,0:T(8,128)S(1)} %get-tuple-element.105, f32[768]{0:T(1024)S(1)} %copy-done.144, f32[768]{0:T(1024)S(1)} %copy-done.111, f32[512]{0:T(512)S(1)} %fusion.148, ...), kind=kOutput, calls=%fused_computation.77 | convolution fusion | flops 1261043712 | bytes 11806720 | tf_op jit(solution)/shard_map/dot_general | solution.py:537
  336.7 3.8 add_convert_fusion.3
  345.8 4.0 fusion.78
  353.0 4.3 pad_maximum_fusion.1
  360.8 6.8 multiply_reduce_fusion.1
  370.8 7.2 multiply_convert_fusion.1
  393.2 4.5 collective-permute-start.12
  401.6 4.7 copy.75
  431.5 4.9 copy.74
  446.2 7.1 add_convert_fusion
  453.3 4.3 fusion.63
  479.9 11.2 %fusion.84 = bf16[6,64,1024]{2,1,0:T(8,128)(2,1)} fusion(bf16[1024,6,64]{0,2,1:T(8,128)(2,1)S(1)} %bitcast.242, f32[6,1024,1024]{1,2,0:T(8,128)} %copy-done, f32[6,1024]{1,0:T(8,128)S(1)} %copy-done.54), kind=kOutput, calls=%fused_computation.179 | convolution fusion | flops 818282496 | bytes 26763264 | tf_op jit(solution)/shard_map/hqk,qhd->khd/dot_general | solution.py:591
  491.1 15.5 %multiply_reduce_fusion = (f32[6,1024]{1,0:T(8,128)S(1)}, f32[6,1024,1024]{1,2,0:T(8,128)}) fusion(f32[6,1024,1024]{1,2,0:T(8,128)} %copy-done, f32[6,1024]{1,0:T(8,128)S(1)} %copy-done.54, bf16[1024,6,64]{0,2,1:T(8,128)(2,1)S(1)} %bitcast.243, bf16[1024,6,64]{0,2,1:T(8,128)(2,1)S(1)} %bitcast.294), kind=kOutput, calls=%fused_computation.1 | convolution fusion | flops 824174592 | bytes 51953664 | tf_op jit(solution)/shard_map/qhd,khd->hqk/dot_general | solution.py:586
  506.7 17.1 %multiply_convert_fusion = bf16[6,1024,1024]{1,2,0:T(8,128)(2,1)S(1)} fusion(f32[6,1024,1024]{1,2,0:T(8,128)} %get-tuple-element.157, f32[6,1024,1024]{1,2,0:T(8,128)} %copy-done, f32[6,1024]{1,0:T(8,128)S(1)} %get-tuple-element.156, f32[6,1024]{1,0:T(8,128)S(1)} %copy-done.54), kind=kLoop, calls=%fused_computation | loop fusion | flops 25165824 | bytes 62963712 | tf_op jit(solution)/shard_map/convert_element_type | solution.py:588
  523.8 4.8 multiply_convert_fusion.5
  548.9 4.3 copy.73
  553.3 4.6 multiply_reduce_fusion.5
  557.9 4.7 fusion.163
  565.8 179.1 %scatter_gradients.1 = f32[48,10880]{1,0:T(8,128)} custom-call(bf16[8,96,1536]{2,1,0:T(8,128)(2,1)} %bitcast.241, bf16[8,96,1536]{2,1,0:T(8,128)(2,1)} %bitcast.240, bf16[8,96,1536]{2,1,0:T(8,128)(2,1)} %bitcast.239, bf16[8,96,3072]{2,1,0:T(8,128)(2,1)} %bitcast.238, bf16[8,96,3072]{2,1,0:T(8,128)(2,1)} %bitcast.237, bf16[8,96,128]{2,1,0:T(8,128)(2,1)} %bitcast.286), custom_call_target="tpu_custom_call" | custom-call | tf_op jit(solution)/shard_map/scatter_gradients/pallas_call | solution.py:484
  776.3 7.4 collective-permute-start.19
  (586 shorter events, 229.7 us)
Async XLA Ops:
  0.7 16.0 %collective-permute-start.4 = (s32[512]{0:T(512)}, s32[512]{0:T(512)S(1)}, u32[]{:S(2)}, u32[]{:S(2)}) collective-permute-start(s32[512]{0:T(512)} %bitcast.304), channel_id=1, source_target_pairs={{0,0},{1,2},{2,1},{3,3},{4,4},{5,6},{6,5},{7,7},{8,8},{9,10},{10,9... | collective-permute-start | bytes 6152 | tf_op jit(solution)/shard_map/ppermute | solution.py:33
  2.1 198.5 %collective-permute-start.6 = (bf16[512,768]{1,0:T(8,128)(2,1)}, bf16[512,768]{1,0:T(8,128)(2,1)S(1)}, u32[]{:S(2)}, u32[]{:S(2)}) collective-permute-start(bf16[512,768]{1,0:T(8,128)(2,1)} %bitcast.306), channel_id=1, source_target_pairs={{0,0},{1,2},{2,1},{3,3},{4,4},{5,6},{6,5},{7,7},{8,8},{9,10},{10,9... | collective-permute-start | bytes 2359304 | tf_op jit(solution)/shard_map/ppermute | solution.py:33
  4.6 193.1 %collective-permute-start.2 = (s32[1536]{0:T(1024)S(1)}, s32[1536]{0:T(1024)S(1)}, u32[]{:S(2)}, u32[]{:S(2)}) collective-permute-start(s32[1536]{0:T(1024)S(1)} %pad_add_fusion), channel_id=1, source_target_pairs={{0,0},{1,2},{2,1},{3,3},{4,4},{5,6},{6,5},{7,7},{8,8},{9,10},{10,9... | collective-permute-start | bytes 18440 | tf_op jit(solution)/shard_map/ppermute | solution.py:33
  5.3 192.5 %collective-permute-start = (bf16[256,768]{1,0:T(8,128)(2,1)}, bf16[256,768]{1,0:T(8,128)(2,1)S(1)}, u32[]{:S(2)}, u32[]{:S(2)}) collective-permute-start(bf16[256,768]{1,0:T(8,128)(2,1)} %bitcast.307), channel_id=1, source_target_pairs={{0,0},{1,2},{2,1},{3,3},{4,4},{5,6},{6,5},{7,7},{8,8},{9,10},{10,9... | collective-permute-start | bytes 1179656 | tf_op jit(solution)/shard_map/ppermute | solution.py:33
  6.9 292.3 %collective-permute-start.13 = (bf16[256,768]{1,0:T(8,128)(2,1)}, bf16[256,768]{1,0:T(8,128)(2,1)}, u32[]{:S(2)}, u32[]{:S(2)}) collective-permute-start(bf16[256,768]{1,0:T(8,128)(2,1)} %bitcast.308), channel_id=1, source_target_pairs={{0,0},{1,2},{2,1},{3,3},{4,4},{5,6},{6,5},{7,7},{8,8},{9,10},{10,9... | collective-permute-start | bytes 1179656 | tf_op jit(solution)/shard_map/ppermute | solution.py:33
  16.6 181.1 %collective-permute-start.5 = (s32[512]{0:T(512)S(1)}, s32[512]{0:T(512)S(1)}, u32[]{:S(2)}, u32[]{:S(2)}) collective-permute-start(s32[512]{0:T(512)S(1)} %collective-permute-done.4), channel_id=1, source_target_pairs={{0,2},{2,0},{1,3},{3,1},{4,6},{6,4},{5,7},{7,5},{8,10},{10,8},{9,1... | collective-permute-start | bytes 6152 | tf_op jit(solution)/shard_map/ppermute | solution.py:37
  197.8 1.8 collective-permute-start.1
  200.6 7.5 collective-permute-start.7
  252.1 12.8 %collective-permute-start.8 = (bf16[1024,768]{1,0:T(8,128)(2,1)S(1)}, bf16[1024,768]{1,0:T(8,128)(2,1)S(1)}, u32[]{:S(2)}, u32[]{:S(2)}) collective-permute-start(bf16[1024,768]{1,0:T(8,128)(2,1)S(1)} %convolution_convert_fusion.4), channel_id=1, source_target_pairs={{0,2},{2,0},{1,3},{3,1},{4,6},{6,4},{5,7},{7,5},{8,10},{10,8},{9,1... | collective-permute-start | bytes 4718600 | tf_op jit(solution)/shard_map/ppermute | solution.py:37
  264.8 34.6 %collective-permute-start.3 = (bf16[512,768]{1,0:T(8,128)(2,1)}, bf16[512,768]{1,0:T(8,128)(2,1)}, u32[]{:S(2)}, u32[]{:S(2)}) collective-permute-start(bf16[512,768]{1,0:T(8,128)(2,1)} %convolution_convert_fusion.13), channel_id=1, source_target_pairs={{0,2},{2,0},{1,3},{3,1},{4,6},{6,4},{5,7},{7,5},{8,10},{10,8},{9,1... | collective-permute-start | bytes 2359304 | tf_op jit(solution)/shard_map/ppermute | solution.py:37
  295.9 8.3 %collective-permute-start.9 = (bf16[1024,768]{1,0:T(8,128)(2,1)}, bf16[1024,768]{1,0:T(8,128)(2,1)}, u32[]{:S(2)}, u32[]{:S(2)}) collective-permute-start(bf16[1024,768]{1,0:T(8,128)(2,1)} %fusion.66), channel_id=1, source_target_pairs={{0,2},{2,0},{1,3},{3,1},{4,6},{6,4},{5,7},{7,5},{8,10},{10,8},{9,1... | collective-permute-start | bytes 4718600 | tf_op jit(solution)/shard_map/ppermute | solution.py:37
  299.2 25.3 %collective-permute-start.14 = (bf16[256,768]{1,0:T(8,128)(2,1)}, bf16[256,768]{1,0:T(8,128)(2,1)S(1)}, u32[]{:S(2)}, u32[]{:S(2)}) collective-permute-start(bf16[256,768]{1,0:T(8,128)(2,1)} %collective-permute-done.13), channel_id=1, source_target_pairs={{0,2},{2,0},{1,3},{3,1},{4,6},{6,4},{5,7},{7,5},{8,10},{10,8},{9,1... | collective-permute-start | bytes 1179656 | tf_op jit(solution)/shard_map/ppermute | solution.py:37
  324.1 2.4 collective-permute-start.10
  345.4 11.9 %collective-permute-start.15 = (bf16[512,768]{1,0:T(8,128)(2,1)S(1)}, bf16[512,768]{1,0:T(8,128)(2,1)S(1)}, u32[]{:S(2)}, u32[]{:S(2)}) collective-permute-start(bf16[512,768]{1,0:T(8,128)(2,1)S(1)} %fusion.75), channel_id=1, source_target_pairs={{0,2},{2,0},{1,3},{3,1},{4,6},{6,4},{5,7},{7,5},{8,10},{10,8},{9,1... | collective-permute-start | bytes 2359304 | tf_op jit(solution)/shard_map/ppermute | solution.py:37
  349.8 41.4 %collective-permute-start.11 = (bf16[512,768]{1,0:T(8,128)(2,1)}, bf16[512,768]{1,0:T(8,128)(2,1)}, u32[]{:S(2)}, u32[]{:S(2)}) collective-permute-start(bf16[512,768]{1,0:T(8,128)(2,1)} %fusion.78), channel_id=1, source_target_pairs={{0,2},{2,0},{1,3},{3,1},{4,6},{6,4},{5,7},{7,5},{8,10},{10,8},{9,1... | collective-permute-start | bytes 2359304 | tf_op jit(solution)/shard_map/ppermute | solution.py:37
  383.9 22.4 %collective-permute-start.20 = (bf16[512,768]{1,0:T(8,128)(2,1)}, bf16[512,768]{1,0:T(8,128)(2,1)}, u32[]{:S(2)}, u32[]{:S(2)}) collective-permute-start(bf16[512,768]{1,0:T(8,128)(2,1)} %convolution_convert_fusion.11), channel_id=1, source_target_pairs={{0,2},{2,0},{1,3},{3,1},{4,6},{6,4},{5,7},{7,5},{8,10},{10,8},{9,1... | collective-permute-start | bytes 2359304 | tf_op jit(solution)/shard_map/ppermute | solution.py:37
  393.2 13.0 %collective-permute-start.12 = (bf16[256,768]{1,0:T(8,128)(2,1)}, bf16[256,768]{1,0:T(8,128)(2,1)}, u32[]{:S(2)}, u32[]{:S(2)}) collective-permute-start(bf16[256,768]{1,0:T(8,128)(2,1)} %fusion.102), channel_id=1, source_target_pairs={{0,0},{1,2},{2,1},{3,3},{4,4},{5,6},{6,5},{7,7},{8,8},{9,10},{10,9... | collective-permute-start | bytes 1179656 | tf_op jit(solution)/shard_map/ppermute | solution.py:33
  398.7 41.2 %collective-permute-start.16 = (bf16[1024,768]{1,0:T(8,128)(2,1)}, bf16[1024,768]{1,0:T(8,128)(2,1)}, u32[]{:S(2)}, u32[]{:S(2)}) collective-permute-start(bf16[1024,768]{1,0:T(8,128)(2,1)} %add_convert_fusion.2), channel_id=1, source_target_pairs={{0,2},{2,0},{1,3},{3,1},{4,6},{6,4},{5,7},{7,5},{8,10},{10,8},{9,1... | collective-permute-start | bytes 4718600 | tf_op jit(solution)/shard_map/ppermute | solution.py:37
  426.2 10.2 %collective-permute-start.21 = (bf16[512,768]{1,0:T(8,128)(2,1)}, bf16[512,768]{1,0:T(8,128)(2,1)}, u32[]{:S(2)}, u32[]{:S(2)}) collective-permute-start(bf16[512,768]{1,0:T(8,128)(2,1)} %add_convert_fusion.8), channel_id=1, source_target_pairs={{0,2},{2,0},{1,3},{3,1},{4,6},{6,4},{5,7},{7,5},{8,10},{10,8},{9,1... | collective-permute-start | bytes 2359304 | tf_op jit(solution)/shard_map/ppermute | solution.py:37
  457.7 14.6 %collective-permute-start.17 = (bf16[1024,768]{1,0:T(8,128)(2,1)S(1)}, bf16[1024,768]{1,0:T(8,128)(2,1)S(1)}, u32[]{:S(2)}, u32[]{:S(2)}) collective-permute-start(bf16[1024,768]{1,0:T(8,128)(2,1)S(1)} %fusion.63), channel_id=1, source_target_pairs={{0,2},{2,0},{1,3},{3,1},{4,6},{6,4},{5,7},{7,5},{8,10},{10,8},{9,1... | collective-permute-start | bytes 4718600 | tf_op jit(solution)/shard_map/ppermute | solution.py:37
  461.1 80.6 %collective-permute-start.22 = (bf16[256,768]{1,0:T(8,128)(2,1)}, bf16[256,768]{1,0:T(8,128)(2,1)S(1)}, u32[]{:S(2)}, u32[]{:S(2)}) collective-permute-start(bf16[256,768]{1,0:T(8,128)(2,1)} %fusion.101), channel_id=1, source_target_pairs={{0,0},{1,2},{2,1},{3,3},{4,4},{5,6},{6,5},{7,7},{8,8},{9,10},{10,9... | collective-permute-start | bytes 1179656 | tf_op jit(solution)/shard_map/ppermute | solution.py:33
  538.6 14.6 %collective-permute-start.18 = (bf16[1024,768]{1,0:T(8,128)(2,1)}, bf16[1024,768]{1,0:T(8,128)(2,1)}, u32[]{:S(2)}, u32[]{:S(2)}) collective-permute-start(bf16[1024,768]{1,0:T(8,128)(2,1)} %add_convert_fusion.1), channel_id=1, source_target_pairs={{0,2},{2,0},{1,3},{3,1},{4,6},{6,4},{5,7},{7,5},{8,10},{10,8},{9,1... | collective-permute-start | bytes 4718600 | tf_op jit(solution)/shard_map/ppermute | solution.py:37
  749.0 3.7 collective-permute-start.28
  752.8 1.3 collective-permute-start.29
  754.1 4.1 collective-permute-start.30
  758.3 4.1 collective-permute-start.31
  759.5 5.1 collective-permute-start.23
  762.4 21.4 %collective-permute-start.32 = (f32[10768]{0:T(1024)S(1)}, f32[10768]{0:T(1024)S(1)}, u32[]{:S(2)}, u32[]{:S(2)}) collective-permute-start(f32[10768]{0:T(1024)S(1)} %add.358), channel_id=1, source_target_pairs={{0,16},{16,0},{8,24},{24,8},{1,17},{17,1},{9,25},{25,9},{2,18},{18... | collective-permute-start | bytes 129224 | tf_op jit(solution)/shard_map/ppermute | solution.py:150
  765.8 3.5 collective-permute-start.25
  769.3 3.5 collective-permute-start.26
  772.9 10.9 %collective-permute-start.27 = (f32[32]{0:T(128)S(1)}, f32[32]{0:T(128)S(1)}, u32[]{:S(2)}, u32[]{:S(2)}) collective-permute-start(f32[32]{0:T(128)S(1)} %add.352), channel_id=1, source_target_pairs={{0,16},{16,0},{8,24},{24,8},{1,17},{17,1},{9,25},{25,9},{2,18},{18... | collective-permute-start | bytes 392 | tf_op jit(solution)/shard_map/ppermute | solution.py:150
  776.3 11.7 %collective-permute-start.19 = (bf16[512,768]{1,0:T(8,128)(2,1)}, bf16[512,768]{1,0:T(8,128)(2,1)}, u32[]{:S(2)}, u32[]{:S(2)}) collective-permute-start(bf16[512,768]{1,0:T(8,128)(2,1)} %dynamic-slice_convert_fusion), channel_id=1, source_target_pairs={{0,0},{1,2},{2,1},{3,3},{4,4},{5,6},{6,5},{7,7},{8,8},{9,10},{10,9... | collective-permute-start | bytes 2359304 | tf_op jit(solution)/shard_map/ppermute | solution.py:33
  (157 other events, 2121.5 us)

commit v3 on v2

--- a/solution.py
+++ b/solution.py
@@ -9,6 +9,7 @@
 from jax.sharding import PartitionSpec as P
 
 HEAD_DIM = 64
+CHUNK = 256
 norm_epsilon = 1e-05
 decay_rate = 1.0 - 2.0 ** (-0.8)
 step_rate = 0.2
@@ -16,17 +17,6 @@
 low = jnp.bfloat16
 wide = jnp.float32
 MESH = pl.DeviceIdType.MESH
-
-
-def gelu_exact(values):
-    return jax.nn.gelu(values, approximate=False)
-
-
-def layer_norm(values, norm_gain, norm_shift):
-    centre = jnp.mean(values, axis=-1, keepdims=True)
-    centred = values - centre
-    spread = jnp.mean(centred * centred, axis=-1, keepdims=True)
-    return centred * lax.rsqrt(spread + norm_epsilon) * norm_gain + norm_shift
 
 
 def swap_chips(array):
@@ -533,157 +523,534 @@
     return [scatter_gradient(group, "xyz") for group in groups]
 
 
-def project(left_side, right_side):
-    return jnp.dot(left_side, right_side, preferred_element_type=wide)
-
-
-def project_back(left_side, right_side):
-    return jnp.einsum("tx,dx->td", left_side, right_side, preferred_element_type=wide)
-
-
-def weight_product(left_side, right_side):
-    return jnp.einsum("td,tx->dx", left_side, right_side, preferred_element_type=wide)
-
-
-def split_heads(matrix):
-    return matrix.reshape(matrix.shape[0], matrix.shape[1] // HEAD_DIM, HEAD_DIM)
-
-
-def block_scores(query_block, key_heads, first_row, key_valid, causal):
-    scores = jnp.einsum(
-        "qhd,khd->hqk", query_block, key_heads, preferred_element_type=wide
-    ) * HEAD_DIM ** (-0.5)
-    allowed = jnp.broadcast_to(key_valid[None, :], (query_block.shape[0], key_valid.shape[0]))
-    if causal:
-        query_place = first_row + lax.broadcasted_iota(jnp.int32, allowed.shape, 0)
-        key_place = lax.broadcasted_iota(jnp.int32, allowed.shape, 1)
-        allowed = allowed & (key_place <= query_place)
-    return jnp.where(allowed[None], scores, masked_score)
-
-
-def attend_forward(query_rows, key_rows, value_rows, key_valid, causal):
-    query_heads = split_heads(query_rows)
-    key_heads = split_heads(key_rows)
-    value_heads = split_heads(value_rows)
-    scores = block_scores(query_heads, key_heads, 0, key_valid, causal)
-    row_peak = jnp.max(scores, axis=-1, keepdims=True)
-    weights = jnp.exp(scores - row_peak)
-    row_total = jnp.sum(weights, axis=-1, keepdims=True)
-    weights_low = (weights / row_total).astype(low)
-    attended = jnp.einsum("hqk,khd->qhd", weights_low, value_heads, preferred_element_type=wide)
-    totals = row_peak[:, :, 0] + jnp.log(row_total[:, :, 0])
-    return attended.astype(low).reshape(query_rows.shape), totals
-
-
-def attend_backward(grad_attended, query_rows, key_rows, value_rows, log_totals, key_valid, causal):
-    query_heads = split_heads(query_rows)
-    key_heads = split_heads(key_rows)
-    value_heads = split_heads(value_rows)
-    grad_heads = split_heads(grad_attended)
-    scale = HEAD_DIM ** (-0.5)
-    scores = block_scores(query_heads, key_heads, 0, key_valid, causal)
-    weights = jnp.exp(scores - log_totals[:, :, None])
-    grad_weights = jnp.einsum("qhd,khd->hqk", grad_heads, value_heads, preferred_element_type=wide)
-    row_dot = jnp.sum(weights * grad_weights, axis=-1, keepdims=True)
-    grad_scores = (weights * (grad_weights - row_dot)).astype(low)
-    grad_query = jnp.einsum("hqk,khd->qhd", grad_scores, key_heads, preferred_element_type=wide)
-    grad_key = jnp.einsum("hqk,qhd->khd", grad_scores, query_heads, preferred_element_type=wide)
-    grad_value = jnp.einsum(
-        "hqk,qhd->khd", weights.astype(low), grad_heads, preferred_element_type=wide
-    )
-    return (
-        (grad_query * scale).reshape(query_rows.shape).astype(low),
-        (grad_key * scale).reshape(key_rows.shape).astype(low),
-        grad_value.reshape(value_rows.shape).astype(low),
-    )
-
-
-def attention_forward(residual, vectors, norm_row, memory_rows, weights, key_valid, causal):
+def dot_nn(left, right):
+    return lax.dot_general(left, right, (((1,), (0,)), ((), ())), preferred_element_type=wide)
+
+
+def dot_nt(left, right):
+    return lax.dot_general(left, right, (((1,), (1,)), ((), ())), preferred_element_type=wide)
+
+
+def turned(block):
+    size = block.shape[1]
+    row = lax.broadcasted_iota(jnp.int32, (size, size), 0)
+    column = lax.broadcasted_iota(jnp.int32, (size, size), 1)
+    return dot_nt((row == column).astype(wide).astype(low), block).astype(low)
+
+
+def turn_into(target, source):
+    rows, columns = source.shape
+    for at in range(0, columns, 256):
+        wide_part = min(256, columns - at)
+        target[at : at + wide_part, :] = turned(source[:, at : at + wide_part])
+
+
+def centre_rows(values):
+    centred = values - jnp.mean(values, axis=-1, keepdims=True)
+    spread = jnp.mean(centred * centred, axis=-1, keepdims=True)
+    return centred * lax.rsqrt(spread + norm_epsilon)
+
+
+def norm_back(x, gain, grads):
+    centred = x - jnp.mean(x, axis=-1, keepdims=True)
+    scale = lax.rsqrt(jnp.mean(centred * centred, axis=-1, keepdims=True) + norm_epsilon)
+    unit = centred * scale
+    inner = grads * gain
+    by_unit = inner * unit
+    back = scale * (
+        inner
+        - jnp.mean(inner, axis=-1, keepdims=True)
+        - unit * jnp.mean(by_unit, axis=-1, keepdims=True)
+    )
+    return back, jnp.sum(grads * unit, axis=0, keepdims=True), jnp.sum(grads, axis=0, keepdims=True)
+
+
+def residual_prologue(norm_row, previous_ref, x_ref, own_ref, other_ref, vec_ref, grad_out, low_ref, vec_out):
+    gain = vec_ref[norm_row : norm_row + 1, :]
+    vec_out[...] = jnp.zeros_like(vec_out)
+
+    @pl.loop(0, x_ref.shape[0] // CHUNK)
+    def _(step):
+        at = pl.ds(pl.multiple_of(step * CHUNK, CHUNK), CHUNK)
+        grads = own_ref[at, :].astype(wide) + other_ref[at, :].astype(wide)
+        back, by_gain, by_shift = norm_back(x_ref[at, :].astype(wide), gain, grads)
+        if previous_ref is not None:
+            back = back + previous_ref[at, :].astype(wide)
+        if grad_out is not None:
+            grad_out[at, :] = back
+        if low_ref is not None:
+            low_ref[at, :] = back.astype(low)
+        vec_out[0:1, :] += by_gain
+        vec_out[1:2, :] += by_shift
+
+
+def erf_ratio(values):
+    x = jnp.clip(values, -4.0, 4.0)
+    square = x * x
+    top = jnp.full_like(square, -2.72614225801306e-10)
+    for term in (
+        2.77068142495902e-08,
+        -2.10102402082508e-06,
+        -5.69250639462346e-05,
+        -7.34990630326855e-04,
+        -2.95459980854025e-03,
+        -1.60960333262415e-02,
+    ):
+        top = top * square + term
+    low_part = jnp.full_like(square, -1.45660718464996e-05)
+    for term in (
+        -2.13374055278905e-04,
+        -1.68282697438203e-03,
+        -7.37332916720468e-03,
+        -1.42647390514189e-02,
+    ):
+        low_part = low_part * square + term
+    return x * top / low_part
+
+
+def gelu_pair(before):
+    phi_whole = 0.5 + 0.5 * erf_ratio(before * 0.7071067811865476)
+    density = jnp.exp(before * before * -0.5) * 0.3989422804014327
+    return before * phi_whole, phi_whole + before * density
+
+
+def chunks(rows):
+    return range(0, rows, CHUNK)
+
+
+def feed_forward_kernel(
+    rows_norm, x_ref, own_ref, other_ref, w_ref, vec_ref, x_out, normed_out, hidden_out, slope_out, part_out
+):
+    units = w_ref.shape[1] // 2
+    gain = vec_ref[rows_norm : rows_norm + 1, :]
+    shift = vec_ref[rows_norm + 1 : rows_norm + 2, :]
+
+    @pl.loop(0, x_ref.shape[0] // CHUNK)
+    def _(step):
+        at = pl.ds(pl.multiple_of(step * CHUNK, CHUNK), CHUNK)
+        x = x_ref[at, :] + (own_ref[at, :].astype(wide) + other_ref[at, :].astype(wide))
+        x_out[at, :] = x
+        normed = (centre_rows(x) * gain + shift).astype(low)
+        normed_out[at, :] = normed
+        part = jnp.zeros((CHUNK, x.shape[1]), wide)
+        for begin in range(0, units, 512):
+            before = dot_nn(normed, w_ref[:, begin : begin + 512])
+            value, slope = gelu_pair(before)
+            hidden = value.astype(low)
+            hidden_out[at, begin : begin + 512] = hidden
+            slope_out[at, begin : begin + 512] = slope.astype(low)
+            part = part + dot_nt(hidden, w_ref[:, units + begin : units + begin + 512])
+        part_out[at, :] = part.astype(low)
+
+
+def params(limit=56):
+    return pltpu.CompilerParams(vmem_limit_bytes=limit << 20)
+
+
+def shaped(rows, columns, kind):
+    return jax.ShapeDtypeStruct((rows, columns), kind)
+
+
+def feed_forward_call(rows_norm, x, own, other, weights, vectors):
+    rows, depth = x.shape
+    units = weights.shape[1] // 2
+    return pl.pallas_call(
+        functools.partial(feed_forward_kernel, rows_norm),
+        out_shape=(
+            shaped(rows, depth, wide),
+            shaped(rows, depth, low),
+            shaped(rows, units, low),
+            shaped(rows, units, low),
+            shaped(rows, depth, low),
+        ),
+        compiler_params=params(),
+        name="feed_forward",
+    )(x, own, other, weights, vectors)
+
+
+def feed_backward_body(normed_ref, hidden_ref, slope_in, w_ref, part_out, grad_out, low_ref, slope_ref, turned_ref, turned_low):
+    rows, depth = low_ref.shape
+    units = w_ref.shape[1] // 2
+    turn_into(turned_low, low_ref)
+    turn_into(turned_ref, normed_ref)
+
+    @pl.loop(0, rows // CHUNK)
+    def _(step):
+        at = pl.ds(pl.multiple_of(step * CHUNK, CHUNK), CHUNK)
+        grads = low_ref[at, :]
+        part = jnp.zeros((CHUNK, depth), wide)
+        for begin in range(0, units, 512):
+            grad = dot_nn(grads, w_ref[:, units + begin : units + begin + 512])
+            grad = (grad * slope_in[at, begin : begin + 512].astype(wide)).astype(low)
+            slope_ref[at, begin : begin + 512] = grad
+            part = part + dot_nt(grad, w_ref[:, begin : begin + 512])
+        part_out[at, :] = part.astype(low)
+
+    for begin in range(0, units, 256):
+        grad_out[:, begin : begin + 256] = dot_nn(
+            turned_ref[...], slope_ref[:, begin : begin + 256]
+        ).astype(low)
+        grad_out[:, units + begin : units + begin + 256] = dot_nn(
+            turned_low[...], hidden_ref[:, begin : begin + 256]
+        ).astype(low)
+
+
+def feed_backward_scratch(rows, depth, units):
+    return [
+        pltpu.VMEM((rows, depth), low),
+        pltpu.VMEM((rows, units), low),
+        pltpu.VMEM((depth, rows), low),
+        pltpu.VMEM((depth, rows), low),
+    ]
+
+
+def whole():
+    return pl.BlockSpec(memory_space=pltpu.VMEM)
+
+
+def scalar():
+    return pl.BlockSpec(memory_space=pltpu.SMEM)
+
+
+def last_feed_backward_kernel(
+    length_ref, cotangent_ref, normed_ref, hidden_ref, slope_in, w_ref, part_out, grad_out, low_ref, *rest
+):
+    rows, depth = cotangent_ref.shape
+    place = lax.broadcasted_iota(jnp.int32, (CHUNK, depth), 0)
+
+    @pl.loop(0, rows // CHUNK)
+    def _(step):
+        first_row = pl.multiple_of(step * CHUNK, CHUNK)
+        at = pl.ds(first_row, CHUNK)
+        rows_here = cotangent_ref[at, :].astype(wide)
+        low_ref[at, :] = jnp.where(first_row + place < length_ref[0], rows_here, 0.0).astype(low)
+
+    feed_backward_body(normed_ref, hidden_ref, slope_in, w_ref, part_out, grad_out, low_ref, *rest)
+
+
+def last_feed_backward_call(length, cotangent, normed, hidden, slope, weights):
+    rows, depth = cotangent.shape
+    units = hidden.shape[1]
+    return pl.pallas_call(
+        last_feed_backward_kernel,
+        out_shape=(shaped(rows, depth, low), shaped(depth, 2 * units, low), shaped(rows, depth, low)),
+        in_specs=[scalar()] + [whole()] * 5,
+        scratch_shapes=feed_backward_scratch(rows, depth, units)[1:],
+        compiler_params=params(),
+        name="last_feed_backward",
+    )(length, cotangent, normed, hidden, slope, weights)
+
+
+def feed_backward_kernel(
+    norm_row, x_ref, own_ref, other_ref, vec_ref, normed_ref, hidden_ref, slope_in, w_ref,
+    part_out, grad_out, g_out, vec_out, low_ref, *rest
+):
+    residual_prologue(norm_row, None, x_ref, own_ref, other_ref, vec_ref, g_out, low_ref, vec_out)
+    feed_backward_body(normed_ref, hidden_ref, slope_in, w_ref, part_out, grad_out, low_ref, *rest)
+
+
+def feed_backward_call(norm_row, x, own, other, vectors, normed, hidden, slope, weights):
+    rows, depth = x.shape
+    units = hidden.shape[1]
+    return pl.pallas_call(
+        functools.partial(feed_backward_kernel, norm_row),
+        out_shape=(
+            shaped(rows, depth, low),
+            shaped(depth, 2 * units, low),
+            shaped(rows, depth, wide),
+            shaped(2, depth, wide),
+        ),
+        scratch_shapes=feed_backward_scratch(rows, depth, units),
+        compiler_params=params(),
+        name="feed_backward",
+    )(x, own, other, vectors, normed, hidden, slope, weights)
+
+
+def half_lanes(shape):
+    return lax.broadcasted_iota(jnp.int32, shape, 1) < 64
+
+
+def one_head(pair, head):
+    first = half_lanes(pair.shape)
+    zero = jnp.zeros_like(pair)
+    return jnp.where(first, pair, zero) if head == 0 else jnp.where(first, zero, pair)
+
+
+def key_bias(keys, length, first_row, causal, rows):
+    place = lax.broadcasted_iota(jnp.int32, (1, keys), 1)
+    if not causal:
+        return jnp.where(place < length, 0.0, masked_score)
+    place = lax.broadcasted_iota(jnp.int32, (rows, keys), 1)
+    row = first_row + lax.broadcasted_iota(jnp.int32, (rows, keys), 0)
+    return jnp.where((place < length) & (place <= row), 0.0, masked_score)
+
+
+def attend_chunk(first_row, length, causal, q_ref, kv_ref, w_ref, attended_out, totals_out, part_out):
+    width = q_ref.shape[1]
+    keys = kv_ref.shape[0]
+    at = pl.ds(first_row, CHUNK)
+    bias = key_bias(keys, length, first_row, causal, CHUNK)
+    lane = lax.broadcasted_iota(jnp.int32, (CHUNK, 128), 1)
+    totals = jnp.zeros((CHUNK, 128), wide)
+    for begin in range(0, width, 128):
+        pair = q_ref[at, begin : begin + 128]
+        key_pair = kv_ref[:, begin : begin + 128]
+        value_pair = kv_ref[:, width + begin : width + begin + 128]
+        results = []
+        for head in range(2):
+            scores = dot_nt(one_head(pair, head), key_pair) + bias
+            peak = jnp.max(scores, axis=-1, keepdims=True)
+            weights = jnp.exp(scores - peak)
+            total = jnp.sum(weights, axis=-1, keepdims=True)
+            results.append(dot_nn(weights.astype(low), value_pair) * (1.0 / total))
+            totals = jnp.where(lane == begin // 64 + head, peak + jnp.log(total), totals)
+        attended_out[at, begin : begin + 128] = jnp.where(
+            lane < 64, results[0], results[1]
+        ).astype(low)
+    totals_out[at, :] = totals
+    part_out[at, :] = dot_nt(attended_out[at, :], w_ref[:, 3 * width :]).astype(low)
+
+
+def self_attention_kernel(
+    rows_norm, causal, length_ref, x_ref, w_ref, vec_ref, normed_out, q_out, kv_out, attended_out, totals_out, part_out
+):
+    width = w_ref.shape[1] // 4
+    gain = vec_ref[rows_norm : rows_norm + 1, :]
+    shift = vec_ref[rows_norm + 1 : rows_norm + 2, :]
+    steps = x_ref.shape[0] // CHUNK
+
+    @pl.loop(0, steps)
+    def _(step):
+        at = pl.ds(pl.multiple_of(step * CHUNK, CHUNK), CHUNK)
+        normed = (centre_rows(x_ref[at, :].astype(wide)) * gain + shift).astype(low)
+        normed_out[at, :] = normed
+        q_out[at, :] = (dot_nn(normed, w_ref[:, :width]).astype(low).astype(wide) * 0.125).astype(low)
+        kv_out[at, :] = dot_nn(normed, w_ref[:, width : 3 * width]).astype(low)
+
+    length = length_ref[0]
+
+    @pl.loop(0, steps)
+    def _(step):
+        attend_chunk(
+            pl.multiple_of(step * CHUNK, CHUNK), length, causal, q_out, kv_out, w_ref, attended_out, totals_out, part_out
+        )
+
+
+def self_attention_call(rows_norm, causal, length, x, weights, vectors):
+    rows, depth = x.shape
     width = weights.shape[1] // 4
-    normed = layer_norm(residual, vectors[norm_row], vectors[norm_row + 1]).astype(low)
-    source_rows = normed if memory_rows is None else memory_rows
-    query_rows = project(normed, weights[:, :width]).astype(low)
-    key_rows = project(source_rows, weights[:, width : 2 * width]).astype(low)
-    value_rows = project(source_rows, weights[:, 2 * width : 3 * width]).astype(low)
-    attended, log_totals = attend_forward(query_rows, key_rows, value_rows, key_valid, causal)
-    branch = core_sum(project_back(attended, weights[:, 3 * width :]))
-    stored = {
-        "normed": normed,
-        "source": source_rows,
-        "query": query_rows,
-        "key": key_rows,
-        "value": value_rows,
-        "attended": attended,
-        "totals": log_totals,
-    }
-    return residual + branch, stored
-
-
-def feed_forward(residual, vectors, norm_row, weights):
-    width = weights.shape[1] // 2
-    normed = layer_norm(residual, vectors[norm_row], vectors[norm_row + 1]).astype(low)
-    before = project(normed, weights[:, :width])
-    hidden = gelu_exact(before).astype(low)
-    branch = core_sum(project_back(hidden, weights[:, width:]))
-    return residual + branch, {"normed": normed, "hidden": hidden, "before": before}
-
-
-def norm_backward(residual, vectors, norm_row, grad_normed):
-    unused_out, norm_back = jax.vjp(layer_norm, residual, vectors[norm_row], vectors[norm_row + 1])
-    return norm_back(grad_normed)
-
-
-def attention_backward(grad_residual, stored, weights, key_valid, causal):
+    whole = pl.BlockSpec(memory_space=pltpu.VMEM)
+    return pl.pallas_call(
+        functools.partial(self_attention_kernel, rows_norm, causal),
+        out_shape=(
+            shaped(rows, depth, low),
+            shaped(rows, width, low),
+            shaped(rows, 2 * width, low),
+            shaped(rows, width, low),
+            shaped(rows, 128, wide),
+            shaped(rows, depth, low),
+        ),
+        in_specs=[pl.BlockSpec(memory_space=pltpu.SMEM), whole, whole, whole],
+        compiler_params=params(),
+        name="self_attention",
+    )(length, x, weights, vectors)
+
+
+def cross_attention_kernel(
+    length_ref, x_ref, own_ref, other_ref, mid_ref, mid_own, mid_other, w_ref, vec_ref,
+    x_out, final_out, memory_out, normed_out, q_out, kv_out, attended_out, totals_out, part_out,
+):
+    width = w_ref.shape[1] // 4
+
+    @pl.loop(0, mid_ref.shape[0] // CHUNK)
+    def _(step):
+        at = pl.ds(pl.multiple_of(step * CHUNK, CHUNK), CHUNK)
+        x = mid_ref[at, :] + (mid_own[at, :].astype(wide) + mid_other[at, :].astype(wide))
+        final_out[at, :] = x
+        memory = (centre_rows(x) * vec_ref[4:5, :] + vec_ref[5:6, :]).astype(low)
+        memory_out[at, :] = memory
+        kv_out[at, :] = dot_nn(memory, w_ref[:, width : 3 * width]).astype(low)
+
+    @pl.loop(0, x_ref.shape[0] // CHUNK)
+    def _(step):
+        at = pl.ds(pl.multiple_of(step * CHUNK, CHUNK), CHUNK)
+        x = x_ref[at, :].astype(wide) + (own_ref[at, :].astype(wide) + other_ref[at, :].astype(wide))
+        x_out[at, :] = x
+        normed = (centre_rows(x) * vec_ref[8:9, :] + vec_ref[9:10, :]).astype(low)
+        normed_out[at, :] = normed
+        q_out[at, :] = (dot_nn(normed, w_ref[:, :width]).astype(low).astype(wide) * 0.125).astype(low)
+
+    length = length_ref[0]
+
+    @pl.loop(0, x_ref.shape[0] // CHUNK)
+    def _(step):
+        attend_chunk(
+            pl.multiple_of(step * CHUNK, CHUNK), length, False, q_out, kv_out, w_ref, attended_out, totals_out, part_out
+        )
+
+
+def cross_attention_call(length, x, own, other, mid, mid_own, mid_other, weights, vectors):
+    rows, depth = x.shape
+    keys = mid.shape[0]
     width = weights.shape[1] // 4
-    grad_branch = grad_residual.astype(low)
-    grad_output = weight_product(grad_branch, stored["attended"])
-    grad_attended = project(grad_branch, weights[:, 3 * width :]).astype(low)
-    grad_query, grad_key, grad_value = attend_backward(
-        grad_attended,
-        stored["query"],
-        stored["key"],
-        stored["value"],
-        stored["totals"],
-        key_valid,
-        causal,
-    )
-    weight_terms = jnp.concatenate(
-        [
-            weight_product(stored["normed"], grad_query).astype(low),
-            weight_product(stored["source"], grad_key).astype(low),
-            weight_product(stored["source"], grad_value).astype(low),
-            grad_output.astype(low),
-        ],
-        axis=1,
-    )
-    from_query = project_back(grad_query, weights[:, :width])
-    from_source = project_back(grad_key, weights[:, width : 2 * width]) + project_back(
-        grad_value, weights[:, 2 * width : 3 * width]
-    )
-    return weight_terms, from_query, from_source
-
-
-def feed_backward(grad_residual, residual, vectors, norm_row, stored, weights):
-    width = weights.shape[1] // 2
-    grad_branch = grad_residual.astype(low)
-    grad_second = weight_product(grad_branch, stored["hidden"])
-    grad_hidden = project(grad_branch, weights[:, width:])
-    unused_value, gelu_back = jax.vjp(gelu_exact, stored["before"])
-    grad_hidden = gelu_back(grad_hidden)[0].astype(low)
-    grad_first = weight_product(stored["normed"], grad_hidden)
-    weight_terms = jnp.concatenate([grad_first.astype(low), grad_second.astype(low)], axis=1)
-    grad_input, grad_gain, grad_shift = norm_backward(
-        residual, vectors, norm_row, core_sum(project_back(grad_hidden, weights[:, :width]))
-    )
-    return grad_residual + grad_input, weight_terms, [grad_gain, grad_shift]
+    whole = pl.BlockSpec(memory_space=pltpu.VMEM)
+    return pl.pallas_call(
+        cross_attention_kernel,
+        out_shape=(
+            shaped(rows, depth, wide),
+            shaped(keys, depth, wide),
+            shaped(keys, depth, low),
+            shaped(rows, depth, low),
+            shaped(rows, width, low),
+            shaped(keys, 2 * width, low),
+            shaped(rows, width, low),
+            shaped(rows, 128, wide),
+            shaped(rows, depth, low),
+        ),
+        in_specs=[pl.BlockSpec(memory_space=pltpu.SMEM)] + [whole] * 8,
+        compiler_params=params(),
+        name="cross_attention",
+    )(length, x, own, other, mid, mid_own, mid_other, weights, vectors)
+
+
+def attention_backward_kernel(
+    causal, cross, norm_row, length_ref, previous_ref, x_ref, own_ref, other_ref, vec_ref,
+    normed_ref, source_ref, q_ref, kv_ref, attended_ref, totals_ref, w_ref, *rest
+):
+    outs = 5 if cross else 4
+    part_out, g_out, vec_out, grad_out = rest[:4]
+    source_part_out = rest[4] if cross else None
+    low_ref, grad_q, grad_kv, turned_k, turned_v, turned_low, turned_normed = rest[outs : outs + 7]
+    turned_source = rest[outs + 7] if cross else turned_normed
+    rows, depth = x_ref.shape
+    keys = kv_ref.shape[0]
+    width = q_ref.shape[1]
+    length = length_ref[0]
+    residual_prologue(norm_row, previous_ref, x_ref, own_ref, other_ref, vec_ref, g_out, low_ref, vec_out)
+    turned_k[...] = jnp.zeros_like(turned_k)
+    turned_v[...] = jnp.zeros_like(turned_v)
+
+    @pl.loop(0, rows // CHUNK)
+    def _(step):
+        first_row = pl.multiple_of(step * CHUNK, CHUNK)
+        at = pl.ds(first_row, CHUNK)
+        grad_attended = dot_nn(low_ref[at, :], w_ref[:, 3 * width :]).astype(low)
+        bias = key_bias(keys, length, first_row, causal, CHUNK)
+        lane = lax.broadcasted_iota(jnp.int32, (CHUNK, 128), 1)
+        totals = totals_ref[at, :]
+        for begin in range(0, width, 128):
+            pair = q_ref[at, begin : begin + 128]
+            key_pair = kv_ref[:, begin : begin + 128]
+            value_pair = kv_ref[:, width + begin : width + begin + 128]
+            grad_pair = grad_attended[:, begin : begin + 128]
+            pair_turned = turned(pair)
+            grad_turned = turned(grad_pair)
+            results = []
+            for head in range(2):
+                number = begin // 64 + head
+                total = jnp.sum(jnp.where(lane == number, totals, 0.0), axis=-1, keepdims=True)
+                scores = dot_nt(one_head(pair, head), key_pair) + bias
+                weights = jnp.exp(scores - total)
+                grad_weights = dot_nt(one_head(grad_pair, head), value_pair)
+                row_dot = jnp.sum(weights * grad_weights, axis=-1, keepdims=True)
+                grad_scores = (weights * (grad_weights - row_dot)).astype(low)
+                results.append(dot_nn(grad_scores, key_pair))
+                span = slice(begin + 64 * head, begin + 64 * head + 64)
+                local = slice(64 * head, 64 * head + 64)
+                turned_k[span, :] += dot_nn(pair_turned[local, :], grad_scores)
+                turned_v[span, :] += dot_nn(grad_turned[local, :], weights.astype(low))
+            grad_q[at, begin : begin + 128] = (
+                jnp.where(lane < 64, results[0], results[1]) * 0.125
+            ).astype(low)
+        if cross:
+            part_out[at, :] = dot_nt(grad_q[at, :], w_ref[:, :width]).astype(low)
+
+    grad_kv[:, :width] = turned(turned_k[...].astype(low))
+    grad_kv[:, width:] = turned(turned_v[...].astype(low))
+
+    @pl.loop(0, keys // CHUNK)
+    def _(step):
+        at = pl.ds(pl.multiple_of(step * CHUNK, CHUNK), CHUNK)
+        from_source = dot_nt(grad_kv[at, :], w_ref[:, width : 3 * width])
+        if cross:
+            source_part_out[at, :] = from_source.astype(low)
+        else:
+            from_query = dot_nt(grad_q[at, :], w_ref[:, :width])
+            part_out[at, :] = (from_source + from_query).astype(low)
+
+    turn_into(turned_low, low_ref)
+    turn_into(turned_normed, normed_ref)
+    if cross:
+        turn_into(turned_source, source_ref)
+    grad_out[:, :width] = dot_nn(turned_normed[...], grad_q[...]).astype(low)
+    grad_out[:, width : 2 * width] = dot_nn(turned_source[...], grad_kv[:, :width]).astype(low)
+    grad_out[:, 2 * width : 3 * width] = dot_nn(turned_source[...], grad_kv[:, width:]).astype(low)
+    grad_out[:, 3 * width :] = dot_nn(turned_low[...], attended_ref[...]).astype(low)
+
+
+def attention_backward_call(
+    causal, norm_row, length, previous, x, own, other, vectors, normed, source, q, kv, attended, totals, weights
+):
+    cross = source is not None
+    rows, depth = x.shape
+    keys = kv.shape[0]
+    width = q.shape[1]
+    outs = [
+        shaped(rows, depth, low),
+        shaped(rows, depth, wide),
+        shaped(2, depth, wide),
+        shaped(depth, 4 * width, low),
+    ]
+    if cross:
+        outs.append(shaped(keys, depth, low))
+    scratch = [
+        pltpu.VMEM((rows, depth), low),
+        pltpu.VMEM((rows, width), low),
+        pltpu.VMEM((keys, 2 * width), low),
+        pltpu.VMEM((width, keys), wide),
+        pltpu.VMEM((width, keys), wide),
+        pltpu.VMEM((depth, rows), low),
+        pltpu.VMEM((depth, rows), low),
+    ]
+    if cross:
+        scratch.append(pltpu.VMEM((depth, keys), low))
+    operands = [length, previous, x, own, other, vectors, normed]
+    if cross:
+        operands.append(source)
+    operands += [q, kv, attended, totals, weights]
+
+    def kernel(*refs):
+        if not cross:
+            refs = refs[:7] + (None,) + refs[7:]
+        attention_backward_kernel(causal, cross, norm_row, *refs)
+
+    return pl.pallas_call(
+        kernel,
+        out_shape=tuple(outs),
+        in_specs=[scalar()] + [whole()] * (len(operands) - 1),
+        scratch_shapes=scratch,
+        compiler_params=params(),
+        name="attention_backward",
+    )(*operands)
+
+
+def finish_kernel(norm_row, previous_ref, x_ref, own_ref, other_ref, vec_ref, g_out, vec_out):
+    residual_prologue(norm_row, previous_ref, x_ref, own_ref, other_ref, vec_ref, g_out, None, vec_out)
+
+
+def finish_call(norm_row, previous, x, own, other, vectors):
+    rows, depth = x.shape
+    return pl.pallas_call(
+        functools.partial(finish_kernel, norm_row),
+        out_shape=(shaped(rows, depth, wide), shaped(2, depth, wide)),
+        compiler_params=params(),
+        name="finish_norm",
+    )(previous, x, own, other, vectors)
 
 
 def factored_step(weights, grads, rows_next, columns_next, row_level, mean_square):
     estimate = rows_next[:, :, None] * columns_next[:, None, :] / row_level[:, None, None]
     return weights - step_rate * jnp.sqrt(mean_square)[:, None, None] * grads * lax.rsqrt(estimate)
-
-
-ORDERS = ("zyx", "zxy", "xyz")
 
 
 def on_device(
@@ -721,8 +1088,8 @@
     source_all = both_halves(source_half)
     flags_all = both_halves(flags_half)
     masks = swap_chips(jnp.concatenate([source_mask[0], target_mask[0]]))
-    source_valid = masks[: source_mask.shape[1]] > 0
-    target_valid = masks[source_mask.shape[1] :] > 0
+    source_length = jnp.sum(masks[: source_mask.shape[1]]).reshape(1)
+    target_length = jnp.sum(masks[source_mask.shape[1] :]).reshape(1)
     target_all = both_halves(swap_chips(target_embed[0]))
     cotangent_all = both_halves(swap_chips(out_cotangent[0]))
 
@@ -735,66 +1102,124 @@
         vector_params[12][None, :],
         jnp.where((flags_all == 2)[:, None], vector_params[13][None, :], source_all.astype(wide)),
     )
-    target_rows = target_all.astype(wide)
-
-    encoder_mid, kept_first = attention_forward(
-        start_rows, vector_params, 0, None, encoder_attention, source_valid, False
-    )
-    decoder_one, kept_third = attention_forward(
-        target_rows, vector_params, 6, None, decoder_attention, target_valid, True
-    )
-    encoder_final, kept_second = feed_forward(encoder_mid, vector_params, 2, encoder_feed)
-    memory_rows = layer_norm(encoder_final, vector_params[4], vector_params[5]).astype(low)
-    decoder_two, kept_fourth = attention_forward(
-        decoder_one, vector_params, 8, memory_rows, cross_attention, source_valid, False
-    )
-    decoder_three, kept_fifth = feed_forward(decoder_two, vector_params, 10, decoder_feed)
+    first_kept = self_attention_call(0, False, source_length, start_rows, encoder_attention, vector_params)
+    first_part = first_kept[5]
+    first_other = other_core(first_part)
+    third_kept = self_attention_call(6, True, target_length, target_all, decoder_attention, vector_params)
+    third_part = third_kept[5]
+    third_other = other_core(third_part)
+    encoder_mid, second_normed, second_hidden, second_slope, second_part = feed_forward_call(
+        2, start_rows, first_part, first_other, encoder_feed, vector_params
+    )
+    second_other = other_core(second_part)
+    decoder_one, encoder_final, memory_rows, *fourth_kept, fourth_part = cross_attention_call(
+        source_length,
+        target_all,
+        third_part,
+        third_other,
+        encoder_mid,
+        second_part,
+        second_other,
+        cross_attention,
+        vector_params,
+    )
+    decoder_two, fifth_normed, fifth_hidden, fifth_slope, fifth_part = feed_forward_call(
+        10, decoder_one, fourth_part, other_core(fourth_part), decoder_feed, vector_params
+    )
+    decoder_three = decoder_two + (fifth_part.astype(wide) + other_core(fifth_part).astype(wide))
 
     def own_half(rows):
         half = rows.shape[0] // 2
         return lax.dynamic_slice_in_dim(rows, core * half, half, 0)
 
-    decoder_out = swap_chips(own_half(decoder_three.astype(low)))
-
-    grad_three = jnp.where(target_valid[:, None], cotangent_all.astype(wide), 0.0)
-    vector_parts = [None] * 14
-    grad_two, decoder_feed_terms, vector_parts[10:12] = feed_backward(
-        grad_three, decoder_two, vector_params, 10, kept_fifth, decoder_feed
-    )
-    cross_terms, from_query, from_source = attention_backward(
-        grad_two, kept_fourth, cross_attention, source_valid, False
-    )
-    grad_memory, vector_parts[4], vector_parts[5] = norm_backward(
-        encoder_final, vector_params, 4, core_sum(from_source)
-    )
-    grad_input, vector_parts[8], vector_parts[9] = norm_backward(
-        decoder_one, vector_params, 8, core_sum(from_query)
-    )
-    grad_one = grad_two + grad_input
-    grad_mid, encoder_feed_terms, vector_parts[2:4] = feed_backward(
-        grad_memory, encoder_mid, vector_params, 2, kept_second, encoder_feed
-    )
-    decoder_terms, from_query, from_source = attention_backward(
-        grad_one, kept_third, decoder_attention, target_valid, True
-    )
-    grad_input, vector_parts[6], vector_parts[7] = norm_backward(
-        target_rows, vector_params, 6, core_sum(from_query + from_source)
-    )
-    target_grad = swap_chips(own_half((grad_one + grad_input).astype(low))).astype(wide)
-    encoder_terms, from_query, from_source = attention_backward(
-        grad_mid, kept_first, encoder_attention, source_valid, False
-    )
-    grad_input, vector_parts[0], vector_parts[1] = norm_backward(
-        start_rows, vector_params, 0, core_sum(from_query + from_source)
-    )
-    grad_start = grad_mid + grad_input
-    vector_parts[12] = jnp.sum(jnp.where((flags_all == 1)[:, None], grad_start, 0.0), axis=0)
-    vector_parts[13] = jnp.sum(jnp.where((flags_all == 2)[:, None], grad_start, 0.0), axis=0)
-    source_grad = swap_chips(own_half(grad_start.astype(low))).astype(wide)
+    decoder_out = swap_chips(own_half(decoder_three).astype(low))
+
+    fifth_back, decoder_feed_terms, grad_three = last_feed_backward_call(
+        target_length, cotangent_all, fifth_normed, fifth_hidden, fifth_slope, decoder_feed
+    )
+    query_back, grad_two, vectors_ten, cross_terms, memory_back = attention_backward_call(
+        False,
+        10,
+        source_length,
+        grad_three,
+        decoder_two,
+        fifth_back,
+        other_core(fifth_back),
+        vector_params,
+        fourth_kept[0],
+        memory_rows,
+        *fourth_kept[1:],
+        cross_attention,
+    )
+    query_other = other_core(query_back)
+    memory_other = other_core(memory_back)
+    third_back, grad_one, vectors_eight, decoder_terms = attention_backward_call(
+        True,
+        8,
+        target_length,
+        grad_two,
+        decoder_one,
+        query_back,
+        query_other,
+        vector_params,
+        third_kept[0],
+        None,
+        *third_kept[1:5],
+        decoder_attention,
+    )
+    third_back_other = other_core(third_back)
+    second_back, encoder_feed_terms, grad_final, vectors_four = feed_backward_call(
+        4,
+        encoder_final,
+        memory_back,
+        memory_other,
+        vector_params,
+        second_normed,
+        second_hidden,
+        second_slope,
+        encoder_feed,
+    )
+    first_back, grad_mid, vectors_two, encoder_terms = attention_backward_call(
+        False,
+        2,
+        source_length,
+        grad_final,
+        encoder_mid,
+        second_back,
+        other_core(second_back),
+        vector_params,
+        first_kept[0],
+        None,
+        *first_kept[1:5],
+        encoder_attention,
+    )
+    grad_target, vectors_six = finish_call(
+        6, grad_one, target_all, third_back, third_back_other, vector_params
+    )
+    target_grad = swap_chips(own_half(grad_target).astype(low)).astype(wide)
+    grad_start, vectors_zero = finish_call(
+        0, grad_mid, start_rows, first_back, other_core(first_back), vector_params
+    )
+    gap_rows = jnp.sum(jnp.where((flags_all == 1)[:, None], grad_start, 0.0), axis=0, keepdims=True)
+    mask_rows = jnp.sum(jnp.where((flags_all == 2)[:, None], grad_start, 0.0), axis=0, keepdims=True)
+    source_grad = swap_chips(own_half(grad_start).astype(low)).astype(wide)
     source_grad = jnp.where((row_flags[0] == 0)[:, None], source_grad, 0.0)
 
-    vector_terms = jnp.stack(vector_parts, axis=1).astype(low)
-    vector_terms = jnp.pad(vector_terms, ((0, 0), (0, 128 - vector_terms.shape[1])))
+    vector_terms = jnp.concatenate(
+        [
+            vectors_zero,
+            vectors_two,
+            vectors_four,
+            vectors_six,
+            vectors_eight,
+            vectors_ten,
+            gap_rows,
+            mask_rows,
+            jnp.zeros((114, depth), wide),
+        ],
+        axis=0,
+    )
+    vector_terms = vector_terms.T.astype(low)
     (encoder_grad, decoder_grad, cross_grad, encoder_feed_grad, decoder_feed_grad, vector_grad) = (
         scatter_groups(
             [

time: 800 us -> 721 us (0.901)
  Pallas kernels: 353 us -> 584 us
  matrix products: 214 us -> 0 us
  other arithmetic: 120 us -> 24.3 us
  waiting for transfers between devices: 13.5 us -> 21.7 us
    pallas_call x0 -> x12, Pallas kernels: none -> 223 us  [the longest x3 90.4 us: attention_backward_call(): pl.pallas_call(kernel, out_shape=tuple(outs), in_specs=[scalar()] + [whol...]
    dot_general x66 -> x0, matrix products: 214 us -> none  [the longest x16 65.9 us: project(): return jnp.dot(left_side, right_side, preferred_element_type=wide)]
    reduce_sum x28 -> x3, other arithmetic: 56.8 us -> 3.52 us  [the longest x1 2.26 us: on_device(): jnp.sum(jnp.where((flags_all == 2)[:, None], grad_start, 0.0), axis=0, ke...]
    convert_element_type x10 -> x1, other arithmetic: 32.7 us -> 1.24 us  [on_device(): decoder_out = swap_chips(own_half(decoder_three).astype(low))]
    slice x1 -> x3, local copies, waits for them, and re-layouts: 0.67 us -> 15.2 us  [the longest x2 14.3 us: gather_groups(): pieces.append(whole[:, begin:begin + group.shape[1]])]
    concatenate x3 -> x1, local copies, waits for them, and re-layouts: 13.9 us -> 1.41 us  [on_device(): jnp.concatenate([vectors_zero, vectors_two, vectors_four, vectors_six, ve...]
    ppermute x17, waiting for transfers between devices: 3 us -> 13.3 us  [other_core(): return lax.ppermute(array, 'c', [(0, 1), (1, 0)])]
    concatenate x5 -> x2, other arithmetic: 11.8 us -> 1.87 us  [both_halves(): jnp.concatenate([jnp.where(first, own_half, received), jnp.where(first, r...]
  transfers between devices with their start and end apart: 33 -> 33, of which waited for: 9 -> 10; matrix products, arithmetic and copies ran while one was open for 39% -> 5% of each run, Pallas kernels for 22% -> 41%
where the time goes in v3:
time: 721 us; the launch traced here: 714 us
  Pallas kernels  584 us (81%)
  starting transfers between devices  43.8 us (6%)
  local copies, waits for them, and re-layouts  38.5 us (5%)
  other arithmetic  24.3 us (3%)
  waiting for transfers between devices  21.7 us (3%)
    pallas_call x1, Pallas kernels, scatter_all(): pl.pallas_call(functools.partial(scatter_kernel, widths), out_shape=jax.S...  183 us
    pallas_call x1, Pallas kernels, gather_all(): pl.pallas_call(gather_kernel, out_shape=jax.ShapeDtypeStruct((8, 2 * rows...  178 us
    pallas_call x3, Pallas kernels, attention_backward_call(): pl.pallas_call(kernel, out_shape=tuple(outs), in_specs=[scalar()] + [whol...  90.4 us
    pallas_call x2, Pallas kernels, feed_forward_call(): pl.pallas_call(functools.partial(feed_forward_kernel, rows_norm), out_sha...  32.6 us
    pallas_call x2, Pallas kernels, self_attention_call(): pl.pallas_call(functools.partial(self_attention_kernel, rows_norm, causal...  32.3 us
    pallas_call x1, Pallas kernels, feed_backward_call(): pl.pallas_call(functools.partial(feed_backward_kernel, norm_row), out_sha...  24.8 us
    ppermute x17, starting transfers between devices, other_core(): return lax.ppermute(array, 'c', [(0, 1), (1, 0)])  19.8 us
    pallas_call x1, Pallas kernels, cross_attention_call(): pl.pallas_call(cross_attention_kernel, out_shape=(shaped(rows, depth, wid...  17.5 us
  transfers between devices with their start and end apart: 33, of which 10 were waited for; matrix products, arithmetic and copies ran while one was open for 5% of the time, Pallas kernels for 41%

profile of v3, /device:TPU:0, one launch (start us, length us, event | category | flops | bytes accessed | tf_op | source)
XLA Modules:
  0.0 714.0 jit_solution(3638803943747227043)
XLA Ops:
  8.4 177.8 %gather_weights.1 = bf16[8,96,10752]{2,1,0:T(8,128)(2,1)} custom-call(bf16[48,10752]{1,0:T(8,128)(2,1)} %copy-done.9), custom_call_target="tpu_custom_call" | custom-call | tf_op jit(solution)/shard_map/gather_weights/pallas_call | solution.py:310
  186.3 6.1 fusion.13
  194.6 3.2 select_select_fusion.x_ref
  197.7 22.2 %self_attention.3 = (bf16[1024,768]{1,0:T(8,128)(2,1)}, bf16[1024,384]{1,0:T(8,128)(2,1)}, bf16[1024,768]{1,0:T(8,128)(2,1)}, bf16[1024,384]{1,0:T(8,128)(2,1)},...) custom-call(s32[1]{0:T(128)} %bitcast.2.length_ref.refs_0_, f32[1024,768]{1,0:T(8,128)} %select_select_fusion.x_ref, ...), custom_call_target="tpu_custom_call" | custom-call | tf_op jit(solution)/shard_map/self_attention/pallas_call | solution.py:843
  221.2 9.0 %collective-permute-start.2 = (bf16[256,768]{1,0:T(8,128)(2,1)S(1)}, bf16[256,768]{1,0:T(8,128)(2,1)S(1)}, u32[]{:S(2)}, u32[]{:S(2)}) collective-permute-start(bf16[256,768]{1,0:T(8,128)(2,1)S(1)} %collective-permute-done.1), channel_id=1, source_target_pairs={{0,2},{2,0},{1,3},{3,1},{4,6},{6,4},{5,7},{7,5},{8,10},{10,8},{9,1... | collective-permute-start | bytes 1179656 | tf_op jit(solution)/shard_map/ppermute | solution.py:27
  230.2 8.2 %fusion.12 = (bf16[768,3072]{1,0:T(8,128)(2,1)}, bf16[768,3072]{1,0:T(8,128)(2,1)}) fusion(bf16[768,10752]{1,0:T(8,128)(2,1)} %bitcast.78), kind=kLoop, calls=%fused_computation.82 | loop fusion | bytes 18874368 | tf_op jit(solution)/shard_map/slice | solution.py:508
  239.6 20.8 %feed_forward.2 = (f32[1024,768]{1,0:T(8,128)}, bf16[1024,768]{1,0:T(8,128)(2,1)}, bf16[1024,1536]{1,0:T(8,128)(2,1)}, bf16[1024,1536]{1,0:T(8,128)(2,1)}, bf16[1024,768]{1,0:T(8,128)(2,1)}) custom-call(f32[1024,768]{1,0:T(8,128)} %select_select_fusion.x_ref, bf16[1024,768]{1,0:T(8,128)(2,1)} %get-tuple-element.71.own_ref, bf16[1024,768]{1,0:T(8,128)(2,1)} %copy-done.7, ...), custom_call_target="tpu_custom_call" | custom-call | tf_op jit(solution)/shard_map/feed_forward/pallas_call | solution.py:657
  262.1 10.1 %self_attention.2 = (bf16[512,768]{1,0:T(8,128)(2,1)}, bf16[512,384]{1,0:T(8,128)(2,1)}, bf16[512,768]{1,0:T(8,128)(2,1)}, bf16[512,384]{1,0:T(8,128)(2,1)}, f32...) custom-call(s32[1]{0:T(128)} %bitcast.4.length_ref.refs_0_, bf16[512,768]{1,0:T(8,128)(2,1)} %pad_maximum_fusion.2.x_ref, ...), custom_call_target="tpu_custom_call" | custom-call | tf_op jit(solution)/shard_map/self_attention/pallas_call | solution.py:843
  273.9 7.9 %collective-permute-start.14 = (bf16[256,768]{1,0:T(8,128)(2,1)S(1)}, bf16[256,768]{1,0:T(8,128)(2,1)S(1)}, u32[]{:S(2)}, u32[]{:S(2)}) collective-permute-start(bf16[256,768]{1,0:T(8,128)(2,1)S(1)} %collective-permute-done.13), channel_id=1, source_target_pairs={{0,2},{2,0},{1,3},{3,1},{4,6},{6,4},{5,7},{7,5},{8,10},{10,8},{9,1... | collective-permute-start | bytes 1179656 | tf_op jit(solution)/shard_map/ppermute | solution.py:27
  283.2 17.5 %cross_attention.1 = (f32[512,768]{1,0:T(8,128)}, f32[1024,768]{1,0:T(8,128)}, bf16[1024,768]{1,0:T(8,128)(2,1)}, bf16[512,768]{1,0:T(8,128)(2,1)}, bf16[512,384...) custom-call(s32[1]{0:T(128)} %bitcast.2.length_ref.refs_0_, ...), custom_call_target="tpu_custom_call" | custom-call | tf_op jit(solution)/shard_map/cross_attention/pallas_call | solution.py:897
  304.1 11.8 %feed_forward.3 = (f32[512,768]{1,0:T(8,128)}, bf16[512,768]{1,0:T(8,128)(2,1)}, bf16[512,1536]{1,0:T(8,128)(2,1)}, bf16[512,1536]{1,0:T(8,128)(2,1)}, bf16[512,768]{1,0:T(8,128)(2,1)}) custom-call(f32[512,768]{1,0:T(8,128)} %get-tuple-element.74.x_ref.refs_2_, bf16[512,768]{1,0:T(8,128)(2,1)} %get-tuple-element.75.own_ref, bf16[512,768]{1,0:T(8,128)(2,1)} %copy-done.14, ...), custom_call_target="tpu_custom_call" | custom-call | tf_op jit(solution)/shard_map/feed_forward/pallas_call | solution.py:657
  315.9 13.3 %last_feed_backward.1 = (bf16[512,768]{1,0:T(8,128)(2,1)}, bf16[768,3072]{1,0:T(8,128)(2,1)}, bf16[512,768]{1,0:T(8,128)(2,1)}) custom-call(s32[1]{0:T(128)} %bitcast.4.length_ref.refs_0_, bf16[512,768]{1,0:T(8,128)(2,1)} %pad_maximum_fusion.3.cotangent_ref, bf16[512,768]{1,0:T(8,128)(2,1)} %get-tuple-element.79.normed_ref, ...), custom_call_target="tpu_custom_call" | custom-call | tf_op jit(solution)/shard_map/last_feed_backward/pallas_call | solution.py:734
  329.4 2.4 collective-permute-done.15.refs_4_
  332.6 28.3 %attention_backward.3 = (bf16[512,768]{1,0:T(8,128)(2,1)}, f32[512,768]{1,0:T(8,128)}, f32[2,768]{1,0:T(2,128)}, bf16[768,1536]{1,0:T(8,128)(2,1)}, bf16[1024,768]{1,0:T(8,128)(2,1)}) custom-call(s32[1]{0:T(128)} %bitcast.2.length_ref.refs_0_, bf16[512,768]{1,0:T(8,128)(2,1)} %get-tuple-element.82.refs_1_, f32[512,768]{1,0:T(8,128)} %get-tuple-element.76.refs_2_, ...), custom_call_target="tpu_custom_call" | custom-call | tf_op jit(solution)/shard_map/attention_backward/pallas_call | solution.py:1027
  361.0 3.5 collective-permute-done.16.other_ref
  365.6 24.8 %feed_backward.1 = (bf16[1024,768]{1,0:T(8,128)(2,1)}, bf16[768,3072]{1,0:T(8,128)(2,1)}, f32[1024,768]{1,0:T(8,128)}, f32[2,768]{1,0:T(2,128)}) custom-call(f32[1024,768]{1,0:T(8,128)} %get-tuple-element.78.x_ref, bf16[1024,768]{1,0:T(8,128)(2,1)} %get-tuple-element.90.own_ref, bf16[1024,768]{1,0:T(8,128)(2,1)} %copy-done.8, f32[14,768]{1,0:T(8,128)} %vec_ref.15, ...), custom_call_target="tpu_custom_call" | custom-call | tf_op jit(solution)/shard_map/feed_backward/pallas_call | solution.py:755
  391.1 4.8 collective-permute-done.20.refs_4_
  396.7 18.9 %attention_backward.5 = (bf16[512,768]{1,0:T(8,128)(2,1)}, f32[512,768]{1,0:T(8,128)}, f32[2,768]{1,0:T(2,128)}, bf16[768,1536]{1,0:T(8,128)(2,1)}) custom-call(s32[1]{0:T(128)} %bitcast.4.length_ref.refs_0_, f32[512,768]{1,0:T(8,128)} %get-tuple-element.104.refs_1_, f32[512,768]{1,0:T(8,128)} %get-tuple-element.74.x_ref.refs_2_, ...), custom_call_target="tpu_custom_call" | custom-call | tf_op jit(solution)/shard_map/attention_backward/pallas_call | solution.py:1027
  417.2 43.2 %attention_backward.4 = (bf16[1024,768]{1,0:T(8,128)(2,1)}, f32[1024,768]{1,0:T(8,128)}, f32[2,768]{1,0:T(2,128)}, bf16[768,1536]{1,0:T(8,128)(2,1)}) custom-call(s32[1]{0:T(128)} %bitcast.2.length_ref.refs_0_, f32[1024,768]{1,0:T(8,128)} %get-tuple-element.94.refs_1_, f32[1024,768]{1,0:T(8,128)} %get-tuple-element.72.mid_ref.refs_2_, ...), custom_call_target="tpu_custom_call" | custom-call | tf_op jit(solution)/shard_map/attention_backward/pallas_call | solution.py:1027
  462.9 4.5 finish_norm.3
  473.0 7.9 %finish_norm.2 = (f32[1024,768]{1,0:T(8,128)}, f32[2,768]{1,0:T(2,128)}) custom-call(f32[1024,768]{1,0:T(8,128)} %get-tuple-element.101.previous_ref, f32[1024,768]{1,0:T(8,128)} %select_select_fusion.x_ref, bf16[1024,768]{1,0:T(8,128)(2,1)} %get-tuple-element.102.own_ref, bf16[1024,768]{1,0:T(8,128)(2,1)} %collective-permute-done.18.other_ref, ...), custom_call_target="tpu_custom_call" | custom-call | tf_op jit(solution)/shard_map/finish_norm/pallas_call | solution.py:1043
  481.8 2.3 select_reduce_fusion
  485.9 182.8 %scatter_gradients.1 = f32[48,10880]{1,0:T(8,128)} custom-call(bf16[8,96,1536]{2,1,0:T(8,128)(2,1)} %bitcast.83, bf16[8,96,1536]{2,1,0:T(8,128)(2,1)} %bitcast.82, bf16[8,96,1536]{2,1,0:T(8,128)(2,1)} %bitcast.81, bf16[8,96,3072]{2,1,0:T(8,128)(2,1)} %bitcast.80, bf16[8,96,3072]{2,1,0:T(8,128)(2,1)} %bitcast.79, bf16[8,96,128]{2,1,0:T(8,128)(2,1)} %bitcast.92), custom_call_target="tpu_custom_call" | custom-call | tf_op jit(solution)/shard_map/scatter_gradients/pallas_call | solution.py:474
  673.7 2.8 collective-permute-done.28
  678.2 2.6 collective-permute-start.30
  680.9 1.9 collective-permute-done.30
  683.0 2.4 dynamic-slice_convert_fusion
  685.3 7.4 %collective-permute-start.19 = (bf16[512,768]{1,0:T(8,128)(2,1)}, bf16[512,768]{1,0:T(8,128)(2,1)}, u32[]{:S(2)}, u32[]{:S(2)}) collective-permute-start(bf16[512,768]{1,0:T(8,128)(2,1)} %dynamic-slice_convert_fusion), channel_id=1, source_target_pairs={{0,0},{1,2},{2,1},{3,3},{4,4},{5,6},{6,5},{7,7},{8,8},{9,10},{10,9... | collective-permute-start | bytes 2359304 | tf_op jit(solution)/shard_map/ppermute | solution.py:23
  694.7 2.1 collective-permute-start.25
  701.8 1.9 collective-permute-start.27
  706.5 2.4 multiply_subtract_fusion.1
  710.5 2.6 select_bitcast_fusion
  (214 shorter events, 55.1 us)
Async XLA Ops:
  1.4 192.4 %collective-permute-start = (s32[1536]{0:T(1024)S(1)}, s32[1536]{0:T(1024)S(1)}, u32[]{:S(2)}, u32[]{:S(2)}) collective-permute-start(s32[1536]{0:T(1024)S(1)} %pad_add_fusion), channel_id=1, source_target_pairs={{0,0},{1,2},{2,1},{3,3},{4,4},{5,6},{6,5},{7,7},{8,8},{9,10},{10,9... | collective-permute-start | bytes 18440 | tf_op jit(solution)/shard_map/ppermute | solution.py:23
  2.0 184.2 %collective-permute-start.6 = (bf16[512,768]{1,0:T(8,128)(2,1)}, bf16[512,768]{1,0:T(8,128)(2,1)S(1)}, u32[]{:S(2)}, u32[]{:S(2)}) collective-permute-start(bf16[512,768]{1,0:T(8,128)(2,1)} %bitcast.101), channel_id=1, source_target_pairs={{0,0},{1,2},{2,1},{3,3},{4,4},{5,6},{6,5},{7,7},{8,8},{9,10},{10,9... | collective-permute-start | bytes 2359304 | tf_op jit(solution)/shard_map/ppermute | solution.py:23
  3.8 188.6 %collective-permute-start.4 = (s32[512]{0:T(512)}, s32[512]{0:T(512)S(1)}, u32[]{:S(2)}, u32[]{:S(2)}) collective-permute-start(s32[512]{0:T(512)} %bitcast.99), channel_id=1, source_target_pairs={{0,0},{1,2},{2,1},{3,3},{4,4},{5,6},{6,5},{7,7},{8,8},{9,10},{10,9... | collective-permute-start | bytes 6152 | tf_op jit(solution)/shard_map/ppermute | solution.py:23
  186.2 8.2 %collective-permute-start.7 = (bf16[512,768]{1,0:T(8,128)(2,1)S(1)}, bf16[512,768]{1,0:T(8,128)(2,1)S(1)}, u32[]{:S(2)}, u32[]{:S(2)}) collective-permute-start(bf16[512,768]{1,0:T(8,128)(2,1)S(1)} %collective-permute-done.6), channel_id=1, source_target_pairs={{0,2},{2,0},{1,3},{3,1},{4,6},{6,4},{5,7},{7,5},{8,10},{10,8},{9,1... | collective-permute-start | bytes 2359304 | tf_op jit(solution)/shard_map/ppermute | solution.py:27
  192.4 1.3 collective-permute-start.5
  219.9 18.5 %collective-permute-start.8 = (bf16[1024,768]{1,0:T(8,128)(2,1)}, bf16[1024,768]{1,0:T(8,128)(2,1)S(1)}, u32[]{:S(2)}, u32[]{:S(2)}) collective-permute-start(bf16[1024,768]{1,0:T(8,128)(2,1)} %get-tuple-element.71.own_ref), channel_id=1, source_target_pairs={{0,2},{2,0},{1,3},{3,1},{4,6},{6,4},{5,7},{7,5},{8,10},{10,8},{9,1... | collective-permute-start | bytes 4718600 | tf_op jit(solution)/shard_map/ppermute | solution.py:27
  221.2 39.9 %collective-permute-start.2 = (bf16[256,768]{1,0:T(8,128)(2,1)S(1)}, bf16[256,768]{1,0:T(8,128)(2,1)S(1)}, u32[]{:S(2)}, u32[]{:S(2)}) collective-permute-start(bf16[256,768]{1,0:T(8,128)(2,1)S(1)} %collective-permute-done.1), channel_id=1, source_target_pairs={{0,2},{2,0},{1,3},{3,1},{4,6},{6,4},{5,7},{7,5},{8,10},{10,8},{9,1... | collective-permute-start | bytes 1179656 | tf_op jit(solution)/shard_map/ppermute | solution.py:27
  260.5 21.3 %collective-permute-start.9 = (bf16[1024,768]{1,0:T(8,128)(2,1)}, bf16[1024,768]{1,0:T(8,128)(2,1)S(1)}, u32[]{:S(2)}, u32[]{:S(2)}) collective-permute-start(bf16[1024,768]{1,0:T(8,128)(2,1)} %get-tuple-element.73.mid_own), channel_id=1, source_target_pairs={{0,2},{2,0},{1,3},{3,1},{4,6},{6,4},{5,7},{7,5},{8,10},{10,8},{9,1... | collective-permute-start | bytes 4718600 | tf_op jit(solution)/shard_map/ppermute | solution.py:27
  272.2 9.6 %collective-permute-start.3 = (bf16[512,768]{1,0:T(8,128)(2,1)}, bf16[512,768]{1,0:T(8,128)(2,1)S(1)}, u32[]{:S(2)}, u32[]{:S(2)}) collective-permute-start(bf16[512,768]{1,0:T(8,128)(2,1)} %get-tuple-element.70.own_ref), channel_id=1, source_target_pairs={{0,2},{2,0},{1,3},{3,1},{4,6},{6,4},{5,7},{7,5},{8,10},{10,8},{9,1... | collective-permute-start | bytes 2359304 | tf_op jit(solution)/shard_map/ppermute | solution.py:27
  272.7 1.2 collective-permute-start.13
  273.9 26.8 %collective-permute-start.14 = (bf16[256,768]{1,0:T(8,128)(2,1)S(1)}, bf16[256,768]{1,0:T(8,128)(2,1)S(1)}, u32[]{:S(2)}, u32[]{:S(2)}) collective-permute-start(bf16[256,768]{1,0:T(8,128)(2,1)S(1)} %collective-permute-done.13), channel_id=1, source_target_pairs={{0,2},{2,0},{1,3},{3,1},{4,6},{6,4},{5,7},{7,5},{8,10},{10,8},{9,1... | collective-permute-start | bytes 1179656 | tf_op jit(solution)/shard_map/ppermute | solution.py:27
  300.7 2.5 collective-permute-start.10
  329.2 2.5 collective-permute-start.15
  360.9 3.6 collective-permute-start.16
  390.4 25.6 %collective-permute-start.17 = (bf16[1024,768]{1,0:T(8,128)(2,1)}, bf16[1024,768]{1,0:T(8,128)(2,1)S(1)}, u32[]{:S(2)}, u32[]{:S(2)}) collective-permute-start(bf16[1024,768]{1,0:T(8,128)(2,1)} %get-tuple-element.95.refs_3_), channel_id=1, source_target_pairs={{0,2},{2,0},{1,3},{3,1},{4,6},{6,4},{5,7},{7,5},{8,10},{10,8},{9,1... | collective-permute-start | bytes 4718600 | tf_op jit(solution)/shard_map/ppermute | solution.py:27
  390.5 5.3 collective-permute-start.20
  390.9 70.0 %collective-permute-start.11 = (bf16[512,768]{1,0:T(8,128)(2,1)}, bf16[512,768]{1,0:T(8,128)(2,1)}, u32[]{:S(2)}, u32[]{:S(2)}) collective-permute-start(bf16[512,768]{1,0:T(8,128)(2,1)} %get-tuple-element.77), channel_id=1, source_target_pairs={{0,2},{2,0},{1,3},{3,1},{4,6},{6,4},{5,7},{7,5},{8,10},{10,8},{9,1... | collective-permute-start | bytes 2359304 | tf_op jit(solution)/shard_map/ppermute | solution.py:27
  415.6 47.2 %collective-permute-start.21 = (bf16[512,768]{1,0:T(8,128)(2,1)}, bf16[512,768]{1,0:T(8,128)(2,1)}, u32[]{:S(2)}, u32[]{:S(2)}) collective-permute-start(bf16[512,768]{1,0:T(8,128)(2,1)} %get-tuple-element.112.own_ref), channel_id=1, source_target_pairs={{0,2},{2,0},{1,3},{3,1},{4,6},{6,4},{5,7},{7,5},{8,10},{10,8},{9,1... | collective-permute-start | bytes 2359304 | tf_op jit(solution)/shard_map/ppermute | solution.py:27
  460.4 12.6 %collective-permute-start.18 = (bf16[1024,768]{1,0:T(8,128)(2,1)}, bf16[1024,768]{1,0:T(8,128)(2,1)}, u32[]{:S(2)}, u32[]{:S(2)}) collective-permute-start(bf16[1024,768]{1,0:T(8,128)(2,1)} %get-tuple-element.102.own_ref), channel_id=1, source_target_pairs={{0,2},{2,0},{1,3},{3,1},{4,6},{6,4},{5,7},{7,5},{8,10},{10,8},{9,1... | collective-permute-start | bytes 4718600 | tf_op jit(solution)/shard_map/ppermute | solution.py:27
  462.2 7.6 %collective-permute-start.12 = (bf16[256,768]{1,0:T(8,128)(2,1)S(1)}, bf16[256,768]{1,0:T(8,128)(2,1)S(1)}, u32[]{:S(2)}, u32[]{:S(2)}) collective-permute-start(bf16[256,768]{1,0:T(8,128)(2,1)S(1)} %fusion), channel_id=1, source_target_pairs={{0,0},{1,2},{2,1},{3,3},{4,4},{5,6},{6,5},{7,7},{8,8},{9,10},{10,9... | collective-permute-start | bytes 1179656 | tf_op jit(solution)/shard_map/ppermute | solution.py:23
  468.7 3.2 collective-permute-start.22
  672.8 3.7 collective-permute-start.28
  676.9 1.3 collective-permute-start.29
  678.2 4.6 collective-permute-start.30
  680.9 11.8 %collective-permute-start.23 = (f32[32]{0:T(128)S(1)}, f32[32]{0:T(128)S(1)}, u32[]{:S(2)}, u32[]{:S(2)}) collective-permute-start(f32[32]{0:T(128)S(1)} %pad_maximum_fusion.6), channel_id=1, source_target_pairs={{0,1},{1,0},{2,3},{3,2},{4,5},{5,4},{6,7},{7,6},{8,9},{9,8},{10,11... | collective-permute-start | bytes 392 | tf_op jit(solution)/shard_map/ppermute | solution.py:144
  682.9 9.9 %collective-permute-start.31 = (f32[10768]{0:T(1024)S(1)}, f32[10768]{0:T(1024)S(1)}, u32[]{:S(2)}, u32[]{:S(2)}) collective-permute-start(f32[10768]{0:T(1024)S(1)} %add.85), channel_id=1, source_target_pairs={{0,8},{8,0},{16,24},{24,16},{1,9},{9,1},{17,25},{25,17},{2,10},{10... | collective-permute-start | bytes 129224 | tf_op jit(solution)/shard_map/ppermute | solution.py:139
  685.3 25.2 %collective-permute-start.19 = (bf16[512,768]{1,0:T(8,128)(2,1)}, bf16[512,768]{1,0:T(8,128)(2,1)}, u32[]{:S(2)}, u32[]{:S(2)}) collective-permute-start(bf16[512,768]{1,0:T(8,128)(2,1)} %dynamic-slice_convert_fusion), channel_id=1, source_target_pairs={{0,0},{1,2},{2,1},{3,3},{4,4},{5,6},{6,5},{7,7},{8,8},{9,10},{10,9... | collective-permute-start | bytes 2359304 | tf_op jit(solution)/shard_map/ppermute | solution.py:23
  692.7 1.9 collective-permute-start.24
  692.8 13.4 %collective-permute-start.32 = (f32[10768]{0:T(1024)S(1)}, f32[10768]{0:T(1024)S(1)}, u32[]{:S(2)}, u32[]{:S(2)}) collective-permute-start(f32[10768]{0:T(1024)S(1)} %add.86), channel_id=1, source_target_pairs={{0,16},{16,0},{8,24},{24,8},{1,17},{17,1},{9,25},{25,9},{2,18},{18... | collective-permute-start | bytes 129224 | tf_op jit(solution)/shard_map/ppermute | solution.py:140
  694.7 3.6 collective-permute-start.25
  698.3 3.5 collective-permute-start.26
  701.8 4.4 collective-permute-start.27
  (34 other events, 460.1 us)

commit v4 on v3

--- a/solution.py
+++ b/solution.py
@@ -152,187 +152,551 @@
     return list(zip(edges[:-1], edges[1:]))
 
 
-class Place:
-    def __init__(self):
-        self.z, self.y, self.c, self.x = (lax.axis_index(name) for name in "zycx")
-        self.holds = self.c == self.x
-
-    def block(self, which):
-        back, same_y = which
-        z = lax.rem(self.z + 4 - back, 4)
-        return z * 2 + (self.y if same_y else 1 - self.y)
-
-    def target(self, axis):
-        if axis == "z":
-            return {"z": lax.rem(self.z + 1, 4)}
-        if axis == "z_back":
-            return {"z": lax.rem(self.z + 3, 4)}
-        return {axis: 1 - getattr(self, axis)}
-
-
-def greet(place):
+def place(name):
+    return lax.axis_index(name)
+
+
+def block_at(which):
+    back, same = which
+    z = lax.rem(place("z") + 4 - back, 4)
+    return z * 2 + (place("y") if same else 1 - place("y"))
+
+
+def target_of(axis):
+    if axis == "z":
+        return {"z": lax.rem(place("z") + 1, 4)}
+    if axis == "z_back":
+        return {"z": lax.rem(place("z") + 3, 4)}
+    if axis == "x_home":
+        return {"c": place("x"), "x": 1 - place("x")}
+    return {axis: 1 - place(axis)}
+
+
+def greet():
     barrier = pltpu.get_barrier_semaphore()
-    for axis in ("c", "x", "y", "z", "z_back"):
-        pl.semaphore_signal(
-            barrier, inc=1, device_id=place.target(axis), device_id_type=MESH
-        )
-    pl.semaphore_wait(barrier, 5)
-
-
-def gather_kernel(own_ref, out_ref, local_sem, send_sems, recv_sems):
-    place = Place()
-    rows = own_ref.shape[0]
-    cuts = column_cuts(own_ref.shape[1])
-    holds = place.holds
-    greet(place)
-    own_block = place.block((0, True))
-    own_rows = out_ref.at[own_block, pl.ds(place.c * rows, rows), :]
-    to_other = pltpu.make_async_remote_copy(
-        src_ref=own_ref,
-        dst_ref=own_rows,
-        send_sem=send_sems.at[72],
-        recv_sem=recv_sems.at[24],
-        device_id=place.target("c"),
-        device_id_type=MESH,
-    )
-    to_self = pltpu.make_async_copy(own_ref, own_rows, local_sem)
-    pl.when(jnp.logical_not(holds))(lambda: to_other.start())
-
-    @pl.when(holds)
-    def _():
-        to_self.start()
-        to_self.wait()
-        to_other.wait_recv()
-
-    pending = []
-
-    def copy(group, which, axis):
-        begin, end = cuts[group]
-        block = place.block(which)
-        piece = out_ref.at[block, :, pl.ds(begin, end - begin)]
-        number = {"z": 0, "y": 1, "x": 2}[axis]
-        return pltpu.make_async_remote_copy(
-            src_ref=piece,
-            dst_ref=piece,
-            send_sem=send_sems.at[(group * 8 + block) * 3 + number],
-            recv_sem=recv_sems.at[group * 8 + block],
-            device_id=place.target(axis),
-            device_id_type=MESH,
-        )
-
-    def send(group, which, axis, who):
-        copy(group, which, axis).start()
-        pending.append((functools.partial(copy, group, which, axis), who))
-
-    def arrive(group, block):
-        copy(group, block, "x").wait_recv()
-
-    here, there = (lambda back: (back, True)), (lambda back: (back, False))
-    first, second, third = 0, 1, 2
-
-    @pl.when(holds)
-    def _():
-        send(first, here(0), "x", True)
-        send(second, here(0), "y", True)
-        send(third, here(0), "z", True)
-        send(third, here(0), "y", True)
-        send(third, here(0), "x", True)
-        send(first, here(0), "z", True)
-        send(first, here(0), "y", True)
-        send(second, here(0), "z", True)
-        send(second, here(0), "x", True)
-
-    @pl.when(jnp.logical_not(holds))
-    def _():
-        arrive(third, here(0))
-        send(third, here(0), "z", False)
-        send(third, here(0), "y", False)
-
-    for back in range(1, 5):
-
-        @pl.when(holds)
-        def _():
-            if back < 4:
-                arrive(first, here(back))
+    targets = [target_of(axis) for axis in ("c", "y", "z", "z_back", "x")]
+    targets.append({"c": 1 - place("c"), "x": 1 - place("x")})
+    for target in targets:
+        pl.semaphore_signal(barrier, inc=1, device_id=target, device_id_type=MESH)
+    pl.semaphore_wait(barrier, len(targets))
+
+
+def here(back):
+    return (back, True)
+
+
+def there(back):
+    return (back, False)
+
+
+class Mover:
+    def __init__(self, send_sems):
+        self.steps = {True: [], False: []}
+        self.sent = {True: [], False: []}
+        self.done = 0
+        self.send_sems = send_sems
+
+    def send(self, home, source, target, recv_sem, device):
+        number = len(self.sent[home])
+
+        def copy():
+            return pltpu.make_async_remote_copy(
+                src_ref=source(),
+                dst_ref=target(),
+                send_sem=self.send_sems.at[number],
+                recv_sem=recv_sem(),
+                device_id=device(),
+                device_id_type=MESH,
+            )
+
+        self.sent[home].append(copy)
+        self.steps[home].append(lambda: copy().start())
+
+    def wait(self, home, target, recv_sem):
+        def step():
+            pltpu.make_async_remote_copy(
+                src_ref=target(),
+                dst_ref=target(),
+                send_sem=self.send_sems.at[0],
+                recv_sem=recv_sem(),
+                device_id=target_of("c"),
+                device_id_type=MESH,
+            ).wait_recv()
+
+        self.steps[home].append(step)
+
+    def local(self, home, step):
+        self.steps[home].append(step)
+
+    def run(self, part, parts):
+        for home in (True, False):
+            steps = self.steps[home]
+            chosen = steps[len(steps) * part // parts : len(steps) * (part + 1) // parts]
+            if not chosen:
+                continue
+            wanted = place("c") == place("x")
+
+            @pl.when(wanted if home else jnp.logical_not(wanted))
+            def _():
+                for step in chosen:
+                    step()
+
+    def finish(self):
+        for home in (True, False):
+            wanted = place("c") == place("x")
+
+            @pl.when(wanted if home else jnp.logical_not(wanted))
+            def _():
+                for copy in self.sent[home]:
+                    copy().wait_send()
+
+
+class Gather(Mover):
+    def __init__(self, own_ref, out_ref, stage_ref, local_sem, send_sems, recv_sems):
+        super().__init__(send_sems)
+        rows, columns = own_ref.shape
+        cuts = column_cuts(columns)
+        (begin_a, end_a), (begin_b, end_b), (begin_c, end_c) = cuts
+        first, second, third = 0, 1, 2
+
+        def out_piece(group, which, parity):
+            begin, end = cuts[group]
+            return out_ref.at[
+                block_at(which), pl.ds(parity() * rows, rows), pl.ds(begin, end - begin)
+            ]
+
+        def out_sem(group, which, parity):
+            return recv_sems.at[(group * 8 + block_at(which)) * 2 + parity()]
+
+        def stage_piece(group, which):
+            begin, end = cuts[group]
+            return stage_ref.at[block_at(which), :, pl.ds(begin, end - begin)]
+
+        def stage_sem(group, which):
+            return recv_sems.at[48 + group * 8 + block_at(which)]
+
+        def core():
+            return place("c")
+
+        def other():
+            return 1 - place("c")
+
+        self_copies = {
+            True: lambda: pltpu.make_async_copy(
+                own_ref, out_ref.at[block_at(here(0)), pl.ds(core() * rows, rows), :], local_sem
+            ),
+        }
+
+        def own_piece(group):
+            begin, end = cuts[group]
+            return own_ref.at[:, pl.ds(begin, end - begin)]
+
+        for home in (True, False):
+            arrived = set()
+
+            def plane(group, which):
+                if which == here(0):
+                    return functools.partial(own_piece, group)
+                if home:
+                    return functools.partial(out_piece, group, which, core)
+                return functools.partial(stage_piece, group, which)
+
+            def plane_target(group, which):
+                if home:
+                    return (
+                        functools.partial(out_piece, group, which, core),
+                        functools.partial(out_sem, group, which, core),
+                    )
+                return (
+                    functools.partial(stage_piece, group, which),
+                    functools.partial(stage_sem, group, which),
+                )
+
+            def plane_send(group, which, axis):
+                target, sem = plane_target(group, which)
+                self.send(home, plane(group, which), target, sem, functools.partial(target_of, axis))
+
+            def plane_wait(group, which):
+                if which == here(0):
+                    return
+                target, sem = plane_target(group, which)
+                self.wait(home, target, sem)
+                if home:
+                    arrived.add((group, which, "core"))
+
+            def deliver(group, which):
+                target = functools.partial(out_piece, group, which, core)
+                sem = functools.partial(out_sem, group, which, core)
+                source = plane(group, which)
+                self.send(home, source, target, sem, functools.partial(target_of, "x_home"))
+                if not home:
+                    self.send(home, source, target, sem, functools.partial(target_of, "c"))
+
+            def core_send(group, which, name, axis):
+                parity = core if name == "core" else other
+                if home and which == here(0) and name == "core":
+                    source = functools.partial(own_piece, group)
+                else:
+                    source = functools.partial(out_piece, group, which, parity)
+                self.send(
+                    home,
+                    source,
+                    functools.partial(out_piece, group, which, parity),
+                    functools.partial(out_sem, group, which, parity),
+                    functools.partial(target_of, axis),
+                )
+
+            def core_wait(group, which, name):
+                if home and which == here(0) and name == "core":
+                    return
+                if (group, which, name) in arrived:
+                    return
+                arrived.add((group, which, name))
+                parity = core if name == "core" else other
+                self.wait(
+                    home,
+                    functools.partial(out_piece, group, which, parity),
+                    functools.partial(out_sem, group, which, parity),
+                )
+
+            if home:
+                self.local(home, lambda: self_copies[True]().start())
+            deliver(third, here(0))
+            plane_send(first, here(0), "z")
+            plane_send(second, here(0), "z")
+            plane_send(first, here(0), "y")
+            deliver(second, here(0))
+            deliver(first, here(0))
+            names = ("core", "other") if home else ("other", "core")
+            for name in names:
+                core_wait(third, here(0), name)
+                core_send(third, here(0), name, "z")
+                core_send(third, here(0), name, "y")
+            for name in names:
+                core_wait(second, here(0), name)
+                core_send(second, here(0), name, "y")
+            for back in (1, 2, 3):
+                plane_wait(first, here(back))
                 if back < 3:
-                    send(first, here(back), "z", True)
-                send(first, here(back), "y", True)
-                send(first, here(back), "x", True)
-                arrive(second, here(back))
+                    plane_send(first, here(back), "z")
+                plane_send(first, here(back), "y")
+                plane_wait(second, here(back))
                 if back < 3:
-                    send(second, here(back), "z", True)
-                send(second, here(back), "x", True)
-                send(second, here(back), "y", True)
-            arrive(first, there(back - 1))
-            send(first, there(back - 1), "x", True)
-
-        @pl.when(jnp.logical_not(holds))
-        def _():
-            arrive(second, here(back - 1))
-            send(second, here(back - 1), "y", False)
-
-        if back < 4:
-            if back == 1:
-                arrive(third, there(0))
-                send(third, there(0), "z", None)
-            arrive(third, here(back))
-            if back < 3:
-                send(third, here(back), "z", None)
-            arrive(third, there(back))
-            if back < 3:
-                send(third, there(back), "z", None)
-    for back in range(4):
-        arrive(second, there(back))
-
-    @pl.when(jnp.logical_not(holds))
-    def _():
-        for back in range(4):
-            arrive(first, here(back))
-            arrive(first, there(back))
-        to_other.wait_send()
-        for one, who in pending:
-            if who is False:
-                one().wait_send()
-
-    @pl.when(holds)
-    def _():
-        for one, who in pending:
-            if who is True:
-                one().wait_send()
-
-    for one, who in pending:
-        if who is None:
-            one().wait_send()
-
-
-def gather_all(own):
+                    plane_send(second, here(back), "z")
+                deliver(second, here(back))
+                deliver(first, here(back))
+                plane_wait(first, there(back - 1))
+                deliver(first, there(back - 1))
+                if back == 1:
+                    for name in names:
+                        core_wait(third, there(0), name)
+                        core_send(third, there(0), name, "z")
+                for which in (here(back), there(back)):
+                    for name in names:
+                        core_wait(third, which, name)
+                        if back < 3:
+                            core_send(third, which, name, "z")
+                for name in names:
+                    core_wait(second, here(back), name)
+                    core_send(second, here(back), name, "y")
+            plane_wait(first, there(3))
+            deliver(first, there(3))
+            for group in (third, second, first):
+                for back in range(4):
+                    for which in (here(back), there(back)):
+                        for name in ("core", "other"):
+                            core_wait(group, which, name)
+            if home:
+                self.local(home, lambda: self_copies[True]().wait())
+
+
+GATHER_SENDS = 64
+
+
+def gather_kernel(own_ref, out_ref, stage_ref, local_sem, send_sems, recv_sems):
+    greet()
+    mover = Gather(own_ref, out_ref, stage_ref, local_sem, send_sems, recv_sems)
+    mover.run(0, 1)
+    mover.finish()
+
+
+def gather_scratch(rows, columns):
+    cuts = column_cuts(columns)
+    return [
+        pltpu.VMEM((8, rows, cuts[1][1]), low),
+        pltpu.SemaphoreType.DMA,
+        pltpu.SemaphoreType.DMA((GATHER_SENDS,)),
+        pltpu.SemaphoreType.DMA((64,)),
+    ]
+
+
+def gather_all(own, number=0):
     rows, columns = own.shape
     return pl.pallas_call(
         gather_kernel,
         out_shape=jax.ShapeDtypeStruct((8, 2 * rows, columns), own.dtype),
         in_specs=[pl.BlockSpec(memory_space=pl.ANY)],
         out_specs=pl.BlockSpec(memory_space=pl.ANY),
-        scratch_shapes=[
-            pltpu.SemaphoreType.DMA,
-            pltpu.SemaphoreType.DMA((73,)),
-            pltpu.SemaphoreType.DMA((25,)),
-        ],
-        compiler_params=pltpu.CompilerParams(collective_id=0, has_side_effects=True),
+        scratch_shapes=gather_scratch(rows, columns),
+        compiler_params=pltpu.CompilerParams(
+            collective_id=number, has_side_effects=True, vmem_limit_bytes=40 << 20
+        ),
         name="gather_weights",
     )(own)
+
+
+class Scatter(Mover):
+    def __init__(self, total, final, stage, x_in, ya_in, yb_in, z_in, zc_in, yc_in, send_sems, recv_sems):
+        super().__init__(send_sems)
+        rows = total.shape[1] // 2
+        columns = total.shape[2]
+        cuts = column_cuts(columns)
+        first, second, third = 0, 1, 2
+        widths = [end - begin for begin, end in cuts]
+
+        def part(group):
+            begin, end = cuts[group]
+            return pl.ds(begin, end - begin)
+
+        def core_piece(group, which, parity=None):
+            if parity is None:
+                return total.at[block_at(which), :, part(group)]
+            return total.at[block_at(which), pl.ds(parity() * rows, rows), part(group)]
+
+        def slot_of(which):
+            return which[0] + (0 if which[1] else 4)
+
+        def x_piece(group, which):
+            return x_in.at[slot_of(which), :, part(group)]
+
+        def stage_piece(group, which):
+            return stage.at[slot_of(which), :, part(group)]
+
+        def sem(number):
+            return lambda: recv_sems.at[number]
+
+        def core():
+            return place("c")
+
+        def other():
+            return 1 - place("c")
+
+        def add_rows(held_of, came_of, count, final_part=None):
+            def step():
+                held, came = held_of(), came_of()
+
+                @pl.loop(0, count // 16)
+                def _(number):
+                    at = pl.ds(pl.multiple_of(number * 16, 16), 16)
+                    if final_part is None:
+                        held[at, :] = held[at, :] + came[at, :]
+                    else:
+                        final[at, final_part] = held[at, :].astype(wide) + came[at, :].astype(wide)
+
+            return step
+
+        for home in (True, False):
+
+            def plane(group, which):
+                if home:
+                    return functools.partial(core_piece, group, which, core)
+                return functools.partial(stage_piece, group, which)
+
+            def x_sends(group, which):
+                number = group * 8 + slot_of(which)
+                if home:
+                    self.send(
+                        home,
+                        functools.partial(core_piece, group, which, other),
+                        functools.partial(stage_piece, group, which),
+                        sem(24 + number),
+                        functools.partial(target_of, "c"),
+                    )
+                    return
+                for parity in (0, 1):
+                    self.send(
+                        home,
+                        functools.partial(core_piece, group, which, functools.partial(parity_value, parity)),
+                        functools.partial(x_piece, group, which),
+                        sem(number),
+                        functools.partial(home_core, parity),
+                    )
+
+            def x_add(group, which, last=False):
+                number = group * 8 + slot_of(which)
+                if not home:
+                    self.wait(home, functools.partial(stage_piece, group, which), sem(24 + number))
+                self.wait(home, functools.partial(x_piece, group, which), sem(number))
+                self.local(
+                    home,
+                    add_rows(
+                        plane(group, which),
+                        functools.partial(x_piece, group, which),
+                        rows,
+                        part(group) if last else None,
+                    ),
+                )
+
+            def z_slot(group, back):
+                return lambda: z_in.at[back, :, part(group)]
+
+            def z_send(group, back):
+                self.send(
+                    home,
+                    plane(group, here(back)),
+                    z_slot(group, back - 1),
+                    sem(60 + group * 4 + back - 1),
+                    functools.partial(target_of, "z_back"),
+                )
+
+            def z_add(group, back):
+                self.wait(home, z_slot(group, back), sem(60 + group * 4 + back))
+                self.local(
+                    home,
+                    add_rows(
+                        plane(group, here(back)),
+                        z_slot(group, back),
+                        rows,
+                        part(group) if back == 0 else None,
+                    ),
+                )
+
+            def ya_slot(back):
+                return lambda: ya_in.at[back]
+
+            def yb_slot(back):
+                return lambda: yb_in.at[back]
+
+            def zc_slot(which):
+                back, same = which
+                return lambda: zc_in.at[back + (0 if same else 3)]
+
+            def zc_send(which):
+                back, same = which
+                self.send(
+                    home,
+                    functools.partial(core_piece, third, which),
+                    zc_slot((back - 1, same)),
+                    sem(72 + back - 1 + (0 if same else 3)),
+                    functools.partial(target_of, "z_back"),
+                )
+
+            def zc_add(which):
+                back, same = which
+                self.wait(home, zc_slot(which), sem(72 + back + (0 if same else 3)))
+                self.local(
+                    home,
+                    add_rows(functools.partial(core_piece, third, which), zc_slot(which), 2 * rows),
+                )
+
+            def second_steps(back):
+                x_add(second, here(back))
+                if back < 3:
+                    z_add(second, back)
+                if back > 0:
+                    z_send(second, back)
+
+            zc_send(there(3))
+            zc_send(here(3))
+            for back in (3, 2, 1, 0):
+                self.send(
+                    home,
+                    functools.partial(core_piece, second, there(back)),
+                    yb_slot(back),
+                    sem(52 + back),
+                    functools.partial(target_of, "y"),
+                )
+                if back > 1:
+                    x_sends(first, there(back))
+                    x_sends(first, here(back))
+            for back in (3, 2, 1, 0):
+                self.wait(home, yb_slot(back), sem(52 + back))
+                self.local(
+                    home,
+                    add_rows(functools.partial(core_piece, second, here(back)), yb_slot(back), 2 * rows),
+                )
+                x_sends(second, here(back))
+                if back > 1:
+                    x_sends(first, there(back - 2))
+                    x_sends(first, here(back - 2))
+                if back < 3:
+                    for which in (there(back), here(back)):
+                        zc_add(which)
+                        if back > 0:
+                            zc_send(which)
+                        elif not which[1]:
+                            self.send(
+                                home,
+                                functools.partial(core_piece, third, there(0)),
+                                lambda: yc_in.at[...],
+                                sem(56),
+                                functools.partial(target_of, "y"),
+                            )
+                x_add(first, there(back))
+                self.send(
+                    home,
+                    plane(first, there(back)),
+                    ya_slot(back),
+                    sem(48 + back),
+                    functools.partial(target_of, "y"),
+                )
+                x_add(first, here(back))
+                if back < 3:
+                    second_steps(back + 1)
+                if back == 0:
+                    self.wait(home, lambda: yc_in.at[...], sem(56))
+                    self.local(
+                        home,
+                        add_rows(
+                            functools.partial(core_piece, third, here(0)),
+                            lambda: yc_in.at[...],
+                            2 * rows,
+                        ),
+                    )
+                    x_sends(third, here(0))
+                self.wait(home, ya_slot(back), sem(48 + back))
+                self.local(home, add_rows(plane(first, here(back)), ya_slot(back), rows))
+                if back < 3:
+                    z_add(first, back)
+                if back > 0:
+                    z_send(first, back)
+            second_steps(0)
+            x_add(third, here(0), last=True)
+
+
+def parity_value(parity):
+    return parity
+
+
+def home_core(parity):
+    return {"c": parity, "x": place("c")}
+
+
+SCATTER_SENDS = 48
+
+
+def scatter_scratch(rows, columns):
+    cuts = column_cuts(columns)
+    widths = [end - begin for begin, end in cuts]
+    return [
+        pltpu.VMEM((8, 2 * rows, columns), low),
+        pltpu.VMEM((8, rows, columns), low),
+        pltpu.VMEM((8, rows, columns), low),
+        pltpu.VMEM((4, rows, widths[0]), low),
+        pltpu.VMEM((4, 2 * rows, widths[1]), low),
+        pltpu.VMEM((4, rows, columns), low),
+        pltpu.VMEM((6, 2 * rows, widths[2]), low),
+        pltpu.VMEM((2 * rows, widths[2]), low),
+        pltpu.SemaphoreType.DMA((SCATTER_SENDS,)),
+        pltpu.SemaphoreType.DMA((80,)),
+    ]
 
 
 def scatter_kernel(widths, *refs):
     count = len(widths)
     grads = refs[:count]
-    out_ref, total, final = refs[count : count + 3]
-    buffers = refs[count + 3 : count + 6]
-    load_sems, send_sems, recv_sems, end_sem = refs[count + 6 :]
-    place = Place()
-    holds = place.holds
-    rows = total.shape[1]
-    columns = total.shape[2]
-    cuts = column_cuts(columns)
+    final, total = refs[count : count + 2]
+    load_sems = refs[-1]
     loads = []
     begin = 0
     for number, width in enumerate(widths):
@@ -342,185 +706,145 @@
         one.start()
         loads.append(one)
         begin += width
-    greet(place)
+    greet()
     for one in loads:
         one.wait()
-    here, there = (lambda back: (back, True)), (lambda back: (back, False))
-    pending = []
-    slots = {}
-
-    def copy(group, which, slot, axis):
-        begin, end = cuts[group]
-        block = place.block(which)
-        return pltpu.make_async_remote_copy(
-            src_ref=total.at[block, :, pl.ds(begin, end - begin)],
-            dst_ref=buffers[group].at[slot],
-            send_sem=send_sems.at[group * 16 + slot],
-            recv_sem=recv_sems.at[group * 16 + slot],
-            device_id=place.target(axis),
-            device_id_type=MESH,
-        )
-
-    def send(group, which, slot, axis, who):
-        copy(group, which, slot, axis).start()
-        pending.append((functools.partial(copy, group, which, slot, axis), who))
-
-    def add(group, which, slot, last=False):
-        copy(group, which, slot, "x").wait_recv()
-        block = place.block(which)
-        begin, end = cuts[group]
-        part = pl.ds(begin, end - begin)
-
-        @pl.loop(0, rows // 16)
-        def _(step):
-            at = pl.ds(pl.multiple_of(step * 16, 16), 16)
-            held = total[block, at, part]
-            came = buffers[group][slot, at, :]
-            if last:
-                final[at, part] = held.astype(wide) + came.astype(wide)
-            else:
-                total[block, at, part] = held + came
-
-    first, second, third = 0, 1, 2
-    for which, offset in ((there, 3), (here, 0)):
-        send(third, which(3), offset + 2, "z_back", None)
-    for back in (3, 2, 1, 0):
-        send(second, there(back), back, "y", None)
-
-    @pl.when(jnp.logical_not(holds))
-    def _():
-        for back in (3, 2, 1, 0):
-            send(first, there(back), 4 + back, "x", False)
-            send(first, here(back), back, "x", False)
-
-    for back in (3, 2, 1, 0):
-        if back < 3:
-            for which, offset in ((there, 3), (here, 0)):
-                add(third, which(back), offset + back)
-                if back > 0:
-                    send(third, which(back), offset + back - 1, "z_back", None)
-                elif offset == 3:
-                    send(third, which(0), 6, "y", None)
-        add(second, here(back), back)
-
-        @pl.when(jnp.logical_not(holds))
-        def _():
-            send(second, here(back), 4 + back, "x", False)
-
-        @pl.when(holds)
-        def _():
-            add(first, there(back), 4 + back)
-            send(first, there(back), 8 + back, "y", True)
-            add(first, here(back), back)
-            add(first, here(back), 8 + back, last=False)
-            if back < 3:
-                add(first, here(back), 12 + back, last=back == 0)
-            if back > 0:
-                send(first, here(back), 12 + back - 1, "z_back", True)
-
-    add(third, here(0), 6)
-
-    @pl.when(jnp.logical_not(holds))
-    def _():
-        send(third, here(0), 7, "x", False)
-
-    end_copy = pltpu.make_async_remote_copy(
-        src_ref=final.at[pl.ds((1 - place.c) * (rows // 2), rows // 2), :],
-        dst_ref=out_ref,
-        send_sem=end_sem.at[0],
-        recv_sem=end_sem.at[1],
-        device_id=place.target("c"),
-        device_id_type=MESH,
-    )
-    keep_copy = pltpu.make_async_copy(
-        final.at[pl.ds(place.c * (rows // 2), rows // 2), :], out_ref, end_sem.at[2]
-    )
-
-    @pl.when(holds)
-    def _():
-        for back in (3, 2, 1, 0):
-            add(second, here(back), 4 + back)
-            if back < 3:
-                add(second, here(back), 8 + back, last=back == 0)
-            if back > 0:
-                send(second, here(back), 8 + back - 1, "z_back", True)
-        add(third, here(0), 7, last=True)
-        end_copy.start()
-        keep_copy.start()
-        keep_copy.wait()
-        end_copy.wait_send()
-        for one, who in pending:
-            if who is True:
-                one().wait_send()
-
-    @pl.when(jnp.logical_not(holds))
-    def _():
-        end_copy.wait_recv()
-        for one, who in pending:
-            if who is False:
-                one().wait_send()
-
-    for one, who in pending:
-        if who is None:
-            one().wait_send()
-
-
-def scatter_all(parts):
+    mover = Scatter(total, final, *refs[count + 2 : -1])
+    mover.run(0, 1)
+    mover.finish()
+
+
+def scatter_all(parts, number=1):
     depth = parts[0].shape[0]
     widths = [part.shape[1] for part in parts]
     columns = sum(widths)
-    rows = depth // 8
-    cuts = column_cuts(columns)
+    rows = depth // 16
     return pl.pallas_call(
         functools.partial(scatter_kernel, widths),
-        out_shape=jax.ShapeDtypeStruct((rows // 2, columns), wide),
+        out_shape=jax.ShapeDtypeStruct((rows, columns), wide),
         in_specs=[pl.BlockSpec(memory_space=pl.ANY)] * len(parts),
-        out_specs=pl.BlockSpec(memory_space=pl.ANY),
-        scratch_shapes=[
-            pltpu.VMEM((8, rows, columns), low),
-            pltpu.VMEM((rows, columns), wide),
-            pltpu.VMEM((15, rows, cuts[0][1] - cuts[0][0]), low),
-            pltpu.VMEM((11, rows, cuts[1][1] - cuts[1][0]), low),
-            pltpu.VMEM((8, rows, cuts[2][1] - cuts[2][0]), low),
-            pltpu.SemaphoreType.DMA((len(parts),)),
-            pltpu.SemaphoreType.DMA((48,)),
-            pltpu.SemaphoreType.DMA((48,)),
-            pltpu.SemaphoreType.DMA((3,)),
-        ],
+        out_specs=pl.BlockSpec(memory_space=pltpu.VMEM),
+        scratch_shapes=scatter_scratch(rows, columns) + [pltpu.SemaphoreType.DMA((len(parts),))],
         compiler_params=pltpu.CompilerParams(
-            collective_id=1, has_side_effects=True, vmem_limit_bytes=56 << 20
+            collective_id=number, has_side_effects=True, vmem_limit_bytes=58 << 20
         ),
         name="scatter_gradients",
-    )(*[part.reshape(8, rows, part.shape[1]) for part in parts])
-
-
-def fits_kernels():
-    return lax.axis_size("z") == 4
-
-
-def gather_groups(groups):
-    if fits_kernels():
-        whole = gather_all(jnp.concatenate(groups, axis=1))
-        whole = whole.reshape(-1, whole.shape[2])
-        pieces = []
-        begin = 0
-        for group in groups:
-            pieces.append(whole[:, begin : begin + group.shape[1]])
-            begin += group.shape[1]
-        return pieces
-    return [gather_weights(group, "zyx") for group in groups]
-
-
-def scatter_groups(groups):
-    if fits_kernels():
-        whole = scatter_all(groups)
-        pieces = []
-        begin = 0
-        for group in groups:
-            pieces.append(whole[:, begin : begin + group.shape[1]])
-            begin += group.shape[1]
-        return pieces
-    return [scatter_gradient(group, "xyz") for group in groups]
+    )(*[part.reshape(8, 2 * rows, part.shape[1]) for part in parts])
+
+
+class Rider:
+    def __init__(self, kind, operand, number):
+        self.kind = kind
+        self.number = number
+        if kind == "gather":
+            rows, columns = operand.shape
+            self.operand = operand
+            self.out = jax.ShapeDtypeStruct((8, 2 * rows, columns), operand.dtype)
+            self.out_spec = pl.BlockSpec(memory_space=pl.ANY)
+            self.scratch = gather_scratch(rows, columns)
+        else:
+            depth, columns = operand.shape
+            rows = depth // 16
+            self.operand = operand.reshape(8, 2 * rows, columns)
+            self.out = jax.ShapeDtypeStruct((rows, columns), wide)
+            self.out_spec = pl.BlockSpec(memory_space=pltpu.VMEM)
+            self.scratch = scatter_scratch(rows, columns) + [pltpu.SemaphoreType.DMA]
+
+
+class Ticks:
+    def __init__(self, rider, operand_ref, out_ref, scratch):
+        self.rider = rider
+        self.refs = (operand_ref, out_ref, scratch)
+        self.mover = None
+
+    def begin(self, parts):
+        if self.rider is None:
+            return
+        operand_ref, out_ref, scratch = self.refs
+        self.parts = parts
+        if self.rider.kind == "gather":
+            self.mover = Gather(operand_ref, out_ref, *scratch)
+        else:
+
+            def load():
+                return pltpu.make_async_copy(operand_ref, scratch[0], scratch[-1])
+
+            load().start()
+            self.mover = Scatter(scratch[0], out_ref, *scratch[1:-1])
+            for home in (True, False):
+                self.mover.steps[home].insert(0, lambda: load().wait())
+        greet()
+
+    def __call__(self, part):
+        if self.mover is not None:
+            self.mover.run(part, self.parts)
+
+    def in_loop(self, step, steps, offset, stride, inner):
+        if self.mover is None:
+            return
+        for number in range(steps):
+
+            @pl.when(step == number)
+            def _():
+                self(offset + number * stride + inner)
+
+    def end(self):
+        if self.mover is not None:
+            self.mover.finish()
+
+
+def ride_call(body, operands, in_specs, outs, scratch, rider, name):
+    count_in, count_out, count_scratch = len(operands), len(outs), len(scratch)
+    out_specs = [pl.BlockSpec(memory_space=pltpu.VMEM)] * count_out
+    options = dict(vmem_limit_bytes=60 << 20)
+    operands, in_specs, outs, scratch = list(operands), list(in_specs), list(outs), list(scratch)
+    if rider is not None:
+        operands.append(rider.operand)
+        in_specs.append(pl.BlockSpec(memory_space=pl.ANY))
+        outs.append(rider.out)
+        out_specs.append(rider.out_spec)
+        scratch += rider.scratch
+        options.update(collective_id=rider.number, has_side_effects=True)
+
+    def kernel(*refs):
+        ins, rest = refs[:count_in], refs[count_in:]
+        operand_ref = out_ref = None
+        extra = ()
+        if rider is not None:
+            operand_ref, rest = rest[0], rest[1:]
+        mine, rest = rest[:count_out], rest[count_out:]
+        if rider is not None:
+            out_ref, rest = rest[0], rest[1:]
+        own, extra = rest[:count_scratch], rest[count_scratch:]
+        ticks = Ticks(rider, operand_ref, out_ref, extra)
+        body(ticks, *ins, *mine, *own)
+        ticks.end()
+
+    return pl.pallas_call(
+        kernel,
+        out_shape=tuple(outs),
+        in_specs=in_specs,
+        out_specs=tuple(out_specs),
+        scratch_shapes=scratch,
+        compiler_params=pltpu.CompilerParams(**options),
+        name=name,
+    )(*operands)
+
+
+def whole():
+    return pl.BlockSpec(memory_space=pltpu.VMEM)
+
+
+def scalar():
+    return pl.BlockSpec(memory_space=pltpu.SMEM)
+
+
+def weight_spec(weights):
+    return pl.BlockSpec(memory_space=pltpu.VMEM)
+
+
+def shaped(rows, columns, kind):
+    return jax.ShapeDtypeStruct((rows, columns), kind)
 
 
 def dot_nn(left, right):
@@ -619,9 +943,12 @@
 
 
 def feed_forward_kernel(
-    rows_norm, x_ref, own_ref, other_ref, w_ref, vec_ref, x_out, normed_out, hidden_out, slope_out, part_out
+    rows_norm, ticks, x_ref, own_ref, other_ref, w_ref, vec_ref, x_out, normed_out, hidden_out, slope_out, part_out
 ):
     units = w_ref.shape[1] // 2
+    steps = x_ref.shape[0] // CHUNK
+    pieces = units // 512
+    ticks.begin(steps * pieces)
     gain = vec_ref[rows_norm : rows_norm + 1, :]
     shift = vec_ref[rows_norm + 1 : rows_norm + 2, :]
 
@@ -634,6 +961,7 @@
         normed_out[at, :] = normed
         part = jnp.zeros((CHUNK, x.shape[1]), wide)
         for begin in range(0, units, 512):
+            ticks.in_loop(step, steps, 0, pieces, begin // 512)
             before = dot_nn(normed, w_ref[:, begin : begin + 512])
             value, slope = gelu_pair(before)
             hidden = value.astype(low)
@@ -643,34 +971,33 @@
         part_out[at, :] = part.astype(low)
 
 
-def params(limit=56):
-    return pltpu.CompilerParams(vmem_limit_bytes=limit << 20)
-
-
-def shaped(rows, columns, kind):
-    return jax.ShapeDtypeStruct((rows, columns), kind)
-
-
-def feed_forward_call(rows_norm, x, own, other, weights, vectors):
+def feed_forward_call(rows_norm, x, own, other, weights, vectors, rider=None):
     rows, depth = x.shape
-    units = weights.shape[1] // 2
-    return pl.pallas_call(
+    units = weights[1] // 2
+    return ride_call(
         functools.partial(feed_forward_kernel, rows_norm),
-        out_shape=(
+        [x, own, other, weights[0], vectors],
+        [whole(), whole(), whole(), weight_spec(weights), whole()],
+        [
             shaped(rows, depth, wide),
             shaped(rows, depth, low),
             shaped(rows, units, low),
             shaped(rows, units, low),
             shaped(rows, depth, low),
-        ),
-        compiler_params=params(),
-        name="feed_forward",
-    )(x, own, other, weights, vectors)
-
-
-def feed_backward_body(normed_ref, hidden_ref, slope_in, w_ref, part_out, grad_out, low_ref, slope_ref, turned_ref, turned_low):
+        ],
+        [],
+        rider,
+        "feed_forward",
+    )
+
+
+def feed_backward_body(ticks, normed_ref, hidden_ref, slope_in, w_ref, part_out, grad_out, low_ref, slope_ref, turned_ref, turned_low):
     rows, depth = low_ref.shape
     units = w_ref.shape[1] // 2
+    steps = rows // CHUNK
+    pieces = units // 512
+    offset = 1 + steps * pieces
+    ticks(0)
     turn_into(turned_low, low_ref)
     turn_into(turned_ref, normed_ref)
 
@@ -680,6 +1007,7 @@
         grads = low_ref[at, :]
         part = jnp.zeros((CHUNK, depth), wide)
         for begin in range(0, units, 512):
+            ticks.in_loop(step, steps, 1, pieces, begin // 512)
             grad = dot_nn(grads, w_ref[:, units + begin : units + begin + 512])
             grad = (grad * slope_in[at, begin : begin + 512].astype(wide)).astype(low)
             slope_ref[at, begin : begin + 512] = grad
@@ -687,6 +1015,7 @@
         part_out[at, :] = part.astype(low)
 
     for begin in range(0, units, 256):
+        ticks(offset + begin // 256)
         grad_out[:, begin : begin + 256] = dot_nn(
             turned_ref[...], slope_ref[:, begin : begin + 256]
         ).astype(low)
@@ -704,16 +1033,8 @@
     ]
 
 
-def whole():
-    return pl.BlockSpec(memory_space=pltpu.VMEM)
-
-
-def scalar():
-    return pl.BlockSpec(memory_space=pltpu.SMEM)
-
-
 def last_feed_backward_kernel(
-    length_ref, cotangent_ref, normed_ref, hidden_ref, slope_in, w_ref, part_out, grad_out, low_ref, *rest
+    ticks, length_ref, cotangent_ref, normed_ref, hidden_ref, slope_in, w_ref, part_out, grad_out, low_ref, *rest
 ):
     rows, depth = cotangent_ref.shape
     place = lax.broadcasted_iota(jnp.int32, (CHUNK, depth), 0)
@@ -725,45 +1046,50 @@
         rows_here = cotangent_ref[at, :].astype(wide)
         low_ref[at, :] = jnp.where(first_row + place < length_ref[0], rows_here, 0.0).astype(low)
 
-    feed_backward_body(normed_ref, hidden_ref, slope_in, w_ref, part_out, grad_out, low_ref, *rest)
-
-
-def last_feed_backward_call(length, cotangent, normed, hidden, slope, weights):
+    feed_backward_body(ticks, normed_ref, hidden_ref, slope_in, w_ref, part_out, grad_out, low_ref, *rest)
+
+
+def last_feed_backward_call(length, cotangent, normed, hidden, slope, weights, rider=None):
     rows, depth = cotangent.shape
     units = hidden.shape[1]
-    return pl.pallas_call(
+    return ride_call(
         last_feed_backward_kernel,
-        out_shape=(shaped(rows, depth, low), shaped(depth, 2 * units, low), shaped(rows, depth, low)),
-        in_specs=[scalar()] + [whole()] * 5,
-        scratch_shapes=feed_backward_scratch(rows, depth, units)[1:],
-        compiler_params=params(),
-        name="last_feed_backward",
-    )(length, cotangent, normed, hidden, slope, weights)
+        [length, cotangent, normed, hidden, slope, weights[0]],
+        [scalar()] + [whole()] * 4 + [weight_spec(weights)],
+        [shaped(rows, depth, low), shaped(depth, 2 * units, low), shaped(rows, depth, low)],
+        feed_backward_scratch(rows, depth, units)[1:],
+        rider,
+        "last_feed_backward",
+    )
 
 
 def feed_backward_kernel(
-    norm_row, x_ref, own_ref, other_ref, vec_ref, normed_ref, hidden_ref, slope_in, w_ref,
+    norm_row, ticks, x_ref, own_ref, other_ref, vec_ref, normed_ref, hidden_ref, slope_in, w_ref,
     part_out, grad_out, g_out, vec_out, low_ref, *rest
 ):
+    units = w_ref.shape[1] // 2
+    ticks.begin(1 + x_ref.shape[0] // CHUNK * (units // 512) + units // 256)
     residual_prologue(norm_row, None, x_ref, own_ref, other_ref, vec_ref, g_out, low_ref, vec_out)
-    feed_backward_body(normed_ref, hidden_ref, slope_in, w_ref, part_out, grad_out, low_ref, *rest)
-
-
-def feed_backward_call(norm_row, x, own, other, vectors, normed, hidden, slope, weights):
+    feed_backward_body(ticks, normed_ref, hidden_ref, slope_in, w_ref, part_out, grad_out, low_ref, *rest)
+
+
+def feed_backward_call(norm_row, x, own, other, vectors, normed, hidden, slope, weights, rider=None):
     rows, depth = x.shape
     units = hidden.shape[1]
-    return pl.pallas_call(
+    return ride_call(
         functools.partial(feed_backward_kernel, norm_row),
-        out_shape=(
+        [x, own, other, vectors, normed, hidden, slope, weights[0]],
+        [whole()] * 7 + [weight_spec(weights)],
+        [
             shaped(rows, depth, low),
             shaped(depth, 2 * units, low),
             shaped(rows, depth, wide),
             shaped(2, depth, wide),
-        ),
-        scratch_shapes=feed_backward_scratch(rows, depth, units),
-        compiler_params=params(),
-        name="feed_backward",
-    )(x, own, other, vectors, normed, hidden, slope, weights)
+        ],
+        feed_backward_scratch(rows, depth, units),
+        rider,
+        "feed_backward",
+    )
 
 
 def half_lanes(shape):
@@ -785,7 +1111,7 @@
     return jnp.where((place < length) & (place <= row), 0.0, masked_score)
 
 
-def attend_chunk(first_row, length, causal, q_ref, kv_ref, w_ref, attended_out, totals_out, part_out):
+def attend_chunk(tick, first_row, length, causal, q_ref, kv_ref, w_ref, attended_out, totals_out, part_out):
     width = q_ref.shape[1]
     keys = kv_ref.shape[0]
     at = pl.ds(first_row, CHUNK)
@@ -793,6 +1119,7 @@
     lane = lax.broadcasted_iota(jnp.int32, (CHUNK, 128), 1)
     totals = jnp.zeros((CHUNK, 128), wide)
     for begin in range(0, width, 128):
+        tick(begin // 128)
         pair = q_ref[at, begin : begin + 128]
         key_pair = kv_ref[:, begin : begin + 128]
         value_pair = kv_ref[:, width + begin : width + begin + 128]
@@ -812,15 +1139,18 @@
 
 
 def self_attention_kernel(
-    rows_norm, causal, length_ref, x_ref, w_ref, vec_ref, normed_out, q_out, kv_out, attended_out, totals_out, part_out
+    rows_norm, causal, ticks, length_ref, x_ref, w_ref, vec_ref, normed_out, q_out, kv_out, attended_out, totals_out, part_out
 ):
     width = w_ref.shape[1] // 4
     gain = vec_ref[rows_norm : rows_norm + 1, :]
     shift = vec_ref[rows_norm + 1 : rows_norm + 2, :]
     steps = x_ref.shape[0] // CHUNK
+    pairs = width // 128
+    ticks.begin(steps * (pairs + 1))
 
     @pl.loop(0, steps)
     def _(step):
+        ticks.in_loop(step, steps, 0, 1, 0)
         at = pl.ds(pl.multiple_of(step * CHUNK, CHUNK), CHUNK)
         normed = (centre_rows(x_ref[at, :].astype(wide)) * gain + shift).astype(low)
         normed_out[at, :] = normed
@@ -832,38 +1162,45 @@
     @pl.loop(0, steps)
     def _(step):
         attend_chunk(
+            functools.partial(ticks.in_loop, step, steps, steps, pairs),
             pl.multiple_of(step * CHUNK, CHUNK), length, causal, q_out, kv_out, w_ref, attended_out, totals_out, part_out
         )
 
 
-def self_attention_call(rows_norm, causal, length, x, weights, vectors):
+def self_attention_call(rows_norm, causal, length, x, weights, vectors, rider=None):
     rows, depth = x.shape
-    width = weights.shape[1] // 4
-    whole = pl.BlockSpec(memory_space=pltpu.VMEM)
-    return pl.pallas_call(
+    width = weights[1] // 4
+    return ride_call(
         functools.partial(self_attention_kernel, rows_norm, causal),
-        out_shape=(
+        [length, x, weights[0], vectors],
+        [scalar(), whole(), weight_spec(weights), whole()],
+        [
             shaped(rows, depth, low),
             shaped(rows, width, low),
             shaped(rows, 2 * width, low),
             shaped(rows, width, low),
             shaped(rows, 128, wide),
             shaped(rows, depth, low),
-        ),
-        in_specs=[pl.BlockSpec(memory_space=pltpu.SMEM), whole, whole, whole],
-        compiler_params=params(),
-        name="self_attention",
-    )(length, x, weights, vectors)
+        ],
+        [],
+        rider,
+        "self_attention",
+    )
 
 
 def cross_attention_kernel(
-    length_ref, x_ref, own_ref, other_ref, mid_ref, mid_own, mid_other, w_ref, vec_ref,
+    ticks, length_ref, x_ref, own_ref, other_ref, mid_ref, mid_own, mid_other, w_ref, vec_ref,
     x_out, final_out, memory_out, normed_out, q_out, kv_out, attended_out, totals_out, part_out,
 ):
     width = w_ref.shape[1] // 4
-
-    @pl.loop(0, mid_ref.shape[0] // CHUNK)
+    first_steps = mid_ref.shape[0] // CHUNK
+    steps = x_ref.shape[0] // CHUNK
+    pairs = width // 128
+    ticks.begin(first_steps + steps * (pairs + 1))
+
+    @pl.loop(0, first_steps)
     def _(step):
+        ticks.in_loop(step, first_steps, 0, 1, 0)
         at = pl.ds(pl.multiple_of(step * CHUNK, CHUNK), CHUNK)
         x = mid_ref[at, :] + (mid_own[at, :].astype(wide) + mid_other[at, :].astype(wide))
         final_out[at, :] = x
@@ -871,8 +1208,9 @@
         memory_out[at, :] = memory
         kv_out[at, :] = dot_nn(memory, w_ref[:, width : 3 * width]).astype(low)
 
-    @pl.loop(0, x_ref.shape[0] // CHUNK)
+    @pl.loop(0, steps)
     def _(step):
+        ticks.in_loop(step, steps, first_steps, 1, 0)
         at = pl.ds(pl.multiple_of(step * CHUNK, CHUNK), CHUNK)
         x = x_ref[at, :].astype(wide) + (own_ref[at, :].astype(wide) + other_ref[at, :].astype(wide))
         x_out[at, :] = x
@@ -882,21 +1220,23 @@
 
     length = length_ref[0]
 
-    @pl.loop(0, x_ref.shape[0] // CHUNK)
+    @pl.loop(0, steps)
     def _(step):
         attend_chunk(
+            functools.partial(ticks.in_loop, step, steps, first_steps + steps, pairs),
             pl.multiple_of(step * CHUNK, CHUNK), length, False, q_out, kv_out, w_ref, attended_out, totals_out, part_out
         )
 
 
-def cross_attention_call(length, x, own, other, mid, mid_own, mid_other, weights, vectors):
+def cross_attention_call(length, x, own, other, mid, mid_own, mid_other, weights, vectors, rider=None):
     rows, depth = x.shape
     keys = mid.shape[0]
-    width = weights.shape[1] // 4
-    whole = pl.BlockSpec(memory_space=pltpu.VMEM)
-    return pl.pallas_call(
+    width = weights[1] // 4
+    return ride_call(
         cross_attention_kernel,
-        out_shape=(
+        [length, x, own, other, mid, mid_own, mid_other, weights[0], vectors],
+        [scalar()] + [whole()] * 6 + [weight_spec(weights), whole()],
+        [
             shaped(rows, depth, wide),
             shaped(keys, depth, wide),
             shaped(keys, depth, low),
@@ -906,15 +1246,15 @@
             shaped(rows, width, low),
             shaped(rows, 128, wide),
             shaped(rows, depth, low),
-        ),
-        in_specs=[pl.BlockSpec(memory_space=pltpu.SMEM)] + [whole] * 8,
-        compiler_params=params(),
-        name="cross_attention",
-    )(length, x, own, other, mid, mid_own, mid_other, weights, vectors)
+        ],
+        [],
+        rider,
+        "cross_attention",
+    )
 
 
 def attention_backward_kernel(
-    causal, cross, norm_row, length_ref, previous_ref, x_ref, own_ref, other_ref, vec_ref,
+    causal, cross, norm_row, ticks, length_ref, previous_ref, x_ref, own_ref, other_ref, vec_ref,
     normed_ref, source_ref, q_ref, kv_ref, attended_ref, totals_ref, w_ref, *rest
 ):
     outs = 5 if cross else 4
@@ -926,7 +1266,14 @@
     keys = kv_ref.shape[0]
     width = q_ref.shape[1]
     length = length_ref[0]
+    steps = rows // CHUNK
+    pairs = width // 128
+    key_steps = keys // CHUNK
+    after = 1 + steps * pairs
+    last = after + key_steps
+    ticks.begin(last + 5)
     residual_prologue(norm_row, previous_ref, x_ref, own_ref, other_ref, vec_ref, g_out, low_ref, vec_out)
+    ticks(0)
     turned_k[...] = jnp.zeros_like(turned_k)
     turned_v[...] = jnp.zeros_like(turned_v)
 
@@ -939,6 +1286,7 @@
         lane = lax.broadcasted_iota(jnp.int32, (CHUNK, 128), 1)
         totals = totals_ref[at, :]
         for begin in range(0, width, 128):
+            ticks.in_loop(step, steps, 1, pairs, begin // 128)
             pair = q_ref[at, begin : begin + 128]
             key_pair = kv_ref[:, begin : begin + 128]
             value_pair = kv_ref[:, width + begin : width + begin + 128]
@@ -970,6 +1318,7 @@
 
     @pl.loop(0, keys // CHUNK)
     def _(step):
+        ticks.in_loop(step, key_steps, after, 1, 0)
         at = pl.ds(pl.multiple_of(step * CHUNK, CHUNK), CHUNK)
         from_source = dot_nt(grad_kv[at, :], w_ref[:, width : 3 * width])
         if cross:
@@ -978,18 +1327,24 @@
             from_query = dot_nt(grad_q[at, :], w_ref[:, :width])
             part_out[at, :] = (from_source + from_query).astype(low)
 
+    ticks(last)
     turn_into(turned_low, low_ref)
     turn_into(turned_normed, normed_ref)
     if cross:
         turn_into(turned_source, source_ref)
+    ticks(last + 1)
     grad_out[:, :width] = dot_nn(turned_normed[...], grad_q[...]).astype(low)
+    ticks(last + 2)
     grad_out[:, width : 2 * width] = dot_nn(turned_source[...], grad_kv[:, :width]).astype(low)
+    ticks(last + 3)
     grad_out[:, 2 * width : 3 * width] = dot_nn(turned_source[...], grad_kv[:, width:]).astype(low)
+    ticks(last + 4)
     grad_out[:, 3 * width :] = dot_nn(turned_low[...], attended_ref[...]).astype(low)
 
 
 def attention_backward_call(
-    causal, norm_row, length, previous, x, own, other, vectors, normed, source, q, kv, attended, totals, weights
+    causal, norm_row, length, previous, x, own, other, vectors, normed, source, q, kv, attended, totals, weights,
+    rider=None,
 ):
     cross = source is not None
     rows, depth = x.shape
@@ -1017,21 +1372,22 @@
     operands = [length, previous, x, own, other, vectors, normed]
     if cross:
         operands.append(source)
-    operands += [q, kv, attended, totals, weights]
-
-    def kernel(*refs):
+    operands += [q, kv, attended, totals, weights[0]]
+
+    def body(ticks, *refs):
         if not cross:
             refs = refs[:7] + (None,) + refs[7:]
-        attention_backward_kernel(causal, cross, norm_row, *refs)
-
-    return pl.pallas_call(
-        kernel,
-        out_shape=tuple(outs),
-        in_specs=[scalar()] + [whole()] * (len(operands) - 1),
-        scratch_shapes=scratch,
-        compiler_params=params(),
-        name="attention_backward",
-    )(*operands)
+        attention_backward_kernel(causal, cross, norm_row, ticks, *refs)
+
+    return ride_call(
+        body,
+        operands,
+        [scalar()] + [whole()] * (len(operands) - 2) + [weight_spec(weights)],
+        outs,
+        scratch,
+        rider,
+        "attention_backward",
+    )
 
 
 def finish_kernel(norm_row, previous_ref, x_ref, own_ref, other_ref, vec_ref, g_out, vec_out):
@@ -1043,9 +1399,13 @@
     return pl.pallas_call(
         functools.partial(finish_kernel, norm_row),
         out_shape=(shaped(rows, depth, wide), shaped(2, depth, wide)),
-        compiler_params=params(),
+        compiler_params=pltpu.CompilerParams(vmem_limit_bytes=40 << 20),
         name="finish_norm",
     )(previous, x, own, other, vectors)
+
+
+def fits_kernels():
+    return lax.axis_size("z") == 4
 
 
 def factored_step(weights, grads, rows_next, columns_next, row_level, mean_square):
@@ -1093,26 +1453,48 @@
     target_all = both_halves(swap_chips(target_embed[0]))
     cotangent_all = both_halves(swap_chips(out_cotangent[0]))
 
-    encoder_attention, decoder_attention, cross_attention, encoder_feed, decoder_feed = gather_groups(
-        [attention_group(0), attention_group(1), attention_group(2), feed_group(0), feed_group(1)]
-    )
+    attention_width, feed_width = 4 * half_width, 2 * half_units
+    fits = fits_kernels()
+
+    def flat(gathered):
+        return gathered.reshape(-1, gathered.shape[-1])
+
+    def ride(kind, operand, number):
+        return Rider(kind, operand, number) if fits else None
+
+    own_groups = [attention_group(0), attention_group(1), attention_group(2), feed_group(0), feed_group(1)]
+    if fits:
+        encoder_attention = (flat(gather_all(own_groups[0], 0)), attention_width)
+    else:
+        (encoder_attention, decoder_attention, cross_attention, encoder_feed, decoder_feed) = [
+            (gather_weights(group, "zyx"), group.shape[1]) for group in own_groups
+        ]
 
     start_rows = jnp.where(
         (flags_all == 1)[:, None],
         vector_params[12][None, :],
         jnp.where((flags_all == 2)[:, None], vector_params[13][None, :], source_all.astype(wide)),
     )
-    first_kept = self_attention_call(0, False, source_length, start_rows, encoder_attention, vector_params)
+    first_kept = self_attention_call(
+        0, False, source_length, start_rows, encoder_attention, vector_params,
+        ride("gather", own_groups[3], 1),
+    )
+    if fits:
+        encoder_feed = (flat(first_kept[6]), feed_width)
     first_part = first_kept[5]
     first_other = other_core(first_part)
+    encoder_mid, second_normed, second_hidden, second_slope, second_part, *rest = feed_forward_call(
+        2, start_rows, first_part, first_other, encoder_feed, vector_params,
+        ride("gather", jnp.concatenate(own_groups[1:3], axis=1), 2),
+    )
+    if fits:
+        decoder_attention = (flat(rest[0])[:, :attention_width], attention_width)
+        cross_attention = (flat(rest[0])[:, attention_width:], attention_width)
+    second_other = other_core(second_part)
     third_kept = self_attention_call(6, True, target_length, target_all, decoder_attention, vector_params)
     third_part = third_kept[5]
     third_other = other_core(third_part)
-    encoder_mid, second_normed, second_hidden, second_slope, second_part = feed_forward_call(
-        2, start_rows, first_part, first_other, encoder_feed, vector_params
-    )
-    second_other = other_core(second_part)
-    decoder_one, encoder_final, memory_rows, *fourth_kept, fourth_part = cross_attention_call(
+    decoder_one, encoder_final, memory_rows, *fourth_kept = cross_attention_call(
         source_length,
         target_all,
         third_part,
@@ -1122,7 +1504,12 @@
         second_other,
         cross_attention,
         vector_params,
-    )
+        ride("gather", own_groups[4], 3),
+    )
+    if fits:
+        decoder_feed = (flat(fourth_kept[6]), feed_width)
+    fourth_part = fourth_kept[5]
+    fourth_kept = fourth_kept[:5]
     decoder_two, fifth_normed, fifth_hidden, fifth_slope, fifth_part = feed_forward_call(
         10, decoder_one, fourth_part, other_core(fourth_part), decoder_feed, vector_params
     )
@@ -1137,7 +1524,7 @@
     fifth_back, decoder_feed_terms, grad_three = last_feed_backward_call(
         target_length, cotangent_all, fifth_normed, fifth_hidden, fifth_slope, decoder_feed
     )
-    query_back, grad_two, vectors_ten, cross_terms, memory_back = attention_backward_call(
+    query_back, grad_two, vectors_ten, cross_terms, memory_back, *decoder_feed_grad = attention_backward_call(
         False,
         10,
         source_length,
@@ -1150,10 +1537,11 @@
         memory_rows,
         *fourth_kept[1:],
         cross_attention,
+        ride("scatter", decoder_feed_terms, 4),
     )
     query_other = other_core(query_back)
     memory_other = other_core(memory_back)
-    third_back, grad_one, vectors_eight, decoder_terms = attention_backward_call(
+    third_back, grad_one, vectors_eight, decoder_terms, *cross_grad = attention_backward_call(
         True,
         8,
         target_length,
@@ -1166,9 +1554,10 @@
         None,
         *third_kept[1:5],
         decoder_attention,
+        ride("scatter", cross_terms, 5),
     )
     third_back_other = other_core(third_back)
-    second_back, encoder_feed_terms, grad_final, vectors_four = feed_backward_call(
+    second_back, encoder_feed_terms, grad_final, vectors_four, *decoder_grad = feed_backward_call(
         4,
         encoder_final,
         memory_back,
@@ -1178,8 +1567,9 @@
         second_hidden,
         second_slope,
         encoder_feed,
-    )
-    first_back, grad_mid, vectors_two, encoder_terms = attention_backward_call(
+        ride("scatter", decoder_terms, 6),
+    )
+    first_back, grad_mid, vectors_two, encoder_terms, *encoder_feed_grad = attention_backward_call(
         False,
         2,
         source_length,
@@ -1192,6 +1582,7 @@
         None,
         *first_kept[1:5],
         encoder_attention,
+        ride("scatter", encoder_feed_terms, 7),
     )
     grad_target, vectors_six = finish_call(
         6, grad_one, target_all, third_back, third_back_other, vector_params
@@ -1220,18 +1611,19 @@
         axis=0,
     )
     vector_terms = vector_terms.T.astype(low)
-    (encoder_grad, decoder_grad, cross_grad, encoder_feed_grad, decoder_feed_grad, vector_grad) = (
-        scatter_groups(
-            [
-                encoder_terms,
-                decoder_terms,
-                cross_terms,
-                encoder_feed_terms,
-                decoder_feed_terms,
-                vector_terms,
-            ]
+    if fits:
+        (decoder_feed_grad,), (cross_grad,), (decoder_grad,), (encoder_feed_grad,) = (
+            decoder_feed_grad, cross_grad, decoder_grad, encoder_feed_grad
         )
-    )
+        last_grads = scatter_all([encoder_terms, vector_terms], 8)
+        encoder_grad, vector_grad = last_grads[:, :attention_width], last_grads[:, attention_width:]
+    else:
+        (encoder_grad, decoder_grad, cross_grad, encoder_feed_grad, decoder_feed_grad, vector_grad) = [
+            scatter_gradient(terms, "xyz")
+            for terms in (
+                encoder_terms, decoder_terms, cross_terms, encoder_feed_terms, decoder_feed_terms, vector_terms
+            )
+        ]
     vector_grad = vector_grad[:, :14].T
 
     def as_matrices(rows, count):

time: 721 us -> 664 us (0.921)
  Pallas kernels: 584 us -> 505 us
  starting transfers between devices: 43.8 us -> 56.1 us
    pallas_call x10, Pallas kernels: 211 us -> 431 us  [ride_call(): pl.pallas_call(kernel, out_shape=tuple(outs), in_specs=in_specs, out_spec...]
    pallas_call x1, Pallas kernels: 178 us -> 29.2 us  [gather_all(): pl.pallas_call(gather_kernel, out_shape=jax.ShapeDtypeStruct((8, 2 * rows...]
    pallas_call x1, Pallas kernels: 183 us -> 38.6 us  [scatter_all(): pl.pallas_call(functools.partial(scatter_kernel, widths), out_shape=jax.S...]
    ppermute x17, starting transfers between devices: 19.8 us -> 31.9 us  [other_core(): return lax.ppermute(array, 'c', [(0, 1), (1, 0)])]
    slice x4 -> x2, local copies, waits for them, and re-layouts: 16.9 us -> 5.91 us  [the longest x1 4.92 us: on_device(): cross_attention = (flat(rest[0])[:, attention_width:], attention_width)]
    unnamed x79 -> x111, local copies, waits for them, and re-layouts: 13.1 us -> 18.7 us
  transfers between devices with their start and end apart: 33 -> 33, of which waited for: 10 -> 10; matrix products, arithmetic and copies ran while one was open for 5% -> 6% of each run, Pallas kernels for 41% -> 33%
where the time goes in v4:
time: 664 us; the launch traced here: 656 us
  Pallas kernels  505 us (76%)
  starting transfers between devices  56.1 us (8%)
  local copies, waits for them, and re-layouts  38.8 us (6%)
  other arithmetic  27.6 us (4%)
  waiting for transfers between devices  26 us (4%)
    pallas_call x10, Pallas kernels, ride_call(): pl.pallas_call(kernel, out_shape=tuple(outs), in_specs=in_specs, out_spec...  431 us
    pallas_call x1, Pallas kernels, scatter_all(): pl.pallas_call(functools.partial(scatter_kernel, widths), out_shape=jax.S...  38.6 us
    ppermute x17, starting transfers between devices, other_core(): return lax.ppermute(array, 'c', [(0, 1), (1, 0)])  31.9 us
    pallas_call x1, Pallas kernels, gather_all(): pl.pallas_call(gather_kernel, out_shape=jax.ShapeDtypeStruct((8, 2 * rows...  29.2 us
    unnamed x111, local copies, waits for them, and re-layouts  18.7 us
    ppermute x8, starting transfers between devices, swap_chips(): return lax.ppermute(array, ('c', 'x'), [(0, 0), (1, 2), (2, 1), (3, 3)])  18.7 us
  transfers between devices with their start and end apart: 33, of which 10 were waited for; matrix products, arithmetic and copies ran while one was open for 6% of the time, Pallas kernels for 33%

profile of v4, /device:TPU:0, one launch (start us, length us, event | category | flops | bytes accessed | tf_op | source)
XLA Modules:
  0.0 655.8 jit_solution(4682187425482763003)
XLA Ops:
  7.7 12.3 %collective-permute-start.6 = (bf16[512,768]{1,0:T(8,128)(2,1)S(1)}, bf16[512,768]{1,0:T(8,128)(2,1)S(1)}, u32[]{:S(2)}, u32[]{:S(2)}) collective-permute-start(bf16[512,768]{1,0:T(8,128)(2,1)S(1)} %collective-permute-done.5), channel_id=1, source_target_pairs={{0,2},{2,0},{1,3},{3,1},{4,6},{6,4},{5,7},{7,5},{8,10},{10,8},{9,1... | collective-permute-start | bytes 2359304 | tf_op jit(solution)/shard_map/ppermute | solution.py:27
  21.0 29.2 %gather_weights.1 = bf16[8,96,1536]{2,1,0:T(8,128)(2,1)S(1)} custom-call(bf16[48,1536]{1,0:T(8,128)(2,1)S(1)} %bitcast.82), custom_call_target="tpu_custom_call" | custom-call | tf_op jit(solution)/shard_map/gather_weights/pallas_call | solution.py:435
  53.0 3.1 select_select_fusion.refs_1_.refs_0_.x_ref
  56.1 51.8 %self_attention.2 = (bf16[1024,768]{1,0:T(8,128)(2,1)}, bf16[1024,384]{1,0:T(8,128)(2,1)}, bf16[1024,768]{1,0:T(8,128)(2,1)}, bf16[1024,384]{1,0:T(8,128)(2,1)},...) custom-call(s32[1]{0:T(128)} %bitcast.2.refs_0_, ...), custom_call_target="tpu_custom_call" | custom-call | tf_op jit(solution)/shard_map/self_attention/pallas_call | solution.py:823
  109.5 8.1 %collective-permute-start.2 = (bf16[256,768]{1,0:T(8,128)(2,1)S(1)}, bf16[256,768]{1,0:T(8,128)(2,1)S(1)}, u32[]{:S(2)}, u32[]{:S(2)}) collective-permute-start(bf16[256,768]{1,0:T(8,128)(2,1)S(1)} %collective-permute-done.1), channel_id=1, source_target_pairs={{0,2},{2,0},{1,3},{3,1},{4,6},{6,4},{5,7},{7,5},{8,10},{10,8},{9,1... | collective-permute-start | bytes 1179656 | tf_op jit(solution)/shard_map/ppermute | solution.py:27
  120.2 57.0 %feed_forward.2 = (f32[1024,768]{1,0:T(8,128)}, bf16[1024,768]{1,0:T(8,128)(2,1)}, bf16[1024,1536]{1,0:T(8,128)(2,1)}, bf16[1024,1536]{1,0:T(8,128)(2,1)}, bf16[...) custom-call(f32[1024,768]{1,0:T(8,128)} %select_select_fusion.refs_1_.refs_0_.x_ref, ...), custom_call_target="tpu_custom_call" | custom-call | tf_op jit(solution)/shard_map/feed_forward/pallas_call | solution.py:823
  178.2 4.9 fusion.12
  183.1 10.1 %self_attention.3 = (bf16[512,768]{1,0:T(8,128)(2,1)}, bf16[512,384]{1,0:T(8,128)(2,1)}, bf16[512,768]{1,0:T(8,128)(2,1)}, bf16[512,384]{1,0:T(8,128)(2,1)}, f32...) custom-call(s32[1]{0:T(128)} %bitcast.4.refs_0_, bf16[512,768]{1,0:T(8,128)(2,1)} %pad_maximum_fusion.2.refs_1_.x_ref, ...), custom_call_target="tpu_custom_call" | custom-call | tf_op jit(solution)/shard_map/self_attention/pallas_call | solution.py:823
  194.6 8.2 %collective-permute-start.14 = (bf16[256,768]{1,0:T(8,128)(2,1)S(1)}, bf16[256,768]{1,0:T(8,128)(2,1)S(1)}, u32[]{:S(2)}, u32[]{:S(2)}) collective-permute-start(bf16[256,768]{1,0:T(8,128)(2,1)S(1)} %collective-permute-done.13), channel_id=1, source_target_pairs={{0,2},{2,0},{1,3},{3,1},{4,6},{6,4},{5,7},{7,5},{8,10},{10,8},{9,1... | collective-permute-start | bytes 1179656 | tf_op jit(solution)/shard_map/ppermute | solution.py:27
  204.9 55.0 %cross_attention.1 = (f32[512,768]{1,0:T(8,128)}, f32[1024,768]{1,0:T(8,128)}, bf16[1024,768]{1,0:T(8,128)(2,1)}, bf16[512,768]{1,0:T(8,128)(2,1)}, bf16[512,384...) custom-call(s32[1]{0:T(128)} %bitcast.2.refs_0_, ...), custom_call_target="tpu_custom_call" | custom-call | tf_op jit(solution)/shard_map/cross_attention/pallas_call | solution.py:823
  263.4 11.7 %feed_forward.3 = (f32[512,768]{1,0:T(8,128)}, bf16[512,768]{1,0:T(8,128)(2,1)}, bf16[512,1536]{1,0:T(8,128)(2,1)}, bf16[512,1536]{1,0:T(8,128)(2,1)}, bf16[512,768]{1,0:T(8,128)(2,1)}) custom-call(f32[512,768]{1,0:T(8,128)} %get-tuple-element.83.refs_0_.refs_2_, bf16[512,768]{1,0:T(8,128)(2,1)} %get-tuple-element.84.refs_1_, bf16[512,768]{1,0:T(8,128)(2,1)} %copy-done.27, ...), custom_call_target="tpu_custom_call" | custom-call | tf_op jit(solution)/shard_map/feed_forward/pallas_call | solution.py:823
  275.1 13.6 %last_feed_backward.1 = (bf16[512,768]{1,0:T(8,128)(2,1)}, bf16[768,3072]{1,0:T(8,128)(2,1)}, bf16[512,768]{1,0:T(8,128)(2,1)}) custom-call(s32[1]{0:T(128)} %bitcast.4.refs_0_, bf16[512,768]{1,0:T(8,128)(2,1)} %pad_maximum_fusion.3.refs_1_, bf16[512,768]{1,0:T(8,128)(2,1)} %get-tuple-element.89.refs_2_, bf16[512,1536]{1,0:T(8,128)(2,1)} %get-tuple-element.90.refs_3_, ...), custom_call_target="tpu_custom_call" | custom-call | tf_op jit(solution)/shard_map/last_feed_backward/pallas_call | solution.py:823
  288.9 2.4 collective-permute-done.15.refs_4_
  292.2 65.5 %attention_backward.3 = (bf16[512,768]{1,0:T(8,128)(2,1)}, f32[512,768]{1,0:T(8,128)}, f32[2,768]{1,0:T(2,128)}, bf16[768,1536]{1,0:T(8,128)(2,1)}, bf16[1024,768]{1,0:T(8,128)(2,1)}, /*index=5*/f32[48,3072]{1,0:T(8,128)}) custom-call(s32[1]{0:T(128)} %bitcast.2.refs_0_, bf16[512,768]{1,0:T(8,128)(2,1)} %get-tuple-element.92.refs_1_, ...), custom_call_target="tpu_custom_call" | custom-call | tf_op jit(solution)/shard_map/attention_backward/pallas_call | solution.py:823
  358.3 4.3 collective-permute-done.17.refs_4_
  363.5 45.8 %attention_backward.4 = (bf16[512,768]{1,0:T(8,128)(2,1)}, f32[512,768]{1,0:T(8,128)}, f32[2,768]{1,0:T(2,128)}, bf16[768,1536]{1,0:T(8,128)(2,1)}, f32[48,1536]{1,0:T(8,128)}) custom-call(s32[1]{0:T(128)} %bitcast.4.refs_0_, f32[512,768]{1,0:T(8,128)} %get-tuple-element.105.refs_1_, f32[512,768]{1,0:T(8,128)} %get-tuple-element.83.refs_0_.refs_2_, ...), custom_call_target="tpu_custom_call" | custom-call | tf_op jit(solution)/shard_map/attention_backward/pallas_call | solution.py:823
  410.5 48.2 %feed_backward.1 = (bf16[1024,768]{1,0:T(8,128)(2,1)}, bf16[768,3072]{1,0:T(8,128)(2,1)}, f32[1024,768]{1,0:T(8,128)}, f32[2,768]{1,0:T(2,128)}, f32[48,1536]{1,0:T(8,128)}) custom-call(f32[1024,768]{1,0:T(8,128)} %get-tuple-element.88.refs_0_, bf16[1024,768]{1,0:T(8,128)(2,1)} %get-tuple-element.101.refs_1_, bf16[1024,768]{1,0:T(8,128)(2,1)} %copy-done.15, ...), custom_call_target="tpu_custom_call" | custom-call | tf_op jit(solution)/shard_map/feed_backward/pallas_call | solution.py:823
  460.2 3.3 collective-permute-done.11
  465.3 4.7 collective-permute-start.12
  470.1 72.2 %attention_backward.5 = (bf16[1024,768]{1,0:T(8,128)(2,1)}, f32[1024,768]{1,0:T(8,128)}, f32[2,768]{1,0:T(2,128)}, bf16[768,1536]{1,0:T(8,128)(2,1)}, f32[48,3072]{1,0:T(8,128)}) custom-call(s32[1]{0:T(128)} %bitcast.2.refs_0_, f32[1024,768]{1,0:T(8,128)} %get-tuple-element.114.refs_1_, f32[1024,768]{1,0:T(8,128)} %get-tuple-element.81.refs_4_.refs_2_, ...), custom_call_target="tpu_custom_call" | custom-call | tf_op jit(solution)/shard_map/attention_backward/pallas_call | solution.py:823
  544.3 2.5 finish_norm.3
  560.2 4.1 finish_norm.2
  570.3 38.6 %scatter_gradients.1 = f32[48,1664]{1,0:T(8,128)} custom-call(bf16[8,96,1536]{2,1,0:T(8,128)(2,1)} %bitcast.91, bf16[8,96,128]{2,1,0:T(8,128)(2,1)} %bitcast.97), custom_call_target="tpu_custom_call" | custom-call | tf_op jit(solution)/shard_map/scatter_gradients/pallas_call | solution.py:722
  612.0 2.8 collective-permute-done.28
  617.7 2.8 collective-permute-done.30
  621.4 2.4 dynamic-slice_convert_fusion
  623.8 7.4 %collective-permute-start.20 = (bf16[512,768]{1,0:T(8,128)(2,1)}, bf16[512,768]{1,0:T(8,128)(2,1)}, u32[]{:S(2)}, u32[]{:S(2)}) collective-permute-start(bf16[512,768]{1,0:T(8,128)(2,1)} %dynamic-slice_convert_fusion), channel_id=1, source_target_pairs={{0,0},{1,2},{2,1},{3,3},{4,4},{5,6},{6,5},{7,7},{8,8},{9,10},{10,9... | collective-permute-start | bytes 2359304 | tf_op jit(solution)/shard_map/ppermute | solution.py:23
  635.2 2.8 collective-permute-done.25
  638.9 2.6 collective-permute-done.26
  643.6 2.4 collective-permute-done.27
  647.0 2.4 multiply_subtract_fusion.1
  651.1 2.5 select_bitcast_fusion
  (244 shorter events, 69.2 us)
Async XLA Ops:
  1.5 50.8 %collective-permute-start = (s32[1536]{0:T(1024)S(1)}, s32[1536]{0:T(1024)S(1)}, u32[]{:S(2)}, u32[]{:S(2)}) collective-permute-start(s32[1536]{0:T(1024)S(1)} %pad_add_fusion), channel_id=1, source_target_pairs={{0,0},{1,2},{2,1},{3,3},{4,4},{5,6},{6,5},{7,7},{8,8},{9,10},{10,9... | collective-permute-start | bytes 18440 | tf_op jit(solution)/shard_map/ppermute | solution.py:23
  2.1 5.5 collective-permute-start.5
  3.9 16.1 %collective-permute-start.3 = (s32[512]{0:T(512)}, s32[512]{0:T(512)S(1)}, u32[]{:S(2)}, u32[]{:S(2)}) collective-permute-start(s32[512]{0:T(512)} %bitcast.106), channel_id=1, source_target_pairs={{0,0},{1,2},{2,1},{3,3},{4,4},{5,6},{6,5},{7,7},{8,8},{9,10},{10,9... | collective-permute-start | bytes 6152 | tf_op jit(solution)/shard_map/ppermute | solution.py:23
  7.7 45.2 %collective-permute-start.6 = (bf16[512,768]{1,0:T(8,128)(2,1)S(1)}, bf16[512,768]{1,0:T(8,128)(2,1)S(1)}, u32[]{:S(2)}, u32[]{:S(2)}) collective-permute-start(bf16[512,768]{1,0:T(8,128)(2,1)S(1)} %collective-permute-done.5), channel_id=1, source_target_pairs={{0,2},{2,0},{1,3},{3,1},{4,6},{6,4},{5,7},{7,5},{8,10},{10,8},{9,1... | collective-permute-start | bytes 2359304 | tf_op jit(solution)/shard_map/ppermute | solution.py:27
  20.0 32.2 %collective-permute-start.4 = (s32[512]{0:T(512)S(1)}, s32[512]{0:T(512)S(1)}, u32[]{:S(2)}, u32[]{:S(2)}) collective-permute-start(s32[512]{0:T(512)S(1)} %collective-permute-done.3), channel_id=1, source_target_pairs={{0,2},{2,0},{1,3},{3,1},{4,6},{6,4},{5,7},{7,5},{8,10},{10,8},{9,1... | collective-permute-start | bytes 6152 | tf_op jit(solution)/shard_map/ppermute | solution.py:27
  108.0 11.1 %collective-permute-start.7 = (bf16[1024,768]{1,0:T(8,128)(2,1)}, bf16[1024,768]{1,0:T(8,128)(2,1)S(1)}, u32[]{:S(2)}, u32[]{:S(2)}) collective-permute-start(bf16[1024,768]{1,0:T(8,128)(2,1)} %get-tuple-element.77.refs_1_), channel_id=1, source_target_pairs={{0,2},{2,0},{1,3},{3,1},{4,6},{6,4},{5,7},{7,5},{8,10},{10,8},{9,1... | collective-permute-start | bytes 4718600 | tf_op jit(solution)/shard_map/ppermute | solution.py:27
  108.3 1.2 collective-permute-start.1
  109.5 9.5 %collective-permute-start.2 = (bf16[256,768]{1,0:T(8,128)(2,1)S(1)}, bf16[256,768]{1,0:T(8,128)(2,1)S(1)}, u32[]{:S(2)}, u32[]{:S(2)}) collective-permute-start(bf16[256,768]{1,0:T(8,128)(2,1)S(1)} %collective-permute-done.1), channel_id=1, source_target_pairs={{0,2},{2,0},{1,3},{3,1},{4,6},{6,4},{5,7},{7,5},{8,10},{10,8},{9,1... | collective-permute-start | bytes 1179656 | tf_op jit(solution)/shard_map/ppermute | solution.py:27
  177.2 26.4 %collective-permute-start.9 = (bf16[1024,768]{1,0:T(8,128)(2,1)}, bf16[1024,768]{1,0:T(8,128)(2,1)S(1)}, u32[]{:S(2)}, u32[]{:S(2)}) collective-permute-start(bf16[1024,768]{1,0:T(8,128)(2,1)} %get-tuple-element.82.refs_5_), channel_id=1, source_target_pairs={{0,2},{2,0},{1,3},{3,1},{4,6},{6,4},{5,7},{7,5},{8,10},{10,8},{9,1... | collective-permute-start | bytes 4718600 | tf_op jit(solution)/shard_map/ppermute | solution.py:27
  193.2 10.4 %collective-permute-start.8 = (bf16[512,768]{1,0:T(8,128)(2,1)}, bf16[512,768]{1,0:T(8,128)(2,1)S(1)}, u32[]{:S(2)}, u32[]{:S(2)}) collective-permute-start(bf16[512,768]{1,0:T(8,128)(2,1)} %get-tuple-element.80.refs_2_), channel_id=1, source_target_pairs={{0,2},{2,0},{1,3},{3,1},{4,6},{6,4},{5,7},{7,5},{8,10},{10,8},{9,1... | collective-permute-start | bytes 2359304 | tf_op jit(solution)/shard_map/ppermute | solution.py:27
  194.6 65.4 %collective-permute-start.14 = (bf16[256,768]{1,0:T(8,128)(2,1)S(1)}, bf16[256,768]{1,0:T(8,128)(2,1)S(1)}, u32[]{:S(2)}, u32[]{:S(2)}) collective-permute-start(bf16[256,768]{1,0:T(8,128)(2,1)S(1)} %collective-permute-done.13), channel_id=1, source_target_pairs={{0,2},{2,0},{1,3},{3,1},{4,6},{6,4},{5,7},{7,5},{8,10},{10,8},{9,1... | collective-permute-start | bytes 1179656 | tf_op jit(solution)/shard_map/ppermute | solution.py:27
  259.9 2.6 collective-permute-start.10
  288.8 2.5 collective-permute-start.15
  357.7 51.6 %collective-permute-start.16 = (bf16[1024,768]{1,0:T(8,128)(2,1)}, bf16[1024,768]{1,0:T(8,128)(2,1)S(1)}, u32[]{:S(2)}, u32[]{:S(2)}) collective-permute-start(bf16[1024,768]{1,0:T(8,128)(2,1)} %get-tuple-element.101.refs_1_), channel_id=1, source_target_pairs={{0,2},{2,0},{1,3},{3,1},{4,6},{6,4},{5,7},{7,5},{8,10},{10,8},{9,1... | collective-permute-start | bytes 4718600 | tf_op jit(solution)/shard_map/ppermute | solution.py:27
  358.2 4.4 collective-permute-start.17
  458.7 11.3 %collective-permute-start.18 = (bf16[1024,768]{1,0:T(8,128)(2,1)}, bf16[1024,768]{1,0:T(8,128)(2,1)}, u32[]{:S(2)}, u32[]{:S(2)}) collective-permute-start(bf16[1024,768]{1,0:T(8,128)(2,1)} %get-tuple-element.115.refs_3_), channel_id=1, source_target_pairs={{0,2},{2,0},{1,3},{3,1},{4,6},{6,4},{5,7},{7,5},{8,10},{10,8},{9,1... | collective-permute-start | bytes 4718600 | tf_op jit(solution)/shard_map/ppermute | solution.py:27
  459.0 4.4 collective-permute-start.11
  459.3 84.9 %collective-permute-start.21 = (bf16[512,768]{1,0:T(8,128)(2,1)S(1)}, bf16[512,768]{1,0:T(8,128)(2,1)}, u32[]{:S(2)}, u32[]{:S(2)}) collective-permute-start(bf16[512,768]{1,0:T(8,128)(2,1)S(1)} %copy-done.9), channel_id=1, source_target_pairs={{0,2},{2,0},{1,3},{3,1},{4,6},{6,4},{5,7},{7,5},{8,10},{10,8},{9,1... | collective-permute-start | bytes 2359304 | tf_op jit(solution)/shard_map/ppermute | solution.py:27
  465.3 83.8 %collective-permute-start.12 = (bf16[256,768]{1,0:T(8,128)(2,1)}, bf16[256,768]{1,0:T(8,128)(2,1)}, u32[]{:S(2)}, u32[]{:S(2)}) collective-permute-start(bf16[256,768]{1,0:T(8,128)(2,1)} %fusion), channel_id=1, source_target_pairs={{0,0},{1,2},{2,1},{3,3},{4,4},{5,6},{6,5},{7,7},{8,8},{9,10},{10,9... | collective-permute-start | bytes 1179656 | tf_op jit(solution)/shard_map/ppermute | solution.py:23
  542.2 14.7 %collective-permute-start.19 = (bf16[1024,768]{1,0:T(8,128)(2,1)}, bf16[1024,768]{1,0:T(8,128)(2,1)}, u32[]{:S(2)}, u32[]{:S(2)}) collective-permute-start(bf16[1024,768]{1,0:T(8,128)(2,1)} %get-tuple-element.123.own_ref), channel_id=1, source_target_pairs={{0,2},{2,0},{1,3},{3,1},{4,6},{6,4},{5,7},{7,5},{8,10},{10,8},{9,1... | collective-permute-start | bytes 4718600 | tf_op jit(solution)/shard_map/ppermute | solution.py:27
  546.9 5.5 collective-permute-start.22
  611.1 3.7 collective-permute-start.28
  615.2 1.3 collective-permute-start.29
  616.5 4.1 collective-permute-start.30
  617.0 14.2 %collective-permute-start.23 = (f32[32]{0:T(128)S(1)}, f32[32]{0:T(128)S(1)}, u32[]{:S(2)}, u32[]{:S(2)}) collective-permute-start(f32[32]{0:T(128)S(1)} %pad_maximum_fusion.7), channel_id=1, source_target_pairs={{0,1},{1,0},{2,3},{3,2},{4,5},{5,4},{6,7},{7,6},{8,9},{9,8},{10,11... | collective-permute-start | bytes 392 | tf_op jit(solution)/shard_map/ppermute | solution.py:144
  620.6 10.7 %collective-permute-start.31 = (f32[10768]{0:T(1024)S(1)}, f32[10768]{0:T(1024)S(1)}, u32[]{:S(2)}, u32[]{:S(2)}) collective-permute-start(f32[10768]{0:T(1024)S(1)} %add.85), channel_id=1, source_target_pairs={{0,8},{8,0},{16,24},{24,16},{1,9},{9,1},{17,25},{25,17},{2,10},{10... | collective-permute-start | bytes 129224 | tf_op jit(solution)/shard_map/ppermute | solution.py:139
  623.8 27.3 %collective-permute-start.20 = (bf16[512,768]{1,0:T(8,128)(2,1)}, bf16[512,768]{1,0:T(8,128)(2,1)}, u32[]{:S(2)}, u32[]{:S(2)}) collective-permute-start(bf16[512,768]{1,0:T(8,128)(2,1)} %dynamic-slice_convert_fusion), channel_id=1, source_target_pairs={{0,0},{1,2},{2,1},{3,3},{4,4},{5,6},{6,5},{7,7},{8,8},{9,10},{10,9... | collective-permute-start | bytes 2359304 | tf_op jit(solution)/shard_map/ppermute | solution.py:23
  631.2 3.1 collective-permute-start.24
  631.3 14.6 %collective-permute-start.32 = (f32[10768]{0:T(1024)S(1)}, f32[10768]{0:T(1024)S(1)}, u32[]{:S(2)}, u32[]{:S(2)}) collective-permute-start(f32[10768]{0:T(1024)S(1)} %add.86), channel_id=1, source_target_pairs={{0,16},{16,0},{8,24},{24,8},{1,17},{17,1},{9,25},{25,9},{2,18},{18... | collective-permute-start | bytes 129224 | tf_op jit(solution)/shard_map/ppermute | solution.py:140
  634.4 3.6 collective-permute-start.25
  638.0 3.5 collective-permute-start.26
  641.5 4.4 collective-permute-start.27
  (52 other events, 957.5 us)

commit v5 on v4

--- a/solution.py
+++ b/solution.py
@@ -152,6 +152,14 @@
     return list(zip(edges[:-1], edges[1:]))
 
 
+def gather_cuts(columns):
+    tiles = columns // 128
+    first = (tiles * 38 + 50) // 100
+    second = (tiles * 39 + 50) // 100
+    edges = [0, first * 128, (first + second) * 128, columns]
+    return list(zip(edges[:-1], edges[1:]))
+
+
 def place(name):
     return lax.axis_index(name)
 
@@ -179,6 +187,15 @@
     for target in targets:
         pl.semaphore_signal(barrier, inc=1, device_id=target, device_id_type=MESH)
     pl.semaphore_wait(barrier, len(targets))
+
+
+class Part:
+    def __init__(self, array, first):
+        self.array, self.first = array, first
+        self.at = self
+
+    def __getitem__(self, index):
+        return self.array.at[self.first + index]
 
 
 def here(back):
@@ -255,15 +272,14 @@
     def __init__(self, own_ref, out_ref, stage_ref, local_sem, send_sems, recv_sems):
         super().__init__(send_sems)
         rows, columns = own_ref.shape
-        cuts = column_cuts(columns)
+        cuts = gather_cuts(columns)
         (begin_a, end_a), (begin_b, end_b), (begin_c, end_c) = cuts
         first, second, third = 0, 1, 2
 
         def out_piece(group, which, parity):
             begin, end = cuts[group]
-            return out_ref.at[
-                block_at(which), pl.ds(parity() * rows, rows), pl.ds(begin, end - begin)
-            ]
+            first_row = (block_at(which) * 2 + parity()) * rows
+            return out_ref.at[pl.ds(first_row, rows), pl.ds(begin, end - begin)]
 
         def out_sem(group, which, parity):
             return recv_sems.at[(group * 8 + block_at(which)) * 2 + parity()]
@@ -283,7 +299,7 @@
 
         self_copies = {
             True: lambda: pltpu.make_async_copy(
-                own_ref, out_ref.at[block_at(here(0)), pl.ds(core() * rows, rows), :], local_sem
+                own_ref, out_ref.at[pl.ds((block_at(here(0)) * 2 + core()) * rows, rows), :], local_sem
             ),
         }
 
@@ -413,41 +429,11 @@
 GATHER_SENDS = 64
 
 
-def gather_kernel(own_ref, out_ref, stage_ref, local_sem, send_sems, recv_sems):
-    greet()
-    mover = Gather(own_ref, out_ref, stage_ref, local_sem, send_sems, recv_sems)
-    mover.run(0, 1)
-    mover.finish()
-
-
-def gather_scratch(rows, columns):
-    cuts = column_cuts(columns)
-    return [
-        pltpu.VMEM((8, rows, cuts[1][1]), low),
-        pltpu.SemaphoreType.DMA,
-        pltpu.SemaphoreType.DMA((GATHER_SENDS,)),
-        pltpu.SemaphoreType.DMA((64,)),
-    ]
-
-
-def gather_all(own, number=0):
-    rows, columns = own.shape
-    return pl.pallas_call(
-        gather_kernel,
-        out_shape=jax.ShapeDtypeStruct((8, 2 * rows, columns), own.dtype),
-        in_specs=[pl.BlockSpec(memory_space=pl.ANY)],
-        out_specs=pl.BlockSpec(memory_space=pl.ANY),
-        scratch_shapes=gather_scratch(rows, columns),
-        compiler_params=pltpu.CompilerParams(
-            collective_id=number, has_side_effects=True, vmem_limit_bytes=40 << 20
-        ),
-        name="gather_weights",
-    )(own)
-
-
 class Scatter(Mover):
-    def __init__(self, total, final, stage, x_in, ya_in, yb_in, z_in, zc_in, yc_in, send_sems, recv_sems):
+    def __init__(self, buffers, final, send_sems, recv_sems):
         super().__init__(send_sems)
+        total, stages, x_ins, z_ins = buffers[0], buffers[1:4], buffers[4:7], buffers[7:9]
+        ya_in, yb_in, zc_in, yc_in = buffers[9:]
         rows = total.shape[1] // 2
         columns = total.shape[2]
         cuts = column_cuts(columns)
@@ -467,10 +453,10 @@
             return which[0] + (0 if which[1] else 4)
 
         def x_piece(group, which):
-            return x_in.at[slot_of(which), :, part(group)]
+            return x_ins[group].at[slot_of(which)]
 
         def stage_piece(group, which):
-            return stage.at[slot_of(which), :, part(group)]
+            return stages[group].at[slot_of(which)]
 
         def sem(number):
             return lambda: recv_sems.at[number]
@@ -503,6 +489,8 @@
                 return functools.partial(stage_piece, group, which)
 
             def x_sends(group, which):
+                if widths[group] == 0:
+                    return
                 number = group * 8 + slot_of(which)
                 if home:
                     self.send(
@@ -523,6 +511,8 @@
                     )
 
             def x_add(group, which, last=False):
+                if widths[group] == 0:
+                    return
                 number = group * 8 + slot_of(which)
                 if not home:
                     self.wait(home, functools.partial(stage_piece, group, which), sem(24 + number))
@@ -538,9 +528,11 @@
                 )
 
             def z_slot(group, back):
-                return lambda: z_in.at[back, :, part(group)]
+                return lambda: z_ins[group].at[back]
 
             def z_send(group, back):
+                if widths[group] == 0:
+                    return
                 self.send(
                     home,
                     plane(group, here(back)),
@@ -550,6 +542,8 @@
                 )
 
             def z_add(group, back):
+                if widths[group] == 0:
+                    return
                 self.wait(home, z_slot(group, back), sem(60 + group * 4 + back))
                 self.local(
                     home,
@@ -599,22 +593,26 @@
             zc_send(there(3))
             zc_send(here(3))
             for back in (3, 2, 1, 0):
-                self.send(
-                    home,
-                    functools.partial(core_piece, second, there(back)),
-                    yb_slot(back),
-                    sem(52 + back),
-                    functools.partial(target_of, "y"),
-                )
+                if widths[second]:
+                    self.send(
+                        home,
+                        functools.partial(core_piece, second, there(back)),
+                        yb_slot(back),
+                        sem(52 + back),
+                        functools.partial(target_of, "y"),
+                    )
                 if back > 1:
                     x_sends(first, there(back))
                     x_sends(first, here(back))
             for back in (3, 2, 1, 0):
-                self.wait(home, yb_slot(back), sem(52 + back))
-                self.local(
-                    home,
-                    add_rows(functools.partial(core_piece, second, here(back)), yb_slot(back), 2 * rows),
-                )
+                if widths[second]:
+                    self.wait(home, yb_slot(back), sem(52 + back))
+                    self.local(
+                        home,
+                        add_rows(
+                            functools.partial(core_piece, second, here(back)), yb_slot(back), 2 * rows
+                        ),
+                    )
                 x_sends(second, here(back))
                 if back > 1:
                     x_sends(first, there(back - 2))
@@ -633,13 +631,14 @@
                                 functools.partial(target_of, "y"),
                             )
                 x_add(first, there(back))
-                self.send(
-                    home,
-                    plane(first, there(back)),
-                    ya_slot(back),
-                    sem(48 + back),
-                    functools.partial(target_of, "y"),
-                )
+                if widths[first]:
+                    self.send(
+                        home,
+                        plane(first, there(back)),
+                        ya_slot(back),
+                        sem(48 + back),
+                        functools.partial(target_of, "y"),
+                    )
                 x_add(first, here(back))
                 if back < 3:
                     second_steps(back + 1)
@@ -654,8 +653,9 @@
                         ),
                     )
                     x_sends(third, here(0))
-                self.wait(home, ya_slot(back), sem(48 + back))
-                self.local(home, add_rows(plane(first, here(back)), ya_slot(back), rows))
+                if widths[first]:
+                    self.wait(home, ya_slot(back), sem(48 + back))
+                    self.local(home, add_rows(plane(first, here(back)), ya_slot(back), rows))
                 if back < 3:
                     z_add(first, back)
                 if back > 0:
@@ -675,168 +675,43 @@
 SCATTER_SENDS = 48
 
 
-def scatter_scratch(rows, columns):
-    cuts = column_cuts(columns)
-    widths = [end - begin for begin, end in cuts]
+SCATTER_BUFFERS = 13
+
+
+def scatter_buffers(rows, columns):
+    first, second, third = [max(end - begin, 128) for begin, end in column_cuts(columns)]
     return [
         pltpu.VMEM((8, 2 * rows, columns), low),
-        pltpu.VMEM((8, rows, columns), low),
-        pltpu.VMEM((8, rows, columns), low),
-        pltpu.VMEM((4, rows, widths[0]), low),
-        pltpu.VMEM((4, 2 * rows, widths[1]), low),
-        pltpu.VMEM((4, rows, columns), low),
-        pltpu.VMEM((6, 2 * rows, widths[2]), low),
-        pltpu.VMEM((2 * rows, widths[2]), low),
-        pltpu.SemaphoreType.DMA((SCATTER_SENDS,)),
-        pltpu.SemaphoreType.DMA((80,)),
+        pltpu.VMEM((8, rows, first), low),
+        pltpu.VMEM((4, rows, second), low),
+        pltpu.VMEM((1, rows, third), low),
+        pltpu.VMEM((8, rows, first), low),
+        pltpu.VMEM((4, rows, second), low),
+        pltpu.VMEM((1, rows, third), low),
+        pltpu.VMEM((3, rows, first), low),
+        pltpu.VMEM((3, rows, second), low),
+        pltpu.VMEM((4, rows, first), low),
+        pltpu.VMEM((4, 2 * rows, second), low),
+        pltpu.VMEM((6, 2 * rows, third), low),
+        pltpu.VMEM((2 * rows, third), low),
     ]
 
-
-def scatter_kernel(widths, *refs):
-    count = len(widths)
-    grads = refs[:count]
-    final, total = refs[count : count + 2]
-    load_sems = refs[-1]
-    loads = []
-    begin = 0
-    for number, width in enumerate(widths):
-        one = pltpu.make_async_copy(
-            grads[number], total.at[:, :, pl.ds(begin, width)], load_sems.at[number]
-        )
-        one.start()
-        loads.append(one)
-        begin += width
-    greet()
-    for one in loads:
-        one.wait()
-    mover = Scatter(total, final, *refs[count + 2 : -1])
-    mover.run(0, 1)
-    mover.finish()
-
-
-def scatter_all(parts, number=1):
-    depth = parts[0].shape[0]
-    widths = [part.shape[1] for part in parts]
-    columns = sum(widths)
-    rows = depth // 16
-    return pl.pallas_call(
-        functools.partial(scatter_kernel, widths),
-        out_shape=jax.ShapeDtypeStruct((rows, columns), wide),
-        in_specs=[pl.BlockSpec(memory_space=pl.ANY)] * len(parts),
-        out_specs=pl.BlockSpec(memory_space=pltpu.VMEM),
-        scratch_shapes=scatter_scratch(rows, columns) + [pltpu.SemaphoreType.DMA((len(parts),))],
-        compiler_params=pltpu.CompilerParams(
-            collective_id=number, has_side_effects=True, vmem_limit_bytes=58 << 20
-        ),
-        name="scatter_gradients",
-    )(*[part.reshape(8, 2 * rows, part.shape[1]) for part in parts])
-
-
-class Rider:
-    def __init__(self, kind, operand, number):
-        self.kind = kind
-        self.number = number
-        if kind == "gather":
-            rows, columns = operand.shape
-            self.operand = operand
-            self.out = jax.ShapeDtypeStruct((8, 2 * rows, columns), operand.dtype)
-            self.out_spec = pl.BlockSpec(memory_space=pl.ANY)
-            self.scratch = gather_scratch(rows, columns)
-        else:
-            depth, columns = operand.shape
-            rows = depth // 16
-            self.operand = operand.reshape(8, 2 * rows, columns)
-            self.out = jax.ShapeDtypeStruct((rows, columns), wide)
-            self.out_spec = pl.BlockSpec(memory_space=pltpu.VMEM)
-            self.scratch = scatter_scratch(rows, columns) + [pltpu.SemaphoreType.DMA]
-
-
-class Ticks:
-    def __init__(self, rider, operand_ref, out_ref, scratch):
-        self.rider = rider
-        self.refs = (operand_ref, out_ref, scratch)
-        self.mover = None
-
-    def begin(self, parts):
-        if self.rider is None:
-            return
-        operand_ref, out_ref, scratch = self.refs
-        self.parts = parts
-        if self.rider.kind == "gather":
-            self.mover = Gather(operand_ref, out_ref, *scratch)
-        else:
-
-            def load():
-                return pltpu.make_async_copy(operand_ref, scratch[0], scratch[-1])
-
-            load().start()
-            self.mover = Scatter(scratch[0], out_ref, *scratch[1:-1])
-            for home in (True, False):
-                self.mover.steps[home].insert(0, lambda: load().wait())
-        greet()
-
-    def __call__(self, part):
-        if self.mover is not None:
-            self.mover.run(part, self.parts)
-
-    def in_loop(self, step, steps, offset, stride, inner):
-        if self.mover is None:
-            return
-        for number in range(steps):
-
-            @pl.when(step == number)
-            def _():
-                self(offset + number * stride + inner)
-
-    def end(self):
-        if self.mover is not None:
-            self.mover.finish()
-
-
 def ride_call(body, operands, in_specs, outs, scratch, rider, name):
-    count_in, count_out, count_scratch = len(operands), len(outs), len(scratch)
-    out_specs = [pl.BlockSpec(memory_space=pltpu.VMEM)] * count_out
-    options = dict(vmem_limit_bytes=60 << 20)
-    operands, in_specs, outs, scratch = list(operands), list(in_specs), list(outs), list(scratch)
-    if rider is not None:
-        operands.append(rider.operand)
-        in_specs.append(pl.BlockSpec(memory_space=pl.ANY))
-        outs.append(rider.out)
-        out_specs.append(rider.out_spec)
-        scratch += rider.scratch
-        options.update(collective_id=rider.number, has_side_effects=True)
-
     def kernel(*refs):
-        ins, rest = refs[:count_in], refs[count_in:]
-        operand_ref = out_ref = None
-        extra = ()
-        if rider is not None:
-            operand_ref, rest = rest[0], rest[1:]
-        mine, rest = rest[:count_out], rest[count_out:]
-        if rider is not None:
-            out_ref, rest = rest[0], rest[1:]
-        own, extra = rest[:count_scratch], rest[count_scratch:]
-        ticks = Ticks(rider, operand_ref, out_ref, extra)
-        body(ticks, *ins, *mine, *own)
-        ticks.end()
+        body(Nothing(), *refs)
 
     return pl.pallas_call(
         kernel,
         out_shape=tuple(outs),
-        in_specs=in_specs,
-        out_specs=tuple(out_specs),
-        scratch_shapes=scratch,
-        compiler_params=pltpu.CompilerParams(**options),
+        in_specs=list(in_specs),
+        scratch_shapes=list(scratch),
+        compiler_params=pltpu.CompilerParams(vmem_limit_bytes=60 << 20),
         name=name,
     )(*operands)
 
 
 def whole():
     return pl.BlockSpec(memory_space=pltpu.VMEM)
-
-
-def scalar():
-    return pl.BlockSpec(memory_space=pltpu.SMEM)
 
 
 def weight_spec(weights):
@@ -889,19 +764,23 @@
     return back, jnp.sum(grads * unit, axis=0, keepdims=True), jnp.sum(grads, axis=0, keepdims=True)
 
 
-def residual_prologue(norm_row, previous_ref, x_ref, own_ref, other_ref, vec_ref, grad_out, low_ref, vec_out):
+def residual_prologue(norm_row, previous_ref, x_ref, own_ref, other_ref, vec_ref, grad_out, low_ref, vec_out, ticks=None):
+    ticks = ticks or Nothing()
+    steps = x_ref.shape[0] // CHUNK
+    ticks.begin(steps)
     gain = vec_ref[norm_row : norm_row + 1, :]
     vec_out[...] = jnp.zeros_like(vec_out)
 
     @pl.loop(0, x_ref.shape[0] // CHUNK)
     def _(step):
         at = pl.ds(pl.multiple_of(step * CHUNK, CHUNK), CHUNK)
+        ticks.in_loop(step, steps, 0, 1, 0)
         grads = own_ref[at, :].astype(wide) + other_ref[at, :].astype(wide)
         back, by_gain, by_shift = norm_back(x_ref[at, :].astype(wide), gain, grads)
         if previous_ref is not None:
             back = back + previous_ref[at, :].astype(wide)
         if grad_out is not None:
-            grad_out[at, :] = back
+            grad_out[at, :] = back.astype(grad_out.dtype)
         if low_ref is not None:
             low_ref[at, :] = back.astype(low)
         vec_out[0:1, :] += by_gain
@@ -991,6 +870,19 @@
     )
 
 
+def store_grad(target, begin, value):
+    value = value.astype(low)
+    span = slice(begin, begin + value.shape[1])
+    if len(target.shape) == 2:
+        target[:, span] = value
+    else:
+        target[:, :, span] = value.reshape(target.shape[0], target.shape[1], value.shape[1])
+
+
+def feed_backward_ticks(rows, units):
+    return 1 + rows // CHUNK * (units // 512) + units // 256
+
+
 def feed_backward_body(ticks, normed_ref, hidden_ref, slope_in, w_ref, part_out, grad_out, low_ref, slope_ref, turned_ref, turned_low):
     rows, depth = low_ref.shape
     units = w_ref.shape[1] // 2
@@ -1016,12 +908,10 @@
 
     for begin in range(0, units, 256):
         ticks(offset + begin // 256)
-        grad_out[:, begin : begin + 256] = dot_nn(
-            turned_ref[...], slope_ref[:, begin : begin + 256]
-        ).astype(low)
-        grad_out[:, units + begin : units + begin + 256] = dot_nn(
-            turned_low[...], hidden_ref[:, begin : begin + 256]
-        ).astype(low)
+        store_grad(grad_out, begin, dot_nn(turned_ref[...], slope_ref[:, begin : begin + 256]))
+        store_grad(
+            grad_out, units + begin, dot_nn(turned_low[...], hidden_ref[:, begin : begin + 256])
+        )
 
 
 def feed_backward_scratch(rows, depth, units):
@@ -1037,14 +927,14 @@
     ticks, length_ref, cotangent_ref, normed_ref, hidden_ref, slope_in, w_ref, part_out, grad_out, low_ref, *rest
 ):
     rows, depth = cotangent_ref.shape
-    place = lax.broadcasted_iota(jnp.int32, (CHUNK, depth), 0)
 
     @pl.loop(0, rows // CHUNK)
     def _(step):
         first_row = pl.multiple_of(step * CHUNK, CHUNK)
         at = pl.ds(first_row, CHUNK)
         rows_here = cotangent_ref[at, :].astype(wide)
-        low_ref[at, :] = jnp.where(first_row + place < length_ref[0], rows_here, 0.0).astype(low)
+        kept = column_of(length_ref, first_row) > 0
+        low_ref[at, :] = jnp.where(kept, rows_here, 0.0).astype(low)
 
     feed_backward_body(ticks, normed_ref, hidden_ref, slope_in, w_ref, part_out, grad_out, low_ref, *rest)
 
@@ -1055,7 +945,7 @@
     return ride_call(
         last_feed_backward_kernel,
         [length, cotangent, normed, hidden, slope, weights[0]],
-        [scalar()] + [whole()] * 4 + [weight_spec(weights)],
+        [whole()] + [whole()] * 4 + [weight_spec(weights)],
         [shaped(rows, depth, low), shaped(depth, 2 * units, low), shaped(rows, depth, low)],
         feed_backward_scratch(rows, depth, units)[1:],
         rider,
@@ -1102,13 +992,13 @@
     return jnp.where(first, pair, zero) if head == 0 else jnp.where(first, zero, pair)
 
 
-def key_bias(keys, length, first_row, causal, rows):
-    place = lax.broadcasted_iota(jnp.int32, (1, keys), 1)
+def key_bias(keys, mask_row, first_row, causal, rows):
+    allowed = jnp.where(mask_row[...] > 0, 0.0, masked_score)
     if not causal:
-        return jnp.where(place < length, 0.0, masked_score)
-    place = lax.broadcasted_iota(jnp.int32, (rows, keys), 1)
+        return allowed
+    column = lax.broadcasted_iota(jnp.int32, (rows, keys), 1)
     row = first_row + lax.broadcasted_iota(jnp.int32, (rows, keys), 0)
-    return jnp.where((place < length) & (place <= row), 0.0, masked_score)
+    return jnp.where(column <= row, allowed, masked_score)
 
 
 def attend_chunk(tick, first_row, length, causal, q_ref, kv_ref, w_ref, attended_out, totals_out, part_out):
@@ -1157,7 +1047,7 @@
         q_out[at, :] = (dot_nn(normed, w_ref[:, :width]).astype(low).astype(wide) * 0.125).astype(low)
         kv_out[at, :] = dot_nn(normed, w_ref[:, width : 3 * width]).astype(low)
 
-    length = length_ref[0]
+    length = length_ref
 
     @pl.loop(0, steps)
     def _(step):
@@ -1173,7 +1063,7 @@
     return ride_call(
         functools.partial(self_attention_kernel, rows_norm, causal),
         [length, x, weights[0], vectors],
-        [scalar(), whole(), weight_spec(weights), whole()],
+        [whole(), whole(), weight_spec(weights), whole()],
         [
             shaped(rows, depth, low),
             shaped(rows, width, low),
@@ -1218,7 +1108,7 @@
         normed_out[at, :] = normed
         q_out[at, :] = (dot_nn(normed, w_ref[:, :width]).astype(low).astype(wide) * 0.125).astype(low)
 
-    length = length_ref[0]
+    length = length_ref
 
     @pl.loop(0, steps)
     def _(step):
@@ -1235,7 +1125,7 @@
     return ride_call(
         cross_attention_kernel,
         [length, x, own, other, mid, mid_own, mid_other, weights[0], vectors],
-        [scalar()] + [whole()] * 6 + [weight_spec(weights), whole()],
+        [whole()] + [whole()] * 6 + [weight_spec(weights), whole()],
         [
             shaped(rows, depth, wide),
             shaped(keys, depth, wide),
@@ -1260,19 +1150,28 @@
     outs = 5 if cross else 4
     part_out, g_out, vec_out, grad_out = rest[:4]
     source_part_out = rest[4] if cross else None
-    low_ref, grad_q, grad_kv, turned_k, turned_v, turned_low, turned_normed = rest[outs : outs + 7]
-    turned_source = rest[outs + 7] if cross else turned_normed
-    rows, depth = x_ref.shape
+    low_ref, scratch = rest[outs], rest[outs + 1 :]
+    residual_prologue(norm_row, previous_ref, x_ref, own_ref, other_ref, vec_ref, g_out, low_ref, vec_out)
+    attention_backward_main(
+        causal, cross, ticks, length_ref, low_ref, normed_ref, source_ref, q_ref, kv_ref, attended_ref, totals_ref,
+        w_ref, part_out, grad_out, source_part_out, *scratch,
+    )
+
+
+def attention_backward_main(
+    causal, cross, ticks, length, low_ref, normed_ref, source_ref, q_ref, kv_ref, attended_ref, totals_ref, w_ref,
+    part_out, grad_out, source_part_out, grad_q, grad_kv, turned_k, turned_v, turned_low, turned_normed, *rest
+):
+    turned_source = rest[0] if cross else turned_normed
+    rows, depth = low_ref.shape
     keys = kv_ref.shape[0]
     width = q_ref.shape[1]
-    length = length_ref[0]
     steps = rows // CHUNK
     pairs = width // 128
     key_steps = keys // CHUNK
     after = 1 + steps * pairs
     last = after + key_steps
     ticks.begin(last + 5)
-    residual_prologue(norm_row, previous_ref, x_ref, own_ref, other_ref, vec_ref, g_out, low_ref, vec_out)
     ticks(0)
     turned_k[...] = jnp.zeros_like(turned_k)
     turned_v[...] = jnp.zeros_like(turned_v)
@@ -1333,13 +1232,28 @@
     if cross:
         turn_into(turned_source, source_ref)
     ticks(last + 1)
-    grad_out[:, :width] = dot_nn(turned_normed[...], grad_q[...]).astype(low)
+    store_grad(grad_out, 0, dot_nn(turned_normed[...], grad_q[...]))
     ticks(last + 2)
-    grad_out[:, width : 2 * width] = dot_nn(turned_source[...], grad_kv[:, :width]).astype(low)
+    store_grad(grad_out, width, dot_nn(turned_source[...], grad_kv[:, :width]))
     ticks(last + 3)
-    grad_out[:, 2 * width : 3 * width] = dot_nn(turned_source[...], grad_kv[:, width:]).astype(low)
+    store_grad(grad_out, 2 * width, dot_nn(turned_source[...], grad_kv[:, width:]))
     ticks(last + 4)
-    grad_out[:, 3 * width :] = dot_nn(turned_low[...], attended_ref[...]).astype(low)
+    store_grad(grad_out, 3 * width, dot_nn(turned_low[...], attended_ref[...]))
+
+
+def attention_backward_scratch(rows, keys, depth, width, cross):
+    scratch = [
+        pltpu.VMEM((rows, depth), low),
+        pltpu.VMEM((rows, width), low),
+        pltpu.VMEM((keys, 2 * width), low),
+        pltpu.VMEM((width, keys), wide),
+        pltpu.VMEM((width, keys), wide),
+        pltpu.VMEM((depth, rows), low),
+        pltpu.VMEM((depth, rows), low),
+    ]
+    if cross:
+        scratch.append(pltpu.VMEM((depth, keys), low))
+    return scratch
 
 
 def attention_backward_call(
@@ -1358,17 +1272,7 @@
     ]
     if cross:
         outs.append(shaped(keys, depth, low))
-    scratch = [
-        pltpu.VMEM((rows, depth), low),
-        pltpu.VMEM((rows, width), low),
-        pltpu.VMEM((keys, 2 * width), low),
-        pltpu.VMEM((width, keys), wide),
-        pltpu.VMEM((width, keys), wide),
-        pltpu.VMEM((depth, rows), low),
-        pltpu.VMEM((depth, rows), low),
-    ]
-    if cross:
-        scratch.append(pltpu.VMEM((depth, keys), low))
+    scratch = attention_backward_scratch(rows, keys, depth, width, cross)
     operands = [length, previous, x, own, other, vectors, normed]
     if cross:
         operands.append(source)
@@ -1382,7 +1286,7 @@
     return ride_call(
         body,
         operands,
-        [scalar()] + [whole()] * (len(operands) - 2) + [weight_spec(weights)],
+        [whole()] + [whole()] * (len(operands) - 2) + [weight_spec(weights)],
         outs,
         scratch,
         rider,
@@ -1404,6 +1308,826 @@
     )(previous, x, own, other, vectors)
 
 
+class Stream:
+    def __init__(self):
+        self.steps = {True: [], False: []}
+        self.begins, self.ends = [], []
+        self.position = {True: 0, False: 0}
+        self.movers = []
+
+    def add(self, mover, overlap=0.0):
+        self.movers.append(mover)
+        begin, end = {}, {}
+        for home in (True, False):
+            had, new = self.steps[home], mover.steps[home]
+            shared = min(int(len(new) * overlap), len(had))
+            kept = len(had) - shared
+            merged = had[:kept]
+            for one, two in zip(had[kept:], new[:shared]):
+                merged += [one, two]
+            merged += new[shared:]
+            for mark in self.ends:
+                if mark[home] > kept:
+                    mark[home] = kept + 2 * (mark[home] - kept)
+            self.steps[home] = merged
+            begin[home], end[home] = kept, len(merged)
+        self.begins.append(begin)
+        self.ends.append(end)
+
+    def between(self, one, two, share):
+        return {home: one[home] + int((two[home] - one[home]) * share) for home in (True, False)}
+
+    def plan(self, marks, shares=(1.0,)):
+        windows, done, start = [], 0.0, dict(self.position)
+        for share in shares:
+            done += share / sum(shares)
+            end = {
+                home: max(
+                    self.position[home],
+                    start[home] + round((marks[home] - start[home]) * done),
+                )
+                for home in (True, False)
+            }
+            windows.append(Window(self, dict(self.position), end))
+            self.position = end
+        return windows
+
+    def run(self, chosen):
+        for home in (True, False):
+            if not chosen[home]:
+                continue
+            wanted = place("c") == place("x")
+
+            @pl.when(wanted if home else jnp.logical_not(wanted))
+            def _():
+                for step in chosen[home]:
+                    step()
+
+    def finish(self):
+        for mover in self.movers:
+            mover.finish()
+
+
+class Window:
+    def __init__(self, stream, start, end):
+        self.stream, self.start, self.end = stream, start, end
+        self.parts = 1
+
+    def begin(self, parts):
+        self.parts = parts
+
+    def __call__(self, part=0):
+        chosen = {}
+        for home in (True, False):
+            start, size = self.start[home], self.end[home] - self.start[home]
+            first = start + size * part // self.parts
+            chosen[home] = self.stream.steps[home][first : start + size * (part + 1) // self.parts]
+        self.stream.run(chosen)
+
+    def in_loop(self, step, steps, offset, stride, inner):
+        if all(self.start[home] == self.end[home] for home in (True, False)):
+            return
+        for number in range(steps):
+
+            @pl.when(step == number)
+            def _():
+                self(offset + number * stride + inner)
+
+
+class Bag:
+    def __init__(self, **entries):
+        self.__dict__.update(entries)
+
+    def names(self):
+        return list(self.__dict__)
+
+    def values(self):
+        return list(self.__dict__.values())
+
+    def joined(self, other):
+        return Bag(**self.__dict__, **other.__dict__)
+
+
+def filled(names, values):
+    return Bag(**dict(zip(names, values)))
+
+
+class Nothing:
+    def begin(self, parts):
+        pass
+
+    def __call__(self, part=0):
+        pass
+
+    def in_loop(self, *unused):
+        pass
+
+
+nothing = Nothing()
+
+
+def vmem_like(ref):
+    return pltpu.VMEM(ref.shape, ref.dtype)
+
+
+class Direct:
+    def __init__(self, ref):
+        self.ref = ref
+
+
+class Swap:
+    def __init__(self, target, send_sem, recv_sem):
+        self.target, self.send_sem, self.recv_sem = target, send_sem, recv_sem
+
+    def copy(self, source):
+        return pltpu.make_async_remote_copy(
+            src_ref=source,
+            dst_ref=self.target,
+            send_sem=self.send_sem,
+            recv_sem=self.recv_sem,
+            device_id=target_of("c"),
+            device_id_type=MESH,
+        )
+
+    def arrive(self):
+        self.copy(self.target).wait_recv()
+
+
+def run_phase(body, sems, ins, outs, scratch=(), swaps=(), before=nothing, after=nothing):
+    moved_in = [ref for ref in ins if not isinstance(ref, Direct)]
+    moved_out = [ref for ref in outs if not isinstance(ref, Direct)]
+
+    def scoped(*refs):
+        own_in, rest = refs[: len(moved_in)], refs[len(moved_in) :]
+        own_out, own_scratch = rest[: len(moved_out)], rest[len(moved_out) :]
+        copies = [
+            pltpu.make_async_copy(ref, own, sems.at[number])
+            for number, (ref, own) in enumerate(zip(moved_in, own_in))
+        ]
+        for copy in copies:
+            copy.start()
+        before()
+        for copy in copies:
+            copy.wait()
+        own_in, own_out = iter(own_in), iter(own_out)
+        all_in = [ref.ref if isinstance(ref, Direct) else next(own_in) for ref in ins]
+        all_out = [ref.ref if isinstance(ref, Direct) else next(own_out) for ref in outs]
+        body(*all_in, *all_out, *own_scratch)
+        copies = []
+        for number, swap in swaps:
+            swap.copy(all_out[number]).start()
+        for ref, own in zip(outs, all_out):
+            if not isinstance(ref, Direct):
+                copy = pltpu.make_async_copy(own, ref, sems.at[16 + len(copies)])
+                copy.start()
+                copies.append(copy)
+        after()
+        for copy in copies:
+            copy.wait()
+        for number, swap in swaps:
+            swap.copy(all_out[number]).wait_send()
+
+    allocations = [vmem_like(ref) for ref in moved_in] + [vmem_like(ref) for ref in moved_out]
+    pl.run_scoped(scoped, *allocations, *scratch)
+
+
+def column_of(row_ref, first_row):
+    size = row_ref.shape[1]
+    lane = lax.broadcasted_iota(jnp.int32, (CHUNK, size), 1)
+    row = first_row + lax.broadcasted_iota(jnp.int32, (CHUNK, size), 0)
+    return jnp.sum(jnp.where(lane == row, row_ref[...], 0), axis=-1, keepdims=True)
+
+
+class Inputs(Mover):
+    def __init__(self, send_sems, recv_sems, local_sems):
+        super().__init__(send_sems)
+        self.recv_sems, self.local_sems = recv_sems, local_sems
+        self.count = 0
+
+    def taken(self):
+        steps = self.steps
+        self.steps = {True: [], False: []}
+        return steps
+
+    def swap(self, source, target):
+        number = self.count
+        self.count += 1
+
+        def diagonal():
+            return {"c": 1 - place("c"), "x": 1 - place("x")}
+
+        def local():
+            return pltpu.make_async_copy(source(), target(True), self.local_sems.at[number])
+
+        self.local(True, lambda: local().start())
+        self.send(
+            False,
+            source,
+            functools.partial(target, False),
+            lambda: self.recv_sems.at[number],
+            diagonal,
+        )
+
+        def arrive():
+            self.local(True, lambda: local().wait())
+            self.wait(False, functools.partial(target, True), lambda: self.recv_sems.at[number])
+
+        return arrive
+
+    def share(self, piece):
+        number = self.count
+        self.count += 1
+
+        def sem():
+            return self.recv_sems.at[number]
+
+        for home in (True, False):
+            self.send(
+                home,
+                functools.partial(piece, True),
+                functools.partial(piece, True),
+                sem,
+                functools.partial(target_of, "c"),
+            )
+
+        def arrive():
+            for home in (True, False):
+                self.wait(home, functools.partial(piece, False), sem)
+
+        return arrive
+
+
+def half_of(ref, own):
+    size = ref.shape[0] // 2
+    core = place("c") if own else 1 - place("c")
+    return ref.at[pl.ds(core * size, size), :]
+
+
+def half_lanes_of(ref, own):
+    size = ref.shape[1] // 2
+    core = place("c") if own else 1 - place("c")
+    return ref.at[:, pl.ds(core * size, size)]
+
+
+def source_mask(marks_row):
+    quarter = marks_row.shape[1] // 4
+    return marks_row.at[:, pl.ds(quarter, 2 * quarter)]
+
+
+def target_mask(marks_row):
+    quarter = marks_row.shape[1] // 4
+    return marks_row.at[:, pl.ds(3 * quarter, quarter)]
+
+
+def any_space():
+    return pl.BlockSpec(memory_space=pl.ANY)
+
+
+def spliced(one, two, at):
+    return {home: one[home][: at[home]] + two[home] + one[home][at[home] :] for home in (True, False)}
+
+
+def shares_of(steps, share):
+    return {home: int(len(steps[home]) * share) for home in (True, False)}
+
+
+def forward_kernel(names_in, names_out, *refs):
+    count_in, count_out = len(names_in), len(names_out)
+    i = filled(names_in, refs[:count_in])
+    o = filled(names_out, refs[count_in : count_in + count_out])
+    (marks_row, flags_row, *rest) = refs[count_in + count_out :]
+    stages, rest = rest[:5], rest[5:]
+    sems, group_send, group_recv, group_local, in_send, in_recv, in_local, swap_sems = rest
+    vec = i.vectors
+    greet()
+
+    start = Inputs(Part(in_send, 0), Part(in_recv, 0), Part(in_local, 0))
+    marks_here = start.swap(lambda: i.marks, lambda own: marks_row)
+    source_here = start.swap(lambda: i.source, functools.partial(half_of, o.source_all))
+    opening = start.taken()
+    marks_here()
+    flags_size = flags_row.shape[1] // 2
+
+    def flags_piece(own):
+        return half_lanes_of(flags_row, own)
+
+    def flags_local():
+        return pltpu.make_async_copy(
+            marks_row.at[:, pl.ds(0, flags_size)], flags_piece(True), in_local.at[8]
+        )
+
+    for home in (True, False):
+        start.local(home, lambda: flags_local().start())
+        start.local(home, lambda: flags_local().wait())
+    flags_there = start.share(flags_piece)
+    source_here()
+    source_there = start.share(functools.partial(half_of, o.source_all))
+    middle = start.taken()
+    flags_there()
+    source_there()
+    closing = start.taken()
+
+    owns = (i.own_1, i.own_3, i.own_2, i.own_4, i.own_5)
+    alls = (o.all_1, o.all_3, o.all_2, o.all_4, o.all_5)
+    gathers = []
+    for number, (own, gathered) in enumerate(zip(owns, alls)):
+        gathers.append(
+            Gather(
+                own,
+                gathered,
+                stages[number],
+                group_local.at[number],
+                Part(group_send, number * GATHER_SENDS),
+                Part(group_recv, number * 64),
+            )
+        )
+    first, second, last = gathers[0], gathers[1], gathers[4]
+    steps = spliced(first.steps, middle, shares_of(first.steps, 0.6))
+    first.steps = {home: opening[home] + steps[home] + closing[home] for home in (True, False)}
+
+    def bring(source, target, first_send, first_recv, first_local):
+        mover = Inputs(Part(in_send, first_send), Part(in_recv, first_recv), Part(in_local, first_local))
+        here_now = mover.swap(lambda: source, functools.partial(half_of, target))
+        begin = mover.taken()
+        here_now()
+        there_now = mover.share(functools.partial(half_of, target))
+        there_now()
+        return mover, begin, mover.taken()
+
+    target_mover, begin, rest = bring(i.target, o.target_all, 16, 8, 9)
+    steps = spliced(second.steps, rest, shares_of(second.steps, 0.4))
+    second.steps = {home: begin[home] + steps[home] for home in (True, False)}
+    cotangent_mover, begin, rest = bring(i.cotangent, o.cotangent_all, 24, 12, 13)
+    steps = spliced(last.steps, begin, shares_of(last.steps, 0.7))
+    last.steps = {home: steps[home] + rest[home] for home in (True, False)}
+    stream = Stream()
+    stream.movers += [start, target_mover, cotangent_mover]
+    for number, mover in enumerate(gathers):
+        stream.add(mover, 0.4 if number > 1 else 0.0)
+    ends = stream.ends
+
+    swap_refs = (o.other_1, o.other_2, o.other_3, o.other_4, o.other_5)
+    swaps = [
+        Swap(ref, swap_sems.at[number], swap_sems.at[8 + number])
+        for number, ref in enumerate(swap_refs)
+    ]
+
+    stream.plan(ends[0])[0]()
+
+    one, ticks, two = stream.plan(stream.between(ends[1], ends[2], 0.25), (1, 7, 1))
+
+    def encoder_attention_body(source_ref, w_ref, x_out, *outs):
+        @pl.loop(0, x_out.shape[0] // CHUNK)
+        def _(step):
+            first_row = pl.multiple_of(step * CHUNK, CHUNK)
+            at = pl.ds(first_row, CHUNK)
+            kind = column_of(flags_row, first_row)
+            x_out[at, :] = jnp.where(
+                kind == 1, vec[12:13, :], jnp.where(kind == 2, vec[13:14, :], source_ref[at, :].astype(wide))
+            )
+
+        self_attention_kernel(0, False, ticks, source_mask(marks_row), x_out, w_ref, vec, *outs)
+
+    run_phase(
+        encoder_attention_body,
+        sems,
+        [o.source_all, o.all_1],
+        [o.start, o.normed_1, o.query_1, o.kv_1, o.attended_1, o.totals_1, o.part_1],
+        swaps=[(6, swaps[0])],
+        before=one,
+        after=two,
+    )
+    one, ticks_two, two = stream.plan(stream.between(ends[1], ends[2], 0.6), (1, 6, 1))
+
+    def decoder_attention_body(x_ref, w_ref, *outs):
+        self_attention_kernel(6, True, ticks_two, target_mask(marks_row), x_ref, w_ref, vec, *outs)
+
+    run_phase(
+        decoder_attention_body,
+        sems,
+        [o.target_all, o.all_3],
+        [o.normed_3, o.query_3, o.kv_3, o.attended_3, o.totals_3, o.part_3],
+        swaps=[(5, swaps[2])],
+        before=one,
+        after=two,
+    )
+    stream.plan(ends[2])[0]()
+    swaps[0].arrive()
+    one, ticks_three, two = stream.plan(stream.between(ends[3], ends[4], 0.2), (1, 5, 1))
+
+    def encoder_feed_body(x_ref, own_ref, other_ref, w_ref, *outs):
+        feed_forward_kernel(2, ticks_three, x_ref, own_ref, other_ref, w_ref, vec, *outs)
+
+    run_phase(
+        encoder_feed_body,
+        sems,
+        [o.start, o.part_1, o.other_1, o.all_2],
+        [o.mid, o.normed_2, o.hidden_2, o.slope_2, o.part_2],
+        swaps=[(4, swaps[1])],
+        before=one,
+        after=two,
+    )
+    stream.plan(ends[3])[0]()
+    swaps[2].arrive()
+    swaps[1].arrive()
+    one, ticks_four, two = stream.plan(ends[4], (1, 5, 1))
+
+    def cross_attention_body(x_ref, own_ref, other_ref, mid_ref, mid_own, mid_other, w_ref, *outs):
+        cross_attention_kernel(
+            ticks_four, source_mask(marks_row), x_ref, own_ref, other_ref, mid_ref, mid_own, mid_other, w_ref, vec, *outs
+        )
+
+    run_phase(
+        cross_attention_body,
+        sems,
+        [o.target_all, o.part_3, o.other_3, o.mid, o.part_2, o.other_2, o.all_4],
+        [o.one, o.final, o.memory, o.normed_4, o.query_4, o.kv_4, o.attended_4, o.totals_4, o.part_4],
+        swaps=[(8, swaps[3])],
+        before=one,
+        after=two,
+    )
+    swaps[3].arrive()
+
+    def decoder_feed_body(x_ref, own_ref, other_ref, w_ref, *outs):
+        feed_forward_kernel(10, nothing, x_ref, own_ref, other_ref, w_ref, vec, *outs)
+
+    run_phase(
+        decoder_feed_body,
+        sems,
+        [o.one, o.part_4, o.other_4, o.all_5],
+        [o.two, o.normed_5, o.hidden_5, o.slope_5, o.part_5],
+        swaps=[(4, swaps[4])],
+    )
+    o.marks_all[...] = marks_row[...]
+    o.flags_all[...] = flags_row[...]
+    swaps[4].arrive()
+    stream.finish()
+
+
+def attention_kept(rows, keys, depth, width):
+    return (
+        shaped(rows, depth, low),
+        shaped(rows, width, low),
+        shaped(keys, 2 * width, low),
+        shaped(rows, width, low),
+        shaped(rows, 128, wide),
+    )
+
+
+def feed_kept(rows, depth, units):
+    return shaped(rows, depth, low), shaped(rows, units, low), shaped(rows, units, low)
+
+
+def specs_of(near, far):
+    return [whole() for unused in near.values()] + [any_space() for unused in far.values()]
+
+
+def dma(count):
+    return pltpu.SemaphoreType.DMA((count,))
+
+
+def forward_call(source, target, cotangent, marks, vectors, groups):
+    depth = vectors.shape[1]
+    rows, few = 2 * source.shape[0], 2 * target.shape[0]
+    block = groups[0].shape[0]
+    width, units = groups[0].shape[1] // 4, groups[1].shape[1] // 2
+    near_in = Bag(marks=marks, vectors=vectors)
+    far_in = Bag(source=source, target=target, cotangent=cotangent)
+    far_in.own_1, far_in.own_2, far_in.own_3, far_in.own_4, far_in.own_5 = groups
+    near_out = Bag(
+        marks_all=jax.ShapeDtypeStruct(marks.shape, marks.dtype),
+        flags_all=jax.ShapeDtypeStruct((1, rows), marks.dtype),
+    )
+    far_out = Bag(
+        source_all=shaped(rows, depth, low),
+        target_all=shaped(few, depth, low),
+        cotangent_all=shaped(few, depth, low),
+        start=shaped(rows, depth, wide),
+        mid=shaped(rows, depth, wide),
+        final=shaped(rows, depth, wide),
+        memory=shaped(rows, depth, low),
+        one=shaped(few, depth, wide),
+        two=shaped(few, depth, wide),
+    )
+    f = far_out
+    f.normed_1, f.query_1, f.kv_1, f.attended_1, f.totals_1 = attention_kept(rows, rows, depth, width)
+    f.normed_3, f.query_3, f.kv_3, f.attended_3, f.totals_3 = attention_kept(few, few, depth, width)
+    f.normed_4, f.query_4, f.kv_4, f.attended_4, f.totals_4 = attention_kept(few, rows, depth, width)
+    f.normed_2, f.hidden_2, f.slope_2 = feed_kept(rows, depth, units)
+    f.normed_5, f.hidden_5, f.slope_5 = feed_kept(few, depth, units)
+    f.part_1 = f.other_1 = f.part_2 = f.other_2 = shaped(rows, depth, low)
+    f.part_3 = f.other_3 = f.part_4 = f.other_4 = f.part_5 = f.other_5 = shaped(few, depth, low)
+    f.all_1, f.all_2, f.all_3, f.all_4, f.all_5 = [
+        shaped(16 * block, group.shape[1], low) for group in groups
+    ]
+    ins, outs = near_in.joined(far_in), near_out.joined(far_out)
+    order = (0, 2, 1, 3, 4)
+    stage = [
+        pltpu.VMEM((8, block, gather_cuts(groups[number].shape[1])[1][1]), low) for number in order
+    ]
+    results = pl.pallas_call(
+        functools.partial(forward_kernel, ins.names(), outs.names()),
+        out_shape=tuple(outs.values()),
+        in_specs=specs_of(near_in, far_in),
+        out_specs=tuple(specs_of(near_out, far_out)),
+        scratch_shapes=[
+            pltpu.VMEM(marks.shape, marks.dtype),
+            pltpu.VMEM((1, rows), marks.dtype),
+            *stage,
+            dma(32),
+            dma(5 * GATHER_SENDS),
+            dma(5 * 64),
+            dma(5),
+            dma(32),
+            dma(16),
+            dma(18),
+            dma(16),
+        ],
+        compiler_params=pltpu.CompilerParams(
+            collective_id=0, has_side_effects=True, vmem_limit_bytes=60 << 20
+        ),
+        name="forward_pass",
+    )(*ins.values())
+    return filled(outs.names(), results)
+
+
+def backward_kernel(names_in, names_out, *refs):
+    count_in, count_out = len(names_in), len(names_out)
+    i = filled(names_in, refs[:count_in])
+    o = filled(names_out, refs[count_in : count_in + count_out])
+    rest = refs[count_in + count_out :]
+    vectors_of, rest = dict(zip((0, 2, 4, 6, 8, 10, 12), rest[:7])), rest[7:]
+    vector_rows, rest = rest[0], rest[1:]
+    buffers = []
+    for unused in range(6):
+        buffers.append(rest[:SCATTER_BUFFERS])
+        rest = rest[SCATTER_BUFFERS:]
+    sems, group_send, group_recv, in_send, in_recv, in_local, swap_sems = rest
+    vec, marks_row, flags_row = i.vectors, i.marks_all, i.flags_all
+    finals = (o.final_5, o.final_4, o.final_3, o.final_2, o.final_1, o.final_vectors)
+    greet()
+    stream = Stream()
+    for number in range(6):
+        mover = Scatter(
+            buffers[number],
+            finals[number],
+            Part(group_send, number * SCATTER_SENDS),
+            Part(group_recv, number * 80),
+        )
+        stream.add(mover, (0.0, 0.15, 0.15, 0.15, 0.1, 0.0)[number])
+    begins, ends = stream.begins, stream.ends
+    swap_refs = (o.other_6, o.other_7, o.other_8, o.other_9, o.other_10, o.other_11)
+    swaps = [
+        Swap(ref, swap_sems.at[number], swap_sems.at[8 + number])
+        for number, ref in enumerate(swap_refs)
+    ]
+
+    def total_of(number):
+        return Direct(buffers[number][0])
+
+    moves = Inputs(Part(in_send, 0), Part(in_recv, 0), Part(in_local, 0))
+
+    swaps_before = []
+
+    def result_body(x_ref, own_ref, other_ref, out):
+        total = own_ref[...].astype(wide) + other_ref[...].astype(wide)
+        out[...] = (x_ref[...] + total).astype(low)
+
+    def last_feed_body(*refs):
+        last_feed_backward_kernel(nothing, target_mask(marks_row), *refs)
+
+    rows, depth = i.cotangent_all.shape
+    units = i.hidden_5.shape[1]
+    run_phase(
+        last_feed_body,
+        sems,
+        [i.cotangent_all, i.normed_5, i.hidden_5, i.slope_5, i.all_5],
+        [o.part_6, total_of(0), o.grad_three],
+        feed_backward_scratch(rows, depth, units)[1:],
+        swaps=[(0, swaps[0])],
+    )
+    run_phase(
+        result_body,
+        sems,
+        [i.two, i.part_5, i.other_5],
+        [o.three],
+        before=stream.plan(stream.between(stream.position, begins[1], 0.15))[0],
+    )
+    result_here = moves.swap(functools.partial(half_of, o.three, True), lambda own: o.decoder_out)
+    stream.run(moves.taken())
+    swaps[0].arrive()
+
+    def residual(norm_row, previous, x, own, other, grad_out, low_ref, before=nothing, ticks=nothing, after=nothing):
+        ins = [x, own, other] + ([previous] if previous is not None else [])
+
+        def body(*refs):
+            if previous is None:
+                x_ref, own_ref, other_ref, grad_ref = refs
+                previous_ref = None
+            else:
+                x_ref, own_ref, other_ref, previous_ref, grad_ref = refs
+            residual_prologue(
+                norm_row, previous_ref, x_ref, own_ref, other_ref, vec, grad_ref, low_ref, vectors_of[norm_row], ticks
+            )
+
+        run_phase(body, sems, ins, [grad_out], before=before, after=after)
+
+    def attention(number, causal, marks, norm_row, previous, x, own, other, grad_out, parts, mask_row, source, kept):
+        rows, depth = x.shape
+        keys, width = kept[2].shape[0], kept[1].shape[1]
+        cross = source is not None
+        early, prologue, late, main_in, ticks, main_out = stream.plan(marks, (1, 1, 1, 1, 8, 1))
+
+        def inner(low_ref):
+            residual(norm_row, previous, x, own, other, grad_out, low_ref, early, prologue, late)
+            ins = [kept[0]] + ([source] if cross else []) + list(kept[1:])
+            outs = [part for part, swap in parts] + [total_of(number)]
+
+            def body(*refs):
+                normed_ref, refs = refs[0], refs[1:]
+                source_ref = None
+                if cross:
+                    source_ref, refs = refs[0], refs[1:]
+                held, refs = refs[:5], refs[5:]
+                part_out, refs = refs[0], refs[1:]
+                source_part = None
+                if cross:
+                    source_part, refs = refs[0], refs[1:]
+                grad_total, scratch = refs[0], refs[1:]
+                attention_backward_main(
+                    causal, cross, ticks, mask_row, low_ref, normed_ref, source_ref, *held,
+                    part_out, grad_total, source_part, *scratch,
+                )
+
+            run_phase(
+                body,
+                sems,
+                ins,
+                outs,
+                attention_backward_scratch(rows, keys, depth, width, cross)[1:],
+                swaps=[(at, swap) for at, (part, swap) in enumerate(parts)],
+                before=main_in,
+                after=main_out,
+            )
+
+        pl.run_scoped(inner, pltpu.VMEM((rows, depth), low))
+
+    attention(
+        1, False, begins[1], 10, o.grad_three, i.two, o.part_6, o.other_6, o.grad_two,
+        [(o.part_7, swaps[1]), (o.part_8, swaps[2])], source_mask(marks_row), i.memory,
+        (i.normed_4, i.query_4, i.kv_4, i.attended_4, i.totals_4, i.all_4),
+    )
+    swaps[1].arrive()
+    attention(
+        2, True, begins[2], 8, o.grad_two, i.one, o.part_7, o.other_7, o.grad_one,
+        [(o.part_9, swaps[3])], target_mask(marks_row), None,
+        (i.normed_3, i.query_3, i.kv_3, i.attended_3, i.totals_3, i.all_3),
+    )
+    swaps[2].arrive()
+    rows, depth = i.final.shape
+    early, prologue, late, main_in, ticks, main_out = stream.plan(begins[3], (1, 1, 1, 1, 6, 1))
+
+    def feed(low_ref):
+        residual(4, None, i.final, o.part_8, o.other_8, o.grad_final, low_ref, early, prologue, late)
+
+        def body(normed_ref, hidden_ref, slope_ref, w_ref, part_out, grad_total, turned_ref, turned_low):
+            ticks.begin(feed_backward_ticks(rows, units))
+            feed_backward_body(
+                ticks, normed_ref, hidden_ref, slope_ref, w_ref, part_out, grad_total, low_ref, slope_ref,
+                turned_ref, turned_low,
+            )
+
+        run_phase(
+            body,
+            sems,
+            [i.normed_2, i.hidden_2, i.slope_2, i.all_2],
+            [o.part_10, total_of(3)],
+            feed_backward_scratch(rows, depth, units)[2:],
+            swaps=[(0, swaps[4])],
+            before=main_in,
+            after=main_out,
+        )
+
+    pl.run_scoped(feed, pltpu.VMEM((rows, depth), low))
+    swaps[3].arrive()
+    residual(
+        6, o.grad_one, i.target_all, o.part_9, o.other_9, o.target_low, None,
+        stream.plan(stream.between(stream.position, begins[4], 0.1))[0],
+    )
+    target_here = moves.swap(functools.partial(half_of, o.target_low, True), lambda own: o.target_grad)
+    stream.run(moves.taken())
+    swaps[4].arrive()
+    attention(
+        4, False, begins[4], 2, o.grad_final, i.mid, o.part_10, o.other_10, o.grad_mid,
+        [(o.part_11, swaps[5])], source_mask(marks_row), None,
+        (i.normed_1, i.query_1, i.kv_1, i.attended_1, i.totals_1, i.all_1),
+    )
+    one, two, three = stream.plan(stream.between(stream.position, ends[4], 0.5), (2, 2, 1))
+    one()
+    swaps[5].arrive()
+
+    def finish_body(previous_ref, x_ref, own_ref, other_ref, grad_out):
+        norms, kinds = vectors_of[0], vectors_of[12]
+        norms[...] = jnp.zeros_like(norms)
+        kinds[...] = jnp.zeros_like(kinds)
+
+        @pl.loop(0, x_ref.shape[0] // CHUNK)
+        def _(step):
+            first_row = pl.multiple_of(step * CHUNK, CHUNK)
+            at = pl.ds(first_row, CHUNK)
+            grads = own_ref[at, :].astype(wide) + other_ref[at, :].astype(wide)
+            back, by_gain, by_shift = norm_back(x_ref[at, :], vec[0:1, :], grads)
+            back = back + previous_ref[at, :]
+            grad_out[at, :] = back.astype(low)
+            norms[0:1, :] += by_gain
+            norms[1:2, :] += by_shift
+            kind = column_of(flags_row, first_row)
+            kinds[0:1, :] += jnp.sum(jnp.where(kind == 1, back, 0.0), axis=0, keepdims=True)
+            kinds[1:2, :] += jnp.sum(jnp.where(kind == 2, back, 0.0), axis=0, keepdims=True)
+
+        vector_rows[...] = jnp.zeros_like(vector_rows)
+        for first, pair in vectors_of.items():
+            vector_rows[first : first + 2, :] = pair[...]
+        every = jnp.concatenate([vector_rows[...], jnp.zeros((112, depth), wide)], axis=0)
+        store_grad(buffers[5][0], 0, turned(every.astype(low)))
+
+    run_phase(
+        finish_body,
+        sems,
+        [o.grad_mid, i.start, o.part_11, o.other_11],
+        [o.source_low],
+        before=two,
+        after=three,
+    )
+    source_here = moves.swap(functools.partial(half_of, o.source_low, True), lambda own: o.source_grad)
+    stream.run(moves.taken())
+    rest = {}
+    for home in (True, False):
+        late = stream.steps[home][stream.position[home] : ends[4][home]]
+        few = stream.steps[home][ends[4][home] :]
+        merged = []
+        for number in range(max(len(late), len(few))):
+            merged += few[number : number + 1] + late[number : number + 1]
+        rest[home] = merged
+    stream.run(rest)
+    result_here()
+    target_here()
+    source_here()
+    stream.run(moves.taken())
+    moves.finish()
+    stream.finish()
+
+
+def backward_call(kept, vectors):
+    rows, depth = kept.start.shape
+    few = kept.one.shape[0]
+    block = depth // 16
+    near_in = Bag(vectors=vectors, marks_all=kept.marks_all, flags_all=kept.flags_all)
+    far_in = Bag(**kept.__dict__)
+    del far_in.marks_all, far_in.flags_all
+    columns = [
+        kept.all_5.shape[1], kept.all_4.shape[1], kept.all_3.shape[1], kept.all_2.shape[1], kept.all_1.shape[1], 128
+    ]
+    near_out = Bag()
+    n = near_out
+    n.final_5, n.final_4, n.final_3, n.final_2, n.final_1, n.final_vectors = [
+        shaped(block, count, wide) for count in columns
+    ]
+    far_out = Bag(
+        grad_three=shaped(few, depth, low),
+        grad_two=shaped(few, depth, wide),
+        grad_one=shaped(few, depth, wide),
+        grad_final=shaped(rows, depth, wide),
+        grad_mid=shaped(rows, depth, wide),
+        target_low=shaped(few, depth, low),
+        source_low=shaped(rows, depth, low),
+        target_grad=shaped(few // 2, depth, low),
+        source_grad=shaped(rows // 2, depth, low),
+        three=shaped(few, depth, low),
+        decoder_out=shaped(few // 2, depth, low),
+    )
+    f = far_out
+    f.part_6 = f.other_6 = f.part_7 = f.other_7 = f.part_9 = f.other_9 = shaped(few, depth, low)
+    f.part_8 = f.other_8 = f.part_10 = f.other_10 = f.part_11 = f.other_11 = shaped(rows, depth, low)
+    ins, outs = near_in.joined(far_in), near_out.joined(far_out)
+    scratch = [pltpu.VMEM((2, depth), wide)] * 7 + [pltpu.VMEM((16, depth), wide)]
+    for count in columns:
+        scratch += scatter_buffers(block, count)
+    results = pl.pallas_call(
+        functools.partial(backward_kernel, ins.names(), outs.names()),
+        out_shape=tuple(outs.values()),
+        in_specs=specs_of(near_in, far_in),
+        out_specs=tuple(specs_of(near_out, far_out)),
+        scratch_shapes=scratch
+        + [dma(32), dma(6 * SCATTER_SENDS), dma(6 * 80), dma(8), dma(8), dma(8), dma(16)],
+        compiler_params=pltpu.CompilerParams(
+            collective_id=1, has_side_effects=True, vmem_limit_bytes=61 << 20
+        ),
+        name="backward_pass",
+    )(*ins.values())
+    return filled(outs.names(), results)
+
+
 def fits_kernels():
     return lax.axis_size("z") == 4
 
@@ -1411,6 +2135,158 @@
 def factored_step(weights, grads, rows_next, columns_next, row_level, mean_square):
     estimate = rows_next[:, :, None] * columns_next[:, None, :] / row_level[:, None, None]
     return weights - step_rate * jnp.sqrt(mean_square)[:, None, None] * grads * lax.rsqrt(estimate)
+
+
+def plain_pass(source, target, cotangent, marks, vectors, own_groups):
+    core = lax.axis_index("c")
+    depth = vectors.shape[1]
+    source_half = swap_chips(source)
+    flags_half = swap_chips(marks[:source.shape[0]])
+    source_all = both_halves(source_half)
+    flags_all = both_halves(flags_half)
+    masks = swap_chips(marks[source.shape[0] :])
+    source_length = masks[None, : 2 * source.shape[0]]
+    target_length = masks[None, 2 * source.shape[0] :]
+    target_all = both_halves(swap_chips(target))
+    cotangent_all = both_halves(swap_chips(cotangent))
+
+    (encoder_attention, encoder_feed, decoder_attention, cross_attention, decoder_feed) = [
+        (gather_weights(group, "zyx"), group.shape[1]) for group in own_groups
+    ]
+
+    start_rows = jnp.where(
+        (flags_all == 1)[:, None],
+        vectors[12][None, :],
+        jnp.where((flags_all == 2)[:, None], vectors[13][None, :], source_all.astype(wide)),
+    )
+    first_kept = self_attention_call(
+        0, False, source_length, start_rows, encoder_attention, vectors,
+    )
+    first_part = first_kept[5]
+    first_other = other_core(first_part)
+    encoder_mid, second_normed, second_hidden, second_slope, second_part, *rest = feed_forward_call(
+        2, start_rows, first_part, first_other, encoder_feed, vectors,
+    )
+    second_other = other_core(second_part)
+    third_kept = self_attention_call(6, True, target_length, target_all, decoder_attention, vectors)
+    third_part = third_kept[5]
+    third_other = other_core(third_part)
+    decoder_one, encoder_final, memory_rows, *fourth_kept = cross_attention_call(
+        source_length,
+        target_all,
+        third_part,
+        third_other,
+        encoder_mid,
+        second_part,
+        second_other,
+        cross_attention,
+        vectors,
+    )
+    fourth_part = fourth_kept[5]
+    fourth_kept = fourth_kept[:5]
+    decoder_two, fifth_normed, fifth_hidden, fifth_slope, fifth_part = feed_forward_call(
+        10, decoder_one, fourth_part, other_core(fourth_part), decoder_feed, vectors
+    )
+    decoder_three = decoder_two + (fifth_part.astype(wide) + other_core(fifth_part).astype(wide))
+
+    def own_half(rows):
+        half = rows.shape[0] // 2
+        return lax.dynamic_slice_in_dim(rows, core * half, half, 0)
+
+    decoder_out = swap_chips(own_half(decoder_three).astype(low))
+
+    fifth_back, decoder_feed_terms, grad_three = last_feed_backward_call(
+        target_length, cotangent_all, fifth_normed, fifth_hidden, fifth_slope, decoder_feed
+    )
+    query_back, grad_two, vectors_ten, cross_terms, memory_back, *decoder_feed_grad = attention_backward_call(
+        False,
+        10,
+        source_length,
+        grad_three,
+        decoder_two,
+        fifth_back,
+        other_core(fifth_back),
+        vectors,
+        fourth_kept[0],
+        memory_rows,
+        *fourth_kept[1:],
+        cross_attention,
+    )
+    query_other = other_core(query_back)
+    memory_other = other_core(memory_back)
+    third_back, grad_one, vectors_eight, decoder_terms, *cross_grad = attention_backward_call(
+        True,
+        8,
+        target_length,
+        grad_two,
+        decoder_one,
+        query_back,
+        query_other,
+        vectors,
+        third_kept[0],
+        None,
+        *third_kept[1:5],
+        decoder_attention,
+    )
+    third_back_other = other_core(third_back)
+    second_back, encoder_feed_terms, grad_final, vectors_four, *decoder_grad = feed_backward_call(
+        4,
+        encoder_final,
+        memory_back,
+        memory_other,
+        vectors,
+        second_normed,
+        second_hidden,
+        second_slope,
+        encoder_feed,
+    )
+    first_back, grad_mid, vectors_two, encoder_terms, *encoder_feed_grad = attention_backward_call(
+        False,
+        2,
+        source_length,
+        grad_final,
+        encoder_mid,
+        second_back,
+        other_core(second_back),
+        vectors,
+        first_kept[0],
+        None,
+        *first_kept[1:5],
+        encoder_attention,
+    )
+    grad_target, vectors_six = finish_call(
+        6, grad_one, target_all, third_back, third_back_other, vectors
+    )
+    target_grad = swap_chips(own_half(grad_target).astype(low)).astype(wide)
+    grad_start, vectors_zero = finish_call(
+        0, grad_mid, start_rows, first_back, other_core(first_back), vectors
+    )
+    gap_rows = jnp.sum(jnp.where((flags_all == 1)[:, None], grad_start, 0.0), axis=0, keepdims=True)
+    mask_rows = jnp.sum(jnp.where((flags_all == 2)[:, None], grad_start, 0.0), axis=0, keepdims=True)
+    source_grad = swap_chips(own_half(grad_start).astype(low)).astype(wide)
+
+    vector_terms = jnp.concatenate(
+        [
+            vectors_zero,
+            vectors_two,
+            vectors_four,
+            vectors_six,
+            vectors_eight,
+            vectors_ten,
+            gap_rows,
+            mask_rows,
+            jnp.zeros((114, depth), wide),
+        ],
+        axis=0,
+    )
+    vector_terms = vector_terms.T.astype(low)
+    grads = [
+        scatter_gradient(terms, "xyz")
+        for terms in (
+            encoder_terms, decoder_terms, cross_terms, encoder_feed_terms, decoder_feed_terms, vector_terms
+        )
+    ]
+    return (decoder_out, source_grad, target_grad, *grads)
 
 
 def on_device(
@@ -1443,187 +2319,24 @@
         part = feed_weights[2 * index : 2 * index + 2].astype(low)
         return part.transpose(1, 0, 2).reshape(local_rows, 2 * half_units)
 
-    source_half = swap_chips(source_embed[0])
-    flags_half = swap_chips(row_flags[0])
-    source_all = both_halves(source_half)
-    flags_all = both_halves(flags_half)
-    masks = swap_chips(jnp.concatenate([source_mask[0], target_mask[0]]))
-    source_length = jnp.sum(masks[: source_mask.shape[1]]).reshape(1)
-    target_length = jnp.sum(masks[source_mask.shape[1] :]).reshape(1)
-    target_all = both_halves(swap_chips(target_embed[0]))
-    cotangent_all = both_halves(swap_chips(out_cotangent[0]))
-
-    attention_width, feed_width = 4 * half_width, 2 * half_units
-    fits = fits_kernels()
-
-    def flat(gathered):
-        return gathered.reshape(-1, gathered.shape[-1])
-
-    def ride(kind, operand, number):
-        return Rider(kind, operand, number) if fits else None
-
-    own_groups = [attention_group(0), attention_group(1), attention_group(2), feed_group(0), feed_group(1)]
-    if fits:
-        encoder_attention = (flat(gather_all(own_groups[0], 0)), attention_width)
+    own_groups = [attention_group(0), feed_group(0), attention_group(1), attention_group(2), feed_group(1)]
+    marks = jnp.concatenate([row_flags[0], source_mask[0], target_mask[0]])
+    if fits_kernels():
+        kept = forward_call(
+            source_embed[0], target_embed[0], out_cotangent[0], marks[None], vector_params, own_groups
+        )
+        back = backward_call(kept, vector_params)
+        decoder_out = back.decoder_out
+        target_grad = back.target_grad.astype(wide)
+        source_grad = back.source_grad.astype(wide)
+        decoder_feed_grad, cross_grad, decoder_grad = back.final_5, back.final_4, back.final_3
+        encoder_feed_grad, encoder_grad, vector_grad = back.final_2, back.final_1, back.final_vectors
     else:
-        (encoder_attention, decoder_attention, cross_attention, encoder_feed, decoder_feed) = [
-            (gather_weights(group, "zyx"), group.shape[1]) for group in own_groups
-        ]
-
-    start_rows = jnp.where(
-        (flags_all == 1)[:, None],
-        vector_params[12][None, :],
-        jnp.where((flags_all == 2)[:, None], vector_params[13][None, :], source_all.astype(wide)),
-    )
-    first_kept = self_attention_call(
-        0, False, source_length, start_rows, encoder_attention, vector_params,
-        ride("gather", own_groups[3], 1),
-    )
-    if fits:
-        encoder_feed = (flat(first_kept[6]), feed_width)
-    first_part = first_kept[5]
-    first_other = other_core(first_part)
-    encoder_mid, second_normed, second_hidden, second_slope, second_part, *rest = feed_forward_call(
-        2, start_rows, first_part, first_other, encoder_feed, vector_params,
-        ride("gather", jnp.concatenate(own_groups[1:3], axis=1), 2),
-    )
-    if fits:
-        decoder_attention = (flat(rest[0])[:, :attention_width], attention_width)
-        cross_attention = (flat(rest[0])[:, attention_width:], attention_width)
-    second_other = other_core(second_part)
-    third_kept = self_attention_call(6, True, target_length, target_all, decoder_attention, vector_params)
-    third_part = third_kept[5]
-    third_other = other_core(third_part)
-    decoder_one, encoder_final, memory_rows, *fourth_kept = cross_attention_call(
-        source_length,
-        target_all,
-        third_part,
-        third_other,
-        encoder_mid,
-        second_part,
-        second_other,
-        cross_attention,
-        vector_params,
-        ride("gather", own_groups[4], 3),
-    )
-    if fits:
-        decoder_feed = (flat(fourth_kept[6]), feed_width)
-    fourth_part = fourth_kept[5]
-    fourth_kept = fourth_kept[:5]
-    decoder_two, fifth_normed, fifth_hidden, fifth_slope, fifth_part = feed_forward_call(
-        10, decoder_one, fourth_part, other_core(fourth_part), decoder_feed, vector_params
-    )
-    decoder_three = decoder_two + (fifth_part.astype(wide) + other_core(fifth_part).astype(wide))
-
-    def own_half(rows):
-        half = rows.shape[0] // 2
-        return lax.dynamic_slice_in_dim(rows, core * half, half, 0)
-
-    decoder_out = swap_chips(own_half(decoder_three).astype(low))
-
-    fifth_back, decoder_feed_terms, grad_three = last_feed_backward_call(
-        target_length, cotangent_all, fifth_normed, fifth_hidden, fifth_slope, decoder_feed
-    )
-    query_back, grad_two, vectors_ten, cross_terms, memory_back, *decoder_feed_grad = attention_backward_call(
-        False,
-        10,
-        source_length,
-        grad_three,
-        decoder_two,
-        fifth_back,
-        other_core(fifth_back),
-        vector_params,
-        fourth_kept[0],
-        memory_rows,
-        *fourth_kept[1:],
-        cross_attention,
-        ride("scatter", decoder_feed_terms, 4),
-    )
-    query_other = other_core(query_back)
-    memory_other = other_core(memory_back)
-    third_back, grad_one, vectors_eight, decoder_terms, *cross_grad = attention_backward_call(
-        True,
-        8,
-        target_length,
-        grad_two,
-        decoder_one,
-        query_back,
-        query_other,
-        vector_params,
-        third_kept[0],
-        None,
-        *third_kept[1:5],
-        decoder_attention,
-        ride("scatter", cross_terms, 5),
-    )
-    third_back_other = other_core(third_back)
-    second_back, encoder_feed_terms, grad_final, vectors_four, *decoder_grad = feed_backward_call(
-        4,
-        encoder_final,
-        memory_back,
-        memory_other,
-        vector_params,
-        second_normed,
-        second_hidden,
-        second_slope,
-        encoder_feed,
-        ride("scatter", decoder_terms, 6),
-    )
-    first_back, grad_mid, vectors_two, encoder_terms, *encoder_feed_grad = attention_backward_call(
-        False,
-        2,
-        source_length,
-        grad_final,
-        encoder_mid,
-        second_back,
-        other_core(second_back),
-        vector_params,
-        first_kept[0],
-        None,
-        *first_kept[1:5],
-        encoder_attention,
-        ride("scatter", encoder_feed_terms, 7),
-    )
-    grad_target, vectors_six = finish_call(
-        6, grad_one, target_all, third_back, third_back_other, vector_params
-    )
-    target_grad = swap_chips(own_half(grad_target).astype(low)).astype(wide)
-    grad_start, vectors_zero = finish_call(
-        0, grad_mid, start_rows, first_back, other_core(first_back), vector_params
-    )
-    gap_rows = jnp.sum(jnp.where((flags_all == 1)[:, None], grad_start, 0.0), axis=0, keepdims=True)
-    mask_rows = jnp.sum(jnp.where((flags_all == 2)[:, None], grad_start, 0.0), axis=0, keepdims=True)
-    source_grad = swap_chips(own_half(grad_start).astype(low)).astype(wide)
+        (
+            decoder_out, source_grad, target_grad,
+            encoder_grad, decoder_grad, cross_grad, encoder_feed_grad, decoder_feed_grad, vector_grad,
+        ) = plain_pass(source_embed[0], target_embed[0], out_cotangent[0], marks, vector_params, own_groups)
     source_grad = jnp.where((row_flags[0] == 0)[:, None], source_grad, 0.0)
-
-    vector_terms = jnp.concatenate(
-        [
-            vectors_zero,
-            vectors_two,
-            vectors_four,
-            vectors_six,
-            vectors_eight,
-            vectors_ten,
-            gap_rows,
-            mask_rows,
-            jnp.zeros((114, depth), wide),
-        ],
-        axis=0,
-    )
-    vector_terms = vector_terms.T.astype(low)
-    if fits:
-        (decoder_feed_grad,), (cross_grad,), (decoder_grad,), (encoder_feed_grad,) = (
-            decoder_feed_grad, cross_grad, decoder_grad, encoder_feed_grad
-        )
-        last_grads = scatter_all([encoder_terms, vector_terms], 8)
-        encoder_grad, vector_grad = last_grads[:, :attention_width], last_grads[:, attention_width:]
-    else:
-        (encoder_grad, decoder_grad, cross_grad, encoder_feed_grad, decoder_feed_grad, vector_grad) = [
-            scatter_gradient(terms, "xyz")
-            for terms in (
-                encoder_terms, decoder_terms, cross_terms, encoder_feed_terms, decoder_feed_terms, vector_terms
-            )
-        ]
     vector_grad = vector_grad[:, :14].T
 
     def as_matrices(rows, count):

time: 664 us -> 503 us (0.76)
  Pallas kernels: 505 us -> 454 us
  starting transfers between devices: 56.1 us -> 8.42 us
  local copies, waits for them, and re-layouts: 38.8 us -> 10.5 us
  other arithmetic: 27.6 us -> 9.73 us
  waiting for transfers between devices: 26 us -> 11.7 us
    pallas_call x14 -> x2, Pallas kernels: 505 us -> 454 us  [the longest x1 258 us: backward_call(): pl.pallas_call(functools.partial(backward_kernel, ins.names(), outs.names...]
    ppermute x17 -> x2, starting transfers between devices: 31.9 us -> 0.14 us  [other_core(): return lax.ppermute(array, 'c', [(0, 1), (1, 0)])]
    ppermute x8 -> x0, starting transfers between devices: 18.7 us -> none  [swap_chips(): return lax.ppermute(array, ('c', 'x'), [(0, 0), (1, 2), (2, 1), (3, 3)])]
    unnamed x111 -> x55, local copies, waits for them, and re-layouts: 18.7 us -> 4.48 us
    ppermute x17 -> x2, waiting for transfers between devices: 12.6 us -> 1.29 us  [other_core(): return lax.ppermute(array, 'c', [(0, 1), (1, 0)])]
    slice x3 -> x0, local copies, waits for them, and re-layouts: 6.75 us -> none  [the longest x1 4.92 us: on_device(): cross_attention = (flat(rest[0])[:, attention_width:], attention_width)]
  transfers between devices with their start and end apart: 33 -> 10, of which waited for: 10 -> 8; matrix products, arithmetic and copies ran while one was open for 6% -> 1% of each run, Pallas kernels for 33% -> 0%
where the time goes in v5:
time: 503 us; the launch traced here: 496 us
  Pallas kernels  454 us (90%)
  waiting for transfers between devices  11.7 us (2%)
  local copies, waits for them, and re-layouts  10.5 us (2%)
  other arithmetic  9.73 us (2%)
  starting transfers between devices  8.42 us (2%)
    pallas_call x1, Pallas kernels, backward_call(): pl.pallas_call(functools.partial(backward_kernel, ins.names(), outs.names...  258 us
    pallas_call x1, Pallas kernels, forward_call(): pl.pallas_call(functools.partial(forward_kernel, ins.names(), outs.names(...  197 us
  transfers between devices with their start and end apart: 10, of which 8 were waited for; matrix products, arithmetic and copies ran while one was open for 1% of the time, Pallas kernels for 0%

profile of v5, /device:TPU:0, one launch (start us, length us, event | category | flops | bytes accessed | tf_op | source)
XLA Modules:
  0.0 495.9 jit_solution(4344046394584150904)
XLA Ops:
  0.7 1.7 multiply_reduce_fusion.3
  2.4 0.7 copy.51
  3.1 0.7 copy.53
  3.8 0.7 copy.54
  4.7 0.7 copy.52
  5.5 0.7 copy.55
  6.2 0.6 pad_add_fusion
  6.8 196.6 %forward_pass.1 = (s32[1,2048]{1,0:T(1,128)}, s32[1,1024]{1,0:T(1,128)}, bf16[1024,768]{1,0:T(8,128)(2,1)}, bf16[512,768]{1,0:T(8,128)(2,1)}, bf16[512,768]{1,0:...) custom-call(s32[1,2048]{1,0:T(1,128)} %bitcast.82, ...), custom_call_target="tpu_custom_call" | custom-call | tf_op jit(solution)/shard_map/forward_pass/pallas_call | solution.py:1828
  203.4 257.7 %backward_pass.1 = (f32[48,3072]{1,0:T(8,128)}, f32[48,1536]{1,0:T(8,128)}, f32[48,1536]{1,0:T(8,128)}, f32[48,3072]{1,0:T(8,128)}, f32[48,1536]{1,0:T(8,128)}, ...) custom-call(f32[14,768]{1,0:T(8,128)} %refs_0_.1, ...), custom_call_target="tpu_custom_call" | custom-call | tf_op jit(solution)/shard_map/backward_pass/pallas_call | solution.py:2116
  461.2 1.0 copy.61
  462.1 1.3 bitcast_bitcast_fusion
  463.8 0.6 copy-done.8
  464.6 1.0 multiply_reduce_fusion.4
  465.8 0.9 bitcast_convert_fusion
  467.0 1.4 select_bitcast_fusion
  468.4 0.8 collective-permute-done.5
  469.7 0.9 collective-permute-done.6
  471.0 3.8 collective-permute-done.7
  474.9 1.2 collective-permute-start
  476.1 2.8 collective-permute-done.8
  479.2 0.7 copy.41
  480.3 1.7 collective-permute-start.2
  481.9 1.9 collective-permute-done.2
  483.8 2.0 collective-permute-start.3
  485.8 0.7 copy.42
  486.5 0.8 collective-permute-done.3
  487.4 2.8 collective-permute-start.4
  490.2 0.7 copy.43
  490.9 0.6 copy.44
  492.1 1.5 multiply_subtract_fusion
  493.7 1.2 multiply_subtract_fusion.1
  494.9 0.7 copy.63
  (96 shorter events, 3.4 us)
Async XLA Ops:
  0.6 3.8 copy-start
  4.7 1.5 copy-start.19
  4.7 1.5 copy-start.20
  4.7 1.5 copy-start.22
  463.5 1.0 copy-start.9
  463.8 28.3 %copy-start.1 = (f32[4,48,1536]{2,1,0:T(8,128)}, f32[4,48,1536]{2,1,0:T(8,128)S(1)}, u32[]{:S(2)}) copy-start(f32[4,48,1536]{2,1,0:T(8,128)S(1)} %get-tuple-element.192) | copy-start | bytes 3538948
  463.8 1.8 copy-start.5
  463.8 1.9 copy-start.7
  464.6 2.3 copy-start.18
  464.6 2.4 copy-start.4
  465.6 3.7 collective-permute-start.5
  465.7 2.6 copy-start.12
  466.7 2.8 copy-start.17
  466.7 2.9 copy-start.21
  467.0 25.1 %copy-start.14 = (f32[4,1536]{1,0:T(4,128)S(1)}, f32[4,1536]{1,0:T(4,128)}, u32[]{:S(2)}) copy-start(f32[4,1536]{1,0:T(4,128)} %param.25) | copy-start | bytes 73732
  467.0 25.1 %copy-start.15 = (f32[12,384]{1,0:T(8,128)S(1)}, f32[12,384]{1,0:T(8,128)}, u32[]{:S(2)}) copy-start(f32[12,384]{1,0:T(8,128)} %param.23) | copy-start | bytes 55300
  469.4 1.3 collective-permute-start.6
  469.6 24.1 %copy-start.13 = (f32[12,48]{1,0:T(8,128)}, f32[12,48]{1,0:T(8,128)S(1)}, u32[]{:S(2)}) copy-start(f32[12,48]{1,0:T(8,128)S(1)} %get-tuple-element.197) | copy-start | bytes 6916
  469.7 24.0 %copy-start.16 = (f32[4,48]{1,0:T(4,128)}, f32[4,48]{1,0:T(4,128)S(1)}, u32[]{:S(2)}) copy-start(f32[4,48]{1,0:T(4,128)S(1)} %get-tuple-element.199) | copy-start | bytes 2308
  470.7 4.1 collective-permute-start.7
  474.8 4.1 collective-permute-start.8
  474.9 4.1 collective-permute-start
  478.9 12.9 %collective-permute-start.9 = (f32[10768]{0:T(1024)S(1)}, f32[10768]{0:T(1024)S(1)}, u32[]{:S(2)}, u32[]{:S(2)}) collective-permute-start(f32[10768]{0:T(1024)S(1)} %add.69), channel_id=1, source_target_pairs={{0,16},{16,0},{8,24},{24,8},{1,17},{17,1},{9,25},{25,9},{2,18},{18... | collective-permute-start | bytes 129224 | tf_op jit(solution)/shard_map/ppermute | solution.py:140
  479.1 1.2 collective-permute-start.1
  480.3 3.5 collective-permute-start.2
  483.8 3.5 collective-permute-start.3
  487.4 4.4 collective-permute-start.4
  492.1 1.6 copy-start.10
  492.1 1.6 copy-start.11
  492.1 1.6 copy-start.2
  492.1 1.6 copy-start.3
  493.7 1.2 copy-start.6
  (1 other events, 1.0 us)

commit v6 on v5

--- a/solution.py
+++ b/solution.py
@@ -583,13 +583,6 @@
                     add_rows(functools.partial(core_piece, third, which), zc_slot(which), 2 * rows),
                 )
 
-            def second_steps(back):
-                x_add(second, here(back))
-                if back < 3:
-                    z_add(second, back)
-                if back > 0:
-                    z_send(second, back)
-
             zc_send(there(3))
             zc_send(here(3))
             for back in (3, 2, 1, 0):
@@ -604,45 +597,44 @@
                 if back > 1:
                     x_sends(first, there(back))
                     x_sends(first, here(back))
-            for back in (3, 2, 1, 0):
-                if widths[second]:
-                    self.wait(home, yb_slot(back), sem(52 + back))
-                    self.local(
-                        home,
-                        add_rows(
-                            functools.partial(core_piece, second, here(back)), yb_slot(back), 2 * rows
-                        ),
-                    )
-                x_sends(second, here(back))
-                if back > 1:
-                    x_sends(first, there(back - 2))
-                    x_sends(first, here(back - 2))
-                if back < 3:
-                    for which in (there(back), here(back)):
-                        zc_add(which)
-                        if back > 0:
-                            zc_send(which)
-                        elif not which[1]:
-                            self.send(
-                                home,
-                                functools.partial(core_piece, third, there(0)),
-                                lambda: yc_in.at[...],
-                                sem(56),
-                                functools.partial(target_of, "y"),
-                            )
-                x_add(first, there(back))
-                if widths[first]:
-                    self.send(
-                        home,
-                        plane(first, there(back)),
-                        ya_slot(back),
-                        sem(48 + back),
-                        functools.partial(target_of, "y"),
-                    )
-                x_add(first, here(back))
-                if back < 3:
-                    second_steps(back + 1)
-                if back == 0:
+            for turn in range(7):
+                back = 3 - turn
+                if back >= 0:
+                    if widths[second]:
+                        self.wait(home, yb_slot(back), sem(52 + back))
+                        self.local(
+                            home,
+                            add_rows(
+                                functools.partial(core_piece, second, here(back)), yb_slot(back), 2 * rows
+                            ),
+                        )
+                    x_sends(second, here(back))
+                    if back > 1:
+                        x_sends(first, there(back - 2))
+                        x_sends(first, here(back - 2))
+                    if back < 3:
+                        for which in (there(back), here(back)):
+                            zc_add(which)
+                            if back > 0:
+                                zc_send(which)
+                            elif not which[1]:
+                                self.send(
+                                    home,
+                                    functools.partial(core_piece, third, there(0)),
+                                    lambda: yc_in.at[...],
+                                    sem(56),
+                                    functools.partial(target_of, "y"),
+                                )
+                    x_add(first, there(back))
+                    if widths[first]:
+                        self.send(
+                            home,
+                            plane(first, there(back)),
+                            ya_slot(back),
+                            sem(48 + back),
+                            functools.partial(target_of, "y"),
+                        )
+                if back == -1:
                     self.wait(home, lambda: yc_in.at[...], sem(56))
                     self.local(
                         home,
@@ -653,14 +645,28 @@
                         ),
                     )
                     x_sends(third, here(0))
-                if widths[first]:
-                    self.wait(home, ya_slot(back), sem(48 + back))
-                    self.local(home, add_rows(plane(first, here(back)), ya_slot(back), rows))
-                if back < 3:
+                back = 4 - turn
+                if 0 <= back < 4:
+                    x_add(first, here(back))
+                    if widths[first]:
+                        self.wait(home, ya_slot(back), sem(48 + back))
+                        self.local(home, add_rows(plane(first, here(back)), ya_slot(back), rows))
+                    if back == 3:
+                        z_send(first, back)
+                back = 5 - turn
+                if 0 <= back < 3:
                     z_add(first, back)
-                if back > 0:
-                    z_send(first, back)
-            second_steps(0)
+                    if back > 0:
+                        z_send(first, back)
+                if 0 <= back < 4:
+                    x_add(second, here(back))
+                    if back == 3:
+                        z_send(second, back)
+                back = 6 - turn
+                if 0 <= back < 3:
+                    z_add(second, back)
+                    if back > 0:
+                        z_send(second, back)
             x_add(third, here(0), last=True)
 
 
@@ -1489,6 +1495,24 @@
 
     allocations = [vmem_like(ref) for ref in moved_in] + [vmem_like(ref) for ref in moved_out]
     pl.run_scoped(scoped, *allocations, *scratch)
+
+
+def prefetched(sems, ins, use):
+    def scoped(*own):
+        copies = [
+            pltpu.make_async_copy(ref, one, sems.at[32 + number])
+            for number, (ref, one) in enumerate(zip(ins, own))
+        ]
+        for copy in copies:
+            copy.start()
+
+        def wait():
+            for copy in copies:
+                copy.wait()
+
+        use([Direct(one) for one in own], wait)
+
+    pl.run_scoped(scoped, *[vmem_like(ref) for ref in ins])
 
 
 def column_of(row_ref, first_row):
@@ -1874,7 +1898,7 @@
             Part(group_send, number * SCATTER_SENDS),
             Part(group_recv, number * 80),
         )
-        stream.add(mover, (0.0, 0.15, 0.15, 0.15, 0.1, 0.0)[number])
+        stream.add(mover, (0.0, 0.85, 0.85, 0.85, 0.5, 0.0)[number])
     begins, ends = stream.begins, stream.ends
     swap_refs = (o.other_6, o.other_7, o.other_8, o.other_9, o.other_10, o.other_11)
     swaps = [
@@ -1938,9 +1962,10 @@
         cross = source is not None
         early, prologue, late, main_in, ticks, main_out = stream.plan(marks, (1, 1, 1, 1, 8, 1))
 
-        def inner(low_ref):
+        def inner(low_ref, ins, wait):
             residual(norm_row, previous, x, own, other, grad_out, low_ref, early, prologue, late)
-            ins = [kept[0]] + ([source] if cross else []) + list(kept[1:])
+            wait()
+            ins = [kept[0]] + ([source] if cross else []) + ins
             outs = [part for part, swap in parts] + [total_of(number)]
 
             def body(*refs):
@@ -1970,7 +1995,10 @@
                 after=main_out,
             )
 
-        pl.run_scoped(inner, pltpu.VMEM((rows, depth), low))
+        pl.run_scoped(
+            lambda low_ref: prefetched(sems, kept[1:], functools.partial(inner, low_ref)),
+            pltpu.VMEM((rows, depth), low),
+        )
 
     attention(
         1, False, begins[1], 10, o.grad_three, i.two, o.part_6, o.other_6, o.grad_two,
@@ -1987,8 +2015,9 @@
     rows, depth = i.final.shape
     early, prologue, late, main_in, ticks, main_out = stream.plan(begins[3], (1, 1, 1, 1, 6, 1))
 
-    def feed(low_ref):
+    def feed(low_ref, ins, wait):
         residual(4, None, i.final, o.part_8, o.other_8, o.grad_final, low_ref, early, prologue, late)
+        wait()
 
         def body(normed_ref, hidden_ref, slope_ref, w_ref, part_out, grad_total, turned_ref, turned_low):
             ticks.begin(feed_backward_ticks(rows, units))
@@ -2000,7 +2029,7 @@
         run_phase(
             body,
             sems,
-            [i.normed_2, i.hidden_2, i.slope_2, i.all_2],
+            [ins[0], i.hidden_2, i.slope_2, ins[1]],
             [o.part_10, total_of(3)],
             feed_backward_scratch(rows, depth, units)[2:],
             swaps=[(0, swaps[4])],
@@ -2008,7 +2037,11 @@
             after=main_out,
         )
 
-    pl.run_scoped(feed, pltpu.VMEM((rows, depth), low))
+    feed_ins = [i.normed_2, i.all_2]
+    pl.run_scoped(
+        lambda low_ref: prefetched(sems, feed_ins, functools.partial(feed, low_ref)),
+        pltpu.VMEM((rows, depth), low),
+    )
     swaps[3].arrive()
     residual(
         6, o.grad_one, i.target_all, o.part_9, o.other_9, o.target_low, None,
@@ -2119,13 +2152,163 @@
         in_specs=specs_of(near_in, far_in),
         out_specs=tuple(specs_of(near_out, far_out)),
         scratch_shapes=scratch
-        + [dma(32), dma(6 * SCATTER_SENDS), dma(6 * 80), dma(8), dma(8), dma(8), dma(16)],
+        + [dma(48), dma(6 * SCATTER_SENDS), dma(6 * 80), dma(8), dma(8), dma(8), dma(16)],
         compiler_params=pltpu.CompilerParams(
             collective_id=1, has_side_effects=True, vmem_limit_bytes=61 << 20
         ),
         name="backward_pass",
     )(*ins.values())
     return filled(outs.names(), results)
+
+
+def lane_slot(number):
+    return number if number < 12 else number + 4
+
+
+def update_kernel(
+    f1, f2, f3, f4, f5, fv, aw, fw, ra, ca, rf, cf, vp, vl, vm,
+    ag, fg, vg, au, fu, vu, ran, can, rfn, cfn, vmn, fng,
+    square, other_square, mine, theirs, line, line_in, send_sems, recv_sems,
+):
+    rows = f1.shape[0]
+    depth = 16 * rows
+    width, units = aw.shape[2], fw.shape[2]
+    barrier = pltpu.get_barrier_semaphore()
+    z = place("z")
+    near = z + 1 - 2 * lax.rem(z, 2)
+    far = lax.rem(z + 2, 4)
+    partners = [target_of("x"), target_of("c"), target_of("y"), {"z": near}, {"z": far}]
+    for partner in partners:
+        pl.semaphore_signal(barrier, inc=1, device_id=partner, device_id_type=MESH)
+    keep, take = decay_rate, 1.0 - decay_rate
+    finals = (f1, f3, f4, f2, f5)
+    matrices = []
+    for number in range(16):
+        if number < 12:
+            final, at, size = finals[number // 4], number % 4 * width, width
+            held = (aw, ag, au, number, ca, can)
+        else:
+            final, at, size = finals[3 + (number - 12) // 2], (number - 12) % 2 * units, units
+            held = (fw, fg, fu, number - 12, cf, cfn)
+        matrices.append((final, at, size, number * width if number < 12 else 12 * width + (number - 12) * units, held))
+    columns = 12 * width + 4 * units
+
+    square[...] = jnp.zeros_like(square)
+    square[0:12, 0:rows] = ra[...]
+    square[16:20, 0:rows] = rf[...]
+    moments = jnp.transpose(square[...])[0:rows, :]
+    other_square[...] = jnp.ones_like(other_square)
+    other_square[0:14, 0:rows] = vm[...]
+    other_square[16:30, 0:rows] = vl[...]
+    scale = jnp.sqrt(jnp.mean(vp[...] * vp[...], axis=1, keepdims=True))
+    other_square[16:30, rows : rows + 128 - rows] = jnp.broadcast_to(scale, (14, 128 - rows))
+    turned_vectors = jnp.transpose(other_square[...])
+    vector_moments = turned_vectors[0:rows, :]
+    shifted = pltpu.roll(turned_vectors, 112, 1)
+    vector_local, vector_scale = shifted[0:rows, :], shifted[rows : rows + 1, :]
+
+    lane = lax.broadcasted_iota(jnp.int32, (rows, 128), 1)
+    one_lane = lax.broadcasted_iota(jnp.int32, (1, 128), 1)
+    row_sums = jnp.zeros((rows, 128), wide)
+    totals = pltpu.roll(jnp.sum(moments, axis=0, keepdims=True) * 0.5, 64, 1)
+    for number, (final, at, size, begin, held) in enumerate(matrices):
+        grads = final[:, at : at + size]
+        squares = grads * grads
+        by_row = jnp.sum(squares, axis=1, keepdims=True)
+        line[:, begin : begin + size] = jnp.sum(squares, axis=0, keepdims=True)
+        weights = held[0][held[3]]
+        by_weight = jnp.sum(jnp.sum(weights * weights, axis=1, keepdims=True), axis=0, keepdims=True)
+        slot = lane_slot(number)
+        row_sums = jnp.where(lane == slot, by_row, row_sums)
+        totals = jnp.where(one_lane == slot, jnp.sum(by_row, axis=0, keepdims=True), totals)
+        totals = jnp.where(one_lane == slot + 32, by_weight, totals)
+        held[1][held[3]] = grads
+    mine[0:rows, :] = row_sums
+    mine[rows : rows + 8, :] = jnp.broadcast_to(totals, (8, 128))
+    pl.semaphore_wait(barrier, len(partners))
+
+    def exchange(source, target, number):
+        copy = pltpu.make_async_remote_copy(
+            src_ref=source,
+            dst_ref=target,
+            send_sem=send_sems.at[number],
+            recv_sem=recv_sems.at[number],
+            device_id=partners[number],
+            device_id_type=MESH,
+        )
+        copy.start()
+        copy.wait()
+
+    exchange(mine, theirs, 0)
+    row_sums = mine[0:rows, :] + theirs[0:rows, :]
+    line[:, columns : columns + 128] = mine[rows : rows + 1, :] + theirs[rows : rows + 1, :]
+    for number in range(1, 5):
+        exchange(line, line_in.at[number - 1], number)
+        line[...] += line_in[number - 1]
+
+    totals = line[:, columns : columns + 128]
+    across = jnp.where(one_lane < 16, float(2 * width), float(2 * units))
+    level = (keep * pltpu.roll(totals, 64, 1) + take * totals / across) / depth
+    size_of = jnp.sqrt(pltpu.roll(totals, 96, 1) / (across * depth))
+    rows_next = keep * moments + take * row_sums / across
+
+    def pick(row, slot):
+        return jnp.sum(jnp.where(lane[0 : row.shape[0], :] == slot, row, 0.0), axis=1, keepdims=True)
+
+    for number, (final, at, size, begin, held) in enumerate(matrices):
+        slot = lane_slot(number)
+        index = held[3]
+        columns_next = keep * held[4][index : index + 1, :] + take * line[:, begin : begin + size] / depth
+        held[5][index : index + 1, :] = columns_next
+        estimate = pick(rows_next, slot) * columns_next / pick(level, slot)
+        step = step_rate * pick(size_of, slot)
+        held[2][index] = held[0][index] - step * final[:, at : at + size] * lax.rsqrt(estimate)
+
+    grads = fv[...]
+    moments_next = keep * vector_moments + take * grads * grads
+    vectors_next = vector_local - step_rate * vector_scale * grads * lax.rsqrt(moments_next)
+    small = jnp.where(lane < 32, rows_next, pltpu.roll(grads, 32, 1))
+    small = jnp.where(lane < 48, small, pltpu.roll(moments_next, 48, 1))
+    small = jnp.where(lane < 64, small, pltpu.roll(vectors_next, 64, 1))
+    small = jnp.where(lane < 80, small, pltpu.roll(grads, 70, 1))
+    square[0:rows, :] = small
+    turned_small = jnp.transpose(square[...])
+    ran[...] = turned_small[0:12, 0:rows]
+    rfn[...] = turned_small[16:20, 0:rows]
+    vg[...] = turned_small[32:46, 0:rows]
+    vmn[...] = turned_small[48:62, 0:rows]
+    vu[...] = turned_small[64:78, 0:rows]
+    fng[...] = turned_small[80:82, 0:rows]
+
+
+def update_call(finals, aw, fw, ra, ca, rf, cf, vp, vl, vm):
+    rows = finals[0].shape[0]
+    columns = 12 * aw.shape[2] + 4 * fw.shape[2]
+
+    def same(array):
+        return jax.ShapeDtypeStruct(array.shape, wide)
+
+    pair = jax.ShapeDtypeStruct((2, rows), wide)
+    return pl.pallas_call(
+        update_kernel,
+        out_shape=tuple(same(a) for a in (aw, fw, vm, aw, fw, vm, ra, ca, rf, cf, vm)) + (pair,),
+        in_specs=[whole()] * 15,
+        out_specs=tuple([whole()] * 12),
+        scratch_shapes=[
+            pltpu.VMEM((128, 128), wide),
+            pltpu.VMEM((128, 128), wide),
+            pltpu.VMEM((rows + 8, 128), wide),
+            pltpu.VMEM((rows + 8, 128), wide),
+            pltpu.VMEM((1, columns + 128), wide),
+            pltpu.VMEM((4, 1, columns + 128), wide),
+            dma(5),
+            dma(5),
+        ],
+        compiler_params=pltpu.CompilerParams(
+            collective_id=2, has_side_effects=True, vmem_limit_bytes=40 << 20
+        ),
+        name="update",
+    )(*finals, aw, fw, ra, ca, rf, cf, vp, vl, vm)
 
 
 def fits_kernels():
@@ -2329,13 +2512,20 @@
         decoder_out = back.decoder_out
         target_grad = back.target_grad.astype(wide)
         source_grad = back.source_grad.astype(wide)
-        decoder_feed_grad, cross_grad, decoder_grad = back.final_5, back.final_4, back.final_3
-        encoder_feed_grad, encoder_grad, vector_grad = back.final_2, back.final_1, back.final_vectors
-    else:
-        (
-            decoder_out, source_grad, target_grad,
-            encoder_grad, decoder_grad, cross_grad, encoder_feed_grad, decoder_feed_grad, vector_grad,
-        ) = plain_pass(source_embed[0], target_embed[0], out_cotangent[0], marks, vector_params, own_groups)
+        source_grad = jnp.where((row_flags[0] == 0)[:, None], source_grad, 0.0)
+        local_width = vector_moments.shape[1]
+        number = (lax.axis_index("z") * 2 + lax.axis_index("y")) * 2 + core
+        vector_local = lax.dynamic_slice_in_dim(vector_params, number * local_width, local_width, 1)
+        updates = update_call(
+            [back.final_1, back.final_2, back.final_3, back.final_4, back.final_5, back.final_vectors],
+            attention_weights, feed_weights, rows_attention, columns_attention, rows_feed, columns_feed,
+            vector_params, vector_local, vector_moments,
+        )
+        return decoder_out[None], source_grad[None], target_grad[None], *updates
+    (
+        decoder_out, source_grad, target_grad,
+        encoder_grad, decoder_grad, cross_grad, encoder_feed_grad, decoder_feed_grad, vector_grad,
+    ) = plain_pass(source_embed[0], target_embed[0], out_cotangent[0], marks, vector_params, own_groups)
     source_grad = jnp.where((row_flags[0] == 0)[:, None], source_grad, 0.0)
     vector_grad = vector_grad[:, :14].T
 

time: 503 us -> 482 us (0.958)
  waiting for transfers between devices: 11.7 us -> 0 us
  starting transfers between devices: 8.42 us -> 0 us
  local copies, waits for them, and re-layouts: 10.5 us -> 18.8 us
  other arithmetic: 9.73 us -> 4.3 us
    pallas_call x1, Pallas kernels: 258 us -> 233 us  [backward_call(): pl.pallas_call(functools.partial(backward_kernel, ins.names(), outs.names...]
    pallas_call x0 -> x1, Pallas kernels: none -> 20.1 us  [update_call(): pl.pallas_call(update_kernel, out_shape=tuple((same(a) for a in (aw, fw,...]
    ppermute x10 -> x0, waiting for transfers between devices: 11.7 us -> none  [the longest x2 5.65 us: data_sum(): values = values + lax.ppermute(values, 'y', [(0, 1), (1, 0)])]
    unnamed x55, local copies, waits for them, and re-layouts: 4.48 us -> 15.2 us
    ppermute x10 -> x0, starting transfers between devices: 8.42 us -> none  [the longest x2 2.98 us: data_sum(): return values + lax.ppermute(values, 'z', [(0, 2), (2, 0), (1, 3), (3, 1)])]
  transfers between devices with their start and end apart: 10 -> 0, of which waited for: 8 -> 0; matrix products, arithmetic and copies ran while one was open for 1% -> 0% of each run, Pallas kernels for 0% -> 0%
where the time goes in v6:
time: 482 us; the launch traced here: 474 us
  Pallas kernels  450 us (93%)
  local copies, waits for them, and re-layouts  18.8 us (4%)
    pallas_call x1, Pallas kernels, backward_call(): pl.pallas_call(functools.partial(backward_kernel, ins.names(), outs.names...  233 us
    pallas_call x1, Pallas kernels, forward_call(): pl.pallas_call(functools.partial(forward_kernel, ins.names(), outs.names(...  197 us
    pallas_call x1, Pallas kernels, update_call(): pl.pallas_call(update_kernel, out_shape=tuple((same(a) for a in (aw, fw,...  20.1 us
    unnamed x55, local copies, waits for them, and re-layouts  15.2 us

profile of v6, /device:TPU:0, one launch (start us, length us, event | category | flops | bytes accessed | tf_op | source)
XLA Modules:
  0.0 473.8 jit_solution(1807063012620401368)
XLA Ops:
  0.7 1.3 convert.10
  2.0 0.7 copy.34
  2.7 0.7 copy.36
  3.4 0.7 copy.37
  4.2 0.7 copy.35
  4.9 0.7 copy.38
  5.7 0.6 pad_add_fusion
  6.3 196.5 %forward_pass.1 = (s32[1,2048]{1,0:T(1,128)}, s32[1,1024]{1,0:T(1,128)}, bf16[1024,768]{1,0:T(8,128)(2,1)}, bf16[512,768]{1,0:T(8,128)(2,1)}, bf16[512,768]{1,0:...) custom-call(s32[1,2048]{1,0:T(1,128)} %bitcast.42, ...), custom_call_target="tpu_custom_call" | custom-call | tf_op jit(solution)/shard_map/forward_pass/pallas_call | solution.py:1852
  202.9 232.9 %backward_pass.1 = (f32[48,3072]{1,0:T(8,128)}, f32[48,1536]{1,0:T(8,128)}, f32[48,1536]{1,0:T(8,128)}, f32[48,3072]{1,0:T(8,128)}, f32[48,1536]{1,0:T(8,128)}, ...) custom-call(f32[14,768]{1,0:T(8,128)} %vp.1, ...), custom_call_target="tpu_custom_call" | custom-call | tf_op jit(solution)/shard_map/backward_pass/pallas_call | solution.py:2149
  435.8 0.1 constant_dynamic-slice_fusion.vl
  436.0 1.1 copy-done.2
  437.0 1.1 copy-done.3
  438.1 1.0 copy-done.5
  439.0 1.0 copy-done.6
  440.0 1.0 copy-done.7
  441.0 0.7 copy-done.10
  441.7 20.1 %update.1 = (f32[12,48,384]{2,1,0:T(8,128)S(1)}, f32[4,48,1536]{2,1,0:T(8,128)S(1)}, f32[14,48]{1,0:T(8,128)S(1)}, f32[12,48,384]{2,1,0:T(8,128)S(1)}, f32[4,48,...) custom-call(f32[48,1536]{1,0:T(8,128)S(1)} %copy-done.7, ...), custom_call_target="tpu_custom_call" | custom-call | tf_op jit(solution)/shard_map/update/pallas_call | solution.py:2292
  461.9 1.4 select_bitcast_fusion
  463.3 0.9 bitcast_convert_fusion
  464.2 0.7 copy.52
  464.9 0.9 copy.53
  465.9 1.0 copy.54
  466.9 0.6 copy.55
  467.5 0.9 copy.56
  468.4 1.0 copy.57
  469.4 0.6 copy.58
  470.0 0.6 copy.59
  470.6 0.6 copy.60
  471.2 0.6 copy.61
  471.8 0.6 copy.62
  472.4 0.6 copy.63
  473.0 0.6 copy.64
  (38 shorter events, 0.2 us)
Async XLA Ops:
  0.6 3.4 copy-start
  4.1 1.6 copy-start.17
  4.1 1.5 copy-start.18
  4.1 1.5 copy-start.19
  202.8 233.0 %copy-start.4 = (f32[14,768]{1,0:T(8,128)S(1)}, f32[14,768]{1,0:T(8,128)}, u32[]{:S(2)}) copy-start(f32[14,768]{1,0:T(8,128)} %vp.1) | copy-start | bytes 129028
  202.8 233.1 %copy-start.1 = (f32[12,48,384]{2,1,0:T(8,128)S(1)}, f32[12,48,384]{2,1,0:T(8,128)}, u32[]{:S(2)}) copy-start(f32[12,48,384]{2,1,0:T(8,128)} %aw.1) | copy-start | bytes 2654212
  202.8 233.1 %copy-start.8 = (f32[12,384]{1,0:T(8,128)S(1)}, f32[12,384]{1,0:T(8,128)}, u32[]{:S(2)}) copy-start(f32[12,384]{1,0:T(8,128)} %ca.1) | copy-start | bytes 55300
  202.8 233.1 %copy-start.9 = (f32[4,1536]{1,0:T(4,128)S(1)}, f32[4,1536]{1,0:T(4,128)}, u32[]{:S(2)}) copy-start(f32[4,1536]{1,0:T(4,128)} %cf.1) | copy-start | bytes 73732
  202.9 233.1 %copy-start.11 = (f32[12,48]{1,0:T(8,128)S(1)}, f32[12,48]{1,0:T(8,128)}, u32[]{:S(2)}) copy-start(f32[12,48]{1,0:T(8,128)} %ra.1) | copy-start | bytes 6916
  202.9 233.1 %copy-start.12 = (f32[14,48]{1,0:T(8,128)S(1)}, f32[14,48]{1,0:T(8,128)}, u32[]{:S(2)}) copy-start(f32[14,48]{1,0:T(8,128)} %vm.1) | copy-start | bytes 8068
  202.9 233.1 %copy-start.13 = (f32[4,48]{1,0:T(4,128)S(1)}, f32[4,48]{1,0:T(4,128)}, u32[]{:S(2)}) copy-start(f32[4,48]{1,0:T(4,128)} %rf.1) | copy-start | bytes 2308
  435.9 1.1 copy-start.2
  437.0 1.1 copy-start.3
  438.1 1.0 copy-start.5
  439.0 1.0 copy-start.6
  440.0 1.0 copy-start.7
  441.0 0.7 copy-start.10
  441.7 20.2 %copy-start.14 = (bf16[512,768]{1,0:T(8,128)(2,1)S(1)}, bf16[512,768]{1,0:T(8,128)(2,1)}, u32[]{:S(2)}) copy-start(bf16[512,768]{1,0:T(8,128)(2,1)} %get-tuple-element.131) | copy-start | bytes 2359300
  461.8 1.4 copy-start.16
  461.9 2.3 copy-start.15

commit v7 on v6

--- a/solution.py
+++ b/solution.py
@@ -180,13 +180,21 @@
     return {axis: 1 - place(axis)}
 
 
-def greet():
+def greet_others():
     barrier = pltpu.get_barrier_semaphore()
     targets = [target_of(axis) for axis in ("c", "y", "z", "z_back", "x")]
     targets.append({"c": 1 - place("c"), "x": 1 - place("x")})
     for target in targets:
         pl.semaphore_signal(barrier, inc=1, device_id=target, device_id_type=MESH)
-    pl.semaphore_wait(barrier, len(targets))
+
+
+def greeted():
+    pl.semaphore_wait(pltpu.get_barrier_semaphore(), 6)
+
+
+def greet():
+    greet_others()
+    greeted()
 
 
 class Part:
@@ -269,9 +277,9 @@
 
 
 class Gather(Mover):
-    def __init__(self, own_ref, out_ref, stage_ref, local_sem, send_sems, recv_sems):
+    def __init__(self, own_ref, out_ref, stage_ref, local_sem, send_sems, recv_sems, first_column, columns):
         super().__init__(send_sems)
-        rows, columns = own_ref.shape
+        rows = own_ref.shape[0]
         cuts = gather_cuts(columns)
         (begin_a, end_a), (begin_b, end_b), (begin_c, end_c) = cuts
         first, second, third = 0, 1, 2
@@ -279,7 +287,7 @@
         def out_piece(group, which, parity):
             begin, end = cuts[group]
             first_row = (block_at(which) * 2 + parity()) * rows
-            return out_ref.at[pl.ds(first_row, rows), pl.ds(begin, end - begin)]
+            return out_ref.at[pl.ds(first_row, rows), pl.ds(first_column + begin, end - begin)]
 
         def out_sem(group, which, parity):
             return recv_sems.at[(group * 8 + block_at(which)) * 2 + parity()]
@@ -299,13 +307,17 @@
 
         self_copies = {
             True: lambda: pltpu.make_async_copy(
-                own_ref, out_ref.at[pl.ds((block_at(here(0)) * 2 + core()) * rows, rows), :], local_sem
+                own_ref.at[:, pl.ds(first_column, columns)],
+                out_ref.at[
+                    pl.ds((block_at(here(0)) * 2 + core()) * rows, rows), pl.ds(first_column, columns)
+                ],
+                local_sem,
             ),
         }
 
         def own_piece(group):
             begin, end = cuts[group]
-            return own_ref.at[:, pl.ds(begin, end - begin)]
+            return own_ref.at[:, pl.ds(first_column + begin, end - begin)]
 
         for home in (True, False):
             arrived = set()
@@ -1620,10 +1632,19 @@
     i = filled(names_in, refs[:count_in])
     o = filled(names_out, refs[count_in : count_in + count_out])
     (marks_row, flags_row, *rest) = refs[count_in + count_out :]
-    stages, rest = rest[:5], rest[5:]
+    stages, owns, rest = rest[:5], rest[5:10], rest[10:]
     sems, group_send, group_recv, group_local, in_send, in_recv, in_local, swap_sems = rest
     vec = i.vectors
-    greet()
+    greet_others()
+    for number in range(12):
+        width = i.attention.shape[2]
+        at = number % 4 * width
+        owns[number // 4][:, at : at + width] = i.attention[number].astype(low)
+    for number in range(4):
+        width = i.feed.shape[2]
+        at = number % 2 * width
+        owns[3 + number // 2][:, at : at + width] = i.feed[number].astype(low)
+    greeted()
 
     start = Inputs(Part(in_send, 0), Part(in_recv, 0), Part(in_local, 0))
     marks_here = start.swap(lambda: i.marks, lambda own: marks_row)
@@ -1651,10 +1672,17 @@
     source_there()
     closing = start.taken()
 
-    owns = (i.own_1, i.own_3, i.own_2, i.own_4, i.own_5)
-    alls = (o.all_1, o.all_3, o.all_2, o.all_4, o.all_5)
+    units = i.feed.shape[2]
     gathers = []
-    for number, (own, gathered) in enumerate(zip(owns, alls)):
+    for number, (own, gathered, first_column, columns) in enumerate(
+        (
+            (owns[0], o.all_1, 0, owns[0].shape[1]),
+            (owns[1], o.all_3, 0, owns[1].shape[1]),
+            (owns[3], o.all_2, 0, 2 * units),
+            (owns[2], o.all_4, 0, owns[2].shape[1]),
+            (owns[4], o.all_5, 0, 2 * units),
+        )
+    ):
         gathers.append(
             Gather(
                 own,
@@ -1663,6 +1691,8 @@
                 group_local.at[number],
                 Part(group_send, number * GATHER_SENDS),
                 Part(group_recv, number * 64),
+                first_column,
+                columns,
             )
         )
     first, second, last = gathers[0], gathers[1], gathers[4]
@@ -1681,9 +1711,8 @@
     target_mover, begin, rest = bring(i.target, o.target_all, 16, 8, 9)
     steps = spliced(second.steps, rest, shares_of(second.steps, 0.4))
     second.steps = {home: begin[home] + steps[home] for home in (True, False)}
-    cotangent_mover, begin, rest = bring(i.cotangent, o.cotangent_all, 24, 12, 13)
-    steps = spliced(last.steps, begin, shares_of(last.steps, 0.7))
-    last.steps = {home: steps[home] + rest[home] for home in (True, False)}
+    cotangent_mover, begin, late_steps = bring(i.cotangent, o.cotangent_all, 24, 12, 13)
+    last.steps = spliced(last.steps, begin, shares_of(last.steps, 0.95))
     stream = Stream()
     stream.movers += [start, target_mover, cotangent_mover]
     for number, mover in enumerate(gathers):
@@ -1782,6 +1811,7 @@
         [o.two, o.normed_5, o.hidden_5, o.slope_5, o.part_5],
         swaps=[(4, swaps[4])],
     )
+    stream.run(late_steps)
     o.marks_all[...] = marks_row[...]
     o.flags_all[...] = flags_row[...]
     swaps[4].arrive()
@@ -1810,14 +1840,12 @@
     return pltpu.SemaphoreType.DMA((count,))
 
 
-def forward_call(source, target, cotangent, marks, vectors, groups):
+def forward_call(source, target, cotangent, marks, vectors, attention, feed):
     depth = vectors.shape[1]
     rows, few = 2 * source.shape[0], 2 * target.shape[0]
-    block = groups[0].shape[0]
-    width, units = groups[0].shape[1] // 4, groups[1].shape[1] // 2
-    near_in = Bag(marks=marks, vectors=vectors)
+    block, width, units = attention.shape[1], attention.shape[2], feed.shape[2]
+    near_in = Bag(marks=marks, vectors=vectors, attention=attention, feed=feed)
     far_in = Bag(source=source, target=target, cotangent=cotangent)
-    far_in.own_1, far_in.own_2, far_in.own_3, far_in.own_4, far_in.own_5 = groups
     near_out = Bag(
         marks_all=jax.ShapeDtypeStruct(marks.shape, marks.dtype),
         flags_all=jax.ShapeDtypeStruct((1, rows), marks.dtype),
@@ -1841,14 +1869,14 @@
     f.normed_5, f.hidden_5, f.slope_5 = feed_kept(few, depth, units)
     f.part_1 = f.other_1 = f.part_2 = f.other_2 = shaped(rows, depth, low)
     f.part_3 = f.other_3 = f.part_4 = f.other_4 = f.part_5 = f.other_5 = shaped(few, depth, low)
-    f.all_1, f.all_2, f.all_3, f.all_4, f.all_5 = [
-        shaped(16 * block, group.shape[1], low) for group in groups
+    f.all_1 = f.all_3 = f.all_4 = shaped(16 * block, 4 * width, low)
+    f.all_2 = f.all_5 = shaped(16 * block, 2 * units, low)
+    ins, outs = near_in.joined(far_in), near_out.joined(far_out)
+    stage = [
+        pltpu.VMEM((8, block, gather_cuts(columns)[1][1]), low)
+        for columns in (4 * width, 4 * width, 2 * units, 4 * width, 2 * units)
     ]
-    ins, outs = near_in.joined(far_in), near_out.joined(far_out)
-    order = (0, 2, 1, 3, 4)
-    stage = [
-        pltpu.VMEM((8, block, gather_cuts(groups[number].shape[1])[1][1]), low) for number in order
-    ]
+    stage += [pltpu.VMEM((block, columns), low) for columns in [4 * width] * 3 + [2 * units] * 2]
     results = pl.pallas_call(
         functools.partial(forward_kernel, ins.names(), outs.names()),
         out_shape=tuple(outs.values()),
@@ -1859,9 +1887,9 @@
             pltpu.VMEM((1, rows), marks.dtype),
             *stage,
             dma(32),
-            dma(5 * GATHER_SENDS),
-            dma(5 * 64),
-            dma(5),
+            dma(6 * GATHER_SENDS),
+            dma(6 * 64),
+            dma(6),
             dma(32),
             dma(16),
             dma(18),
@@ -2166,10 +2194,20 @@
 
 
 def update_kernel(
-    f1, f2, f3, f4, f5, fv, aw, fw, ra, ca, rf, cf, vp, vl, vm,
+    f1_far, f2_far, f3_far, f4_far, f5_far, aw_far, fw_far, fv, ra, ca, rf, cf, vp, vl, vm,
     ag, fg, vg, au, fu, vu, ran, can, rfn, cfn, vmn, fng,
-    square, other_square, mine, theirs, line, line_in, send_sems, recv_sems,
+    f1, f2, f3, f4, f5, aw, fw, square, other_square, mine, theirs, line, line_in, send_sems, recv_sems, load_sems,
 ):
+    loads = [
+        pltpu.make_async_copy(source, target, load_sems.at[number])
+        for number, (source, target) in enumerate(
+            (
+                (f1_far, f1), (f2_far, f2), (f3_far, f3), (f4_far, f4), (f5_far, f5), (aw_far, aw), (fw_far, fw),
+            )
+        )
+    ]
+    for load in loads:
+        load.start()
     rows = f1.shape[0]
     depth = 16 * rows
     width, units = aw.shape[2], fw.shape[2]
@@ -2207,6 +2245,8 @@
     shifted = pltpu.roll(turned_vectors, 112, 1)
     vector_local, vector_scale = shifted[0:rows, :], shifted[rows : rows + 1, :]
 
+    for load in loads:
+        load.wait()
     lane = lax.broadcasted_iota(jnp.int32, (rows, 128), 1)
     one_lane = lax.broadcasted_iota(jnp.int32, (1, 128), 1)
     row_sums = jnp.zeros((rows, 128), wide)
@@ -2289,12 +2329,14 @@
         return jax.ShapeDtypeStruct(array.shape, wide)
 
     pair = jax.ShapeDtypeStruct((2, rows), wide)
+    far = [*finals[:5], aw, fw]
     return pl.pallas_call(
         update_kernel,
         out_shape=tuple(same(a) for a in (aw, fw, vm, aw, fw, vm, ra, ca, rf, cf, vm)) + (pair,),
-        in_specs=[whole()] * 15,
+        in_specs=[any_space()] * 7 + [whole()] * 8,
         out_specs=tuple([whole()] * 12),
-        scratch_shapes=[
+        scratch_shapes=[vmem_like(array) for array in far]
+        + [
             pltpu.VMEM((128, 128), wide),
             pltpu.VMEM((128, 128), wide),
             pltpu.VMEM((rows + 8, 128), wide),
@@ -2303,12 +2345,13 @@
             pltpu.VMEM((4, 1, columns + 128), wide),
             dma(5),
             dma(5),
+            dma(7),
         ],
         compiler_params=pltpu.CompilerParams(
-            collective_id=2, has_side_effects=True, vmem_limit_bytes=40 << 20
+            collective_id=2, has_side_effects=True, vmem_limit_bytes=60 << 20
         ),
         name="update",
-    )(*finals, aw, fw, ra, ca, rf, cf, vp, vl, vm)
+    )(*far, finals[5], ra, ca, rf, cf, vp, vl, vm)
 
 
 def fits_kernels():
@@ -2502,11 +2545,10 @@
         part = feed_weights[2 * index : 2 * index + 2].astype(low)
         return part.transpose(1, 0, 2).reshape(local_rows, 2 * half_units)
 
-    own_groups = [attention_group(0), feed_group(0), attention_group(1), attention_group(2), feed_group(1)]
     marks = jnp.concatenate([row_flags[0], source_mask[0], target_mask[0]])
     if fits_kernels():
         kept = forward_call(
-            source_embed[0], target_embed[0], out_cotangent[0], marks[None], vector_params, own_groups
+            source_embed[0], target_embed[0], out_cotangent[0], marks[None], vector_params, attention_weights, feed_weights
         )
         back = backward_call(kept, vector_params)
         decoder_out = back.decoder_out
@@ -2522,6 +2564,7 @@
             vector_params, vector_local, vector_moments,
         )
         return decoder_out[None], source_grad[None], target_grad[None], *updates
+    own_groups = [attention_group(0), feed_group(0), attention_group(1), attention_group(2), feed_group(1)]
     (
         decoder_out, source_grad, target_grad,
         encoder_grad, decoder_grad, cross_grad, encoder_feed_grad, decoder_feed_grad, vector_grad,

time: 482 us -> 481 us (level)
  local copies, waits for them, and re-layouts: 18.8 us -> 10.8 us
  Pallas kernels: 450 us -> 457 us
    unnamed x55 -> x45, local copies, waits for them, and re-layouts: 15.2 us -> 9.41 us
where the time goes in v7:
time: 481 us; the launch traced here: 472 us
  Pallas kernels  457 us (95%)
  local copies, waits for them, and re-layouts  10.8 us (2%)
    pallas_call x1, Pallas kernels, backward_call(): pl.pallas_call(functools.partial(backward_kernel, ins.names(), outs.names...  234 us
    pallas_call x1, Pallas kernels, forward_call(): pl.pallas_call(functools.partial(forward_kernel, ins.names(), outs.names(...  200 us
    pallas_call x1, Pallas kernels, update_call(): pl.pallas_call(update_kernel, out_shape=tuple((same(a) for a in (aw, fw,...  22.7 us

profile of v7, /device:TPU:0, one launch (start us, length us, event | category | flops | bytes accessed | tf_op | source)
XLA Modules:
  0.0 472.2 jit_solution(7049305649810163185)
XLA Ops:
  0.6 1.3 pad_add_fusion
  2.0 199.7 %forward_pass.1 = (s32[1,2048]{1,0:T(1,128)}, s32[1,1024]{1,0:T(1,128)}, bf16[1024,768]{1,0:T(8,128)(2,1)}, bf16[512,768]{1,0:T(8,128)(2,1)}, bf16[512,768]{1,0:...) custom-call(s32[1,2048]{1,0:T(1,128)} %bitcast.17, ...), custom_call_target="tpu_custom_call" | custom-call | tf_op jit(solution)/shard_map/forward_pass/pallas_call | solution.py:1880
  201.7 234.4 %backward_pass.1 = (f32[48,3072]{1,0:T(8,128)}, f32[48,1536]{1,0:T(8,128)}, f32[48,1536]{1,0:T(8,128)}, f32[48,3072]{1,0:T(8,128)}, f32[48,1536]{1,0:T(8,128)}, ...) custom-call(f32[14,768]{1,0:T(8,128)} %vp.1, ...), custom_call_target="tpu_custom_call" | custom-call | tf_op jit(solution)/shard_map/backward_pass/pallas_call | solution.py:2177
  436.0 1.4 constant_dynamic-slice_fusion.vl
  437.4 22.7 %update.1 = (f32[12,48,384]{2,1,0:T(8,128)}, f32[4,48,1536]{2,1,0:T(8,128)}, f32[14,48]{1,0:T(8,128)}, f32[12,48,384]{2,1,0:T(8,128)}, f32[4,48,1536]{2,1,0:T(8,...) custom-call(f32[48,1536]{1,0:T(8,128)} %get-tuple-element.133.f1_far, ...), custom_call_target="tpu_custom_call" | custom-call | tf_op jit(solution)/shard_map/update/pallas_call | solution.py:2333
  460.2 0.0 copy-start.6
  460.2 0.0 copy-done.13
  460.2 0.0 copy-done.4
  460.2 0.0 copy-start.5
  460.2 1.4 select_bitcast_fusion
  461.6 0.0 copy-done.6
  461.6 0.9 bitcast_convert_fusion
  462.5 0.0 copy-done.5
  462.5 0.7 copy.42
  463.3 0.0 copy-done.3
  463.3 0.9 copy.43
  464.2 0.0 copy-done.1
  464.2 1.0 copy.44
  465.2 0.0 copy-done.12
  465.2 0.6 copy.45
  465.8 0.0 copy-done.2
  465.8 0.9 copy.46
  466.7 0.0 copy-done
  466.8 1.0 copy.47
  467.8 0.6 copy.48
  468.4 0.6 copy.49
  469.0 0.6 copy.50
  469.6 0.0 copy-done.14
  469.6 0.6 copy.51
  470.2 0.6 copy.52
  470.8 0.6 copy.53
  471.4 0.6 copy.54
  (21 shorter events, 0.0 us)
Async XLA Ops:
  437.4 22.7 %copy-start.13 = (s32[1,512]{1,0:T(1,128)S(1)}, s32[1,512]{1,0:T(1,128)}, u32[]{:S(2)}) copy-start(s32[1,512]{1,0:T(1,128)} %param.17) | copy-start | bytes 6148
  437.4 22.7 %copy-start.4 = (bf16[512,768]{1,0:T(8,128)(2,1)S(1)}, bf16[512,768]{1,0:T(8,128)(2,1)}, u32[]{:S(2)}) copy-start(bf16[512,768]{1,0:T(8,128)(2,1)} %get-tuple-element.131) | copy-start | bytes 2359300
  460.2 1.4 copy-start.6
  460.2 2.3 copy-start.5
  461.6 1.7 copy-start.3
  462.5 1.7 copy-start.1
  464.2 1.0 copy-start.12
  464.2 1.6 copy-start.2
  464.2 2.5 copy-start
  466.7 1.1 copy-start.11
  466.7 1.7 copy-start.10
  466.7 2.3 copy-start.8
  466.7 2.9 copy-start.14
  466.8 3.4 copy-start.7
  466.8 4.0 copy-start.9
  466.8 4.6 copy-start.15
